TPU v7x, 32 devices: a whole 2x2x4 slice. The times are simulated.
32 devices in a mesh: groups: 2 (over y), tm: 4 (over z), param: 4 (over x, core).
Axes of the slice: x: 2, y: 2, z: 4, core: 2. Of those that a mesh axis runs over, the one named last changes fastest.
Arguments:
- design: float32 [3, 512, 40960], P(None, ('groups', 'tm'), 'param'), parts along dimension 1, may hold values from -0.03125 to 0.03125
- filter_taps: float32 [3, 512], replicated, may hold values from -0.25 to 0.25
- probes: float32 [40960, 256], P('param', ('groups', 'tm')), parts along dimension 1, may hold values from -6 to 6
Outputs:
- normal_product: float32 [40960, 256], P('param', ('groups', 'tm')), parts along dimension 1
There are 2 independent parts, one for each index of `groups`. A program takes and returns all parts, laid end to end along the dimension named above; an argument that names none is the same for every part. Nothing has to cross between parts.
All inputs are finite; a program needn't handle non-finite values.
Results may differ from a plain program's by a relative error of at most 0.000071.
Values sent between devices are 32-bit elements; how exact they have to be, the bound alone decides.
No kernel may reach another device: no remote copies, remote signals or barrier semaphores. Data moves between devices by JAX's collectives and lax.ppermute only.
A program may use at most 128 MiB of HBM per device.

v0:
```python
import math

import jax
import jax.numpy as jnp
import numpy as np
from jax import lax
from jax.sharding import PartitionSpec as P


def passed_along(value, axis, by):
    length = lax.axis_size(axis)
    pairs = [(i, i + by) for i in range(length) if 0 <= i + by < length]
    return lax.ppermute(value, axis, pairs)


def block_taps(filter_taps, epochs, block_total, forward):
    shape = (block_total, epochs, epochs)
    distance = lax.broadcasted_iota(jnp.int32, shape, 0)
    source = lax.broadcasted_iota(jnp.int32, shape, 1)
    target = lax.broadcasted_iota(jnp.int32, shape, 2)
    if forward:
        lag_index = distance * epochs + target - source
    else:
        lag_index = distance * epochs + source - target
    tap_count = filter_taps.shape[1]
    inside = (lag_index >= 0) & (lag_index < tap_count)
    values = jnp.take(filter_taps, jnp.clip(lag_index, 0, tap_count - 1), axis=1)
    return jnp.where(inside[None], values, 0.0)


def apply_blocks(stacked, matrices):
    return jnp.einsum("ckdbe,cdef->ckbf", stacked, matrices, precision=lax.Precision.HIGHEST)


def body(design, filter_taps, probes):
    highest = lax.Precision.HIGHEST
    components, epochs, coefficients = design.shape
    tap_count = filter_taps.shape[1]
    blocks_back = (tap_count - 1 + epochs - 1) // epochs
    block_total = blocks_back + 1
    block_width = math.gcd(coefficients, 512)
    block_count = coefficients // block_width
    forward_taps = block_taps(filter_taps, epochs, block_total, True)
    backward_taps = block_taps(filter_taps, epochs, block_total, False)
    columns = lax.all_gather(probes, "tm", axis=1, tiled=True)

    def accumulate(step_index, running):
        start = step_index * block_width
        design_block = lax.dynamic_slice_in_dim(design, start, block_width, 2)
        column_block = lax.dynamic_slice_in_dim(columns, start, block_width, 0)
        return running + jnp.einsum("ctp,pk->ckt", design_block, column_block, precision=highest)

    initial = jnp.zeros((components, columns.shape[1], epochs), jnp.float32)
    projected = lax.fori_loop(0, block_count, accumulate, initial)
    projected = lax.psum_scatter(projected, "param", scatter_dimension=1, tiled=True)
    probe_count = projected.shape[1]
    before = [passed_along(projected, "tm", distance) for distance in range(blocks_back, 0, -1)]
    extended = jnp.stack(before + [projected], axis=2)
    pick_forward = np.array([[blocks_back - d] for d in range(block_total)], np.int32)
    filtered = apply_blocks(extended[:, :, pick_forward], forward_taps)
    filtered = filtered.reshape(components, probe_count, epochs)
    trailing = [passed_along(filtered, "tm", -distance) for distance in range(1, blocks_back + 1)]
    extended = jnp.stack([filtered] + trailing, axis=2)
    weighted = apply_blocks(extended[:, :, :, None], backward_taps)
    weighted = weighted.reshape(components, probe_count, epochs)
    weighted = lax.all_gather(weighted, "param", axis=1, tiled=True)

    def block_product(step_index):
        design_block = lax.dynamic_slice_in_dim(design, step_index * block_width, block_width, 2)
        return jnp.einsum("ctp,ckt->pk", design_block, weighted, precision=highest)

    stacked = lax.map(block_product, jnp.arange(block_count, dtype=jnp.int32))
    partial_value = stacked.reshape(coefficients, weighted.shape[1])
    result = lax.psum_scatter(partial_value, "tm", scatter_dimension=1, tiled=True)
    return result


def solution(mesh):
    in_specs = (P(None, ("groups", "tm"), "param"), P(), P("param", ("groups", "tm")))
    out_specs = P("param", ("groups", "tm"))
    return jax.shard_map(body, mesh=mesh, in_specs=in_specs, out_specs=out_specs, check_vma=False)
```

profile of v0, /device:TPU:8, one launch (start us, length us, event | category | flops | bytes accessed | tf_op | source)
XLA Modules:
  0.0 657.7 jit_solution(4134613164685531167)
XLA Ops:
  7.7 97.6 %all-gather.2.cloned.1.call-done = f32[10240,128]{0,1:T(8,128)} async-done(((f32[10240,32]{0,1:T(8,128)}), f32[10240,128]{0,1:T(8,128)}) %all-gather.2.cloned.1.call-update) | async-done | bytes 5242896 | tf_op jit(solution)/shard_map/all_gather | solution.py:45
  105.4 32.3 %while.25 = (s32[]{:T(128)}, f32[3,128,64]{1,2,0:T(8,128)S(1)}, f32[10240,128]{0,1:T(8,128)}, f32[3,64,10240]{2,1,0:T(8,128)}, s32[]{:T(128)}, /*index=5*/s32[]{:T(128)}, s32[]{:T(128)}, s32[]{:T(128)}) while((s32[]{:T(128)}, f32[3,128,64]{1,2,0:T(8,128)S(1)}, f32[10240,128]{0,1:T(8,128)}, f32[3,64,10240]{2,1,0:T(8,128)}, ...), condition=%wide.region_1.2_spmd.clone, body=%wide.region_0.1_spmd.clone.sunk | while | flops 151044096 | bytes 853644 | solution.py:54
  140.4 31.4 %all-reduce.3.cloned.1.call-done = f32[3,128,64]{2,0,1:T(4,128)} async-done(((f32[3,128,64]{2,0,1:T(4,128)}), f32[3,128,64]{2,0,1:T(4,128)}) %all-reduce.3.cloned.1.call-update) | async-done | bytes 98320
  173.6 121.7 %gather_fusion.1 = f32[36864,3]{1,0:T(8,128)} fusion(f32[3,512]{0,1:T(8,128)S(1)} %copy.26, s32[36864]{0:T(1024)S(1)} %broadcast_clamp_fusion.1), kind=kCustom, calls=%fused_computation.clone | custom fusion | bytes 1032192 | tf_op jit(solution)/shard_map/jit(_take)/gather | solution.py:27
  295.3 11.0 %copy.27 = f32[9,64,64,3]{2,1,3,0:T(8,128)S(1)} copy(f32[9,64,64,3]{3,2,1,0:T(8,128)} %bitcast.74) | data formatting | bytes 884736 | tf_op jit(solution)/shard_map/jit(_take)/gather | solution.py:27
  307.1 4.9 collective-permute-start.2
  322.8 121.7 %gather_fusion.2 = f32[36864,3]{1,0:T(8,128)} fusion(f32[3,512]{0,1:T(8,128)S(1)} %copy.26, s32[36864]{0:T(1024)S(1)} %broadcast_clamp_fusion), kind=kCustom, calls=%fused_computation.1.clone | custom fusion | bytes 1032192 | tf_op jit(solution)/shard_map/jit(_take)/gather | solution.py:27
  444.5 11.0 %copy.30 = f32[9,64,64,3]{2,1,3,0:T(8,128)S(1)} copy(f32[9,64,64,3]{3,2,1,0:T(8,128)} %bitcast.73) | data formatting | bytes 884736 | tf_op jit(solution)/shard_map/jit(_take)/gather | solution.py:27
  458.2 4.2 collective-permute-done.5
  463.4 5.6 all_gather.7
  469.1 82.8 %while.24 = (s32[]{:T(128)}, f32[20,512,128]{2,1,0:T(8,128)}, s32[20]{0:T(128)S(1)}, f32[3,64,10240]{2,1,0:T(8,128)}, f32[3,128,64]{1,2,0:T(8,128)S(1)}, /*index=5*/s32[]{:T(128)}, s32[1]{0:T(128)}, s32[]{:T(128)}, s32[]{:T(128)}) while((s32[]{:T(128)}, f32[20,512,128]{2,1,0:T(8,128)}, s32[20]{0:T(128)S(1)}, f32[3,64,10240]{2,1,0:T(8,128)}, ...), condition=%wide.region_4.6_spmd, body=%wide.region_3.5_spmd.sunk | while | flops 150994944 | bytes 754331 | solution.py:72
  470.5 2.8 fusion.34
  474.6 2.8 fusion.34
  478.7 2.8 fusion.34
  482.9 2.8 fusion.34
  487.0 2.8 fusion.34
  491.2 2.8 fusion.34
  495.3 2.8 fusion.34
  499.4 2.8 fusion.34
  503.6 2.8 fusion.34
  507.7 2.8 fusion.34
  511.8 2.8 fusion.34
  520.1 2.8 fusion.34
  524.3 2.8 fusion.34
  528.4 2.8 fusion.34
  532.6 2.8 fusion.34
  536.7 2.8 fusion.34
  540.8 2.8 fusion.34
  545.0 2.8 fusion.34
  549.1 2.8 fusion.34
  551.9 5.9 copy.37
  557.8 93.4 %reduce-scatter.4.cloned.1.call-done = f32[32,10240]{1,0:T(8,128)} async-done(((f32[128,10240]{1,0:T(8,128)}), f32[32,10240]{1,0:T(8,128)}) %reduce-scatter.4.cloned.1.call-update) | async-done | bytes 1310736
  (103 shorter events, 67.6 us)
Async XLA Ops:
  6.5 132.5 %copy-start.2 = (u32[32]{0:T(128)S(1)}, u32[32]{0:T(128)}, u32[]{:S(2)}) copy-start(u32[32]{0:T(128)} %constant.76) | copy-start | bytes 388
  6.5 166.8 %copy-start.1 = (s32[9]{0:T(128)S(1)}, s32[9]{0:T(128)}, u32[]{:S(2)}) copy-start(s32[9]{0:T(128)} %constant.73) | copy-start | bytes 112
  6.5 166.9 %copy-start = (f32[3,512]{1,0:T(4,128)S(1)}, f32[3,512]{1,0:T(4,128)}, u32[]{:S(2)}) copy-start(f32[3,512]{1,0:T(4,128)} %param.12) | copy-start | bytes 18436
  6.5 98.8 %all-gather.2.cloned.1.call-start = ((), (), s32[]{:S(2)}) async-start(), calls=%async_computation.1 | async-start | bytes 6553600 | tf_op jit(solution)/shard_map/all_gather | solution.py:45
  7.3 164.6 %all-reduce.3.cloned.1.call-start = ((), (), s32[]{:S(2)}) async-start(), calls=%async_computation.3 | async-start | bytes 524288
  138.5 512.6 %reduce-scatter.4.cloned.1.call-start = ((), (), s32[]{:S(2)}) async-start(), calls=%async_computation.2 | async-start | bytes 6553600
  172.7 141.3 %collective-permute-start = (f32[3,32,64]{2,0,1:T(4,128)S(1)}, f32[3,32,64]{2,0,1:T(4,128)S(1)}, u32[]{:S(2)}, u32[]{:S(2)}) collective-permute-start(f32[3,32,64]{2,0,1:T(4,128)S(1)} %constant_dynamic-slice_fusion), channel_id=1, source_target_pairs={} | collective-permute-start | bytes 73736 | tf_op jit(solution)/shard_map/ppermute | solution.py:13
  306.4 7.7 %collective-permute-start.1 = (f32[3,32,64]{2,0,1:T(4,128)S(1)}, f32[3,32,64]{2,0,1:T(4,128)S(1)}, u32[]{:S(2)}, u32[]{:S(2)}) collective-permute-start(f32[3,32,64]{2,0,1:T(4,128)S(1)} %constant_dynamic-slice_fusion), channel_id=1, source_target_pairs={{0,12},{1,13},{2,14},{3,15},{16,28},{17,29},{18,30},{19,31}} | collective-permute-start | bytes 73736 | tf_op jit(solution)/shard_map/ppermute | solution.py:13
  307.1 8.4 %collective-permute-start.2 = (f32[3,32,64]{2,0,1:T(4,128)S(1)}, f32[3,32,64]{2,0,1:T(4,128)S(1)}, u32[]{:S(2)}, u32[]{:S(2)}) collective-permute-start(f32[3,32,64]{2,0,1:T(4,128)S(1)} %constant_dynamic-slice_fusion), channel_id=1, source_target_pairs={{0,8},{4,12},{1,9},{5,13},{2,10},{6,14},{3,11},{7,15},{16,24},{20,... | collective-permute-start | bytes 73736 | tf_op jit(solution)/shard_map/ppermute | solution.py:13
  312.0 6.2 collective-permute-start.3
  320.8 137.3 %collective-permute-start.4 = (f32[3,32,64]{2,1,0:T(8,128)S(1)}, f32[3,32,64]{2,1,0:T(8,128)S(1)}, u32[]{:S(2)}, u32[]{:S(2)}) collective-permute-start(f32[3,32,64]{2,1,0:T(8,128)S(1)} %bitcast.77), channel_id=1, source_target_pairs={{4,0},{8,4},{12,8},{5,1},{9,5},{13,9},{6,2},{10,6},{14,10},{7,3},{... | collective-permute-start | bytes 73736 | tf_op jit(solution)/shard_map/ppermute | solution.py:13
  455.5 6.9 %collective-permute-start.5 = (f32[3,32,64]{2,1,0:T(8,128)S(1)}, f32[3,32,64]{2,1,0:T(8,128)S(1)}, u32[]{:S(2)}, u32[]{:S(2)}) collective-permute-start(f32[3,32,64]{2,1,0:T(8,128)S(1)} %bitcast.78), channel_id=1, source_target_pairs={{8,0},{12,4},{9,1},{13,5},{10,2},{14,6},{11,3},{15,7},{24,16},{28,... | collective-permute-start | bytes 73736 | tf_op jit(solution)/shard_map/ppermute | solution.py:13
  456.8 5.6 collective-permute-start.6
  457.5 4.9 collective-permute-start.7
Sparse Core Ops, SparseCore 0:
  8.9 96.3 all-gather.1
  138.7 33.1 all-reduce.2
  557.9 93.2 reduce-scatter.3
where the time goes:
time: 661 us; the launch traced here: 658 us
  local copies, waits for them, and re-layouts  289 us (44%)
  waiting for transfers between devices  231 us (35%)
  matrix products  89 us (13%)
  loops' own time  14.6 us (2%)
  between operations  14.2 us (2%)
  starting transfers between devices  12.8 us (2%)
    gather x4, local copies, waits for them, and re-layouts, block_taps(): jnp.take(filter_taps, jnp.clip(lag_index, 0, tap_count - 1), axis=1)  265 us
    unnamed x5, waiting for transfers between devices  126 us
    all_gather x1, waiting for transfers between devices, body(): columns = lax.all_gather(probes, 'tm', axis=1, tiled=True)  97.6 us
    dot_general x20, matrix products, block_product(): return jnp.einsum('ctp,ckt->pk', design_block, weighted, precision=highest)  55.6 us
    dot_general x20, matrix products, accumulate(): jnp.einsum('ctp,pk->ckt', design_block, column_block, precision=highest)  31.7 us
    another operation x1, loops' own time, body(): stacked = lax.map(block_product, jnp.arange(block_count, dtype=jnp.int32))  14 us
  transfers between devices with their start and end apart: 11, of which 6 were waited for; matrix products, arithmetic and copies ran while one was open for 41% of the time, Pallas kernels for 0%

commit v1 on v0

v1 whole, which is shorter than its diff:
```python
import jax
import jax.numpy as jnp
from jax import lax
from jax.experimental import pallas as pl
from jax.experimental.pallas import tpu as pltpu
from jax.sharding import PartitionSpec as P

HIGHEST = lax.Precision.HIGHEST
HIGH = lax.Precision.HIGH


def normal_rows(filter_taps, block_index, epochs, total):
    components, tap_count = filter_taps.shape
    lanes = -(-(total + tap_count) // 128) * 128
    pad = jnp.zeros((components, lanes - tap_count), jnp.float32)
    ascending = jnp.concatenate([filter_taps, pad], axis=1)[:, None, :]
    descending = jnp.concatenate([filter_taps[:, ::-1], pad], axis=1)[:, None, :]

    def kernel(index_ref, ascending_ref, descending_ref, out_ref, forward_ref):
        rising = jnp.broadcast_to(ascending_ref[0], (epochs, lanes))
        falling = jnp.broadcast_to(descending_ref[0], (epochs, lanes))
        for block in range(total // epochs):
            shift = (block * epochs - (tap_count - 1)) % lanes
            rolled = pltpu.roll(falling, shift, 1, stride=1, stride_axis=0)
            forward_ref[block * epochs : (block + 1) * epochs, :] = rolled[:, :total]
        staggered = pltpu.roll(rising, 0, 1, stride=1, stride_axis=0)
        backward = pltpu.roll(staggered, index_ref[0] * epochs, 1)[:, :total]
        out_ref[0] = jnp.dot(backward, forward_ref[...], precision=HIGHEST, preferred_element_type=jnp.float32)

    return pl.pallas_call(
        kernel,
        grid_spec=pltpu.PrefetchScalarGridSpec(
            num_scalar_prefetch=1,
            grid=(components,),
            in_specs=[
                pl.BlockSpec((1, 1, lanes), lambda c, index: (c, 0, 0)),
                pl.BlockSpec((1, 1, lanes), lambda c, index: (c, 0, 0)),
            ],
            out_specs=pl.BlockSpec((1, epochs, total), lambda c, index: (c, 0, 0)),
            scratch_shapes=[pltpu.VMEM((total, total), jnp.float32)],
        ),
        out_shape=jax.ShapeDtypeStruct((components, epochs, total), jnp.float32),
        name="normal_rows",
    )(jnp.reshape(block_index, (1,)).astype(jnp.int32), ascending, descending)


def body(design, filter_taps, probes):
    components, epochs, coefficients = design.shape
    blocks = lax.axis_size("tm")
    total = blocks * epochs
    rows = normal_rows(filter_taps, lax.axis_index("tm"), epochs, total)
    columns = lax.all_gather(probes.T, "tm", axis=0, tiled=True)
    flat = design.reshape(components * epochs, coefficients)
    partial = lax.dot_general(flat, columns, (((1,), (1,)), ((), ())), precision=HIGH)
    shares = lax.all_gather(partial, "param", axis=0)
    projected = jnp.sum(shares, axis=0).reshape(components, epochs, -1)
    everything = lax.all_gather(projected, "tm", axis=1, tiled=True)
    weighted = jnp.einsum("cts,csk->ctk", rows, everything, precision=HIGHEST)
    weighted = weighted.reshape(components * epochs, -1)
    product = lax.dot_general(weighted, flat, (((0,), (0,)), ((), ())), precision=HIGH)
    result = lax.psum_scatter(product, "tm", scatter_dimension=0, tiled=True)
    return result.T


def solution(mesh):
    in_specs = (P(None, ("groups", "tm"), "param"), P(), P("param", ("groups", "tm")))
    out_specs = P("param", ("groups", "tm"))
    return jax.shard_map(body, mesh=mesh, in_specs=in_specs, out_specs=out_specs, check_vma=False)
```

time: 661 us -> 247 us (0.37)
  local copies, waits for them, and re-layouts: 289 us -> 3.53 us
  matrix products: 89 us -> 16.8 us
  waiting for transfers between devices: 231 us -> 187 us
  blocking collectives: 5.61 us -> 21.4 us
  loops' own time: 14.6 us -> 0 us
  starting transfers between devices: 12.8 us -> 0.04 us
    gather x5 -> x0, local copies, waits for them, and re-layouts: 266 us -> none  [the longest x4 265 us: block_taps(): jnp.take(filter_taps, jnp.clip(lag_index, 0, tap_count - 1), axis=1)]
    unnamed x5 -> x2, waiting for transfers between devices: 126 us -> 0.73 us
    reduce_scatter x0 -> x1, waiting for transfers between devices: none -> 95.1 us  [body(): result = lax.psum_scatter(product, 'tm', scatter_dimension=0, tiled=True)]
    dot_general x42 -> x3, matrix products: 89 us -> 16.8 us  [the longest x1 8.37 us: body(): lax.dot_general(weighted, flat, (((0,), (0,)), ((), ())), precision=HIGH)]
    all_gather x1 -> x2, blocking collectives: 5.61 us -> 21.4 us  [the longest x1 14.7 us: body(): everything = lax.all_gather(projected, 'tm', axis=1, tiled=True)]
    another operation x2 -> x0, loops' own time: 14.6 us -> none  [the longest x1 14 us: body(): stacked = lax.map(block_product, jnp.arange(block_count, dtype=jnp.int32))]
    dynamic_slice x20 -> x0, local copies, waits for them, and re-layouts: 13.2 us -> none  [body(): stacked = lax.map(block_product, jnp.arange(block_count, dtype=jnp.int32))]
    ppermute x8 -> x0, starting transfers between devices: 12.7 us -> none  [passed_along(): return lax.ppermute(value, axis, pairs)]
  transfers between devices with their start and end apart: 11 -> 2, of which waited for: 6 -> 2; matrix products, arithmetic and copies ran while one was open for 41% -> 1% of each run, Pallas kernels for 0% -> 1%
where the time goes in v1:
time: 247 us; the launch traced here: 245 us
  waiting for transfers between devices  187 us (76%)
  blocking collectives  21.4 us (9%)
  matrix products  16.8 us (7%)
  between operations  13.4 us (5%)
  local copies, waits for them, and re-layouts  3.53 us (1%)
  Pallas kernels  2.88 us (1%)
    reduce_scatter x1, waiting for transfers between devices, body(): result = lax.psum_scatter(product, 'tm', scatter_dimension=0, tiled=True)  95.1 us
    all_gather x1, waiting for transfers between devices, body(): columns = lax.all_gather(probes.T, 'tm', axis=0, tiled=True)  91.6 us
    all_gather x1, blocking collectives, body(): everything = lax.all_gather(projected, 'tm', axis=1, tiled=True)  14.7 us
    dot_general x1, matrix products, body(): lax.dot_general(weighted, flat, (((0,), (0,)), ((), ())), precision=HIGH)  8.37 us
    dot_general x1, matrix products, body(): lax.dot_general(flat, columns, (((1,), (1,)), ((), ())), precision=HIGH)  8.02 us
    all_gather x1, blocking collectives, body(): shares = lax.all_gather(partial, 'param', axis=0)  6.68 us
  transfers between devices with their start and end apart: 2, of which 2 were waited for; matrix products, arithmetic and copies ran while one was open for 1% of the time, Pallas kernels for 1%

profile of v1, /device:TPU:8, one launch (start us, length us, event | category | flops | bytes accessed | tf_op | source)
XLA Modules:
  0.0 245.5 jit_solution(9793061325811180782)
XLA Ops:
  6.5 0.0 all-gather.3.cloned.1.call-start
  6.5 0.7 all-gather.3.cloned.1.call-update
  7.3 0.0 reduce-scatter.2.cloned.1.call-start
  7.3 1.6 rev.3
  8.9 0.7 concatenate.6
  9.6 0.6 broadcast_in_dim.8.descending_ref
  10.2 0.6 broadcast_in_dim.7.ascending_ref
  10.8 2.9 %normal_rows.1 = f32[3,64,256]{2,1,0:T(8,128)} custom-call(s32[1]{0:T(128)} %bitcast.index_ref, f32[3,1,768]{2,1,0:T(1,128)} %broadcast_in_dim.7.ascending_ref, f32[3,1,768]{2,1,0:T(1,128)} %broadcast_in_dim.8.descending_ref), custom_call_target="tpu_custom_call" | custom-call | tf_op jit(solution)/shard_map/normal_rows/pallas_call | solution.py:30
  13.7 91.6 %all-gather.3.cloned.1.call-done = f32[128,10240]{1,0:T(8,128)} async-done(((f32[32,10240]{1,0:T(8,128)}), f32[128,10240]{1,0:T(8,128)}) %all-gather.3.cloned.1.call-update) | async-done | bytes 5242896 | tf_op jit(solution)/shard_map/all_gather | solution.py:52
  105.3 0.0 copy-start
  105.3 8.0 %fusion = f32[192,128]{1,0:T(8,128)S(1)} fusion(f32[192,10240]{1,0:T(8,128)} %bitcast.14, f32[128,10240]{1,0:T(8,128)} %all-gather.3.cloned.1.call-done), kind=kOutput, calls=%fused_computation.1 | convolution fusion | flops 1509949440 | bytes 13205504 | tf_op jit(solution)/shard_map/dot_general | solution.py:54
  113.4 6.7 %all-gather = f32[768,128]{1,0:T(8,128)S(1)} all-gather(f32[192,128]{1,0:T(8,128)S(1)} %fusion), channel_id=2, replica_groups=mesh['groups'=2,'tm'=4,'param'=4] {'param'}, dimensions={0}, use_global_device_ids=true | all-gather | bytes 491520 | tf_op jit(solution)/shard_map/all_gather | solution.py:55
  120.1 14.7 %all_gather.15 = f32[3,256,128]{2,1,0:T(8,128)S(1)} all-gather(f32[3,64,128]{2,1,0:T(8,128)S(1)} %bitcast.17), channel_id=1, replica_groups=mesh['groups'=2,'tm'=4,'param'=4] {'tm'}, dimensions={1}, use_global_device_ids=true | all-gather | bytes 491520 | tf_op jit(solution)/shard_map/all_gather | solution.py:57
  134.8 0.0 copy-done
  134.8 0.4 fusion.1
  135.1 8.4 %convolution_bitcast_fusion = f32[128,10240]{1,0:T(8,128)} fusion(f32[3,64,128]{2,1,0:T(8,128)S(1)} %fusion.1, f32[3,64,10240]{2,1,0:T(8,128)} %param.3), kind=kOutput, calls=%fused_computation | convolution fusion | flops 1509949440 | bytes 13205504 | tf_op jit(solution)/shard_map/dot_general | solution.py:60
  143.5 0.0 reduce-scatter.2.cloned.1.call-update
  143.5 95.1 %reduce-scatter.2.cloned.1.call-done = f32[32,10240]{1,0:T(8,128)} async-done(((f32[128,10240]{1,0:T(8,128)}), f32[32,10240]{1,0:T(8,128)}) %reduce-scatter.2.cloned.1.call-update) | async-done | bytes 1310736 | tf_op jit(solution)/shard_map/reduce_scatter | solution.py:61
  (2 shorter events, 0.0 us)
Async XLA Ops:
  6.5 98.8 %all-gather.3.cloned.1.call-start = ((), (), s32[]{:S(2)}) async-start(), calls=%async_computation.1 | async-start | bytes 6553600 | tf_op jit(solution)/shard_map/all_gather | solution.py:52
  7.3 231.4 %reduce-scatter.2.cloned.1.call-start = ((), (), s32[]{:S(2)}) async-start(), calls=%async_computation.2 | async-start | bytes 6553600 | tf_op jit(solution)/shard_map/reduce_scatter | solution.py:61
  105.3 29.4 %copy-start = (f32[3,64,256]{2,1,0:T(8,128)S(1)}, f32[3,64,256]{2,1,0:T(8,128)}, u32[]{:S(2)}) copy-start(f32[3,64,256]{2,1,0:T(8,128)} %normal_rows.1) | copy-start | bytes 589828
Sparse Core Ops, SparseCore 0:
  8.9 96.3 all-gather.2
  143.7 94.9 reduce-scatter.1

commit v2 on v1

--- a/solution.py
+++ b/solution.py
@@ -1,3 +1,5 @@
+import math
+
 import jax
 import jax.numpy as jnp
 from jax import lax
@@ -6,7 +8,23 @@
 from jax.sharding import PartitionSpec as P
 
 HIGHEST = lax.Precision.HIGHEST
-HIGH = lax.Precision.HIGH
+ALONG = (((1,), (1,)), ((), ()))
+ACROSS = (((1,), (0,)), ((), ()))
+
+
+def split(value):
+    high = value.astype(jnp.bfloat16)
+    return high, (value - high.astype(jnp.float32)).astype(jnp.bfloat16)
+
+
+def three_passes(left, right, dimensions):
+    left_high, left_low = split(left)
+    right_high, right_low = split(right)
+    height = left.shape[0]
+    both = jnp.concatenate([left_high, left_low], axis=0)
+    first = lax.dot_general(both, right_high, dimensions, preferred_element_type=jnp.float32)
+    last = lax.dot_general(left_high, right_low, dimensions, preferred_element_type=jnp.float32)
+    return first[:height] + (first[height:] + last)
 
 
 def normal_rows(filter_taps, block_index, epochs, total):
@@ -44,22 +62,158 @@
     )(jnp.reshape(block_index, (1,)).astype(jnp.int32), ascending, descending)
 
 
+def project(design, own, chunk, arrivals, shards):
+    components, epochs, coefficients = design.shape
+    samples = components * epochs
+    slots = len(arrivals) + 1
+    rows = arrivals[0][0].shape[0]
+    width = math.gcd(coefficients, 2048)
+    counts = [len(pieces) for pieces in arrivals]
+    pieces = [piece for group in arrivals for piece in group]
+
+    def kernel(shard_ref, design_ref, own_ref, *refs):
+        *piece_refs, out_ref = refs
+        values = [own_ref[...]]
+        start = 0
+        for count in counts:
+            value = piece_refs[start][...]
+            for ref in piece_refs[start + 1 : start + count]:
+                value = value + ref[...]
+            values.append(value)
+            start += count
+        block = design_ref[...].reshape(samples, width)
+        part = three_passes(jnp.concatenate(values, axis=0), block, ALONG)
+
+        @pl.when(pl.program_id(0) == 0)
+        def _():
+            out_ref[...] = jnp.zeros_like(out_ref)
+
+        for slot in range(slots):
+            out_ref[shard_ref[slot]] += part[slot * rows : (slot + 1) * rows]
+
+    return pl.pallas_call(
+        kernel,
+        grid_spec=pltpu.PrefetchScalarGridSpec(
+            num_scalar_prefetch=1,
+            grid=(coefficients // width,),
+            in_specs=[
+                pl.BlockSpec((components, epochs, width), lambda p, shard: (0, 0, p)),
+                pl.BlockSpec((rows, width), lambda p, shard: (chunk, p)),
+            ]
+            + [pl.BlockSpec((rows, width), lambda p, shard: (0, p)) for _ in pieces],
+            out_specs=pl.BlockSpec((slots, rows, samples), lambda p, shard: (0, 0, 0)),
+        ),
+        out_shape=jax.ShapeDtypeStruct((slots, rows, samples), jnp.float32),
+        name="project",
+    )(shards, design, own, *pieces)
+
+
+def multiply(design, taps, everything, shards):
+    components, epochs, coefficients = design.shape
+    samples = components * epochs
+    blocks, slots, rows, _ = everything.shape
+    width = math.gcd(coefficients, 2048)
+
+    def kernel(shard_ref, design_ref, taps_ref, everything_ref, *refs):
+        *out_refs, weighted_ref = refs
+
+        @pl.when(pl.program_id(0) == 0)
+        def _():
+            sums = [0.0] * components
+            for source in range(blocks):
+                block = everything_ref[source].reshape(slots * rows, samples)
+                for c in range(components):
+                    piece = block[:, c * epochs : (c + 1) * epochs]
+                    factor = taps_ref[c, :, source * epochs : (source + 1) * epochs]
+                    sums[c] = sums[c] + lax.dot_general(
+                        piece, factor, ALONG, precision=HIGHEST, preferred_element_type=jnp.float32
+                    )
+            weighted_ref[...] = jnp.concatenate(sums, axis=1).reshape(slots, rows, samples)
+
+        weighted = jnp.concatenate([weighted_ref[shard_ref[slot]] for slot in range(slots)], axis=0)
+        block = design_ref[...].reshape(samples, width)
+        product = three_passes(weighted, block, ACROSS)
+        for slot in range(slots):
+            out_refs[slot][...] = product[slot * rows : (slot + 1) * rows]
+
+    return pl.pallas_call(
+        kernel,
+        grid_spec=pltpu.PrefetchScalarGridSpec(
+            num_scalar_prefetch=1,
+            grid=(coefficients // width,),
+            in_specs=[
+                pl.BlockSpec((components, epochs, width), lambda p, shard: (0, 0, p)),
+                pl.BlockSpec(taps.shape, lambda p, shard: (0, 0, 0)),
+                pl.BlockSpec(everything.shape, lambda p, shard: (0, 0, 0, 0)),
+            ],
+            out_specs=[pl.BlockSpec((rows, width), lambda p, shard: (0, p)) for _ in range(slots)],
+            scratch_shapes=[pltpu.VMEM((slots, rows, samples), jnp.float32)],
+        ),
+        out_shape=[jax.ShapeDtypeStruct((rows, coefficients), jnp.float32) for _ in range(slots)],
+        name="multiply",
+    )(shards, design, taps, everything)
+
+
+def step_pairs(length, step, parity):
+    pairs = []
+    for low in range(parity, length - 1, 2):
+        if low - step + 1 >= 0:
+            pairs.append((low, low + 1))
+        if low + step < length:
+            pairs.append((low + 1, low))
+    return pairs
+
+
+def gather_along(value, length):
+    arrived = {(0, 0): value, (1, 0): value}
+    for step in range(1, length):
+        for parity in (0, 1):
+            pairs = step_pairs(length, step, parity)
+            source = arrived.get((1 - parity, step - 1))
+            if pairs:
+                arrived[parity, step] = lax.ppermute(source, "tm", pairs)
+    return [
+        [arrived[key] for key in ((0, slot), (1, length - slot)) if key in arrived] for slot in range(1, length)
+    ]
+
+
+def reduce_along(slots, length):
+    pending = {}
+    for step in range(length - 1, 0, -1):
+        for parity in (0, 1):
+            pairs = step_pairs(length, step, parity)
+            if pairs:
+                value = slots[step] if parity == 0 else slots[length - step]
+                if (1 - parity, step + 1) in pending:
+                    value = value + pending[1 - parity, step + 1]
+                pending[parity, step] = lax.ppermute(value, "tm", [(b, a) for a, b in pairs])
+    result = slots[0]
+    for parity in (0, 1):
+        if (parity, 1) in pending:
+            result = result + pending[parity, 1]
+    return result
+
+
 def body(design, filter_taps, probes):
     components, epochs, coefficients = design.shape
-    blocks = lax.axis_size("tm")
-    total = blocks * epochs
-    rows = normal_rows(filter_taps, lax.axis_index("tm"), epochs, total)
-    columns = lax.all_gather(probes.T, "tm", axis=0, tiled=True)
-    flat = design.reshape(components * epochs, coefficients)
-    partial = lax.dot_general(flat, columns, (((1,), (1,)), ((), ())), precision=HIGH)
-    shares = lax.all_gather(partial, "param", axis=0)
-    projected = jnp.sum(shares, axis=0).reshape(components, epochs, -1)
-    everything = lax.all_gather(projected, "tm", axis=1, tiled=True)
-    weighted = jnp.einsum("cts,csk->ctk", rows, everything, precision=HIGHEST)
-    weighted = weighted.reshape(components * epochs, -1)
-    product = lax.dot_general(weighted, flat, (((0,), (0,)), ((), ())), precision=HIGH)
-    result = lax.psum_scatter(product, "tm", scatter_dimension=0, tiled=True)
-    return result.T
+    length = lax.axis_size("tm")
+    place = lax.axis_index("tm")
+    own = probes.T
+    columns = own.shape[0]
+    chunks = 2 if columns % 16 == 0 else 1
+    rows = columns // chunks
+    direction = 1 - 2 * (place % 2)
+    shards = (place + direction * jnp.arange(length, dtype=jnp.int32)) % length
+    taps = normal_rows(filter_taps, place, epochs, length * epochs)
+    results = []
+    for chunk in range(chunks):
+        arrivals = gather_along(own[chunk * rows : (chunk + 1) * rows], length)
+        partial = project(design, own, chunk, arrivals, shards)
+        projected = jnp.sum(lax.all_gather(partial, "param", axis=0), axis=0)
+        everything = lax.all_gather(projected, "tm", axis=0)
+        slots = multiply(design, taps, everything, shards)
+        results.append(reduce_along(slots, length))
+    return jnp.concatenate(results, axis=0).T
 
 
 def solution(mesh):

time: 247 us -> 228 us (0.923)
  waiting for transfers between devices: 187 us -> 94.8 us
  starting transfers between devices: 0.04 us -> 40.5 us
  Pallas kernels: 2.88 us -> 36.6 us
  blocking collectives: 21.4 us -> 47.8 us
  matrix products: 16.8 us -> 0 us
  between operations: 13.4 us -> 0.36 us
    reduce_scatter x1 -> x0, waiting for transfers between devices: 95.1 us -> none  [body(): result = lax.psum_scatter(product, 'tm', scatter_dimension=0, tiled=True)]
    ppermute x0 -> x20, waiting for transfers between devices: none -> 94.8 us  [the longest x10 56.1 us: reduce_along(): lax.ppermute(value, 'tm', [(b, a) for a, b in pairs])]
    all_gather x1 -> x0, waiting for transfers between devices: 91.6 us -> none  [body(): columns = lax.all_gather(probes.T, 'tm', axis=0, tiled=True)]
    ppermute x0 -> x20, starting transfers between devices: none -> 40.5 us  [the longest x10 23.3 us: gather_along(): arrived[parity, step] = lax.ppermute(source, 'tm', pairs)]
    pallas_call x0 -> x4, Pallas kernels: none -> 33.8 us  [the longest x2 17.5 us: multiply(): pl.pallas_call(kernel, grid_spec=pltpu.PrefetchScalarGridSpec(num_scalar_...]
    all_gather x2 -> x4, blocking collectives: 21.4 us -> 47.8 us  [the longest x2 35.8 us: body(): everything = lax.all_gather(projected, 'tm', axis=0)]
    dot_general x3 -> x0, matrix products: 16.8 us -> none  [the longest x1 8.37 us: body(): lax.dot_general(weighted, flat, (((0,), (0,)), ((), ())), precision=HIGH)]
  transfers between devices with their start and end apart: 2 -> 20, of which waited for: 2 -> 10; matrix products, arithmetic and copies ran while one was open for 1% -> 1% of each run, Pallas kernels for 1% -> 16%
where the time goes in v2:
time: 228 us; the launch traced here: 226 us
  waiting for transfers between devices  94.8 us (42%)
  blocking collectives  47.8 us (21%)
  starting transfers between devices  40.5 us (18%)
  Pallas kernels  36.6 us (16%)
  local copies, waits for them, and re-layouts  3.84 us (2%)
  other arithmetic  2.3 us (1%)
    ppermute x10, waiting for transfers between devices, reduce_along(): lax.ppermute(value, 'tm', [(b, a) for a, b in pairs])  56.1 us
    ppermute x10, waiting for transfers between devices, gather_along(): arrived[parity, step] = lax.ppermute(source, 'tm', pairs)  38.7 us
    all_gather x2, blocking collectives, body(): everything = lax.all_gather(projected, 'tm', axis=0)  35.8 us
    ppermute x10, starting transfers between devices, gather_along(): arrived[parity, step] = lax.ppermute(source, 'tm', pairs)  23.3 us
    pallas_call x2, Pallas kernels, multiply(): pl.pallas_call(kernel, grid_spec=pltpu.PrefetchScalarGridSpec(num_scalar_...  17.5 us
    ppermute x10, starting transfers between devices, reduce_along(): lax.ppermute(value, 'tm', [(b, a) for a, b in pairs])  17.2 us
    pallas_call x2, Pallas kernels, project(): pl.pallas_call(kernel, grid_spec=pltpu.PrefetchScalarGridSpec(num_scalar_...  16.3 us
    all_gather x2, blocking collectives, body(): projected = jnp.sum(lax.all_gather(partial, 'param', axis=0), axis=0)  12 us
  transfers between devices with their start and end apart: 20, of which 10 were waited for; matrix products, arithmetic and copies ran while one was open for 1% of the time, Pallas kernels for 16%

profile of v2, /device:TPU:8, one launch (start us, length us, event | category | flops | bytes accessed | tf_op | source)
XLA Modules:
  0.0 226.3 jit_solution(12370042890137521975)
XLA Ops:
  0.0 2.2 fusion.1
  2.2 2.0 collective-permute-start
  4.2 3.5 %collective-permute-start.11 = (f32[16,10240]{1,0:T(8,128)S(1)}, f32[16,10240]{1,0:T(8,128)S(1)}, u32[]{:S(2)}, u32[]{:S(2)}) collective-permute-start(f32[16,10240]{1,0:T(8,128)S(1)} %get-tuple-element.22), channel_id=1, source_target_pairs={{4,8},{8,4},{5,9},{9,5},{6,10},{10,6},{7,11},{11,7},{20,24},{24,20... | collective-permute-start | bytes 1966088 | tf_op jit(solution)/shard_map/ppermute | solution.py:174
  7.7 12.1 %collective-permute-done.10.refs_0_ = f32[16,10240]{1,0:T(8,128)S(1)} collective-permute-done((f32[16,10240]{1,0:T(8,128)S(1)}, f32[16,10240]{1,0:T(8,128)S(1)}, u32[]{:S(2)}, u32[]{:S(2)}) %collective-permute-start.10) | collective-permute-done | bytes 655392 | tf_op jit(solution)/shard_map/ppermute | solution.py:174
  19.8 3.5 %collective-permute-start.13 = (f32[16,10240]{1,0:T(8,128)S(1)}, f32[16,10240]{1,0:T(8,128)}, u32[]{:S(2)}, u32[]{:S(2)}) collective-permute-start(f32[16,10240]{1,0:T(8,128)S(1)} %collective-permute-done.10.refs_0_), channel_id=1, source_target_pairs={{4,8},{8,4},{5,9},{9,5},{6,10},{10,6},{7,11},{11,7},{20,24},{24,20... | collective-permute-start | bytes 1966088 | tf_op jit(solution)/shard_map/ppermute | solution.py:174
  23.3 2.4 %collective-permute-start.1 = (f32[16,10240]{1,0:T(8,128)}, f32[16,10240]{1,0:T(8,128)S(1)}, u32[]{:S(2)}, u32[]{:S(2)}) collective-permute-start(f32[16,10240]{1,0:T(8,128)} %get-tuple-element.21), channel_id=1, source_target_pairs={{4,8},{8,4},{5,9},{9,5},{6,10},{10,6},{7,11},{11,7},{20,24},{24,20... | collective-permute-start | bytes 1966088 | tf_op jit(solution)/shard_map/ppermute | solution.py:174
  25.7 7.0 %collective-permute-done.refs_0_ = f32[16,10240]{1,0:T(8,128)S(1)} collective-permute-done((f32[16,10240]{1,0:T(8,128)}, f32[16,10240]{1,0:T(8,128)S(1)}, u32[]{:S(2)}, u32[]{:S(2)}) %collective-permute-start) | collective-permute-done | bytes 655392 | tf_op jit(solution)/shard_map/ppermute | solution.py:174
  32.7 3.5 %collective-permute-start.3 = (f32[16,10240]{1,0:T(8,128)S(1)}, f32[16,10240]{1,0:T(8,128)S(1)}, u32[]{:S(2)}, u32[]{:S(2)}) collective-permute-start(f32[16,10240]{1,0:T(8,128)S(1)} %collective-permute-done.refs_0_), channel_id=1, source_target_pairs={{4,8},{8,4},{5,9},{9,5},{6,10},{10,6},{7,11},{11,7},{20,24},{24,20... | collective-permute-start | bytes 1966088 | tf_op jit(solution)/shard_map/ppermute | solution.py:174
  36.2 2.2 collective-permute-start.12
  39.5 2.1 collective-permute-start.14
  43.7 9.7 %collective-permute-done.1.refs_4_ = f32[16,10240]{1,0:T(8,128)S(1)} collective-permute-done((f32[16,10240]{1,0:T(8,128)}, f32[16,10240]{1,0:T(8,128)S(1)}, u32[]{:S(2)}, u32[]{:S(2)}) %collective-permute-start.1) | collective-permute-done | bytes 655392 | tf_op jit(solution)/shard_map/ppermute | solution.py:174
  53.4 2.1 collective-permute-start.2
  55.6 8.7 %collective-permute-done.3.refs_2_ = f32[16,10240]{1,0:T(8,128)S(1)} collective-permute-done((f32[16,10240]{1,0:T(8,128)S(1)}, f32[16,10240]{1,0:T(8,128)S(1)}, u32[]{:S(2)}, u32[]{:S(2)}) %collective-permute-start.3) | collective-permute-done | bytes 655392 | tf_op jit(solution)/shard_map/ppermute | solution.py:174
  64.3 2.1 collective-permute-start.4
  66.4 2.9 %normal_rows.1.taps_ref = f32[3,64,256]{2,1,0:T(8,128)} custom-call(s32[1]{0:T(128)} %bitcast.index_ref, f32[3,1,768]{2,1,0:T(1,128)} %broadcast_in_dim.7.ascending_ref, f32[3,1,768]{2,1,0:T(1,128)} %broadcast_in_dim.8.descending_ref), custom_call_target="tpu_custom_call" | custom-call | tf_op jit(solution)/shard_map/normal_rows/pallas_call | solution.py:48
  69.3 8.1 %project.3 = f32[4,16,192]{2,1,0:T(8,128)} custom-call(s32[4]{0:T(128)} %and_select_fusion.shard_ref, f32[3,64,10240]{2,1,0:T(8,128)} %design_ref.7, f32[32,10240]{1,0:T(8,128)} %bitcast.9, f32[16,10240]{1,0:T(8,128)} %copy-done.3, f32[16,10240]{1,0:T(8,128)} %collective-permute-done.12.refs_1_, f32[16,10240]{1,0:T(8,128)} %collective-permute-done.13.refs_2_, ...), custom_call_target="tpu_custom_call" | custom-call | tf_op jit(solution)/shard_map/project/pallas_call | solution.py:94
  77.4 6.0 %all-gather.2 = f32[16,16,192]{2,1,0:T(8,128)S(1)} all-gather(f32[4,16,192]{2,1,0:T(8,128)} %project.3), channel_id=4, replica_groups=mesh['groups'=2,'tm'=4,'param'=4] {'param'}, dimensions={0}, use_global_device_ids=true | all-gather | bytes 245760 | tf_op jit(solution)/shard_map/all_gather | solution.py:212
  83.5 20.3 %all-gather.3 = f32[16,16,192]{2,1,0:T(8,128)} all-gather(f32[4,16,192]{2,1,0:T(8,128)S(1)} %reduce_sum.19), channel_id=5, replica_groups=mesh['groups'=2,'tm'=4,'param'=4] {'tm'}, dimensions={0}, use_global_device_ids=true | all-gather | bytes 245760 | tf_op jit(solution)/shard_map/all_gather | solution.py:213
  103.7 8.7 %multiply.3 = (f32[16,10240]{1,0:T(8,128)}, f32[16,10240]{1,0:T(8,128)}, f32[16,10240]{1,0:T(8,128)}, f32[16,10240]{1,0:T(8,128)}) custom-call(s32[4]{0:T(128)} %and_select_fusion.shard_ref, f32[3,64,10240]{2,1,0:T(8,128)} %design_ref.7, f32[3,64,256]{2,1,0:T(8,128)} %normal_rows.1.taps_ref, f32[4,4,16,192]{3,2,1,0:T(8,128)} %bitcast.12), custom_call_target="tpu_custom_call" | custom-call | tf_op jit(solution)/shard_map/multiply/pallas_call | solution.py:139
  113.7 8.1 %project.2 = f32[4,16,192]{2,1,0:T(8,128)} custom-call(s32[4]{0:T(128)} %and_select_fusion.shard_ref, f32[3,64,10240]{2,1,0:T(8,128)} %design_ref.7, f32[32,10240]{1,0:T(8,128)} %bitcast.10, f32[16,10240]{1,0:T(8,128)} %copy-done, f32[16,10240]{1,0:T(8,128)} %collective-permute-done.2.refs_1_, f32[16,10240]{1,0:T(8,128)} %copy-done.2, ...), custom_call_target="tpu_custom_call" | custom-call | tf_op jit(solution)/shard_map/project/pallas_call | solution.py:94
  121.8 6.0 %all-gather = f32[16,16,192]{2,1,0:T(8,128)S(1)} all-gather(f32[4,16,192]{2,1,0:T(8,128)} %project.2), channel_id=2, replica_groups=mesh['groups'=2,'tm'=4,'param'=4] {'param'}, dimensions={0}, use_global_device_ids=true | all-gather | bytes 245760 | tf_op jit(solution)/shard_map/all_gather | solution.py:212
  127.8 15.6 %all-gather.1 = f32[16,16,192]{2,1,0:T(8,128)} all-gather(f32[4,16,192]{2,1,0:T(8,128)S(1)} %reduce_sum.18), channel_id=3, replica_groups=mesh['groups'=2,'tm'=4,'param'=4] {'tm'}, dimensions={0}, use_global_device_ids=true | all-gather | bytes 245760 | tf_op jit(solution)/shard_map/all_gather | solution.py:213
  143.4 8.8 %multiply.2 = (f32[16,10240]{1,0:T(8,128)}, f32[16,10240]{1,0:T(8,128)}, f32[16,10240]{1,0:T(8,128)}, f32[16,10240]{1,0:T(8,128)}) custom-call(s32[4]{0:T(128)} %and_select_fusion.shard_ref, f32[3,64,10240]{2,1,0:T(8,128)} %design_ref.7, f32[3,64,256]{2,1,0:T(8,128)} %normal_rows.1.taps_ref, f32[4,4,16,192]{3,2,1,0:T(8,128)} %bitcast.11), custom_call_target="tpu_custom_call" | custom-call | tf_op jit(solution)/shard_map/multiply/pallas_call | solution.py:139
  155.1 2.9 %collective-permute-start.16 = (f32[16,10240]{1,0:T(8,128)S(1)}, f32[16,10240]{1,0:T(8,128)S(1)}, u32[]{:S(2)}, u32[]{:S(2)}) collective-permute-start(f32[16,10240]{1,0:T(8,128)S(1)} %add.59), channel_id=1, source_target_pairs={{8,4},{4,8},{9,5},{5,9},{10,6},{6,10},{11,7},{7,11},{24,20},{20,24... | collective-permute-start | bytes 1966088 | tf_op jit(solution)/shard_map/ppermute | solution.py:189
  159.3 12.8 %collective-permute-done.5 = f32[16,10240]{1,0:T(8,128)S(1)} collective-permute-done((f32[16,10240]{1,0:T(8,128)}, f32[16,10240]{1,0:T(8,128)S(1)}, u32[]{:S(2)}, u32[]{:S(2)}) %collective-permute-start.5) | collective-permute-done | bytes 655392 | tf_op jit(solution)/shard_map/ppermute | solution.py:189
  172.2 2.9 %collective-permute-start.6 = (f32[16,10240]{1,0:T(8,128)S(1)}, f32[16,10240]{1,0:T(8,128)S(1)}, u32[]{:S(2)}, u32[]{:S(2)}) collective-permute-start(f32[16,10240]{1,0:T(8,128)S(1)} %add.54), channel_id=1, source_target_pairs={{8,4},{4,8},{9,5},{5,9},{10,6},{6,10},{11,7},{7,11},{24,20},{20,24... | collective-permute-start | bytes 1966088 | tf_op jit(solution)/shard_map/ppermute | solution.py:189
  175.2 11.0 %collective-permute-done.18 = f32[16,10240]{1,0:T(8,128)S(1)} collective-permute-done((f32[16,10240]{1,0:T(8,128)S(1)}, f32[16,10240]{1,0:T(8,128)S(1)}, u32[]{:S(2)}, u32[]{:S(2)}) %collective-permute-start.18) | collective-permute-done | bytes 655392 | tf_op jit(solution)/shard_map/ppermute | solution.py:189
  186.2 2.9 %collective-permute-start.19 = (f32[16,10240]{1,0:T(8,128)S(1)}, f32[16,10240]{1,0:T(8,128)S(1)}, u32[]{:S(2)}, u32[]{:S(2)}) collective-permute-start(f32[16,10240]{1,0:T(8,128)S(1)} %add.62), channel_id=1, source_target_pairs={{8,4},{4,8},{9,5},{5,9},{10,6},{6,10},{11,7},{7,11},{24,20},{20,24... | collective-permute-start | bytes 1966088 | tf_op jit(solution)/shard_map/ppermute | solution.py:189
  189.4 10.8 %collective-permute-done.8 = f32[16,10240]{1,0:T(8,128)S(1)} collective-permute-done((f32[16,10240]{1,0:T(8,128)S(1)}, f32[16,10240]{1,0:T(8,128)S(1)}, u32[]{:S(2)}, u32[]{:S(2)}) %collective-permute-start.8) | collective-permute-done | bytes 655392 | tf_op jit(solution)/shard_map/ppermute | solution.py:189
  200.3 2.9 %collective-permute-start.9 = (f32[16,10240]{1,0:T(8,128)S(1)}, f32[16,10240]{1,0:T(8,128)S(1)}, u32[]{:S(2)}, u32[]{:S(2)}) collective-permute-start(f32[16,10240]{1,0:T(8,128)S(1)} %add.57), channel_id=1, source_target_pairs={{8,4},{4,8},{9,5},{5,9},{10,6},{6,10},{11,7},{7,11},{24,20},{20,24... | collective-permute-start | bytes 1966088 | tf_op jit(solution)/shard_map/ppermute | solution.py:189
  203.4 10.8 %collective-permute-done.17 = f32[16,10240]{1,0:T(8,128)S(1)} collective-permute-done((f32[16,10240]{1,0:T(8,128)S(1)}, f32[16,10240]{1,0:T(8,128)S(1)}, u32[]{:S(2)}, u32[]{:S(2)}) %collective-permute-start.17) | collective-permute-done | bytes 655392 | tf_op jit(solution)/shard_map/ppermute | solution.py:189
  214.4 10.6 %collective-permute-done.7 = f32[16,10240]{1,0:T(8,128)S(1)} collective-permute-done((f32[16,10240]{1,0:T(8,128)S(1)}, f32[16,10240]{1,0:T(8,128)S(1)}, u32[]{:S(2)}, u32[]{:S(2)}) %collective-permute-start.7) | collective-permute-done | bytes 655392 | tf_op jit(solution)/shard_map/ppermute | solution.py:189
  (63 shorter events, 10.5 us)
Async XLA Ops:
  0.0 41.6 %copy-start.13 = (f32[3,512]{1,0:T(4,128)S(1)}, f32[3,512]{1,0:T(4,128)}, u32[]{:S(2)}) copy-start(f32[3,512]{1,0:T(4,128)} %param.4) | copy-start | bytes 18436
  2.2 17.6 %collective-permute-start.10 = (f32[16,10240]{1,0:T(8,128)S(1)}, f32[16,10240]{1,0:T(8,128)S(1)}, u32[]{:S(2)}, u32[]{:S(2)}) collective-permute-start(f32[16,10240]{1,0:T(8,128)S(1)} %get-tuple-element.22), channel_id=1, source_target_pairs={{0,4},{4,0},{8,12},{12,8},{1,5},{5,1},{9,13},{13,9},{2,6},{6,2},{1... | collective-permute-start | bytes 1966088 | tf_op jit(solution)/shard_map/ppermute | solution.py:174
  2.2 30.5 %collective-permute-start = (f32[16,10240]{1,0:T(8,128)}, f32[16,10240]{1,0:T(8,128)S(1)}, u32[]{:S(2)}, u32[]{:S(2)}) collective-permute-start(f32[16,10240]{1,0:T(8,128)} %get-tuple-element.21), channel_id=1, source_target_pairs={{0,4},{4,0},{8,12},{12,8},{1,5},{5,1},{9,13},{13,9},{2,6},{6,2},{1... | collective-permute-start | bytes 1966088 | tf_op jit(solution)/shard_map/ppermute | solution.py:174
  4.2 32.0 %collective-permute-start.11 = (f32[16,10240]{1,0:T(8,128)S(1)}, f32[16,10240]{1,0:T(8,128)S(1)}, u32[]{:S(2)}, u32[]{:S(2)}) collective-permute-start(f32[16,10240]{1,0:T(8,128)S(1)} %get-tuple-element.22), channel_id=1, source_target_pairs={{4,8},{8,4},{5,9},{9,5},{6,10},{10,6},{7,11},{11,7},{20,24},{24,20... | collective-permute-start | bytes 1966088 | tf_op jit(solution)/shard_map/ppermute | solution.py:174
  19.8 49.4 %copy-start.3 = (f32[16,10240]{1,0:T(8,128)}, f32[16,10240]{1,0:T(8,128)S(1)}, u32[]{:S(2)}) copy-start(f32[16,10240]{1,0:T(8,128)S(1)} %collective-permute-done.10.refs_0_) | copy-start | bytes 1966084
  19.8 19.7 %collective-permute-start.13 = (f32[16,10240]{1,0:T(8,128)S(1)}, f32[16,10240]{1,0:T(8,128)}, u32[]{:S(2)}, u32[]{:S(2)}) collective-permute-start(f32[16,10240]{1,0:T(8,128)S(1)} %collective-permute-done.10.refs_0_), channel_id=1, source_target_pairs={{4,8},{8,4},{5,9},{9,5},{6,10},{10,6},{7,11},{11,7},{20,24},{24,20... | collective-permute-start | bytes 1966088 | tf_op jit(solution)/shard_map/ppermute | solution.py:174
  23.3 30.1 %collective-permute-start.1 = (f32[16,10240]{1,0:T(8,128)}, f32[16,10240]{1,0:T(8,128)S(1)}, u32[]{:S(2)}, u32[]{:S(2)}) collective-permute-start(f32[16,10240]{1,0:T(8,128)} %get-tuple-element.21), channel_id=1, source_target_pairs={{4,8},{8,4},{5,9},{9,5},{6,10},{10,6},{7,11},{11,7},{20,24},{24,20... | collective-permute-start | bytes 1966088 | tf_op jit(solution)/shard_map/ppermute | solution.py:174
  32.7 44.7 %copy-start = (f32[16,10240]{1,0:T(8,128)}, f32[16,10240]{1,0:T(8,128)S(1)}, u32[]{:S(2)}) copy-start(f32[16,10240]{1,0:T(8,128)S(1)} %collective-permute-done.refs_0_) | copy-start | bytes 1966084
  32.7 31.5 %collective-permute-start.3 = (f32[16,10240]{1,0:T(8,128)S(1)}, f32[16,10240]{1,0:T(8,128)S(1)}, u32[]{:S(2)}, u32[]{:S(2)}) collective-permute-start(f32[16,10240]{1,0:T(8,128)S(1)} %collective-permute-done.refs_0_), channel_id=1, source_target_pairs={{4,8},{8,4},{5,9},{9,5},{6,10},{10,6},{7,11},{11,7},{20,24},{24,20... | collective-permute-start | bytes 1966088 | tf_op jit(solution)/shard_map/ppermute | solution.py:174
  36.2 33.0 %copy-start.4 = (f32[16,10240]{1,0:T(8,128)}, f32[16,10240]{1,0:T(8,128)S(1)}, u32[]{:S(2)}) copy-start(f32[16,10240]{1,0:T(8,128)S(1)} %collective-permute-done.11.refs_4_) | copy-start | bytes 1966084
  36.2 33.0 %collective-permute-start.12 = (f32[16,10240]{1,0:T(8,128)S(1)}, f32[16,10240]{1,0:T(8,128)}, u32[]{:S(2)}, u32[]{:S(2)}) collective-permute-start(f32[16,10240]{1,0:T(8,128)S(1)} %collective-permute-done.11.refs_4_), channel_id=1, source_target_pairs={{4,0},{8,12},{5,1},{9,13},{6,2},{10,14},{7,3},{11,15},{20,16},{24,... | collective-permute-start | bytes 1966088 | tf_op jit(solution)/shard_map/ppermute | solution.py:174
  39.5 29.7 %collective-permute-start.14 = (f32[16,10240]{1,0:T(8,128)}, f32[16,10240]{1,0:T(8,128)}, u32[]{:S(2)}, u32[]{:S(2)}) collective-permute-start(f32[16,10240]{1,0:T(8,128)} %collective-permute-done.13.refs_2_), channel_id=1, source_target_pairs={{4,0},{8,12},{5,1},{9,13},{6,2},{10,14},{7,3},{11,15},{20,16},{24,... | collective-permute-start | bytes 1966088 | tf_op jit(solution)/shard_map/ppermute | solution.py:174
  53.4 24.0 %copy-start.1 = (f32[16,10240]{1,0:T(8,128)}, f32[16,10240]{1,0:T(8,128)S(1)}, u32[]{:S(2)}) copy-start(f32[16,10240]{1,0:T(8,128)S(1)} %collective-permute-done.1.refs_4_) | copy-start | bytes 1966084
  53.4 60.2 %collective-permute-start.2 = (f32[16,10240]{1,0:T(8,128)S(1)}, f32[16,10240]{1,0:T(8,128)}, u32[]{:S(2)}, u32[]{:S(2)}) collective-permute-start(f32[16,10240]{1,0:T(8,128)S(1)} %collective-permute-done.1.refs_4_), channel_id=1, source_target_pairs={{4,0},{8,12},{5,1},{9,13},{6,2},{10,14},{7,3},{11,15},{20,16},{24,... | collective-permute-start | bytes 1966088 | tf_op jit(solution)/shard_map/ppermute | solution.py:174
  64.3 13.1 %copy-start.2 = (f32[16,10240]{1,0:T(8,128)}, f32[16,10240]{1,0:T(8,128)S(1)}, u32[]{:S(2)}) copy-start(f32[16,10240]{1,0:T(8,128)S(1)} %collective-permute-done.3.refs_2_) | copy-start | bytes 1966084
  64.3 49.4 %collective-permute-start.4 = (f32[16,10240]{1,0:T(8,128)S(1)}, f32[16,10240]{1,0:T(8,128)}, u32[]{:S(2)}, u32[]{:S(2)}) collective-permute-start(f32[16,10240]{1,0:T(8,128)S(1)} %collective-permute-done.3.refs_2_), channel_id=1, source_target_pairs={{4,0},{8,12},{5,1},{9,13},{6,2},{10,14},{7,3},{11,15},{20,16},{24,... | collective-permute-start | bytes 1966088 | tf_op jit(solution)/shard_map/ppermute | solution.py:174
  112.4 42.6 %collective-permute-start.15 = (f32[16,10240]{1,0:T(8,128)}, f32[16,10240]{1,0:T(8,128)S(1)}, u32[]{:S(2)}, u32[]{:S(2)}) collective-permute-start(f32[16,10240]{1,0:T(8,128)} %get-tuple-element.20), channel_id=1, source_target_pairs={{0,4},{12,8},{1,5},{13,9},{2,6},{14,10},{3,7},{15,11},{16,20},{28,... | collective-permute-start | bytes 1966088 | tf_op jit(solution)/shard_map/ppermute | solution.py:189
  152.2 19.9 %collective-permute-start.5 = (f32[16,10240]{1,0:T(8,128)}, f32[16,10240]{1,0:T(8,128)S(1)}, u32[]{:S(2)}, u32[]{:S(2)}) collective-permute-start(f32[16,10240]{1,0:T(8,128)} %get-tuple-element.16), channel_id=1, source_target_pairs={{0,4},{12,8},{1,5},{13,9},{2,6},{14,10},{3,7},{15,11},{16,20},{28,... | collective-permute-start | bytes 1966088 | tf_op jit(solution)/shard_map/ppermute | solution.py:189
  153.7 32.5 %collective-permute-start.18 = (f32[16,10240]{1,0:T(8,128)S(1)}, f32[16,10240]{1,0:T(8,128)S(1)}, u32[]{:S(2)}, u32[]{:S(2)}) collective-permute-start(f32[16,10240]{1,0:T(8,128)S(1)} %copy-done.10), channel_id=1, source_target_pairs={{0,4},{12,8},{1,5},{13,9},{2,6},{14,10},{3,7},{15,11},{16,20},{28,... | collective-permute-start | bytes 1966088 | tf_op jit(solution)/shard_map/ppermute | solution.py:189
  155.0 31.1 %copy-start.9 = (f32[16,10240]{1,0:T(8,128)S(1)}, f32[16,10240]{1,0:T(8,128)}, u32[]{:S(2)}) copy-start(f32[16,10240]{1,0:T(8,128)} %get-tuple-element.20) | copy-start | bytes 1966084
  155.1 34.2 %collective-permute-start.16 = (f32[16,10240]{1,0:T(8,128)S(1)}, f32[16,10240]{1,0:T(8,128)S(1)}, u32[]{:S(2)}, u32[]{:S(2)}) collective-permute-start(f32[16,10240]{1,0:T(8,128)S(1)} %add.59), channel_id=1, source_target_pairs={{8,4},{4,8},{9,5},{5,9},{10,6},{6,10},{11,7},{7,11},{24,20},{20,24... | collective-permute-start | bytes 1966088 | tf_op jit(solution)/shard_map/ppermute | solution.py:189
  158.0 42.2 %collective-permute-start.8 = (f32[16,10240]{1,0:T(8,128)S(1)}, f32[16,10240]{1,0:T(8,128)S(1)}, u32[]{:S(2)}, u32[]{:S(2)}) collective-permute-start(f32[16,10240]{1,0:T(8,128)S(1)} %copy-done.12), channel_id=1, source_target_pairs={{0,4},{12,8},{1,5},{13,9},{2,6},{14,10},{3,7},{15,11},{16,20},{28,... | collective-permute-start | bytes 1966088 | tf_op jit(solution)/shard_map/ppermute | solution.py:189
  172.2 17.0 %copy-start.7 = (f32[16,10240]{1,0:T(8,128)S(1)}, f32[16,10240]{1,0:T(8,128)}, u32[]{:S(2)}) copy-start(f32[16,10240]{1,0:T(8,128)} %get-tuple-element.18) | copy-start | bytes 1966084
  172.2 31.0 %collective-permute-start.6 = (f32[16,10240]{1,0:T(8,128)S(1)}, f32[16,10240]{1,0:T(8,128)S(1)}, u32[]{:S(2)}, u32[]{:S(2)}) collective-permute-start(f32[16,10240]{1,0:T(8,128)S(1)} %add.54), channel_id=1, source_target_pairs={{8,4},{4,8},{9,5},{5,9},{10,6},{6,10},{11,7},{7,11},{24,20},{20,24... | collective-permute-start | bytes 1966088 | tf_op jit(solution)/shard_map/ppermute | solution.py:189
  186.2 14.0 %copy-start.11 = (f32[16,10240]{1,0:T(8,128)S(1)}, f32[16,10240]{1,0:T(8,128)}, u32[]{:S(2)}) copy-start(f32[16,10240]{1,0:T(8,128)} %get-tuple-element.16) | copy-start | bytes 1966084
  186.2 17.2 %collective-permute-start.19 = (f32[16,10240]{1,0:T(8,128)S(1)}, f32[16,10240]{1,0:T(8,128)S(1)}, u32[]{:S(2)}, u32[]{:S(2)}) collective-permute-start(f32[16,10240]{1,0:T(8,128)S(1)} %add.62), channel_id=1, source_target_pairs={{8,4},{4,8},{9,5},{5,9},{10,6},{6,10},{11,7},{7,11},{24,20},{20,24... | collective-permute-start | bytes 1966088 | tf_op jit(solution)/shard_map/ppermute | solution.py:189
  189.3 14.0 %copy-start.8 = (f32[16,10240]{1,0:T(8,128)S(1)}, f32[16,10240]{1,0:T(8,128)}, u32[]{:S(2)}) copy-start(f32[16,10240]{1,0:T(8,128)} %get-tuple-element.14) | copy-start | bytes 1966084
  189.3 24.9 %collective-permute-start.17 = (f32[16,10240]{1,0:T(8,128)S(1)}, f32[16,10240]{1,0:T(8,128)S(1)}, u32[]{:S(2)}, u32[]{:S(2)}) collective-permute-start(f32[16,10240]{1,0:T(8,128)S(1)} %add.60), channel_id=1, source_target_pairs={{4,0},{0,4},{12,8},{8,12},{5,1},{1,5},{13,9},{9,13},{6,2},{2,6},{1... | collective-permute-start | bytes 1966088 | tf_op jit(solution)/shard_map/ppermute | solution.py:189
  200.3 14.0 %copy-start.5 = (f32[16,10240]{1,0:T(8,128)S(1)}, f32[16,10240]{1,0:T(8,128)}, u32[]{:S(2)}) copy-start(f32[16,10240]{1,0:T(8,128)} %get-tuple-element.17) | copy-start | bytes 1966084
  200.3 14.1 %collective-permute-start.9 = (f32[16,10240]{1,0:T(8,128)S(1)}, f32[16,10240]{1,0:T(8,128)S(1)}, u32[]{:S(2)}, u32[]{:S(2)}) collective-permute-start(f32[16,10240]{1,0:T(8,128)S(1)} %add.57), channel_id=1, source_target_pairs={{8,4},{4,8},{9,5},{5,9},{10,6},{6,10},{11,7},{7,11},{24,20},{20,24... | collective-permute-start | bytes 1966088 | tf_op jit(solution)/shard_map/ppermute | solution.py:189
  203.3 21.7 %collective-permute-start.7 = (f32[16,10240]{1,0:T(8,128)S(1)}, f32[16,10240]{1,0:T(8,128)S(1)}, u32[]{:S(2)}, u32[]{:S(2)}) collective-permute-start(f32[16,10240]{1,0:T(8,128)S(1)} %add.55), channel_id=1, source_target_pairs={{4,0},{0,4},{12,8},{8,12},{5,1},{1,5},{13,9},{9,13},{6,2},{2,6},{1... | collective-permute-start | bytes 1966088 | tf_op jit(solution)/shard_map/ppermute | solution.py:189
  214.3 10.8 %copy-start.6 = (f32[16,10240]{1,0:T(8,128)S(1)}, f32[16,10240]{1,0:T(8,128)}, u32[]{:S(2)}) copy-start(f32[16,10240]{1,0:T(8,128)} %get-tuple-element.13) | copy-start | bytes 1966084
  (2 other events, 16.0 us)

commit v3 on v2

--- a/solution.py
+++ b/solution.py
@@ -17,14 +17,37 @@
     return high, (value - high.astype(jnp.float32)).astype(jnp.bfloat16)
 
 
-def three_passes(left, right, dimensions):
+def three_passes(left, right_high, right_low):
     left_high, left_low = split(left)
-    right_high, right_low = split(right)
     height = left.shape[0]
     both = jnp.concatenate([left_high, left_low], axis=0)
-    first = lax.dot_general(both, right_high, dimensions, preferred_element_type=jnp.float32)
-    last = lax.dot_general(left_high, right_low, dimensions, preferred_element_type=jnp.float32)
+    first = lax.dot_general(both, right_high, ACROSS, preferred_element_type=jnp.float32)
+    last = lax.dot_general(left_high, right_low, ACROSS, preferred_element_type=jnp.float32)
     return first[:height] + (first[height:] + last)
+
+
+def split_design(design):
+    components, epochs, coefficients = design.shape
+    samples = components * epochs
+    width = math.gcd(coefficients, 2048)
+
+    def kernel(design_ref, high_ref, low_ref, tall_high_ref, tall_low_ref):
+        block = design_ref[...].reshape(samples, width)
+        high_ref[...], low_ref[...] = split(block)
+        tall_high_ref[...], tall_low_ref[...] = split(block.T)
+
+    flat = jax.ShapeDtypeStruct((samples, coefficients), jnp.bfloat16)
+    tall = jax.ShapeDtypeStruct((coefficients, samples), jnp.bfloat16)
+    return pl.pallas_call(
+        kernel,
+        grid=(coefficients // width,),
+        in_specs=[pl.BlockSpec((components, epochs, width), lambda p: (0, 0, p))],
+        out_specs=[pl.BlockSpec((samples, width), lambda p: (0, p))] * 2
+        + [pl.BlockSpec((width, samples), lambda p: (p, 0))] * 2,
+        out_shape=[flat, flat, tall, tall],
+        compiler_params=pltpu.CompilerParams(vmem_limit_bytes=16 << 20),
+        name="split_design",
+    )(design)
 
 
 def normal_rows(filter_taps, block_index, epochs, total):
@@ -43,7 +66,9 @@
             forward_ref[block * epochs : (block + 1) * epochs, :] = rolled[:, :total]
         staggered = pltpu.roll(rising, 0, 1, stride=1, stride_axis=0)
         backward = pltpu.roll(staggered, index_ref[0] * epochs, 1)[:, :total]
-        out_ref[0] = jnp.dot(backward, forward_ref[...], precision=HIGHEST, preferred_element_type=jnp.float32)
+        rows = jnp.dot(backward, forward_ref[...], precision=HIGHEST, preferred_element_type=jnp.float32)
+        for block in range(total // epochs):
+            out_ref[block, 0] = rows[:, block * epochs : (block + 1) * epochs]
 
     return pl.pallas_call(
         kernel,
@@ -54,24 +79,24 @@
                 pl.BlockSpec((1, 1, lanes), lambda c, index: (c, 0, 0)),
                 pl.BlockSpec((1, 1, lanes), lambda c, index: (c, 0, 0)),
             ],
-            out_specs=pl.BlockSpec((1, epochs, total), lambda c, index: (c, 0, 0)),
+            out_specs=pl.BlockSpec((total // epochs, 1, epochs, epochs), lambda c, index: (0, c, 0, 0)),
             scratch_shapes=[pltpu.VMEM((total, total), jnp.float32)],
         ),
-        out_shape=jax.ShapeDtypeStruct((components, epochs, total), jnp.float32),
+        out_shape=jax.ShapeDtypeStruct((total // epochs, components, epochs, epochs), jnp.float32),
+        compiler_params=pltpu.CompilerParams(vmem_limit_bytes=(4 << 20) + 4 * total * total),
         name="normal_rows",
     )(jnp.reshape(block_index, (1,)).astype(jnp.int32), ascending, descending)
 
 
-def project(design, own, chunk, arrivals, shards):
-    components, epochs, coefficients = design.shape
-    samples = components * epochs
+def project(tall_high, tall_low, own, chunk, arrivals, shards):
+    coefficients, samples = tall_high.shape
     slots = len(arrivals) + 1
     rows = arrivals[0][0].shape[0]
-    width = math.gcd(coefficients, 2048)
+    width = math.gcd(coefficients, 5120)
     counts = [len(pieces) for pieces in arrivals]
     pieces = [piece for group in arrivals for piece in group]
 
-    def kernel(shard_ref, design_ref, own_ref, *refs):
+    def kernel(shard_ref, high_ref, low_ref, own_ref, *refs):
         *piece_refs, out_ref = refs
         values = [own_ref[...]]
         start = 0
@@ -81,8 +106,7 @@
                 value = value + ref[...]
             values.append(value)
             start += count
-        block = design_ref[...].reshape(samples, width)
-        part = three_passes(jnp.concatenate(values, axis=0), block, ALONG)
+        part = three_passes(jnp.concatenate(values, axis=0), high_ref[...], low_ref[...])
 
         @pl.when(pl.program_id(0) == 0)
         def _():
@@ -97,61 +121,67 @@
             num_scalar_prefetch=1,
             grid=(coefficients // width,),
             in_specs=[
-                pl.BlockSpec((components, epochs, width), lambda p, shard: (0, 0, p)),
+                pl.BlockSpec((width, samples), lambda p, shard: (p, 0)),
+                pl.BlockSpec((width, samples), lambda p, shard: (p, 0)),
                 pl.BlockSpec((rows, width), lambda p, shard: (chunk, p)),
             ]
             + [pl.BlockSpec((rows, width), lambda p, shard: (0, p)) for _ in pieces],
             out_specs=pl.BlockSpec((slots, rows, samples), lambda p, shard: (0, 0, 0)),
         ),
         out_shape=jax.ShapeDtypeStruct((slots, rows, samples), jnp.float32),
+        compiler_params=pltpu.CompilerParams(vmem_limit_bytes=24 << 20),
         name="project",
-    )(shards, design, own, *pieces)
-
-
-def multiply(design, taps, everything, shards):
-    components, epochs, coefficients = design.shape
-    samples = components * epochs
-    blocks, slots, rows, _ = everything.shape
-    width = math.gcd(coefficients, 2048)
-
-    def kernel(shard_ref, design_ref, taps_ref, everything_ref, *refs):
-        *out_refs, weighted_ref = refs
+    )(shards, tall_high, tall_low, own, *pieces)
+
+
+def multiply(high, low, taps, blocks, places, shards):
+    samples, coefficients = high.shape
+    _, components, epochs, _ = taps.shape
+    slots, rows, _ = blocks[0].shape
+    width = math.gcd(coefficients, 5120)
+    count = len(blocks)
+
+    def kernel(shard_ref, place_ref, high_ref, low_ref, taps_ref, *refs):
+        block_refs = refs[:count]
+        out_refs = refs[count:-1]
+        weighted_ref = refs[-1]
 
         @pl.when(pl.program_id(0) == 0)
         def _():
             sums = [0.0] * components
-            for source in range(blocks):
-                block = everything_ref[source].reshape(slots * rows, samples)
+            for source in range(count):
+                block = block_refs[source][...].reshape(slots * rows, samples)
                 for c in range(components):
                     piece = block[:, c * epochs : (c + 1) * epochs]
-                    factor = taps_ref[c, :, source * epochs : (source + 1) * epochs]
+                    factor = taps_ref[place_ref[source], c]
                     sums[c] = sums[c] + lax.dot_general(
                         piece, factor, ALONG, precision=HIGHEST, preferred_element_type=jnp.float32
                     )
             weighted_ref[...] = jnp.concatenate(sums, axis=1).reshape(slots, rows, samples)
 
         weighted = jnp.concatenate([weighted_ref[shard_ref[slot]] for slot in range(slots)], axis=0)
-        block = design_ref[...].reshape(samples, width)
-        product = three_passes(weighted, block, ACROSS)
+        product = three_passes(weighted, high_ref[...], low_ref[...])
         for slot in range(slots):
             out_refs[slot][...] = product[slot * rows : (slot + 1) * rows]
 
     return pl.pallas_call(
         kernel,
         grid_spec=pltpu.PrefetchScalarGridSpec(
-            num_scalar_prefetch=1,
+            num_scalar_prefetch=2,
             grid=(coefficients // width,),
             in_specs=[
-                pl.BlockSpec((components, epochs, width), lambda p, shard: (0, 0, p)),
-                pl.BlockSpec(taps.shape, lambda p, shard: (0, 0, 0)),
-                pl.BlockSpec(everything.shape, lambda p, shard: (0, 0, 0, 0)),
-            ],
-            out_specs=[pl.BlockSpec((rows, width), lambda p, shard: (0, p)) for _ in range(slots)],
+                pl.BlockSpec((samples, width), lambda p, shard, place: (0, p)),
+                pl.BlockSpec((samples, width), lambda p, shard, place: (0, p)),
+                pl.BlockSpec(taps.shape, lambda p, shard, place: (0, 0, 0, 0)),
+            ]
+            + [pl.BlockSpec((slots, rows, samples), lambda p, shard, place: (0, 0, 0)) for _ in blocks],
+            out_specs=[pl.BlockSpec((rows, width), lambda p, shard, place: (0, p)) for _ in range(slots)],
             scratch_shapes=[pltpu.VMEM((slots, rows, samples), jnp.float32)],
         ),
         out_shape=[jax.ShapeDtypeStruct((rows, coefficients), jnp.float32) for _ in range(slots)],
+        compiler_params=pltpu.CompilerParams(vmem_limit_bytes=24 << 20),
         name="multiply",
-    )(shards, design, taps, everything)
+    )(shards, places, high, low, taps, *blocks)
 
 
 def step_pairs(length, step, parity):
@@ -194,6 +224,14 @@
     return result
 
 
+def exchange(value, length):
+    if length <= 8 and length & (length - 1) == 0:
+        others = [lax.ppermute(value, "tm", [(i, i ^ by) for i in range(length)]) for by in range(1, length)]
+        return [value] + others, lax.axis_index("tm") ^ jnp.arange(length, dtype=jnp.int32)
+    gathered = lax.all_gather(value, "tm", axis=0)
+    return [gathered[i] for i in range(length)], jnp.arange(length, dtype=jnp.int32)
+
+
 def body(design, filter_taps, probes):
     components, epochs, coefficients = design.shape
     length = lax.axis_size("tm")
@@ -205,13 +243,14 @@
     direction = 1 - 2 * (place % 2)
     shards = (place + direction * jnp.arange(length, dtype=jnp.int32)) % length
     taps = normal_rows(filter_taps, place, epochs, length * epochs)
+    high, low, tall_high, tall_low = split_design(design)
     results = []
     for chunk in range(chunks):
         arrivals = gather_along(own[chunk * rows : (chunk + 1) * rows], length)
-        partial = project(design, own, chunk, arrivals, shards)
+        partial = project(tall_high, tall_low, own, chunk, arrivals, shards)
         projected = jnp.sum(lax.all_gather(partial, "param", axis=0), axis=0)
-        everything = lax.all_gather(projected, "tm", axis=0)
-        slots = multiply(design, taps, everything, shards)
+        blocks, places = exchange(projected, length)
+        slots = multiply(high, low, taps, blocks, places, shards)
         results.append(reduce_along(slots, length))
     return jnp.concatenate(results, axis=0).T
 

time: 228 us -> 217 us (0.952)
  blocking collectives: 47.8 us -> 11.7 us
  local copies, waits for them, and re-layouts: 3.84 us -> 20.5 us
  Pallas kernels: 36.6 us -> 21.6 us
  starting transfers between devices: 40.5 us -> 53 us
  waiting for transfers between devices: 94.8 us -> 105 us
    all_gather x2 -> x0, blocking collectives: 35.8 us -> none  [body(): everything = lax.all_gather(projected, 'tm', axis=0)]
    ppermute x0 -> x6, waiting for transfers between devices: none -> 20.8 us  [exchange(): lax.ppermute(value, 'tm', [(i, i ^ by) for i in range(length)])]
    unnamed x28 -> x42, local copies, waits for them, and re-layouts: 0.06 us -> 17.9 us
    ppermute x0 -> x6, starting transfers between devices: none -> 9.52 us  [exchange(): lax.ppermute(value, 'tm', [(i, i ^ by) for i in range(length)])]
    pallas_call x2, Pallas kernels: 17.5 us -> 8.13 us  [multiply(): pl.pallas_call(kernel, grid_spec=pltpu.PrefetchScalarGridSpec(num_scalar_...]
    pallas_call x2, Pallas kernels: 16.3 us -> 7.64 us  [project(): pl.pallas_call(kernel, grid_spec=pltpu.PrefetchScalarGridSpec(num_scalar_...]
    ppermute x10, waiting for transfers between devices: 38.7 us -> 30.4 us  [gather_along(): arrived[parity, step] = lax.ppermute(source, 'tm', pairs)]
    pallas_call x0 -> x1, Pallas kernels: none -> 4.26 us  [split_design(): pl.pallas_call(kernel, grid=(coefficients // width,), in_specs=[pl.BlockS...]
  transfers between devices with their start and end apart: 20 -> 26, of which waited for: 10 -> 17; matrix products, arithmetic and copies ran while one was open for 1% -> 1% of each run, Pallas kernels for 16% -> 10%
where the time goes in v3:
time: 217 us; the launch traced here: 216 us
  waiting for transfers between devices  105 us (48%)
  starting transfers between devices  53 us (24%)
  Pallas kernels  21.6 us (10%)
  local copies, waits for them, and re-layouts  20.5 us (9%)
  blocking collectives  11.7 us (5%)
  other arithmetic  4.11 us (2%)
    ppermute x10, waiting for transfers between devices, reduce_along(): lax.ppermute(value, 'tm', [(b, a) for a, b in pairs])  53.4 us
    ppermute x10, waiting for transfers between devices, gather_along(): arrived[parity, step] = lax.ppermute(source, 'tm', pairs)  30.4 us
    ppermute x10, starting transfers between devices, gather_along(): arrived[parity, step] = lax.ppermute(source, 'tm', pairs)  24.1 us
    ppermute x6, waiting for transfers between devices, exchange(): lax.ppermute(value, 'tm', [(i, i ^ by) for i in range(length)])  20.8 us
    ppermute x10, starting transfers between devices, reduce_along(): lax.ppermute(value, 'tm', [(b, a) for a, b in pairs])  19.4 us
    unnamed x42, local copies, waits for them, and re-layouts  17.9 us
    all_gather x2, blocking collectives, body(): projected = jnp.sum(lax.all_gather(partial, 'param', axis=0), axis=0)  11.7 us
    ppermute x6, starting transfers between devices, exchange(): lax.ppermute(value, 'tm', [(i, i ^ by) for i in range(length)])  9.52 us
  transfers between devices with their start and end apart: 26, of which 17 were waited for; matrix products, arithmetic and copies ran while one was open for 1% of the time, Pallas kernels for 10%

profile of v3, /device:TPU:8, one launch (start us, length us, event | category | flops | bytes accessed | tf_op | source)
XLA Modules:
  0.0 215.8 jit_solution(13091492744816821984)
XLA Ops:
  4.2 3.5 %collective-permute-start.1 = (f32[16,10240]{1,0:T(8,128)S(1)}, f32[16,10240]{1,0:T(8,128)}, u32[]{:S(2)}, u32[]{:S(2)}) collective-permute-start(f32[16,10240]{1,0:T(8,128)S(1)} %get-tuple-element.29), channel_id=1, source_target_pairs={{4,8},{8,4},{5,9},{9,5},{6,10},{10,6},{7,11},{11,7},{20,24},{24,20... | collective-permute-start | bytes 1966088 | tf_op jit(solution)/shard_map/ppermute | solution.py:204
  7.7 12.1 %collective-permute-done.refs_0_ = f32[16,10240]{1,0:T(8,128)S(1)} collective-permute-done((f32[16,10240]{1,0:T(8,128)S(1)}, f32[16,10240]{1,0:T(8,128)S(1)}, u32[]{:S(2)}, u32[]{:S(2)}) %collective-permute-start) | collective-permute-done | bytes 655392 | tf_op jit(solution)/shard_map/ppermute | solution.py:204
  19.8 3.5 %collective-permute-start.3 = (f32[16,10240]{1,0:T(8,128)S(1)}, f32[16,10240]{1,0:T(8,128)}, u32[]{:S(2)}, u32[]{:S(2)}) collective-permute-start(f32[16,10240]{1,0:T(8,128)S(1)} %collective-permute-done.refs_0_), channel_id=1, source_target_pairs={{4,8},{8,4},{5,9},{9,5},{6,10},{10,6},{7,11},{11,7},{20,24},{24,20... | collective-permute-start | bytes 1966088 | tf_op jit(solution)/shard_map/ppermute | solution.py:204
  24.2 2.3 %collective-permute-start.14 = (f32[16,10240]{1,0:T(8,128)}, f32[16,10240]{1,0:T(8,128)S(1)}, u32[]{:S(2)}, u32[]{:S(2)}) collective-permute-start(f32[16,10240]{1,0:T(8,128)} %get-tuple-element.30), channel_id=1, source_target_pairs={{4,8},{8,4},{5,9},{9,5},{6,10},{10,6},{7,11},{11,7},{20,24},{24,20... | collective-permute-start | bytes 1966088 | tf_op jit(solution)/shard_map/ppermute | solution.py:204
  26.5 6.2 %collective-permute-done.13.refs_0_ = f32[16,10240]{1,0:T(8,128)S(1)} collective-permute-done((f32[16,10240]{1,0:T(8,128)}, f32[16,10240]{1,0:T(8,128)S(1)}, u32[]{:S(2)}, u32[]{:S(2)}) %collective-permute-start.13) | collective-permute-done | bytes 655392 | tf_op jit(solution)/shard_map/ppermute | solution.py:204
  32.7 3.5 %collective-permute-start.16 = (f32[16,10240]{1,0:T(8,128)S(1)}, f32[16,10240]{1,0:T(8,128)}, u32[]{:S(2)}, u32[]{:S(2)}) collective-permute-start(f32[16,10240]{1,0:T(8,128)S(1)} %collective-permute-done.13.refs_0_), channel_id=1, source_target_pairs={{4,8},{8,4},{5,9},{9,5},{6,10},{10,6},{7,11},{11,7},{20,24},{24,20... | collective-permute-start | bytes 1966088 | tf_op jit(solution)/shard_map/ppermute | solution.py:204
  41.6 3.2 %copy-done.11 = f32[3,64,10240]{2,1,0:T(8,128)S(1)} copy-done((f32[3,64,10240]{2,1,0:T(8,128)S(1)}, f32[3,64,10240]{2,1,0:T(8,128)}, u32[]{:S(2)}) %copy-start.11) | copy-done | bytes 7864344
  44.9 4.3 %split_design.1 = (bf16[192,10240]{1,0:T(8,128)(2,1)S(1)}, bf16[192,10240]{1,0:T(8,128)(2,1)S(1)}, bf16[10240,192]{1,0:T(8,128)(2,1)S(1)}, bf16[10240,192]{1,0:T(8,128)(2,1)S(1)}) custom-call(f32[3,64,10240]{2,1,0:T(8,128)S(1)} %copy-done.11), custom_call_target="tpu_custom_call" | custom-call | tf_op jit(solution)/shard_map/split_design/pallas_call | solution.py:41
  51.1 2.3 %collective-permute-done.14.refs_4_ = f32[16,10240]{1,0:T(8,128)S(1)} collective-permute-done((f32[16,10240]{1,0:T(8,128)}, f32[16,10240]{1,0:T(8,128)S(1)}, u32[]{:S(2)}, u32[]{:S(2)}) %collective-permute-start.14) | collective-permute-done | bytes 655392 | tf_op jit(solution)/shard_map/ppermute | solution.py:204
  53.4 2.9 %collective-permute-start.15 = (f32[16,10240]{1,0:T(8,128)S(1)}, f32[16,10240]{1,0:T(8,128)}, u32[]{:S(2)}, u32[]{:S(2)}) collective-permute-start(f32[16,10240]{1,0:T(8,128)S(1)} %collective-permute-done.14.refs_4_), channel_id=1, source_target_pairs={{4,0},{8,12},{5,1},{9,13},{6,2},{10,14},{7,3},{11,15},{20,16},{24,... | collective-permute-start | bytes 1966088 | tf_op jit(solution)/shard_map/ppermute | solution.py:204
  56.3 8.2 %collective-permute-done.16.refs_2_ = f32[16,10240]{1,0:T(8,128)} collective-permute-done((f32[16,10240]{1,0:T(8,128)S(1)}, f32[16,10240]{1,0:T(8,128)}, u32[]{:S(2)}, u32[]{:S(2)}) %collective-permute-start.16) | collective-permute-done | bytes 655392 | tf_op jit(solution)/shard_map/ppermute | solution.py:204
  67.1 3.8 %project.2 = f32[4,16,192]{2,1,0:T(8,128)S(1)} custom-call(s32[4]{0:T(128)S(1)} %and_select_fusion.shard_ref, bf16[10240,192]{1,0:T(8,128)(2,1)S(1)} %get-tuple-element.19.high_ref, bf16[10240,192]{1,0:T(8,128)(2,1)S(1)} %get-tuple-element.20.low_ref, f32[32,10240]{1,0:T(8,128)S(1)} %bitcast.7, f32[16,10240]{1,0:T(8,128)S(1)} %copy-done.13, ...), custom_call_target="tpu_custom_call" | custom-call | tf_op jit(solution)/shard_map/project/pallas_call | solution.py:118
  70.9 5.8 %all-gather = f32[16,16,192]{2,1,0:T(8,128)S(1)} all-gather(f32[4,16,192]{2,1,0:T(8,128)S(1)} %project.2), channel_id=2, replica_groups=mesh['groups'=2,'tm'=4,'param'=4] {'param'}, dimensions={0}, use_global_device_ids=true | all-gather | bytes 245760 | tf_op jit(solution)/shard_map/all_gather | solution.py:251
  76.7 2.5 %collective-permute-start.5 = (f32[4,16,192]{2,1,0:T(8,128)S(1)}, f32[4,16,192]{2,1,0:T(8,128)S(1)}, u32[]{:S(2)}, u32[]{:S(2)}) collective-permute-start(f32[4,16,192]{2,1,0:T(8,128)S(1)} %reduce_sum.18.refs_0_), channel_id=1, source_target_pairs={{0,4},{4,0},{8,12},{12,8},{1,5},{5,1},{9,13},{13,9},{2,6},{6,2},{1... | collective-permute-start | bytes 147464 | tf_op jit(solution)/shard_map/ppermute | solution.py:229
  83.1 14.2 %collective-permute-done.5.refs_1_ = f32[4,16,192]{2,1,0:T(8,128)S(1)} collective-permute-done((f32[4,16,192]{2,1,0:T(8,128)S(1)}, f32[4,16,192]{2,1,0:T(8,128)S(1)}, u32[]{:S(2)}, u32[]{:S(2)}) %collective-permute-start.5) | collective-permute-done | bytes 49184 | tf_op jit(solution)/shard_map/ppermute | solution.py:229
  101.5 4.4 %multiply.2 = (f32[16,10240]{1,0:T(8,128)S(1)}, f32[16,10240]{1,0:T(8,128)S(1)}, f32[16,10240]{1,0:T(8,128)S(1)}, f32[16,10240]{1,0:T(8,128)}) custom-call(s32[4]{0:T(128)S(1)} %and_select_fusion.shard_ref, s32[4]{0:T(128)S(1)} %iota_xor_fusion.place_ref, bf16[192,10240]{1,0:T(8,128)(2,1)S(1)} %copy-done.5, bf16[192,10240]{1,0:T(8,128)(2,1)S(1)} %copy-done.8, ...), custom_call_target="tpu_custom_call" | custom-call | tf_op jit(solution)/shard_map/multiply/pallas_call | solution.py:167
  108.1 2.5 %copy-done.3 = bf16[10240,192]{1,0:T(8,128)(2,1)S(1)} copy-done((bf16[10240,192]{1,0:T(8,128)(2,1)S(1)}, bf16[10240,192]{1,0:T(8,128)(2,1)}, u32[]{:S(2)}) %copy-start.3) | copy-done | bytes 3932184
  110.6 3.8 %project.3 = f32[4,16,192]{2,1,0:T(8,128)S(1)} custom-call(s32[4]{0:T(128)S(1)} %and_select_fusion.shard_ref, bf16[10240,192]{1,0:T(8,128)(2,1)S(1)} %copy-done.1, bf16[10240,192]{1,0:T(8,128)(2,1)S(1)} %copy-done.3, f32[32,10240]{1,0:T(8,128)S(1)} %bitcast.8, f32[16,10240]{1,0:T(8,128)S(1)} %collective-permute-done.13.refs_0_, ...), custom_call_target="tpu_custom_call" | custom-call | tf_op jit(solution)/shard_map/project/pallas_call | solution.py:118
  114.4 5.9 %all-gather.1 = f32[16,16,192]{2,1,0:T(8,128)S(1)} all-gather(f32[4,16,192]{2,1,0:T(8,128)S(1)} %project.3), channel_id=3, replica_groups=mesh['groups'=2,'tm'=4,'param'=4] {'param'}, dimensions={0}, use_global_device_ids=true | all-gather | bytes 245760 | tf_op jit(solution)/shard_map/all_gather | solution.py:251
  120.4 3.5 %collective-permute-start.18 = (f32[4,16,192]{2,1,0:T(8,128)S(1)}, f32[4,16,192]{2,1,0:T(8,128)S(1)}, u32[]{:S(2)}, u32[]{:S(2)}) collective-permute-start(f32[4,16,192]{2,1,0:T(8,128)S(1)} %reduce_sum.19.refs_0_), channel_id=1, source_target_pairs={{0,4},{4,0},{8,12},{12,8},{1,5},{5,1},{9,13},{13,9},{2,6},{6,2},{1... | collective-permute-start | bytes 147464 | tf_op jit(solution)/shard_map/ppermute | solution.py:229
  126.9 3.3 %collective-permute-done.19.refs_2_ = f32[4,16,192]{2,1,0:T(8,128)S(1)} collective-permute-done((f32[4,16,192]{2,1,0:T(8,128)S(1)}, f32[4,16,192]{2,1,0:T(8,128)S(1)}, u32[]{:S(2)}, u32[]{:S(2)}) %collective-permute-start.19) | collective-permute-done | bytes 49184 | tf_op jit(solution)/shard_map/ppermute | solution.py:229
  136.4 3.7 %multiply.3 = (f32[16,10240]{1,0:T(8,128)S(1)}, f32[16,10240]{1,0:T(8,128)S(1)}, f32[16,10240]{1,0:T(8,128)S(1)}, f32[16,10240]{1,0:T(8,128)S(1)}) custom-call(s32[4]{0:T(128)S(1)} %and_select_fusion.shard_ref, s32[4]{0:T(128)S(1)} %iota_xor_fusion.place_ref, bf16[192,10240]{1,0:T(8,128)(2,1)S(1)} %copy-done.6, bf16[192,10240]{1,0:T(8,128)(2,1)S(1)} %copy-done.9, ...), custom_call_target="tpu_custom_call" | custom-call | tf_op jit(solution)/shard_map/multiply/pallas_call | solution.py:167
  143.9 3.4 %collective-permute-start.9 = (f32[16,10240]{1,0:T(8,128)S(1)}, f32[16,10240]{1,0:T(8,128)S(1)}, u32[]{:S(2)}, u32[]{:S(2)}) collective-permute-start(f32[16,10240]{1,0:T(8,128)S(1)} %add.54), channel_id=1, source_target_pairs={{8,4},{4,8},{9,5},{5,9},{10,6},{6,10},{11,7},{7,11},{24,20},{20,24... | collective-permute-start | bytes 1966088 | tf_op jit(solution)/shard_map/ppermute | solution.py:219
  148.6 11.0 %collective-permute-done.21 = f32[16,10240]{1,0:T(8,128)S(1)} collective-permute-done((f32[16,10240]{1,0:T(8,128)S(1)}, f32[16,10240]{1,0:T(8,128)S(1)}, u32[]{:S(2)}, u32[]{:S(2)}) %collective-permute-start.21) | collective-permute-done | bytes 655392 | tf_op jit(solution)/shard_map/ppermute | solution.py:219
  159.7 3.6 %collective-permute-start.22 = (f32[16,10240]{1,0:T(8,128)S(1)}, f32[16,10240]{1,0:T(8,128)S(1)}, u32[]{:S(2)}, u32[]{:S(2)}) collective-permute-start(f32[16,10240]{1,0:T(8,128)S(1)} %add.59), channel_id=1, source_target_pairs={{8,4},{4,8},{9,5},{5,9},{10,6},{6,10},{11,7},{7,11},{24,20},{20,24... | collective-permute-start | bytes 1966088 | tf_op jit(solution)/shard_map/ppermute | solution.py:219
  163.3 10.4 %collective-permute-done.11 = f32[16,10240]{1,0:T(8,128)S(1)} collective-permute-done((f32[16,10240]{1,0:T(8,128)S(1)}, f32[16,10240]{1,0:T(8,128)S(1)}, u32[]{:S(2)}, u32[]{:S(2)}) %collective-permute-start.11) | collective-permute-done | bytes 655392 | tf_op jit(solution)/shard_map/ppermute | solution.py:219
  174.8 3.5 %collective-permute-start.12 = (f32[16,10240]{1,0:T(8,128)S(1)}, f32[16,10240]{1,0:T(8,128)S(1)}, u32[]{:S(2)}, u32[]{:S(2)}) collective-permute-start(f32[16,10240]{1,0:T(8,128)S(1)} %add.57), channel_id=1, source_target_pairs={{8,4},{4,8},{9,5},{5,9},{10,6},{6,10},{11,7},{7,11},{24,20},{20,24... | collective-permute-start | bytes 1966088 | tf_op jit(solution)/shard_map/ppermute | solution.py:219
  178.5 9.2 %collective-permute-done.24 = f32[16,10240]{1,0:T(8,128)S(1)} collective-permute-done((f32[16,10240]{1,0:T(8,128)S(1)}, f32[16,10240]{1,0:T(8,128)S(1)}, u32[]{:S(2)}, u32[]{:S(2)}) %collective-permute-start.24) | collective-permute-done | bytes 655392 | tf_op jit(solution)/shard_map/ppermute | solution.py:219
  187.8 3.6 %collective-permute-start.25 = (f32[16,10240]{1,0:T(8,128)S(1)}, f32[16,10240]{1,0:T(8,128)S(1)}, u32[]{:S(2)}, u32[]{:S(2)}) collective-permute-start(f32[16,10240]{1,0:T(8,128)S(1)} %add.62), channel_id=1, source_target_pairs={{8,4},{4,8},{9,5},{5,9},{10,6},{6,10},{11,7},{7,11},{24,20},{20,24... | collective-permute-start | bytes 1966088 | tf_op jit(solution)/shard_map/ppermute | solution.py:219
  191.8 10.0 %collective-permute-done.10 = f32[16,10240]{1,0:T(8,128)S(1)} collective-permute-done((f32[16,10240]{1,0:T(8,128)S(1)}, f32[16,10240]{1,0:T(8,128)S(1)}, u32[]{:S(2)}, u32[]{:S(2)}) %collective-permute-start.10) | collective-permute-done | bytes 655392 | tf_op jit(solution)/shard_map/ppermute | solution.py:219
  201.9 3.1 %collective-permute-done.25 = f32[16,10240]{1,0:T(8,128)S(1)} collective-permute-done((f32[16,10240]{1,0:T(8,128)S(1)}, f32[16,10240]{1,0:T(8,128)S(1)}, u32[]{:S(2)}, u32[]{:S(2)}) %collective-permute-start.25) | collective-permute-done | bytes 655392 | tf_op jit(solution)/shard_map/ppermute | solution.py:219
  205.0 9.6 %collective-permute-done.23 = f32[16,10240]{1,0:T(8,128)S(1)} collective-permute-done((f32[16,10240]{1,0:T(8,128)S(1)}, f32[16,10240]{1,0:T(8,128)S(1)}, u32[]{:S(2)}, u32[]{:S(2)}) %collective-permute-start.23) | collective-permute-done | bytes 655392 | tf_op jit(solution)/shard_map/ppermute | solution.py:219
  (89 shorter events, 42.7 us)
Async XLA Ops:
  2.2 17.6 %collective-permute-start = (f32[16,10240]{1,0:T(8,128)S(1)}, f32[16,10240]{1,0:T(8,128)S(1)}, u32[]{:S(2)}, u32[]{:S(2)}) collective-permute-start(f32[16,10240]{1,0:T(8,128)S(1)} %get-tuple-element.29), channel_id=1, source_target_pairs={{0,4},{4,0},{8,12},{12,8},{1,5},{5,1},{9,13},{13,9},{2,6},{6,2},{1... | collective-permute-start | bytes 1966088 | tf_op jit(solution)/shard_map/ppermute | solution.py:204
  2.2 30.5 %collective-permute-start.13 = (f32[16,10240]{1,0:T(8,128)}, f32[16,10240]{1,0:T(8,128)S(1)}, u32[]{:S(2)}, u32[]{:S(2)}) collective-permute-start(f32[16,10240]{1,0:T(8,128)} %get-tuple-element.30), channel_id=1, source_target_pairs={{0,4},{4,0},{8,12},{12,8},{1,5},{5,1},{9,13},{13,9},{2,6},{6,2},{1... | collective-permute-start | bytes 1966088 | tf_op jit(solution)/shard_map/ppermute | solution.py:204
  4.2 32.0 %collective-permute-start.1 = (f32[16,10240]{1,0:T(8,128)S(1)}, f32[16,10240]{1,0:T(8,128)}, u32[]{:S(2)}, u32[]{:S(2)}) collective-permute-start(f32[16,10240]{1,0:T(8,128)S(1)} %get-tuple-element.29), channel_id=1, source_target_pairs={{4,8},{8,4},{5,9},{9,5},{6,10},{10,6},{7,11},{11,7},{20,24},{24,20... | collective-permute-start | bytes 1966088 | tf_op jit(solution)/shard_map/ppermute | solution.py:204
  19.8 19.7 %collective-permute-start.3 = (f32[16,10240]{1,0:T(8,128)S(1)}, f32[16,10240]{1,0:T(8,128)}, u32[]{:S(2)}, u32[]{:S(2)}) collective-permute-start(f32[16,10240]{1,0:T(8,128)S(1)} %collective-permute-done.refs_0_), channel_id=1, source_target_pairs={{4,8},{8,4},{5,9},{9,5},{6,10},{10,6},{7,11},{11,7},{20,24},{24,20... | collective-permute-start | bytes 1966088 | tf_op jit(solution)/shard_map/ppermute | solution.py:204
  24.2 29.3 %collective-permute-start.14 = (f32[16,10240]{1,0:T(8,128)}, f32[16,10240]{1,0:T(8,128)S(1)}, u32[]{:S(2)}, u32[]{:S(2)}) collective-permute-start(f32[16,10240]{1,0:T(8,128)} %get-tuple-element.30), channel_id=1, source_target_pairs={{4,8},{8,4},{5,9},{9,5},{6,10},{10,6},{7,11},{11,7},{20,24},{24,20... | collective-permute-start | bytes 1966088 | tf_op jit(solution)/shard_map/ppermute | solution.py:204
  32.7 31.7 %collective-permute-start.16 = (f32[16,10240]{1,0:T(8,128)S(1)}, f32[16,10240]{1,0:T(8,128)}, u32[]{:S(2)}, u32[]{:S(2)}) collective-permute-start(f32[16,10240]{1,0:T(8,128)S(1)} %collective-permute-done.13.refs_0_), channel_id=1, source_target_pairs={{4,8},{8,4},{5,9},{9,5},{6,10},{10,6},{7,11},{11,7},{20,24},{24,20... | collective-permute-start | bytes 1966088 | tf_op jit(solution)/shard_map/ppermute | solution.py:204
  36.2 30.4 %collective-permute-start.2 = (f32[16,10240]{1,0:T(8,128)}, f32[16,10240]{1,0:T(8,128)}, u32[]{:S(2)}, u32[]{:S(2)}) collective-permute-start(f32[16,10240]{1,0:T(8,128)} %collective-permute-done.1.refs_4_), channel_id=1, source_target_pairs={{4,0},{8,12},{5,1},{9,13},{6,2},{10,14},{7,3},{11,15},{20,16},{24,... | collective-permute-start | bytes 1966088 | tf_op jit(solution)/shard_map/ppermute | solution.py:204
  39.5 27.6 %collective-permute-start.4 = (f32[16,10240]{1,0:T(8,128)}, f32[16,10240]{1,0:T(8,128)}, u32[]{:S(2)}, u32[]{:S(2)}) collective-permute-start(f32[16,10240]{1,0:T(8,128)} %collective-permute-done.3.refs_2_), channel_id=1, source_target_pairs={{4,0},{8,12},{5,1},{9,13},{6,2},{10,14},{7,3},{11,15},{20,16},{24,... | collective-permute-start | bytes 1966088 | tf_op jit(solution)/shard_map/ppermute | solution.py:204
  44.9 22.2 %copy-start.10 = (f32[10240,32]{0,1:T(8,128)S(1)}, f32[10240,32]{0,1:T(8,128)}, u32[]{:S(2)}) copy-start(f32[10240,32]{0,1:T(8,128)} %param.5) | copy-start | bytes 3932164
  44.9 22.2 %copy-start.13 = (f32[16,10240]{1,0:T(8,128)S(1)}, f32[16,10240]{1,0:T(8,128)}, u32[]{:S(2)}) copy-start(f32[16,10240]{1,0:T(8,128)} %copy-done.12) | copy-start | bytes 1966084
  51.1 19.8 %copy-start = (bf16[10240,192]{1,0:T(8,128)(2,1)}, bf16[10240,192]{1,0:T(8,128)(2,1)S(1)}, u32[]{:S(2)}) copy-start(bf16[10240,192]{1,0:T(8,128)(2,1)S(1)} %get-tuple-element.19.high_ref) | copy-start | bytes 11796484
  51.1 19.8 %copy-start.2 = (bf16[10240,192]{1,0:T(8,128)(2,1)}, bf16[10240,192]{1,0:T(8,128)(2,1)S(1)}, u32[]{:S(2)}) copy-start(bf16[10240,192]{1,0:T(8,128)(2,1)S(1)} %get-tuple-element.20.low_ref) | copy-start | bytes 11796484
  51.1 19.8 %copy-start.7 = (bf16[192,10240]{1,0:T(8,128)(2,1)}, bf16[192,10240]{1,0:T(8,128)(2,1)S(1)}, u32[]{:S(2)}) copy-start(bf16[192,10240]{1,0:T(8,128)(2,1)S(1)} %get-tuple-element.18.low_ref) | copy-start | bytes 11796484
  53.4 54.6 %collective-permute-start.15 = (f32[16,10240]{1,0:T(8,128)S(1)}, f32[16,10240]{1,0:T(8,128)}, u32[]{:S(2)}, u32[]{:S(2)}) collective-permute-start(f32[16,10240]{1,0:T(8,128)S(1)} %collective-permute-done.14.refs_4_), channel_id=1, source_target_pairs={{4,0},{8,12},{5,1},{9,13},{6,2},{10,14},{7,3},{11,15},{20,16},{24,... | collective-permute-start | bytes 1966088 | tf_op jit(solution)/shard_map/ppermute | solution.py:204
  64.5 43.6 %collective-permute-start.17 = (f32[16,10240]{1,0:T(8,128)}, f32[16,10240]{1,0:T(8,128)}, u32[]{:S(2)}, u32[]{:S(2)}) collective-permute-start(f32[16,10240]{1,0:T(8,128)} %collective-permute-done.16.refs_2_), channel_id=1, source_target_pairs={{4,0},{8,12},{5,1},{9,13},{6,2},{10,14},{7,3},{11,15},{20,16},{24,... | collective-permute-start | bytes 1966088 | tf_op jit(solution)/shard_map/ppermute | solution.py:204
  76.7 20.5 %collective-permute-start.5 = (f32[4,16,192]{2,1,0:T(8,128)S(1)}, f32[4,16,192]{2,1,0:T(8,128)S(1)}, u32[]{:S(2)}, u32[]{:S(2)}) collective-permute-start(f32[4,16,192]{2,1,0:T(8,128)S(1)} %reduce_sum.18.refs_0_), channel_id=1, source_target_pairs={{0,4},{4,0},{8,12},{12,8},{1,5},{5,1},{9,13},{13,9},{2,6},{6,2},{1... | collective-permute-start | bytes 147464 | tf_op jit(solution)/shard_map/ppermute | solution.py:229
  79.3 18.0 %collective-permute-start.6 = (f32[4,16,192]{2,1,0:T(8,128)S(1)}, f32[4,16,192]{2,1,0:T(8,128)S(1)}, u32[]{:S(2)}, u32[]{:S(2)}) collective-permute-start(f32[4,16,192]{2,1,0:T(8,128)S(1)} %reduce_sum.18.refs_0_), channel_id=1, source_target_pairs={{0,8},{4,12},{8,0},{12,4},{1,9},{5,13},{9,1},{13,5},{2,10},{6,14},... | collective-permute-start | bytes 147464 | tf_op jit(solution)/shard_map/ppermute | solution.py:229
  80.6 16.7 %collective-permute-start.7 = (f32[4,16,192]{2,1,0:T(8,128)S(1)}, f32[4,16,192]{2,1,0:T(8,128)S(1)}, u32[]{:S(2)}, u32[]{:S(2)}) collective-permute-start(f32[4,16,192]{2,1,0:T(8,128)S(1)} %reduce_sum.18.refs_0_), channel_id=1, source_target_pairs={{0,12},{4,8},{8,4},{12,0},{1,13},{5,9},{9,5},{13,1},{2,14},{6,10},... | collective-permute-start | bytes 147464 | tf_op jit(solution)/shard_map/ppermute | solution.py:229
  106.8 35.9 %collective-permute-start.8 = (f32[16,10240]{1,0:T(8,128)}, f32[16,10240]{1,0:T(8,128)}, u32[]{:S(2)}, u32[]{:S(2)}) collective-permute-start(f32[16,10240]{1,0:T(8,128)} %get-tuple-element.24), channel_id=1, source_target_pairs={{0,4},{12,8},{1,5},{13,9},{2,6},{14,10},{3,7},{15,11},{16,20},{28,... | collective-permute-start | bytes 1966088 | tf_op jit(solution)/shard_map/ppermute | solution.py:219
  114.4 27.0 %copy-start.19 = (f32[16,10240]{1,0:T(8,128)S(1)}, f32[16,10240]{1,0:T(8,128)}, u32[]{:S(2)}) copy-start(f32[16,10240]{1,0:T(8,128)} %copy-done.18) | copy-start | bytes 1966084
  120.4 6.5 %collective-permute-start.18 = (f32[4,16,192]{2,1,0:T(8,128)S(1)}, f32[4,16,192]{2,1,0:T(8,128)S(1)}, u32[]{:S(2)}, u32[]{:S(2)}) collective-permute-start(f32[4,16,192]{2,1,0:T(8,128)S(1)} %reduce_sum.19.refs_0_), channel_id=1, source_target_pairs={{0,4},{4,0},{8,12},{12,8},{1,5},{5,1},{9,13},{13,9},{2,6},{6,2},{1... | collective-permute-start | bytes 147464 | tf_op jit(solution)/shard_map/ppermute | solution.py:229
  123.9 6.3 %collective-permute-start.19 = (f32[4,16,192]{2,1,0:T(8,128)S(1)}, f32[4,16,192]{2,1,0:T(8,128)S(1)}, u32[]{:S(2)}, u32[]{:S(2)}) collective-permute-start(f32[4,16,192]{2,1,0:T(8,128)S(1)} %reduce_sum.19.refs_0_), channel_id=1, source_target_pairs={{0,8},{4,12},{8,0},{12,4},{1,9},{5,13},{9,1},{13,5},{2,10},{6,14},... | collective-permute-start | bytes 147464 | tf_op jit(solution)/shard_map/ppermute | solution.py:229
  125.1 7.0 %collective-permute-start.20 = (f32[4,16,192]{2,1,0:T(8,128)S(1)}, f32[4,16,192]{2,1,0:T(8,128)S(1)}, u32[]{:S(2)}, u32[]{:S(2)}) collective-permute-start(f32[4,16,192]{2,1,0:T(8,128)S(1)} %reduce_sum.19.refs_0_), channel_id=1, source_target_pairs={{0,12},{4,8},{8,4},{12,0},{1,13},{5,9},{9,5},{13,1},{2,14},{6,10},... | collective-permute-start | bytes 147464 | tf_op jit(solution)/shard_map/ppermute | solution.py:229
  140.1 19.5 %collective-permute-start.21 = (f32[16,10240]{1,0:T(8,128)S(1)}, f32[16,10240]{1,0:T(8,128)S(1)}, u32[]{:S(2)}, u32[]{:S(2)}) collective-permute-start(f32[16,10240]{1,0:T(8,128)S(1)} %get-tuple-element.28), channel_id=1, source_target_pairs={{0,4},{12,8},{1,5},{13,9},{2,6},{14,10},{3,7},{15,11},{16,20},{28,... | collective-permute-start | bytes 1966088 | tf_op jit(solution)/shard_map/ppermute | solution.py:219
  141.4 32.3 %collective-permute-start.11 = (f32[16,10240]{1,0:T(8,128)S(1)}, f32[16,10240]{1,0:T(8,128)S(1)}, u32[]{:S(2)}, u32[]{:S(2)}) collective-permute-start(f32[16,10240]{1,0:T(8,128)S(1)} %copy-done.19), channel_id=1, source_target_pairs={{0,4},{12,8},{1,5},{13,9},{2,6},{14,10},{3,7},{15,11},{16,20},{28,... | collective-permute-start | bytes 1966088 | tf_op jit(solution)/shard_map/ppermute | solution.py:219
  143.9 34.4 %collective-permute-start.9 = (f32[16,10240]{1,0:T(8,128)S(1)}, f32[16,10240]{1,0:T(8,128)S(1)}, u32[]{:S(2)}, u32[]{:S(2)}) collective-permute-start(f32[16,10240]{1,0:T(8,128)S(1)} %add.54), channel_id=1, source_target_pairs={{8,4},{4,8},{9,5},{5,9},{10,6},{6,10},{11,7},{7,11},{24,20},{20,24... | collective-permute-start | bytes 1966088 | tf_op jit(solution)/shard_map/ppermute | solution.py:219
  147.3 40.4 %collective-permute-start.24 = (f32[16,10240]{1,0:T(8,128)S(1)}, f32[16,10240]{1,0:T(8,128)S(1)}, u32[]{:S(2)}, u32[]{:S(2)}) collective-permute-start(f32[16,10240]{1,0:T(8,128)S(1)} %get-tuple-element.27), channel_id=1, source_target_pairs={{0,4},{12,8},{1,5},{13,9},{2,6},{14,10},{3,7},{15,11},{16,20},{28,... | collective-permute-start | bytes 1966088 | tf_op jit(solution)/shard_map/ppermute | solution.py:219
  159.7 31.7 %collective-permute-start.22 = (f32[16,10240]{1,0:T(8,128)S(1)}, f32[16,10240]{1,0:T(8,128)S(1)}, u32[]{:S(2)}, u32[]{:S(2)}) collective-permute-start(f32[16,10240]{1,0:T(8,128)S(1)} %add.59), channel_id=1, source_target_pairs={{8,4},{4,8},{9,5},{5,9},{10,6},{6,10},{11,7},{7,11},{24,20},{20,24... | collective-permute-start | bytes 1966088 | tf_op jit(solution)/shard_map/ppermute | solution.py:219
  174.8 17.0 %collective-permute-start.12 = (f32[16,10240]{1,0:T(8,128)S(1)}, f32[16,10240]{1,0:T(8,128)S(1)}, u32[]{:S(2)}, u32[]{:S(2)}) collective-permute-start(f32[16,10240]{1,0:T(8,128)S(1)} %add.57), channel_id=1, source_target_pairs={{8,4},{4,8},{9,5},{5,9},{10,6},{6,10},{11,7},{7,11},{24,20},{20,24... | collective-permute-start | bytes 1966088 | tf_op jit(solution)/shard_map/ppermute | solution.py:219
  178.4 23.4 %collective-permute-start.10 = (f32[16,10240]{1,0:T(8,128)S(1)}, f32[16,10240]{1,0:T(8,128)S(1)}, u32[]{:S(2)}, u32[]{:S(2)}) collective-permute-start(f32[16,10240]{1,0:T(8,128)S(1)} %add.55), channel_id=1, source_target_pairs={{4,0},{0,4},{12,8},{8,12},{5,1},{1,5},{13,9},{9,13},{6,2},{2,6},{1... | collective-permute-start | bytes 1966088 | tf_op jit(solution)/shard_map/ppermute | solution.py:219
  187.8 17.2 %collective-permute-start.25 = (f32[16,10240]{1,0:T(8,128)S(1)}, f32[16,10240]{1,0:T(8,128)S(1)}, u32[]{:S(2)}, u32[]{:S(2)}) collective-permute-start(f32[16,10240]{1,0:T(8,128)S(1)} %add.62), channel_id=1, source_target_pairs={{8,4},{4,8},{9,5},{5,9},{10,6},{6,10},{11,7},{7,11},{24,20},{20,24... | collective-permute-start | bytes 1966088 | tf_op jit(solution)/shard_map/ppermute | solution.py:219
  191.5 23.0 %collective-permute-start.23 = (f32[16,10240]{1,0:T(8,128)S(1)}, f32[16,10240]{1,0:T(8,128)S(1)}, u32[]{:S(2)}, u32[]{:S(2)}) collective-permute-start(f32[16,10240]{1,0:T(8,128)S(1)} %add.60), channel_id=1, source_target_pairs={{4,0},{0,4},{12,8},{8,12},{5,1},{1,5},{13,9},{9,13},{6,2},{2,6},{1... | collective-permute-start | bytes 1966088 | tf_op jit(solution)/shard_map/ppermute | solution.py:219
  (15 other events, 86.2 us)

commit v4 on v3

--- a/solution.py
+++ b/solution.py
@@ -7,6 +7,7 @@
 from jax.experimental.pallas import tpu as pltpu
 from jax.sharding import PartitionSpec as P
 
+SHORT = pl.CostEstimate(flops=1, bytes_accessed=1, transcendentals=0)
 HIGHEST = lax.Precision.HIGHEST
 ALONG = (((1,), (1,)), ((), ()))
 ACROSS = (((1,), (0,)), ((), ()))
@@ -46,6 +47,7 @@
         + [pl.BlockSpec((width, samples), lambda p: (p, 0))] * 2,
         out_shape=[flat, flat, tall, tall],
         compiler_params=pltpu.CompilerParams(vmem_limit_bytes=16 << 20),
+        cost_estimate=SHORT,
         name="split_design",
     )(design)
 
@@ -84,6 +86,7 @@
         ),
         out_shape=jax.ShapeDtypeStruct((total // epochs, components, epochs, epochs), jnp.float32),
         compiler_params=pltpu.CompilerParams(vmem_limit_bytes=(4 << 20) + 4 * total * total),
+        cost_estimate=SHORT,
         name="normal_rows",
     )(jnp.reshape(block_index, (1,)).astype(jnp.int32), ascending, descending)
 
@@ -130,6 +133,7 @@
         ),
         out_shape=jax.ShapeDtypeStruct((slots, rows, samples), jnp.float32),
         compiler_params=pltpu.CompilerParams(vmem_limit_bytes=24 << 20),
+        cost_estimate=SHORT,
         name="project",
     )(shards, tall_high, tall_low, own, *pieces)
 
@@ -180,8 +184,27 @@
         ),
         out_shape=[jax.ShapeDtypeStruct((rows, coefficients), jnp.float32) for _ in range(slots)],
         compiler_params=pltpu.CompilerParams(vmem_limit_bytes=24 << 20),
+        cost_estimate=SHORT,
         name="multiply",
     )(shards, places, high, low, taps, *blocks)
+
+
+def add_up(shares):
+    count, slots, rows, samples = shares.shape
+
+    def kernel(shares_ref, out_ref):
+        value = shares_ref[0]
+        for share in range(1, count):
+            value = value + shares_ref[share]
+        out_ref[...] = value
+
+    return pl.pallas_call(
+        kernel,
+        out_shape=jax.ShapeDtypeStruct((slots, rows, samples), jnp.float32),
+        compiler_params=pltpu.CompilerParams(vmem_limit_bytes=8 << 20),
+        cost_estimate=SHORT,
+        name="add_up",
+    )(shares)
 
 
 def step_pairs(length, step, parity):
@@ -194,42 +217,85 @@
     return pairs
 
 
-def gather_along(value, length):
-    arrived = {(0, 0): value, (1, 0): value}
-    for step in range(1, length):
+def after(value, *others):
+    return lax.optimization_barrier((value,) + others)[0]
+
+
+class Gather:
+    def __init__(self, value, length):
+        self.length = length
+        self.arrived = {(0, 0): value, (1, 0): value}
+        self.done = 0
+        self.latest = [value]
+
+    def step(self, count=1):
+        for _ in range(count):
+            if self.done == self.length - 1:
+                return
+            self.done += 1
+            self.latest = []
+            for parity in (0, 1):
+                pairs = step_pairs(self.length, self.done, parity)
+                if pairs:
+                    value = lax.ppermute(self.arrived[1 - parity, self.done - 1], "tm", pairs)
+                    self.arrived[parity, self.done] = value
+                    self.latest.append(value)
+
+    def slots(self):
+        self.step(self.length)
+        return [
+            [self.arrived[key] for key in ((0, slot), (1, self.length - slot)) if key in self.arrived]
+            for slot in range(1, self.length)
+        ]
+
+
+class Reduction:
+    def __init__(self, slots, length):
+        self.length = length
+        self.slots = slots
+        self.pending = {}
+        self.left = length - 1
+        self.latest = []
+
+    def step(self, count=1):
+        for _ in range(count):
+            if self.left == 0:
+                return
+            self.latest = []
+            for parity in (0, 1):
+                pairs = step_pairs(self.length, self.left, parity)
+                if pairs:
+                    value = self.slots[self.left] if parity == 0 else self.slots[self.length - self.left]
+                    if (1 - parity, self.left + 1) in self.pending:
+                        value = value + self.pending[1 - parity, self.left + 1]
+                    value = lax.ppermute(value, "tm", [(b, a) for a, b in pairs])
+                    self.pending[parity, self.left] = value
+                    self.latest.append(value)
+            self.left -= 1
+
+    def result(self):
+        self.step(self.length)
+        value = self.slots[0]
         for parity in (0, 1):
-            pairs = step_pairs(length, step, parity)
-            source = arrived.get((1 - parity, step - 1))
-            if pairs:
-                arrived[parity, step] = lax.ppermute(source, "tm", pairs)
-    return [
-        [arrived[key] for key in ((0, slot), (1, length - slot)) if key in arrived] for slot in range(1, length)
-    ]
-
-
-def reduce_along(slots, length):
-    pending = {}
-    for step in range(length - 1, 0, -1):
-        for parity in (0, 1):
-            pairs = step_pairs(length, step, parity)
-            if pairs:
-                value = slots[step] if parity == 0 else slots[length - step]
-                if (1 - parity, step + 1) in pending:
-                    value = value + pending[1 - parity, step + 1]
-                pending[parity, step] = lax.ppermute(value, "tm", [(b, a) for a, b in pairs])
-    result = slots[0]
-    for parity in (0, 1):
-        if (parity, 1) in pending:
-            result = result + pending[parity, 1]
-    return result
+            if (parity, 1) in self.pending:
+                value = value + self.pending[parity, 1]
+        return value
+
+
+def is_direct(length):
+    return length <= 8 and length & (length - 1) == 0
+
+
+def places_of(length):
+    numbers = jnp.arange(length, dtype=jnp.int32)
+    return lax.axis_index("tm") ^ numbers if is_direct(length) else numbers
 
 
 def exchange(value, length):
-    if length <= 8 and length & (length - 1) == 0:
-        others = [lax.ppermute(value, "tm", [(i, i ^ by) for i in range(length)]) for by in range(1, length)]
-        return [value] + others, lax.axis_index("tm") ^ jnp.arange(length, dtype=jnp.int32)
+    if is_direct(length):
+        return [value] + [lax.ppermute(value, "tm", [(i, i ^ by) for i in range(length)]) for by in range(1, length)]
     gathered = lax.all_gather(value, "tm", axis=0)
-    return [gathered[i] for i in range(length)], jnp.arange(length, dtype=jnp.int32)
+    return [gathered[i] for i in range(length)]
 
 
 def body(design, filter_taps, probes):
@@ -243,16 +309,35 @@
     direction = 1 - 2 * (place % 2)
     shards = (place + direction * jnp.arange(length, dtype=jnp.int32)) % length
     taps = normal_rows(filter_taps, place, epochs, length * epochs)
-    high, low, tall_high, tall_low = split_design(design)
+    places = places_of(length)
+    high, low, tall_high, tall_low = split_design(after(design, taps, shards, places))
+    parts = []
+    for chunk in range(chunks):
+        value = own[chunk * rows : (chunk + 1) * rows]
+        if parts:
+            value = after(value, *last_source)
+        gather = Gather(value, length)
+        if chunk == 0:
+            gather.step(length - 2)
+            last_source = gather.latest
+            gather.step()
+        parts.append(gather)
     results = []
-    for chunk in range(chunks):
-        arrivals = gather_along(own[chunk * rows : (chunk + 1) * rows], length)
-        partial = project(tall_high, tall_low, own, chunk, arrivals, shards)
-        projected = jnp.sum(lax.all_gather(partial, "param", axis=0), axis=0)
-        blocks, places = exchange(projected, length)
-        slots = multiply(high, low, taps, blocks, places, shards)
-        results.append(reduce_along(slots, length))
-    return jnp.concatenate(results, axis=0).T
+    for chunk, gather in enumerate(parts):
+        behind = parts[chunk + 1] if chunk + 1 < chunks else (results[-1] if results else None)
+        if behind is not None:
+            behind.step()
+        partial = project(tall_high, tall_low, own, chunk, gather.slots(), shards)
+        if behind is not None:
+            partial = after(partial, *behind.latest)
+            behind.step()
+        projected = add_up(lax.all_gather(partial, "param", axis=0))
+        blocks = exchange(projected, length)
+        if behind is not None:
+            blocks[-1] = after(blocks[-1], *behind.latest)
+            behind.step()
+        results.append(Reduction(multiply(high, low, taps, blocks, places, shards), length))
+    return jnp.concatenate([reduction.result() for reduction in results], axis=0).T
 
 
 def solution(mesh):

time: 217 us -> 202 us (0.931)
  local copies, waits for them, and re-layouts: 20.5 us -> 7.55 us
  waiting for transfers between devices: 105 us -> 111 us
  starting transfers between devices: 53 us -> 49.5 us
  other arithmetic: 4.11 us -> 1.93 us
    ppermute x20, waiting for transfers between devices: 83.8 us -> 99.8 us  [the longest x10 61.6 us: step(): value = lax.ppermute(value, 'tm', [(b, a) for a, b in pairs])]
    unnamed x42 -> x18, local copies, waits for them, and re-layouts: 17.9 us -> 5.75 us
    ppermute x6, waiting for transfers between devices: 20.8 us -> 11 us  [exchange(): lax.ppermute(value, 'tm', [(i, i ^ by) for i in range(length)])]
    ppermute x20, starting transfers between devices: 43.4 us -> 41.1 us  [the longest x10 25.2 us: step(): value = lax.ppermute(self.arrived[1 - parity, self.done - 1], 'tm', pairs)]
    add x8, other arithmetic: 2.92 us -> 0.73 us  [the longest x6 0.47 us: step(): value = value + self.pending[1 - parity, self.left + 1]]
  transfers between devices with their start and end apart: 26 -> 26, of which waited for: 17 -> 15; matrix products, arithmetic and copies ran while one was open for 1% -> 1% of each run, Pallas kernels for 10% -> 6%
where the time goes in v4:
time: 202 us
  waiting for transfers between devices  111 us (55%)
  starting transfers between devices  49.5 us (25%)
  Pallas kernels  19.8 us (10%)
  blocking collectives  11.6 us (6%)
  local copies, waits for them, and re-layouts  7.55 us (4%)
    ppermute x10, waiting for transfers between devices, step(): value = lax.ppermute(value, 'tm', [(b, a) for a, b in pairs])  61.6 us
    ppermute x10, waiting for transfers between devices, step(): value = lax.ppermute(self.arrived[1 - parity, self.done - 1], 'tm', pairs)  38.2 us
    ppermute x10, starting transfers between devices, step(): value = lax.ppermute(self.arrived[1 - parity, self.done - 1], 'tm', pairs)  25.2 us
    ppermute x10, starting transfers between devices, step(): value = lax.ppermute(value, 'tm', [(b, a) for a, b in pairs])  15.8 us
    all_gather x2, blocking collectives, body(): projected = add_up(lax.all_gather(partial, 'param', axis=0))  11.6 us
    ppermute x6, waiting for transfers between devices, exchange(): lax.ppermute(value, 'tm', [(i, i ^ by) for i in range(length)])  11 us
    ppermute x6, starting transfers between devices, exchange(): lax.ppermute(value, 'tm', [(i, i ^ by) for i in range(length)])  8.47 us
    pallas_call x2, Pallas kernels, multiply(): pl.pallas_call(kernel, grid_spec=pltpu.PrefetchScalarGridSpec(num_scalar_...  7.48 us
  transfers between devices with their start and end apart: 26, of which 15 were waited for; matrix products, arithmetic and copies ran while one was open for 1% of the time, Pallas kernels for 6%

profile of v4, /device:TPU:8, one launch (start us, length us, event | category | flops | bytes accessed | tf_op | source)
XLA Modules:
  0.0 201.5 jit_solution(1585932625616981058)
XLA Ops:
  1.4 3.5 %collective-permute-start.1 = (f32[16,10240]{1,0:T(8,128)S(1)}, f32[16,10240]{1,0:T(8,128)S(1)}, u32[]{:S(2)}, u32[]{:S(2)}) collective-permute-start(f32[16,10240]{1,0:T(8,128)S(1)} %get-tuple-element.41), channel_id=1, source_target_pairs={{4,8},{8,4},{5,9},{9,5},{6,10},{10,6},{7,11},{11,7},{20,24},{24,20... | collective-permute-start | bytes 1966088 | tf_op jit(solution)/shard_map/ppermute | solution.py:240
  5.0 14.8 %collective-permute-done.1.refs_4_ = f32[16,10240]{1,0:T(8,128)S(1)} collective-permute-done((f32[16,10240]{1,0:T(8,128)S(1)}, f32[16,10240]{1,0:T(8,128)S(1)}, u32[]{:S(2)}, u32[]{:S(2)}) %collective-permute-start.1) | collective-permute-done | bytes 655392 | tf_op jit(solution)/shard_map/ppermute | solution.py:240
  21.9 3.5 %collective-permute-start.3 = (f32[16,10240]{1,0:T(8,128)S(1)}, f32[16,10240]{1,0:T(8,128)}, u32[]{:S(2)}, u32[]{:S(2)}) collective-permute-start(f32[16,10240]{1,0:T(8,128)S(1)} %collective-permute-done.refs_0_), channel_id=1, source_target_pairs={{4,8},{8,4},{5,9},{9,5},{6,10},{10,6},{7,11},{11,7},{20,24},{24,20... | collective-permute-start | bytes 1966088 | tf_op jit(solution)/shard_map/ppermute | solution.py:240
  26.3 8.2 %collective-permute-done.2.refs_1_ = f32[16,10240]{1,0:T(8,128)S(1)} collective-permute-done((f32[16,10240]{1,0:T(8,128)S(1)}, f32[16,10240]{1,0:T(8,128)S(1)}, u32[]{:S(2)}, u32[]{:S(2)}) %collective-permute-start.2) | collective-permute-done | bytes 655392 | tf_op jit(solution)/shard_map/ppermute | solution.py:240
  35.3 4.2 %collective-permute-done.3.refs_2_ = f32[16,10240]{1,0:T(8,128)} collective-permute-done((f32[16,10240]{1,0:T(8,128)S(1)}, f32[16,10240]{1,0:T(8,128)}, u32[]{:S(2)}, u32[]{:S(2)}) %collective-permute-start.3) | collective-permute-done | bytes 655392 | tf_op jit(solution)/shard_map/ppermute | solution.py:240
  39.5 3.5 %collective-permute-start.6 = (f32[16,10240]{1,0:T(8,128)S(1)}, f32[16,10240]{1,0:T(8,128)S(1)}, u32[]{:S(2)}, u32[]{:S(2)}) collective-permute-start(f32[16,10240]{1,0:T(8,128)S(1)} %get-tuple-element.28), channel_id=1, source_target_pairs={{4,8},{8,4},{5,9},{9,5},{6,10},{10,6},{7,11},{11,7},{20,24},{24,20... | collective-permute-start | bytes 1966088 | tf_op jit(solution)/shard_map/ppermute | solution.py:240
  43.1 4.8 %collective-permute-start.4 = (f32[16,10240]{1,0:T(8,128)}, f32[16,10240]{1,0:T(8,128)}, u32[]{:S(2)}, u32[]{:S(2)}) collective-permute-start(f32[16,10240]{1,0:T(8,128)} %collective-permute-done.3.refs_2_), channel_id=1, source_target_pairs={{4,0},{8,12},{5,1},{9,13},{6,2},{10,14},{7,3},{11,15},{20,16},{24,... | collective-permute-start | bytes 1966088 | tf_op jit(solution)/shard_map/ppermute | solution.py:240
  47.9 8.2 %collective-permute-done.6.refs_4_ = f32[16,10240]{1,0:T(8,128)S(1)} collective-permute-done((f32[16,10240]{1,0:T(8,128)S(1)}, f32[16,10240]{1,0:T(8,128)S(1)}, u32[]{:S(2)}, u32[]{:S(2)}) %collective-permute-start.6) | collective-permute-done | bytes 655392 | tf_op jit(solution)/shard_map/ppermute | solution.py:240
  58.3 2.6 %collective-permute-start.11 = (f32[16,10240]{1,0:T(8,128)S(1)}, f32[16,10240]{1,0:T(8,128)S(1)}, u32[]{:S(2)}, u32[]{:S(2)}) collective-permute-start(f32[16,10240]{1,0:T(8,128)S(1)} %collective-permute-done.5.refs_0_), channel_id=1, source_target_pairs={{4,8},{8,4},{5,9},{9,5},{6,10},{10,6},{7,11},{11,7},{20,24},{24,20... | collective-permute-start | bytes 1966088 | tf_op jit(solution)/shard_map/ppermute | solution.py:240
  63.0 3.2 %copy-done.1 = f32[3,64,10240]{2,1,0:T(8,128)S(1)} copy-done((f32[3,64,10240]{2,1,0:T(8,128)S(1)}, f32[3,64,10240]{2,1,0:T(8,128)}, u32[]{:S(2)}) %copy-start.1) | copy-done | bytes 7864344
  66.2 4.3 %split_design.1 = (bf16[192,10240]{1,0:T(8,128)(2,1)S(1)}, bf16[192,10240]{1,0:T(8,128)(2,1)S(1)}, bf16[10240,192]{1,0:T(8,128)(2,1)S(1)}, bf16[10240,192]{1,0:T(8,128)(2,1)S(1)}) custom-call(f32[3,64,10240]{2,1,0:T(8,128)S(1)} %copy-done.1), custom_call_target="tpu_custom_call" | custom-call | flops 1 | bytes 1 | tf_op jit(solution)/shard_map/split_design/pallas_call | solution.py:42
  72.4 3.6 %project.2 = f32[4,16,192]{2,1,0:T(8,128)S(1)} custom-call(s32[4]{0:T(128)S(1)} %and_select_fusion.shard_ref, bf16[10240,192]{1,0:T(8,128)(2,1)S(1)} %get-tuple-element.26.high_ref, bf16[10240,192]{1,0:T(8,128)(2,1)S(1)} %get-tuple-element.27.low_ref, f32[32,10240]{1,0:T(8,128)S(1)} %bitcast.7, f32[16,10240]{1,0:T(8,128)S(1)} %copy-done.5, ...), custom_call_target="tpu_custom_call" | custom-call | flops 1 | bytes 1 | tf_op jit(solution)/shard_map/project/pallas_call | solution.py:121
  76.1 5.8 %all-gather = f32[16,16,192]{2,1,0:T(8,128)S(1)} all-gather(f32[4,16,192]{2,1,0:T(8,128)S(1)} %project.2), channel_id=2, replica_groups=mesh['groups'=2,'tm'=4,'param'=4] {'param'}, dimensions={0}, use_global_device_ids=true | all-gather | bytes 245760 | tf_op jit(solution)/shard_map/all_gather | solution.py:334
  82.4 3.4 %collective-permute-start.7 = (f32[4,16,192]{2,1,0:T(8,128)S(1)}, f32[4,16,192]{2,1,0:T(8,128)S(1)}, u32[]{:S(2)}, u32[]{:S(2)}) collective-permute-start(f32[4,16,192]{2,1,0:T(8,128)S(1)} %add_up.2.refs_0_), channel_id=1, source_target_pairs={{0,4},{4,0},{8,12},{12,8},{1,5},{5,1},{9,13},{13,9},{2,6},{6,2},{1... | collective-permute-start | bytes 147464 | tf_op jit(solution)/shard_map/ppermute | solution.py:296
  86.8 3.3 %collective-permute-done.7.refs_1_ = f32[4,16,192]{2,1,0:T(8,128)S(1)} collective-permute-done((f32[4,16,192]{2,1,0:T(8,128)S(1)}, f32[4,16,192]{2,1,0:T(8,128)S(1)}, u32[]{:S(2)}, u32[]{:S(2)}) %collective-permute-start.7) | collective-permute-done | bytes 49184 | tf_op jit(solution)/shard_map/ppermute | solution.py:296
  91.9 3.7 %multiply.2 = (f32[16,10240]{1,0:T(8,128)S(1)}, f32[16,10240]{1,0:T(8,128)S(1)}, f32[16,10240]{1,0:T(8,128)S(1)}, f32[16,10240]{1,0:T(8,128)S(1)}) custom-call(s32[4]{0:T(128)S(1)} %and_select_fusion.shard_ref, s32[4]{0:T(128)S(1)} %iota_xor_fusion.place_ref, bf16[192,10240]{1,0:T(8,128)(2,1)S(1)} %get-tuple-element.24.high_ref, ...), custom_call_target="tpu_custom_call" | custom-call | flops 1 | bytes 1 | tf_op jit(solution)/shard_map/multiply/pallas_call | solution.py:171
  97.0 4.6 %collective-permute-start.17 = (f32[16,10240]{1,0:T(8,128)S(1)}, f32[16,10240]{1,0:T(8,128)S(1)}, u32[]{:S(2)}, u32[]{:S(2)}) collective-permute-start(f32[16,10240]{1,0:T(8,128)S(1)} %collective-permute-done.11.refs_2_), channel_id=1, source_target_pairs={{4,0},{8,12},{5,1},{9,13},{6,2},{10,14},{7,3},{11,15},{20,16},{24,... | collective-permute-start | bytes 1966088 | tf_op jit(solution)/shard_map/ppermute | solution.py:240
  102.9 12.3 %collective-permute-done.12 = f32[16,10240]{1,0:T(8,128)S(1)} collective-permute-done((f32[16,10240]{1,0:T(8,128)S(1)}, f32[16,10240]{1,0:T(8,128)S(1)}, u32[]{:S(2)}, u32[]{:S(2)}) %collective-permute-start.12) | collective-permute-done | bytes 655392 | tf_op jit(solution)/shard_map/ppermute | solution.py:271
  115.3 2.5 %collective-permute-start.13 = (f32[16,10240]{1,0:T(8,128)S(1)}, f32[16,10240]{1,0:T(8,128)S(1)}, u32[]{:S(2)}, u32[]{:S(2)}) collective-permute-start(f32[16,10240]{1,0:T(8,128)S(1)} %add.54), channel_id=1, source_target_pairs={{8,4},{4,8},{9,5},{5,9},{10,6},{6,10},{11,7},{7,11},{24,20},{20,24... | collective-permute-start | bytes 1966088 | tf_op jit(solution)/shard_map/ppermute | solution.py:271
  117.9 2.8 %project.3 = f32[4,16,192]{2,1,0:T(8,128)S(1)} custom-call(s32[4]{0:T(128)S(1)} %and_select_fusion.shard_ref, bf16[10240,192]{1,0:T(8,128)(2,1)S(1)} %get-tuple-element.26.high_ref, bf16[10240,192]{1,0:T(8,128)(2,1)S(1)} %get-tuple-element.27.low_ref, f32[32,10240]{1,0:T(8,128)S(1)} %bitcast.8, f32[16,10240]{1,0:T(8,128)S(1)} %collective-permute-done.5.refs_0_, ...), custom_call_target="tpu_custom_call" | custom-call | flops 1 | bytes 1 | tf_op jit(solution)/shard_map/project/pallas_call | solution.py:121
  120.6 5.8 %all-gather.1 = f32[16,16,192]{2,1,0:T(8,128)S(1)} all-gather(f32[4,16,192]{2,1,0:T(8,128)S(1)} %project.3), channel_id=3, replica_groups=mesh['groups'=2,'tm'=4,'param'=4] {'param'}, dimensions={0}, use_global_device_ids=true | all-gather | bytes 245760 | tf_op jit(solution)/shard_map/all_gather | solution.py:334
  128.0 2.0 %collective-permute-start.19 = (f32[4,16,192]{2,1,0:T(8,128)S(1)}, f32[4,16,192]{2,1,0:T(8,128)S(1)}, u32[]{:S(2)}, u32[]{:S(2)}) collective-permute-start(f32[4,16,192]{2,1,0:T(8,128)S(1)} %add_up.3.refs_0_), channel_id=1, source_target_pairs={{0,8},{4,12},{8,0},{12,4},{1,9},{5,13},{9,1},{13,5},{2,10},{6,14},... | collective-permute-start | bytes 147464 | tf_op jit(solution)/shard_map/ppermute | solution.py:296
  130.0 5.9 %collective-permute-done.20.refs_3_ = f32[4,16,192]{2,1,0:T(8,128)S(1)} collective-permute-done((f32[4,16,192]{2,1,0:T(8,128)S(1)}, f32[4,16,192]{2,1,0:T(8,128)S(1)}, u32[]{:S(2)}, u32[]{:S(2)}) %collective-permute-start.20) | collective-permute-done | bytes 49184 | tf_op jit(solution)/shard_map/ppermute | solution.py:296
  135.9 3.7 %multiply.3 = (f32[16,10240]{1,0:T(8,128)S(1)}, f32[16,10240]{1,0:T(8,128)S(1)}, f32[16,10240]{1,0:T(8,128)S(1)}, f32[16,10240]{1,0:T(8,128)S(1)}) custom-call(s32[4]{0:T(128)S(1)} %and_select_fusion.shard_ref, s32[4]{0:T(128)S(1)} %iota_xor_fusion.place_ref, bf16[192,10240]{1,0:T(8,128)(2,1)S(1)} %get-tuple-element.24.high_ref, ...), custom_call_target="tpu_custom_call" | custom-call | flops 1 | bytes 1 | tf_op jit(solution)/shard_map/multiply/pallas_call | solution.py:171
  142.2 17.0 %collective-permute-done.21 = f32[16,10240]{1,0:T(8,128)S(1)} collective-permute-done((f32[16,10240]{1,0:T(8,128)S(1)}, f32[16,10240]{1,0:T(8,128)S(1)}, u32[]{:S(2)}, u32[]{:S(2)}) %collective-permute-start.21) | collective-permute-done | bytes 655392 | tf_op jit(solution)/shard_map/ppermute | solution.py:271
  159.3 2.2 %collective-permute-start.22 = (f32[16,10240]{1,0:T(8,128)S(1)}, f32[16,10240]{1,0:T(8,128)S(1)}, u32[]{:S(2)}, u32[]{:S(2)}) collective-permute-start(f32[16,10240]{1,0:T(8,128)S(1)} %add.59), channel_id=1, source_target_pairs={{8,4},{4,8},{9,5},{5,9},{10,6},{6,10},{11,7},{7,11},{24,20},{20,24... | collective-permute-start | bytes 1966088 | tf_op jit(solution)/shard_map/ppermute | solution.py:271
  161.5 3.7 %collective-permute-start.16 = (f32[16,10240]{1,0:T(8,128)S(1)}, f32[16,10240]{1,0:T(8,128)S(1)}, u32[]{:S(2)}, u32[]{:S(2)}) collective-permute-start(f32[16,10240]{1,0:T(8,128)S(1)} %add.57), channel_id=1, source_target_pairs={{8,4},{4,8},{9,5},{5,9},{10,6},{6,10},{11,7},{7,11},{24,20},{20,24... | collective-permute-start | bytes 1966088 | tf_op jit(solution)/shard_map/ppermute | solution.py:271
  165.4 7.9 %collective-permute-done.24 = f32[16,10240]{1,0:T(8,128)S(1)} collective-permute-done((f32[16,10240]{1,0:T(8,128)S(1)}, f32[16,10240]{1,0:T(8,128)S(1)}, u32[]{:S(2)}, u32[]{:S(2)}) %collective-permute-start.24) | collective-permute-done | bytes 655392 | tf_op jit(solution)/shard_map/ppermute | solution.py:271
  173.3 2.2 %collective-permute-start.25 = (f32[16,10240]{1,0:T(8,128)S(1)}, f32[16,10240]{1,0:T(8,128)S(1)}, u32[]{:S(2)}, u32[]{:S(2)}) collective-permute-start(f32[16,10240]{1,0:T(8,128)S(1)} %add.62), channel_id=1, source_target_pairs={{8,4},{4,8},{9,5},{5,9},{10,6},{6,10},{11,7},{7,11},{24,20},{20,24... | collective-permute-start | bytes 1966088 | tf_op jit(solution)/shard_map/ppermute | solution.py:271
  175.5 3.3 %collective-permute-done.22 = f32[16,10240]{1,0:T(8,128)S(1)} collective-permute-done((f32[16,10240]{1,0:T(8,128)S(1)}, f32[16,10240]{1,0:T(8,128)S(1)}, u32[]{:S(2)}, u32[]{:S(2)}) %collective-permute-start.22) | collective-permute-done | bytes 655392 | tf_op jit(solution)/shard_map/ppermute | solution.py:271
  179.0 13.9 %collective-permute-done.16 = f32[16,10240]{1,0:T(8,128)S(1)} collective-permute-done((f32[16,10240]{1,0:T(8,128)S(1)}, f32[16,10240]{1,0:T(8,128)S(1)}, u32[]{:S(2)}, u32[]{:S(2)}) %collective-permute-start.16) | collective-permute-done | bytes 655392 | tf_op jit(solution)/shard_map/ppermute | solution.py:271
  193.1 7.2 %collective-permute-done.25 = f32[16,10240]{1,0:T(8,128)S(1)} collective-permute-done((f32[16,10240]{1,0:T(8,128)S(1)}, f32[16,10240]{1,0:T(8,128)S(1)}, u32[]{:S(2)}, u32[]{:S(2)}) %collective-permute-start.25) | collective-permute-done | bytes 655392 | tf_op jit(solution)/shard_map/ppermute | solution.py:271
  (65 shorter events, 23.6 us)
Async XLA Ops:
  0.0 60.9 %copy-start.8 = (f32[3,512]{1,0:T(4,128)S(1)}, f32[3,512]{1,0:T(4,128)}, u32[]{:S(2)}) copy-start(f32[3,512]{1,0:T(4,128)} %param.4) | copy-start | bytes 18436
  1.4 18.4 %collective-permute-start.1 = (f32[16,10240]{1,0:T(8,128)S(1)}, f32[16,10240]{1,0:T(8,128)S(1)}, u32[]{:S(2)}, u32[]{:S(2)}) collective-permute-start(f32[16,10240]{1,0:T(8,128)S(1)} %get-tuple-element.41), channel_id=1, source_target_pairs={{4,8},{8,4},{5,9},{9,5},{6,10},{10,6},{7,11},{11,7},{20,24},{24,20... | collective-permute-start | bytes 1966088 | tf_op jit(solution)/shard_map/ppermute | solution.py:240
  4.9 17.0 %collective-permute-start = (f32[16,10240]{1,0:T(8,128)S(1)}, f32[16,10240]{1,0:T(8,128)S(1)}, u32[]{:S(2)}, u32[]{:S(2)}) collective-permute-start(f32[16,10240]{1,0:T(8,128)S(1)} %get-tuple-element.41), channel_id=1, source_target_pairs={{0,4},{4,0},{8,12},{12,8},{1,5},{5,1},{9,13},{13,9},{2,6},{6,2},{1... | collective-permute-start | bytes 1966088 | tf_op jit(solution)/shard_map/ppermute | solution.py:240
  19.8 14.7 %collective-permute-start.2 = (f32[16,10240]{1,0:T(8,128)S(1)}, f32[16,10240]{1,0:T(8,128)S(1)}, u32[]{:S(2)}, u32[]{:S(2)}) collective-permute-start(f32[16,10240]{1,0:T(8,128)S(1)} %collective-permute-done.1.refs_4_), channel_id=1, source_target_pairs={{4,0},{8,12},{5,1},{9,13},{6,2},{10,14},{7,3},{11,15},{20,16},{24,... | collective-permute-start | bytes 1966088 | tf_op jit(solution)/shard_map/ppermute | solution.py:240
  21.9 17.6 %collective-permute-start.3 = (f32[16,10240]{1,0:T(8,128)S(1)}, f32[16,10240]{1,0:T(8,128)}, u32[]{:S(2)}, u32[]{:S(2)}) collective-permute-start(f32[16,10240]{1,0:T(8,128)S(1)} %collective-permute-done.refs_0_), channel_id=1, source_target_pairs={{4,8},{8,4},{5,9},{9,5},{6,10},{10,6},{7,11},{11,7},{20,24},{24,20... | collective-permute-start | bytes 1966088 | tf_op jit(solution)/shard_map/ppermute | solution.py:240
  39.5 16.6 %collective-permute-start.6 = (f32[16,10240]{1,0:T(8,128)S(1)}, f32[16,10240]{1,0:T(8,128)S(1)}, u32[]{:S(2)}, u32[]{:S(2)}) collective-permute-start(f32[16,10240]{1,0:T(8,128)S(1)} %get-tuple-element.28), channel_id=1, source_target_pairs={{4,8},{8,4},{5,9},{9,5},{6,10},{10,6},{7,11},{11,7},{20,24},{24,20... | collective-permute-start | bytes 1966088 | tf_op jit(solution)/shard_map/ppermute | solution.py:240
  43.0 15.3 %collective-permute-start.5 = (f32[16,10240]{1,0:T(8,128)S(1)}, f32[16,10240]{1,0:T(8,128)S(1)}, u32[]{:S(2)}, u32[]{:S(2)}) collective-permute-start(f32[16,10240]{1,0:T(8,128)S(1)} %get-tuple-element.28), channel_id=1, source_target_pairs={{0,4},{4,0},{8,12},{12,8},{1,5},{5,1},{9,13},{13,9},{2,6},{6,2},{1... | collective-permute-start | bytes 1966088 | tf_op jit(solution)/shard_map/ppermute | solution.py:240
  43.1 29.3 %collective-permute-start.4 = (f32[16,10240]{1,0:T(8,128)}, f32[16,10240]{1,0:T(8,128)}, u32[]{:S(2)}, u32[]{:S(2)}) collective-permute-start(f32[16,10240]{1,0:T(8,128)} %collective-permute-done.3.refs_2_), channel_id=1, source_target_pairs={{4,0},{8,12},{5,1},{9,13},{6,2},{10,14},{7,3},{11,15},{20,16},{24,... | collective-permute-start | bytes 1966088 | tf_op jit(solution)/shard_map/ppermute | solution.py:240
  56.1 30.7 %collective-permute-start.10 = (f32[16,10240]{1,0:T(8,128)S(1)}, f32[16,10240]{1,0:T(8,128)S(1)}, u32[]{:S(2)}, u32[]{:S(2)}) collective-permute-start(f32[16,10240]{1,0:T(8,128)S(1)} %collective-permute-done.6.refs_4_), channel_id=1, source_target_pairs={{4,0},{8,12},{5,1},{9,13},{6,2},{10,14},{7,3},{11,15},{20,16},{24,... | collective-permute-start | bytes 1966088 | tf_op jit(solution)/shard_map/ppermute | solution.py:240
  58.3 28.6 %collective-permute-start.11 = (f32[16,10240]{1,0:T(8,128)S(1)}, f32[16,10240]{1,0:T(8,128)S(1)}, u32[]{:S(2)}, u32[]{:S(2)}) collective-permute-start(f32[16,10240]{1,0:T(8,128)S(1)} %collective-permute-done.5.refs_0_), channel_id=1, source_target_pairs={{4,8},{8,4},{5,9},{9,5},{6,10},{10,6},{7,11},{11,7},{20,24},{24,20... | collective-permute-start | bytes 1966088 | tf_op jit(solution)/shard_map/ppermute | solution.py:240
  63.0 3.2 %copy-start.1 = (f32[3,64,10240]{2,1,0:T(8,128)S(1)}, f32[3,64,10240]{2,1,0:T(8,128)}, u32[]{:S(2)}) copy-start(f32[3,64,10240]{2,1,0:T(8,128)} %design_ref) | copy-start | bytes 23592964
  66.2 6.2 %copy-start = (f32[10240,32]{0,1:T(8,128)S(1)}, f32[10240,32]{0,1:T(8,128)}, u32[]{:S(2)}) copy-start(f32[10240,32]{0,1:T(8,128)} %param.5) | copy-start | bytes 3932164
  66.2 6.2 %copy-start.3 = (f32[16,10240]{1,0:T(8,128)S(1)}, f32[16,10240]{1,0:T(8,128)}, u32[]{:S(2)}) copy-start(f32[16,10240]{1,0:T(8,128)} %copy-done.2) | copy-start | bytes 1966084
  66.2 6.2 %copy-start.5 = (f32[16,10240]{1,0:T(8,128)S(1)}, f32[16,10240]{1,0:T(8,128)}, u32[]{:S(2)}) copy-start(f32[16,10240]{1,0:T(8,128)} %copy-done.4) | copy-start | bytes 1966084
  66.2 6.2 %copy-start.7 = (f32[16,10240]{1,0:T(8,128)S(1)}, f32[16,10240]{1,0:T(8,128)}, u32[]{:S(2)}) copy-start(f32[16,10240]{1,0:T(8,128)} %copy-done.6) | copy-start | bytes 1966084
  81.9 4.9 %collective-permute-start.9 = (f32[4,16,192]{2,1,0:T(8,128)S(1)}, f32[4,16,192]{2,1,0:T(8,128)S(1)}, u32[]{:S(2)}, u32[]{:S(2)}) collective-permute-start(f32[4,16,192]{2,1,0:T(8,128)S(1)} %add_up.2.refs_0_), channel_id=1, source_target_pairs={{0,12},{4,8},{8,4},{12,0},{1,13},{5,9},{9,5},{13,1},{2,14},{6,10},... | collective-permute-start | bytes 147464 | tf_op jit(solution)/shard_map/ppermute | solution.py:296
  82.4 7.7 %collective-permute-start.7 = (f32[4,16,192]{2,1,0:T(8,128)S(1)}, f32[4,16,192]{2,1,0:T(8,128)S(1)}, u32[]{:S(2)}, u32[]{:S(2)}) collective-permute-start(f32[4,16,192]{2,1,0:T(8,128)S(1)} %add_up.2.refs_0_), channel_id=1, source_target_pairs={{0,4},{4,0},{8,12},{12,8},{1,5},{5,1},{9,13},{13,9},{2,6},{6,2},{1... | collective-permute-start | bytes 147464 | tf_op jit(solution)/shard_map/ppermute | solution.py:296
  85.8 6.1 %collective-permute-start.8 = (f32[4,16,192]{2,1,0:T(8,128)S(1)}, f32[4,16,192]{2,1,0:T(8,128)S(1)}, u32[]{:S(2)}, u32[]{:S(2)}) collective-permute-start(f32[4,16,192]{2,1,0:T(8,128)S(1)} %add_up.2.refs_0_), channel_id=1, source_target_pairs={{0,8},{4,12},{8,0},{12,4},{1,9},{5,13},{9,1},{13,5},{2,10},{6,14},... | collective-permute-start | bytes 147464 | tf_op jit(solution)/shard_map/ppermute | solution.py:296
  95.7 19.6 %collective-permute-start.12 = (f32[16,10240]{1,0:T(8,128)S(1)}, f32[16,10240]{1,0:T(8,128)S(1)}, u32[]{:S(2)}, u32[]{:S(2)}) collective-permute-start(f32[16,10240]{1,0:T(8,128)S(1)} %get-tuple-element.34), channel_id=1, source_target_pairs={{0,4},{12,8},{1,5},{13,9},{2,6},{14,10},{3,7},{15,11},{16,20},{28,... | collective-permute-start | bytes 1966088 | tf_op jit(solution)/shard_map/ppermute | solution.py:271
  97.0 20.9 %collective-permute-start.17 = (f32[16,10240]{1,0:T(8,128)S(1)}, f32[16,10240]{1,0:T(8,128)S(1)}, u32[]{:S(2)}, u32[]{:S(2)}) collective-permute-start(f32[16,10240]{1,0:T(8,128)S(1)} %collective-permute-done.11.refs_2_), channel_id=1, source_target_pairs={{4,0},{8,12},{5,1},{9,13},{6,2},{10,14},{7,3},{11,15},{20,16},{24,... | collective-permute-start | bytes 1966088 | tf_op jit(solution)/shard_map/ppermute | solution.py:240
  101.6 28.4 %collective-permute-start.15 = (f32[16,10240]{1,0:T(8,128)S(1)}, f32[16,10240]{1,0:T(8,128)S(1)}, u32[]{:S(2)}, u32[]{:S(2)}) collective-permute-start(f32[16,10240]{1,0:T(8,128)S(1)} %get-tuple-element.33), channel_id=1, source_target_pairs={{0,4},{12,8},{1,5},{13,9},{2,6},{14,10},{3,7},{15,11},{16,20},{28,... | collective-permute-start | bytes 1966088 | tf_op jit(solution)/shard_map/ppermute | solution.py:271
  115.3 20.5 %collective-permute-start.13 = (f32[16,10240]{1,0:T(8,128)S(1)}, f32[16,10240]{1,0:T(8,128)S(1)}, u32[]{:S(2)}, u32[]{:S(2)}) collective-permute-start(f32[16,10240]{1,0:T(8,128)S(1)} %add.54), channel_id=1, source_target_pairs={{8,4},{4,8},{9,5},{5,9},{10,6},{6,10},{11,7},{7,11},{24,20},{20,24... | collective-permute-start | bytes 1966088 | tf_op jit(solution)/shard_map/ppermute | solution.py:271
  126.4 9.4 %collective-permute-start.20 = (f32[4,16,192]{2,1,0:T(8,128)S(1)}, f32[4,16,192]{2,1,0:T(8,128)S(1)}, u32[]{:S(2)}, u32[]{:S(2)}) collective-permute-start(f32[4,16,192]{2,1,0:T(8,128)S(1)} %add_up.3.refs_0_), channel_id=1, source_target_pairs={{0,12},{4,8},{8,4},{12,0},{1,13},{5,9},{9,5},{13,1},{2,14},{6,10},... | collective-permute-start | bytes 147464 | tf_op jit(solution)/shard_map/ppermute | solution.py:296
  128.0 7.9 %collective-permute-start.18 = (f32[4,16,192]{2,1,0:T(8,128)S(1)}, f32[4,16,192]{2,1,0:T(8,128)S(1)}, u32[]{:S(2)}, u32[]{:S(2)}) collective-permute-start(f32[4,16,192]{2,1,0:T(8,128)S(1)} %add_up.3.refs_0_), channel_id=1, source_target_pairs={{0,4},{4,0},{8,12},{12,8},{1,5},{5,1},{9,13},{13,9},{2,6},{6,2},{1... | collective-permute-start | bytes 147464 | tf_op jit(solution)/shard_map/ppermute | solution.py:296
  128.0 7.9 %collective-permute-start.19 = (f32[4,16,192]{2,1,0:T(8,128)S(1)}, f32[4,16,192]{2,1,0:T(8,128)S(1)}, u32[]{:S(2)}, u32[]{:S(2)}) collective-permute-start(f32[4,16,192]{2,1,0:T(8,128)S(1)} %add_up.3.refs_0_), channel_id=1, source_target_pairs={{0,8},{4,12},{8,0},{12,4},{1,9},{5,13},{9,1},{13,5},{2,10},{6,14},... | collective-permute-start | bytes 147464 | tf_op jit(solution)/shard_map/ppermute | solution.py:296
  139.6 19.6 %collective-permute-start.21 = (f32[16,10240]{1,0:T(8,128)S(1)}, f32[16,10240]{1,0:T(8,128)S(1)}, u32[]{:S(2)}, u32[]{:S(2)}) collective-permute-start(f32[16,10240]{1,0:T(8,128)S(1)} %get-tuple-element.40), channel_id=1, source_target_pairs={{0,4},{12,8},{1,5},{13,9},{2,6},{14,10},{3,7},{15,11},{16,20},{28,... | collective-permute-start | bytes 1966088 | tf_op jit(solution)/shard_map/ppermute | solution.py:271
  140.9 32.3 %collective-permute-start.24 = (f32[16,10240]{1,0:T(8,128)S(1)}, f32[16,10240]{1,0:T(8,128)S(1)}, u32[]{:S(2)}, u32[]{:S(2)}) collective-permute-start(f32[16,10240]{1,0:T(8,128)S(1)} %get-tuple-element.39), channel_id=1, source_target_pairs={{0,4},{12,8},{1,5},{13,9},{2,6},{14,10},{3,7},{15,11},{16,20},{28,... | collective-permute-start | bytes 1966088 | tf_op jit(solution)/shard_map/ppermute | solution.py:271
  159.3 19.6 %collective-permute-start.22 = (f32[16,10240]{1,0:T(8,128)S(1)}, f32[16,10240]{1,0:T(8,128)S(1)}, u32[]{:S(2)}, u32[]{:S(2)}) collective-permute-start(f32[16,10240]{1,0:T(8,128)S(1)} %add.59), channel_id=1, source_target_pairs={{8,4},{4,8},{9,5},{5,9},{10,6},{6,10},{11,7},{7,11},{24,20},{20,24... | collective-permute-start | bytes 1966088 | tf_op jit(solution)/shard_map/ppermute | solution.py:271
  161.5 31.3 %collective-permute-start.16 = (f32[16,10240]{1,0:T(8,128)S(1)}, f32[16,10240]{1,0:T(8,128)S(1)}, u32[]{:S(2)}, u32[]{:S(2)}) collective-permute-start(f32[16,10240]{1,0:T(8,128)S(1)} %add.57), channel_id=1, source_target_pairs={{8,4},{4,8},{9,5},{5,9},{10,6},{6,10},{11,7},{7,11},{24,20},{20,24... | collective-permute-start | bytes 1966088 | tf_op jit(solution)/shard_map/ppermute | solution.py:271
  165.3 27.6 %collective-permute-start.14 = (f32[16,10240]{1,0:T(8,128)S(1)}, f32[16,10240]{1,0:T(8,128)S(1)}, u32[]{:S(2)}, u32[]{:S(2)}) collective-permute-start(f32[16,10240]{1,0:T(8,128)S(1)} %add.55), channel_id=1, source_target_pairs={{4,0},{0,4},{12,8},{8,12},{5,1},{1,5},{13,9},{9,13},{6,2},{2,6},{1... | collective-permute-start | bytes 1966088 | tf_op jit(solution)/shard_map/ppermute | solution.py:271
  173.3 26.9 %collective-permute-start.25 = (f32[16,10240]{1,0:T(8,128)S(1)}, f32[16,10240]{1,0:T(8,128)S(1)}, u32[]{:S(2)}, u32[]{:S(2)}) collective-permute-start(f32[16,10240]{1,0:T(8,128)S(1)} %add.62), channel_id=1, source_target_pairs={{8,4},{4,8},{9,5},{5,9},{10,6},{6,10},{11,7},{7,11},{24,20},{20,24... | collective-permute-start | bytes 1966088 | tf_op jit(solution)/shard_map/ppermute | solution.py:271
  178.9 21.3 %collective-permute-start.23 = (f32[16,10240]{1,0:T(8,128)S(1)}, f32[16,10240]{1,0:T(8,128)S(1)}, u32[]{:S(2)}, u32[]{:S(2)}) collective-permute-start(f32[16,10240]{1,0:T(8,128)S(1)} %add.60), channel_id=1, source_target_pairs={{4,0},{0,4},{12,8},{8,12},{5,1},{1,5},{13,9},{9,13},{6,2},{2,6},{1... | collective-permute-start | bytes 1966088 | tf_op jit(solution)/shard_map/ppermute | solution.py:271
  (3 other events, 2.5 us)

commit v5 on v4

--- a/solution.py
+++ b/solution.py
@@ -7,7 +7,13 @@
 from jax.experimental.pallas import tpu as pltpu
 from jax.sharding import PartitionSpec as P
 
-SHORT = pl.CostEstimate(flops=1, bytes_accessed=1, transcendentals=0)
+
+def cost(size):
+    return pl.CostEstimate(flops=1, bytes_accessed=size, transcendentals=0)
+
+
+SHORT = cost(1)
+LONG = cost(12_000_000)
 HIGHEST = lax.Precision.HIGHEST
 ALONG = (((1,), (1,)), ((), ()))
 ACROSS = (((1,), (0,)), ((), ()))
@@ -55,40 +61,34 @@
 def normal_rows(filter_taps, block_index, epochs, total):
     components, tap_count = filter_taps.shape
     lanes = -(-(total + tap_count) // 128) * 128
-    pad = jnp.zeros((components, lanes - tap_count), jnp.float32)
-    ascending = jnp.concatenate([filter_taps, pad], axis=1)[:, None, :]
-    descending = jnp.concatenate([filter_taps[:, ::-1], pad], axis=1)[:, None, :]
-
-    def kernel(index_ref, ascending_ref, descending_ref, out_ref, forward_ref):
-        rising = jnp.broadcast_to(ascending_ref[0], (epochs, lanes))
-        falling = jnp.broadcast_to(descending_ref[0], (epochs, lanes))
-        for block in range(total // epochs):
-            shift = (block * epochs - (tap_count - 1)) % lanes
-            rolled = pltpu.roll(falling, shift, 1, stride=1, stride_axis=0)
-            forward_ref[block * epochs : (block + 1) * epochs, :] = rolled[:, :total]
-        staggered = pltpu.roll(rising, 0, 1, stride=1, stride_axis=0)
-        backward = pltpu.roll(staggered, index_ref[0] * epochs, 1)[:, :total]
-        rows = jnp.dot(backward, forward_ref[...], precision=HIGHEST, preferred_element_type=jnp.float32)
-        for block in range(total // epochs):
-            out_ref[block, 0] = rows[:, block * epochs : (block + 1) * epochs]
+
+    def kernel(index_ref, taps_ref, out_ref, lag_ref):
+        for c in range(components):
+            row = jnp.concatenate([taps_ref[c : c + 1], jnp.zeros((1, lanes - tap_count), jnp.float32)], axis=1)
+            square = jnp.broadcast_to(row, (epochs, lanes))
+            for block in range(total // epochs):
+                rolled = pltpu.roll(square, block * epochs, 1, stride=1, stride_axis=0)
+                lag_ref[block * epochs : (block + 1) * epochs, :] = rolled[:, :total]
+            staggered = pltpu.roll(square, 0, 1, stride=1, stride_axis=0)
+            weight = pltpu.roll(staggered, index_ref[0] * epochs, 1)[:, :total]
+            rows = lax.dot_general(weight, lag_ref[...], ALONG, precision=HIGHEST, preferred_element_type=jnp.float32)
+            for block in range(total // epochs):
+                out_ref[block, c] = rows[:, block * epochs : (block + 1) * epochs]
 
     return pl.pallas_call(
         kernel,
         grid_spec=pltpu.PrefetchScalarGridSpec(
             num_scalar_prefetch=1,
-            grid=(components,),
-            in_specs=[
-                pl.BlockSpec((1, 1, lanes), lambda c, index: (c, 0, 0)),
-                pl.BlockSpec((1, 1, lanes), lambda c, index: (c, 0, 0)),
-            ],
-            out_specs=pl.BlockSpec((total // epochs, 1, epochs, epochs), lambda c, index: (0, c, 0, 0)),
+            grid=(1,),
+            in_specs=[pl.BlockSpec((components, tap_count), lambda c, index: (0, 0))],
+            out_specs=pl.BlockSpec((total // epochs, components, epochs, epochs), lambda c, index: (0, 0, 0, 0)),
             scratch_shapes=[pltpu.VMEM((total, total), jnp.float32)],
         ),
         out_shape=jax.ShapeDtypeStruct((total // epochs, components, epochs, epochs), jnp.float32),
-        compiler_params=pltpu.CompilerParams(vmem_limit_bytes=(4 << 20) + 4 * total * total),
+        compiler_params=pltpu.CompilerParams(vmem_limit_bytes=(8 << 20) + 6 * total * total),
         cost_estimate=SHORT,
         name="normal_rows",
-    )(jnp.reshape(block_index, (1,)).astype(jnp.int32), ascending, descending)
+    )(jnp.reshape(block_index, (1,)).astype(jnp.int32), filter_taps)
 
 
 def project(tall_high, tall_low, own, chunk, arrivals, shards):
@@ -133,7 +133,7 @@
         ),
         out_shape=jax.ShapeDtypeStruct((slots, rows, samples), jnp.float32),
         compiler_params=pltpu.CompilerParams(vmem_limit_bytes=24 << 20),
-        cost_estimate=SHORT,
+        cost_estimate=LONG,
         name="project",
     )(shards, tall_high, tall_low, own, *pieces)
 
@@ -207,6 +207,28 @@
     )(shares)
 
 
+def total_of(values):
+    rows, coefficients = values[0].shape
+    width = math.gcd(coefficients, 5120)
+
+    def kernel(*refs):
+        value = refs[0][...]
+        for ref in refs[1:-1]:
+            value = value + ref[...]
+        refs[-1][...] = value
+
+    return pl.pallas_call(
+        kernel,
+        grid=(coefficients // width,),
+        in_specs=[pl.BlockSpec((rows, width), lambda p: (0, p)) for _ in values],
+        out_specs=pl.BlockSpec((rows, width), lambda p: (0, p)),
+        out_shape=jax.ShapeDtypeStruct((rows, coefficients), jnp.float32),
+        compiler_params=pltpu.CompilerParams(vmem_limit_bytes=8 << 20),
+        cost_estimate=LONG,
+        name="total_of",
+    )(*values)
+
+
 def step_pairs(length, step, parity):
     pairs = []
     for low in range(parity, length - 1, 2):
@@ -228,25 +250,29 @@
         self.done = 0
         self.latest = [value]
 
-    def step(self, count=1):
-        for _ in range(count):
-            if self.done == self.length - 1:
-                return
+    def step(self, count=1, behind=()):
+        for _ in range(min(count, self.length - 1 - self.done)):
             self.done += 1
             self.latest = []
             for parity in (0, 1):
                 pairs = step_pairs(self.length, self.done, parity)
                 if pairs:
-                    value = lax.ppermute(self.arrived[1 - parity, self.done - 1], "tm", pairs)
+                    value = self.arrived[1 - parity, self.done - 1]
+                    if behind:
+                        value = after(value, *behind)
+                    value = lax.ppermute(value, "tm", pairs)
                     self.arrived[parity, self.done] = value
                     self.latest.append(value)
 
-    def slots(self):
+    def slots(self, behind=()):
         self.step(self.length)
-        return [
+        slots = [
             [self.arrived[key] for key in ((0, slot), (1, self.length - slot)) if key in self.arrived]
             for slot in range(1, self.length)
         ]
+        if behind:
+            slots[-1][-1] = after(slots[-1][-1], *behind)
+        return slots
 
 
 class Reduction:
@@ -257,17 +283,18 @@
         self.left = length - 1
         self.latest = []
 
-    def step(self, count=1):
-        for _ in range(count):
-            if self.left == 0:
-                return
+    def step(self, count=1, behind=()):
+        for _ in range(min(count, self.left)):
             self.latest = []
             for parity in (0, 1):
                 pairs = step_pairs(self.length, self.left, parity)
                 if pairs:
                     value = self.slots[self.left] if parity == 0 else self.slots[self.length - self.left]
                     if (1 - parity, self.left + 1) in self.pending:
-                        value = value + self.pending[1 - parity, self.left + 1]
+                        waiting = self.pending[1 - parity, self.left + 1]
+                        if behind:
+                            waiting = after(waiting, *behind)
+                        value = value + waiting
                     value = lax.ppermute(value, "tm", [(b, a) for a, b in pairs])
                     self.pending[parity, self.left] = value
                     self.latest.append(value)
@@ -275,11 +302,7 @@
 
     def result(self):
         self.step(self.length)
-        value = self.slots[0]
-        for parity in (0, 1):
-            if (parity, 1) in self.pending:
-                value = value + self.pending[parity, 1]
-        return value
+        return total_of([self.slots[0]] + [self.pending[key] for key in ((0, 1), (1, 1)) if key in self.pending])
 
 
 def is_direct(length):
@@ -308,36 +331,41 @@
     rows = columns // chunks
     direction = 1 - 2 * (place % 2)
     shards = (place + direction * jnp.arange(length, dtype=jnp.int32)) % length
+    places = places_of(length)
     taps = normal_rows(filter_taps, place, epochs, length * epochs)
-    places = places_of(length)
     high, low, tall_high, tall_low = split_design(after(design, taps, shards, places))
-    parts = []
-    for chunk in range(chunks):
-        value = own[chunk * rows : (chunk + 1) * rows]
-        if parts:
-            value = after(value, *last_source)
-        gather = Gather(value, length)
-        if chunk == 0:
-            gather.step(length - 2)
-            last_source = gather.latest
-            gather.step()
-        parts.append(gather)
-    results = []
-    for chunk, gather in enumerate(parts):
-        behind = parts[chunk + 1] if chunk + 1 < chunks else (results[-1] if results else None)
-        if behind is not None:
-            behind.step()
-        partial = project(tall_high, tall_low, own, chunk, gather.slots(), shards)
-        if behind is not None:
-            partial = after(partial, *behind.latest)
-            behind.step()
-        projected = add_up(lax.all_gather(partial, "param", axis=0))
-        blocks = exchange(projected, length)
-        if behind is not None:
-            blocks[-1] = after(blocks[-1], *behind.latest)
-            behind.step()
-        results.append(Reduction(multiply(high, low, taps, blocks, places, shards), length))
-    return jnp.concatenate([reduction.result() for reduction in results], axis=0).T
+
+    def summed(partial):
+        return add_up(lax.all_gather(partial, "param", axis=0))
+
+    def multiplied(blocks):
+        return Reduction(multiply(high, low, taps, blocks, places, shards), length)
+
+    first = Gather(own[:rows], length)
+    first.step()
+    first.step(behind=[high])
+    waited = first.latest
+    first.step(length)
+    if chunks == 1:
+        partial = project(tall_high, tall_low, own, 0, first.slots(), shards)
+        return multiplied(exchange(summed(partial), length)).result().T
+    second = Gather(after(own[rows:], *waited), length)
+    second.step()
+    partial = project(tall_high, tall_low, own, 0, first.slots(), shards)
+    projected = summed(partial)
+    second.step(behind=[projected])
+    ahead = multiplied(exchange(projected, length))
+    ahead.step()
+    second.step(length, behind=[ahead.slots[0]])
+    partial = project(tall_high, tall_low, own, 1, second.slots(behind=ahead.latest[:1]), shards)
+    ahead.step()
+    projected = summed(partial)
+    ahead.step(length, behind=[projected])
+    start = ahead.result()
+    trailing = multiplied(exchange(projected, length))
+    trailing.step()
+    trailing.step(behind=[start])
+    return jnp.concatenate([start, trailing.result()], axis=0).T
 
 
 def solution(mesh):

time: 202 us -> 210 us (1.040)
  waiting for transfers between devices: 111 us -> 123 us
  local copies, waits for them, and re-layouts: 7.55 us -> 4.62 us
    ppermute x6, waiting for transfers between devices: 11 us -> 20.1 us  [exchange(): lax.ppermute(value, 'tm', [(i, i ^ by) for i in range(length)])]
    ppermute x10, waiting for transfers between devices: 61.6 us -> 64.4 us  [step(): value = lax.ppermute(value, 'tm', [(b, a) for a, b in pairs])]
    unnamed x18 -> x6, local copies, waits for them, and re-layouts: 5.75 us -> 3.24 us
  transfers between devices with their start and end apart: 26 -> 26, of which waited for: 15 -> 17; matrix products, arithmetic and copies ran while one was open for 1% -> 0% of each run, Pallas kernels for 6% -> 9%
where the time goes in v5:
time: 210 us; the launch traced here: 208 us
  waiting for transfers between devices  123 us (59%)
  starting transfers between devices  48.2 us (23%)
  Pallas kernels  19.1 us (9%)
  blocking collectives  11.6 us (6%)
  local copies, waits for them, and re-layouts  4.62 us (2%)
    ppermute x10, waiting for transfers between devices, step(): value = lax.ppermute(value, 'tm', [(b, a) for a, b in pairs])  64.4 us
    ppermute x10, waiting for transfers between devices, step(): value = lax.ppermute(value, 'tm', pairs)  38.3 us
    ppermute x10, starting transfers between devices, step(): value = lax.ppermute(value, 'tm', pairs)  25.2 us
    ppermute x6, waiting for transfers between devices, exchange(): lax.ppermute(value, 'tm', [(i, i ^ by) for i in range(length)])  20.1 us
    ppermute x10, starting transfers between devices, step(): value = lax.ppermute(value, 'tm', [(b, a) for a, b in pairs])  15.4 us
    all_gather x2, blocking collectives, summed(): return add_up(lax.all_gather(partial, 'param', axis=0))  11.6 us
    ppermute x6, starting transfers between devices, exchange(): lax.ppermute(value, 'tm', [(i, i ^ by) for i in range(length)])  7.64 us
    pallas_call x2, Pallas kernels, multiply(): pl.pallas_call(kernel, grid_spec=pltpu.PrefetchScalarGridSpec(num_scalar_...  7.46 us
  transfers between devices with their start and end apart: 26, of which 17 were waited for; matrix products, arithmetic and copies ran while one was open for 0% of the time, Pallas kernels for 9%

profile of v5, /device:TPU:8, one launch (start us, length us, event | category | flops | bytes accessed | tf_op | source)
XLA Modules:
  0.0 208.4 jit_solution(8978602330950202766)
XLA Ops:
  1.5 5.0 %collective-permute-start.1 = (f32[16,10240]{1,0:T(8,128)S(1)}, f32[16,10240]{1,0:T(8,128)S(1)}, u32[]{:S(2)}, u32[]{:S(2)}) collective-permute-start(f32[16,10240]{1,0:T(8,128)S(1)} %get-tuple-element.51), channel_id=1, source_target_pairs={{4,8},{8,4},{5,9},{9,5},{6,10},{10,6},{7,11},{11,7},{20,24},{24,20... | collective-permute-start | bytes 1966088 | tf_op jit(solution)/shard_map/ppermute | solution.py:263
  7.7 3.2 %copy-done.1 = f32[3,64,10240]{2,1,0:T(8,128)S(1)} copy-done((f32[3,64,10240]{2,1,0:T(8,128)S(1)}, f32[3,64,10240]{2,1,0:T(8,128)}, u32[]{:S(2)}) %copy-start.1) | copy-done | bytes 7864344
  11.0 4.3 %split_design.1 = (bf16[192,10240]{1,0:T(8,128)(2,1)S(1)}, bf16[192,10240]{1,0:T(8,128)(2,1)S(1)}, bf16[10240,192]{1,0:T(8,128)(2,1)S(1)}, bf16[10240,192]{1,0:T(8,128)(2,1)S(1)}) custom-call(f32[3,64,10240]{2,1,0:T(8,128)S(1)} %copy-done.1), custom_call_target="tpu_custom_call" | custom-call | flops 1 | bytes 1 | tf_op jit(solution)/shard_map/split_design/pallas_call | solution.py:48
  15.2 2.7 %collective-permute-done.refs_0_ = f32[16,10240]{1,0:T(8,128)S(1)} collective-permute-done((f32[16,10240]{1,0:T(8,128)S(1)}, f32[16,10240]{1,0:T(8,128)S(1)}, u32[]{:S(2)}, u32[]{:S(2)}) %collective-permute-start) | collective-permute-done | bytes 655392 | tf_op jit(solution)/shard_map/ppermute | solution.py:263
  17.9 3.5 %collective-permute-start.3 = (f32[16,10240]{1,0:T(8,128)S(1)}, f32[16,10240]{1,0:T(8,128)S(1)}, u32[]{:S(2)}, u32[]{:S(2)}) collective-permute-start(f32[16,10240]{1,0:T(8,128)S(1)} %collective-permute-done.refs_0_), channel_id=1, source_target_pairs={{4,8},{8,4},{5,9},{9,5},{6,10},{10,6},{7,11},{11,7},{20,24},{24,20... | collective-permute-start | bytes 1966088 | tf_op jit(solution)/shard_map/ppermute | solution.py:263
  22.8 12.7 %collective-permute-done.3.refs_2_ = f32[16,10240]{1,0:T(8,128)S(1)} collective-permute-done((f32[16,10240]{1,0:T(8,128)S(1)}, f32[16,10240]{1,0:T(8,128)S(1)}, u32[]{:S(2)}, u32[]{:S(2)}) %collective-permute-start.3) | collective-permute-done | bytes 655392 | tf_op jit(solution)/shard_map/ppermute | solution.py:263
  38.9 2.7 %collective-permute-start.11 = (f32[16,10240]{1,0:T(8,128)S(1)}, f32[16,10240]{1,0:T(8,128)S(1)}, u32[]{:S(2)}, u32[]{:S(2)}) collective-permute-start(f32[16,10240]{1,0:T(8,128)S(1)} %get-tuple-element.39), channel_id=1, source_target_pairs={{4,8},{8,4},{5,9},{9,5},{6,10},{10,6},{7,11},{11,7},{20,24},{24,20... | collective-permute-start | bytes 1966088 | tf_op jit(solution)/shard_map/ppermute | solution.py:263
  41.7 10.2 %collective-permute-done.4.refs_3_ = f32[16,10240]{1,0:T(8,128)S(1)} collective-permute-done((f32[16,10240]{1,0:T(8,128)S(1)}, f32[16,10240]{1,0:T(8,128)S(1)}, u32[]{:S(2)}, u32[]{:S(2)}) %collective-permute-start.4) | collective-permute-done | bytes 655392 | tf_op jit(solution)/shard_map/ppermute | solution.py:263
  51.9 2.8 %project.2 = f32[4,16,192]{2,1,0:T(8,128)S(1)} custom-call(s32[4]{0:T(128)S(1)} %and_select_fusion.shard_ref, bf16[10240,192]{1,0:T(8,128)(2,1)S(1)} %get-tuple-element.31.high_ref, bf16[10240,192]{1,0:T(8,128)(2,1)S(1)} %get-tuple-element.32.low_ref, f32[32,10240]{1,0:T(8,128)S(1)} %bitcast.7, f32[16,10240]{1,0:T(8,128)S(1)} %collective-permute-done.refs_0_, ...), custom_call_target="tpu_custom_call" | custom-call | flops 1 | bytes 12000000 | tf_op jit(solution)/shard_map/project/pallas_call | solution.py:121
  54.7 5.8 %all-gather = f32[16,16,192]{2,1,0:T(8,128)S(1)} all-gather(f32[4,16,192]{2,1,0:T(8,128)S(1)} %project.2), channel_id=2, replica_groups=mesh['groups'=2,'tm'=4,'param'=4] {'param'}, dimensions={0}, use_global_device_ids=true | all-gather | bytes 245760 | tf_op jit(solution)/shard_map/all_gather | solution.py:339
  60.5 3.4 %collective-permute-done.10.refs_0_ = f32[16,10240]{1,0:T(8,128)S(1)} collective-permute-done((f32[16,10240]{1,0:T(8,128)S(1)}, f32[16,10240]{1,0:T(8,128)S(1)}, u32[]{:S(2)}, u32[]{:S(2)}) %collective-permute-start.10) | collective-permute-done | bytes 655392 | tf_op jit(solution)/shard_map/ppermute | solution.py:263
  63.9 3.1 %collective-permute-start.13 = (f32[16,10240]{1,0:T(8,128)S(1)}, f32[16,10240]{1,0:T(8,128)S(1)}, u32[]{:S(2)}, u32[]{:S(2)}) collective-permute-start(f32[16,10240]{1,0:T(8,128)S(1)} %collective-permute-done.10.refs_0_), channel_id=1, source_target_pairs={{4,8},{8,4},{5,9},{9,5},{6,10},{10,6},{7,11},{11,7},{20,24},{24,20... | collective-permute-start | bytes 1966088 | tf_op jit(solution)/shard_map/ppermute | solution.py:263
  67.2 2.2 %collective-permute-start.6 = (f32[4,16,192]{2,1,0:T(8,128)S(1)}, f32[4,16,192]{2,1,0:T(8,128)S(1)}, u32[]{:S(2)}, u32[]{:S(2)}) collective-permute-start(f32[4,16,192]{2,1,0:T(8,128)S(1)} %add_up.2.refs_0_), channel_id=1, source_target_pairs={{0,8},{4,12},{8,0},{12,4},{1,9},{5,13},{9,1},{13,5},{2,10},{6,14},... | collective-permute-start | bytes 147464 | tf_op jit(solution)/shard_map/ppermute | solution.py:319
  71.4 12.5 %collective-permute-done.6.refs_2_ = f32[4,16,192]{2,1,0:T(8,128)S(1)} collective-permute-done((f32[4,16,192]{2,1,0:T(8,128)S(1)}, f32[4,16,192]{2,1,0:T(8,128)S(1)}, u32[]{:S(2)}, u32[]{:S(2)}) %collective-permute-start.6) | collective-permute-done | bytes 49184 | tf_op jit(solution)/shard_map/ppermute | solution.py:319
  83.8 2.3 %collective-permute-done.7.refs_3_ = f32[4,16,192]{2,1,0:T(8,128)S(1)} collective-permute-done((f32[4,16,192]{2,1,0:T(8,128)S(1)}, f32[4,16,192]{2,1,0:T(8,128)S(1)}, u32[]{:S(2)}, u32[]{:S(2)}) %collective-permute-start.7) | collective-permute-done | bytes 49184 | tf_op jit(solution)/shard_map/ppermute | solution.py:319
  86.1 3.7 %multiply.2 = (f32[16,10240]{1,0:T(8,128)S(1)}, f32[16,10240]{1,0:T(8,128)S(1)}, f32[16,10240]{1,0:T(8,128)S(1)}, f32[16,10240]{1,0:T(8,128)S(1)}) custom-call(s32[4]{0:T(128)S(1)} %and_select_fusion.shard_ref, s32[4]{0:T(128)S(1)} %iota_xor_fusion.place_ref, bf16[192,10240]{1,0:T(8,128)(2,1)S(1)} %get-tuple-element.29.high_ref, ...), custom_call_target="tpu_custom_call" | custom-call | flops 1 | bytes 1 | tf_op jit(solution)/shard_map/multiply/pallas_call | solution.py:171
  91.2 4.6 %collective-permute-start.12 = (f32[16,10240]{1,0:T(8,128)S(1)}, f32[16,10240]{1,0:T(8,128)S(1)}, u32[]{:S(2)}, u32[]{:S(2)}) collective-permute-start(f32[16,10240]{1,0:T(8,128)S(1)} %collective-permute-done.11.refs_4_), channel_id=1, source_target_pairs={{4,0},{8,12},{5,1},{9,13},{6,2},{10,14},{7,3},{11,15},{20,16},{24,... | collective-permute-start | bytes 1966088 | tf_op jit(solution)/shard_map/ppermute | solution.py:263
  98.5 11.0 %collective-permute-done.8 = f32[16,10240]{1,0:T(8,128)S(1)} collective-permute-done((f32[16,10240]{1,0:T(8,128)S(1)}, f32[16,10240]{1,0:T(8,128)S(1)}, u32[]{:S(2)}, u32[]{:S(2)}) %collective-permute-start.8) | collective-permute-done | bytes 655392 | tf_op jit(solution)/shard_map/ppermute | solution.py:298
  109.5 2.8 %collective-permute-start.9 = (f32[16,10240]{1,0:T(8,128)S(1)}, f32[16,10240]{1,0:T(8,128)S(1)}, u32[]{:S(2)}, u32[]{:S(2)}) collective-permute-start(f32[16,10240]{1,0:T(8,128)S(1)} %add.38), channel_id=1, source_target_pairs={{8,4},{4,8},{9,5},{5,9},{10,6},{6,10},{11,7},{7,11},{24,20},{20,24... | collective-permute-start | bytes 1966088 | tf_op jit(solution)/shard_map/ppermute | solution.py:298
  112.3 9.3 %collective-permute-done.14.refs_3_ = f32[16,10240]{1,0:T(8,128)S(1)} collective-permute-done((f32[16,10240]{1,0:T(8,128)S(1)}, f32[16,10240]{1,0:T(8,128)S(1)}, u32[]{:S(2)}, u32[]{:S(2)}) %collective-permute-start.14) | collective-permute-done | bytes 655392 | tf_op jit(solution)/shard_map/ppermute | solution.py:263
  121.6 2.8 %project.3 = f32[4,16,192]{2,1,0:T(8,128)S(1)} custom-call(s32[4]{0:T(128)S(1)} %and_select_fusion.shard_ref, bf16[10240,192]{1,0:T(8,128)(2,1)S(1)} %get-tuple-element.31.high_ref, bf16[10240,192]{1,0:T(8,128)(2,1)S(1)} %get-tuple-element.32.low_ref, f32[32,10240]{1,0:T(8,128)S(1)} %bitcast.8, f32[16,10240]{1,0:T(8,128)S(1)} %collective-permute-done.10.refs_0_, ...), custom_call_target="tpu_custom_call" | custom-call | flops 1 | bytes 12000000 | tf_op jit(solution)/shard_map/project/pallas_call | solution.py:121
  124.4 5.8 %all-gather.1 = f32[16,16,192]{2,1,0:T(8,128)S(1)} all-gather(f32[4,16,192]{2,1,0:T(8,128)S(1)} %project.3), channel_id=3, replica_groups=mesh['groups'=2,'tm'=4,'param'=4] {'param'}, dimensions={0}, use_global_device_ids=true | all-gather | bytes 245760 | tf_op jit(solution)/shard_map/all_gather | solution.py:339
  130.2 2.5 %collective-permute-start.18 = (f32[4,16,192]{2,1,0:T(8,128)S(1)}, f32[4,16,192]{2,1,0:T(8,128)S(1)}, u32[]{:S(2)}, u32[]{:S(2)}) collective-permute-start(f32[4,16,192]{2,1,0:T(8,128)S(1)} %add_up.3.refs_0_), channel_id=1, source_target_pairs={{0,4},{4,0},{8,12},{12,8},{1,5},{5,1},{9,13},{13,9},{2,6},{6,2},{1... | collective-permute-start | bytes 147464 | tf_op jit(solution)/shard_map/ppermute | solution.py:319
  134.4 2.4 %collective-permute-start.17 = (f32[16,10240]{1,0:T(8,128)S(1)}, f32[16,10240]{1,0:T(8,128)S(1)}, u32[]{:S(2)}, u32[]{:S(2)}) collective-permute-start(f32[16,10240]{1,0:T(8,128)S(1)} %add.40), channel_id=1, source_target_pairs={{8,4},{4,8},{9,5},{5,9},{10,6},{6,10},{11,7},{7,11},{24,20},{20,24... | collective-permute-start | bytes 1966088 | tf_op jit(solution)/shard_map/ppermute | solution.py:298
  138.4 3.0 %collective-permute-done.20.refs_3_ = f32[4,16,192]{2,1,0:T(8,128)S(1)} collective-permute-done((f32[4,16,192]{2,1,0:T(8,128)S(1)}, f32[4,16,192]{2,1,0:T(8,128)S(1)}, u32[]{:S(2)}, u32[]{:S(2)}) %collective-permute-start.20) | collective-permute-done | bytes 49184 | tf_op jit(solution)/shard_map/ppermute | solution.py:319
  141.3 3.7 %multiply.3 = (f32[16,10240]{1,0:T(8,128)S(1)}, f32[16,10240]{1,0:T(8,128)S(1)}, f32[16,10240]{1,0:T(8,128)S(1)}, f32[16,10240]{1,0:T(8,128)S(1)}) custom-call(s32[4]{0:T(128)S(1)} %and_select_fusion.shard_ref, s32[4]{0:T(128)S(1)} %iota_xor_fusion.place_ref, bf16[192,10240]{1,0:T(8,128)(2,1)S(1)} %get-tuple-element.29.high_ref, ...), custom_call_target="tpu_custom_call" | custom-call | flops 1 | bytes 1 | tf_op jit(solution)/shard_map/multiply/pallas_call | solution.py:171
  147.9 6.9 %collective-permute-done.17.refs_2_ = f32[16,10240]{1,0:T(8,128)S(1)} collective-permute-done((f32[16,10240]{1,0:T(8,128)S(1)}, f32[16,10240]{1,0:T(8,128)S(1)}, u32[]{:S(2)}, u32[]{:S(2)}) %collective-permute-start.17) | collective-permute-done | bytes 655392 | tf_op jit(solution)/shard_map/ppermute | solution.py:298
  154.8 8.1 %collective-permute-done.15.refs_1_ = f32[16,10240]{1,0:T(8,128)S(1)} collective-permute-done((f32[16,10240]{1,0:T(8,128)S(1)}, f32[16,10240]{1,0:T(8,128)S(1)}, u32[]{:S(2)}, u32[]{:S(2)}) %collective-permute-start.15) | collective-permute-done | bytes 655392 | tf_op jit(solution)/shard_map/ppermute | solution.py:298
  163.3 13.7 %collective-permute-done.21 = f32[16,10240]{1,0:T(8,128)S(1)} collective-permute-done((f32[16,10240]{1,0:T(8,128)S(1)}, f32[16,10240]{1,0:T(8,128)S(1)}, u32[]{:S(2)}, u32[]{:S(2)}) %collective-permute-start.21) | collective-permute-done | bytes 655392 | tf_op jit(solution)/shard_map/ppermute | solution.py:298
  179.2 9.7 %collective-permute-done.24 = f32[16,10240]{1,0:T(8,128)S(1)} collective-permute-done((f32[16,10240]{1,0:T(8,128)S(1)}, f32[16,10240]{1,0:T(8,128)S(1)}, u32[]{:S(2)}, u32[]{:S(2)}) %collective-permute-start.24) | collective-permute-done | bytes 655392 | tf_op jit(solution)/shard_map/ppermute | solution.py:298
  189.0 2.7 %collective-permute-start.25 = (f32[16,10240]{1,0:T(8,128)S(1)}, f32[16,10240]{1,0:T(8,128)S(1)}, u32[]{:S(2)}, u32[]{:S(2)}) collective-permute-start(f32[16,10240]{1,0:T(8,128)S(1)} %add.43), channel_id=1, source_target_pairs={{8,4},{4,8},{9,5},{5,9},{10,6},{6,10},{11,7},{7,11},{24,20},{20,24... | collective-permute-start | bytes 1966088 | tf_op jit(solution)/shard_map/ppermute | solution.py:298
  191.9 13.7 %collective-permute-done.25.refs_2_ = f32[16,10240]{1,0:T(8,128)S(1)} collective-permute-done((f32[16,10240]{1,0:T(8,128)S(1)}, f32[16,10240]{1,0:T(8,128)S(1)}, u32[]{:S(2)}, u32[]{:S(2)}) %collective-permute-start.25) | collective-permute-done | bytes 655392 | tf_op jit(solution)/shard_map/ppermute | solution.py:298
  (48 shorter events, 25.1 us)
Async XLA Ops:
  0.0 6.5 %copy-start.2 = (f32[3,512]{1,0:T(4,128)S(1)}, f32[3,512]{1,0:T(4,128)}, u32[]{:S(2)}) copy-start(f32[3,512]{1,0:T(4,128)} %taps_ref.1) | copy-start | bytes 18436
  1.4 16.5 %collective-permute-start = (f32[16,10240]{1,0:T(8,128)S(1)}, f32[16,10240]{1,0:T(8,128)S(1)}, u32[]{:S(2)}, u32[]{:S(2)}) collective-permute-start(f32[16,10240]{1,0:T(8,128)S(1)} %get-tuple-element.51), channel_id=1, source_target_pairs={{0,4},{4,0},{8,12},{12,8},{1,5},{5,1},{9,13},{13,9},{2,6},{6,2},{1... | collective-permute-start | bytes 1966088 | tf_op jit(solution)/shard_map/ppermute | solution.py:263
  1.5 19.9 %collective-permute-start.1 = (f32[16,10240]{1,0:T(8,128)S(1)}, f32[16,10240]{1,0:T(8,128)S(1)}, u32[]{:S(2)}, u32[]{:S(2)}) collective-permute-start(f32[16,10240]{1,0:T(8,128)S(1)} %get-tuple-element.51), channel_id=1, source_target_pairs={{4,8},{8,4},{5,9},{9,5},{6,10},{10,6},{7,11},{11,7},{20,24},{24,20... | collective-permute-start | bytes 1966088 | tf_op jit(solution)/shard_map/ppermute | solution.py:263
  7.7 3.2 %copy-start.1 = (f32[3,64,10240]{2,1,0:T(8,128)S(1)}, f32[3,64,10240]{2,1,0:T(8,128)}, u32[]{:S(2)}) copy-start(f32[3,64,10240]{2,1,0:T(8,128)} %design_ref) | copy-start | bytes 23592964
  11.0 40.9 %copy-start = (f32[10240,32]{0,1:T(8,128)S(1)}, f32[10240,32]{0,1:T(8,128)}, u32[]{:S(2)}) copy-start(f32[10240,32]{0,1:T(8,128)} %param.5) | copy-start | bytes 3932164
  17.9 17.5 %collective-permute-start.3 = (f32[16,10240]{1,0:T(8,128)S(1)}, f32[16,10240]{1,0:T(8,128)S(1)}, u32[]{:S(2)}, u32[]{:S(2)}) collective-permute-start(f32[16,10240]{1,0:T(8,128)S(1)} %collective-permute-done.refs_0_), channel_id=1, source_target_pairs={{4,8},{8,4},{5,9},{9,5},{6,10},{10,6},{7,11},{11,7},{20,24},{24,20... | collective-permute-start | bytes 1966088 | tf_op jit(solution)/shard_map/ppermute | solution.py:263
  21.4 15.3 %collective-permute-start.2 = (f32[16,10240]{1,0:T(8,128)S(1)}, f32[16,10240]{1,0:T(8,128)S(1)}, u32[]{:S(2)}, u32[]{:S(2)}) collective-permute-start(f32[16,10240]{1,0:T(8,128)S(1)} %collective-permute-done.1.refs_4_), channel_id=1, source_target_pairs={{4,0},{8,12},{5,1},{9,13},{6,2},{10,14},{7,3},{11,15},{20,16},{24,... | collective-permute-start | bytes 1966088 | tf_op jit(solution)/shard_map/ppermute | solution.py:263
  35.4 16.5 %collective-permute-start.4 = (f32[16,10240]{1,0:T(8,128)S(1)}, f32[16,10240]{1,0:T(8,128)S(1)}, u32[]{:S(2)}, u32[]{:S(2)}) collective-permute-start(f32[16,10240]{1,0:T(8,128)S(1)} %collective-permute-done.3.refs_2_), channel_id=1, source_target_pairs={{4,0},{8,12},{5,1},{9,13},{6,2},{10,14},{7,3},{11,15},{20,16},{24,... | collective-permute-start | bytes 1966088 | tf_op jit(solution)/shard_map/ppermute | solution.py:263
  36.7 27.2 %collective-permute-start.10 = (f32[16,10240]{1,0:T(8,128)S(1)}, f32[16,10240]{1,0:T(8,128)S(1)}, u32[]{:S(2)}, u32[]{:S(2)}) collective-permute-start(f32[16,10240]{1,0:T(8,128)S(1)} %get-tuple-element.39), channel_id=1, source_target_pairs={{0,4},{4,0},{8,12},{12,8},{1,5},{5,1},{9,13},{13,9},{2,6},{6,2},{1... | collective-permute-start | bytes 1966088 | tf_op jit(solution)/shard_map/ppermute | solution.py:263
  38.9 52.3 %collective-permute-start.11 = (f32[16,10240]{1,0:T(8,128)S(1)}, f32[16,10240]{1,0:T(8,128)S(1)}, u32[]{:S(2)}, u32[]{:S(2)}) collective-permute-start(f32[16,10240]{1,0:T(8,128)S(1)} %get-tuple-element.39), channel_id=1, source_target_pairs={{4,8},{8,4},{5,9},{9,5},{6,10},{10,6},{7,11},{11,7},{20,24},{24,20... | collective-permute-start | bytes 1966088 | tf_op jit(solution)/shard_map/ppermute | solution.py:263
  63.9 31.9 %collective-permute-start.13 = (f32[16,10240]{1,0:T(8,128)S(1)}, f32[16,10240]{1,0:T(8,128)S(1)}, u32[]{:S(2)}, u32[]{:S(2)}) collective-permute-start(f32[16,10240]{1,0:T(8,128)S(1)} %collective-permute-done.10.refs_0_), channel_id=1, source_target_pairs={{4,8},{8,4},{5,9},{9,5},{6,10},{10,6},{7,11},{11,7},{20,24},{24,20... | collective-permute-start | bytes 1966088 | tf_op jit(solution)/shard_map/ppermute | solution.py:263
  67.0 4.3 %collective-permute-start.5 = (f32[4,16,192]{2,1,0:T(8,128)S(1)}, f32[4,16,192]{2,1,0:T(8,128)S(1)}, u32[]{:S(2)}, u32[]{:S(2)}) collective-permute-start(f32[4,16,192]{2,1,0:T(8,128)S(1)} %add_up.2.refs_0_), channel_id=1, source_target_pairs={{0,4},{4,0},{8,12},{12,8},{1,5},{5,1},{9,13},{13,9},{2,6},{6,2},{1... | collective-permute-start | bytes 147464 | tf_op jit(solution)/shard_map/ppermute | solution.py:319
  67.2 16.7 %collective-permute-start.6 = (f32[4,16,192]{2,1,0:T(8,128)S(1)}, f32[4,16,192]{2,1,0:T(8,128)S(1)}, u32[]{:S(2)}, u32[]{:S(2)}) collective-permute-start(f32[4,16,192]{2,1,0:T(8,128)S(1)} %add_up.2.refs_0_), channel_id=1, source_target_pairs={{0,8},{4,12},{8,0},{12,4},{1,9},{5,13},{9,1},{13,5},{2,10},{6,14},... | collective-permute-start | bytes 147464 | tf_op jit(solution)/shard_map/ppermute | solution.py:319
  69.4 16.8 %collective-permute-start.7 = (f32[4,16,192]{2,1,0:T(8,128)S(1)}, f32[4,16,192]{2,1,0:T(8,128)S(1)}, u32[]{:S(2)}, u32[]{:S(2)}) collective-permute-start(f32[4,16,192]{2,1,0:T(8,128)S(1)} %add_up.2.refs_0_), channel_id=1, source_target_pairs={{0,12},{4,8},{8,4},{12,0},{1,13},{5,9},{9,5},{13,1},{2,14},{6,10},... | collective-permute-start | bytes 147464 | tf_op jit(solution)/shard_map/ppermute | solution.py:319
  89.9 19.6 %collective-permute-start.8 = (f32[16,10240]{1,0:T(8,128)S(1)}, f32[16,10240]{1,0:T(8,128)S(1)}, u32[]{:S(2)}, u32[]{:S(2)}) collective-permute-start(f32[16,10240]{1,0:T(8,128)S(1)} %get-tuple-element.38), channel_id=1, source_target_pairs={{0,4},{12,8},{1,5},{13,9},{2,6},{14,10},{3,7},{15,11},{16,20},{28,... | collective-permute-start | bytes 1966088 | tf_op jit(solution)/shard_map/ppermute | solution.py:298
  91.2 21.1 %collective-permute-start.12 = (f32[16,10240]{1,0:T(8,128)S(1)}, f32[16,10240]{1,0:T(8,128)S(1)}, u32[]{:S(2)}, u32[]{:S(2)}) collective-permute-start(f32[16,10240]{1,0:T(8,128)S(1)} %collective-permute-done.11.refs_4_), channel_id=1, source_target_pairs={{4,0},{8,12},{5,1},{9,13},{6,2},{10,14},{7,3},{11,15},{20,16},{24,... | collective-permute-start | bytes 1966088 | tf_op jit(solution)/shard_map/ppermute | solution.py:263
  95.8 25.7 %collective-permute-start.14 = (f32[16,10240]{1,0:T(8,128)S(1)}, f32[16,10240]{1,0:T(8,128)S(1)}, u32[]{:S(2)}, u32[]{:S(2)}) collective-permute-start(f32[16,10240]{1,0:T(8,128)S(1)} %collective-permute-done.13.refs_2_), channel_id=1, source_target_pairs={{4,0},{8,12},{5,1},{9,13},{6,2},{10,14},{7,3},{11,15},{20,16},{24,... | collective-permute-start | bytes 1966088 | tf_op jit(solution)/shard_map/ppermute | solution.py:263
  97.2 37.1 %collective-permute-start.16 = (f32[16,10240]{1,0:T(8,128)S(1)}, f32[16,10240]{1,0:T(8,128)S(1)}, u32[]{:S(2)}, u32[]{:S(2)}) collective-permute-start(f32[16,10240]{1,0:T(8,128)S(1)} %get-tuple-element.37), channel_id=1, source_target_pairs={{0,4},{12,8},{1,5},{13,9},{2,6},{14,10},{3,7},{15,11},{16,20},{28,... | collective-permute-start | bytes 1966088 | tf_op jit(solution)/shard_map/ppermute | solution.py:298
  109.5 35.6 %collective-permute-start.9 = (f32[16,10240]{1,0:T(8,128)S(1)}, f32[16,10240]{1,0:T(8,128)S(1)}, u32[]{:S(2)}, u32[]{:S(2)}) collective-permute-start(f32[16,10240]{1,0:T(8,128)S(1)} %add.38), channel_id=1, source_target_pairs={{8,4},{4,8},{9,5},{5,9},{10,6},{6,10},{11,7},{7,11},{24,20},{20,24... | collective-permute-start | bytes 1966088 | tf_op jit(solution)/shard_map/ppermute | solution.py:298
  130.2 6.6 %collective-permute-start.18 = (f32[4,16,192]{2,1,0:T(8,128)S(1)}, f32[4,16,192]{2,1,0:T(8,128)S(1)}, u32[]{:S(2)}, u32[]{:S(2)}) collective-permute-start(f32[4,16,192]{2,1,0:T(8,128)S(1)} %add_up.3.refs_0_), channel_id=1, source_target_pairs={{0,4},{4,0},{8,12},{12,8},{1,5},{5,1},{9,13},{13,9},{2,6},{6,2},{1... | collective-permute-start | bytes 147464 | tf_op jit(solution)/shard_map/ppermute | solution.py:319
  132.7 5.7 %collective-permute-start.19 = (f32[4,16,192]{2,1,0:T(8,128)S(1)}, f32[4,16,192]{2,1,0:T(8,128)S(1)}, u32[]{:S(2)}, u32[]{:S(2)}) collective-permute-start(f32[4,16,192]{2,1,0:T(8,128)S(1)} %add_up.3.refs_0_), channel_id=1, source_target_pairs={{0,8},{4,12},{8,0},{12,4},{1,9},{5,13},{9,1},{13,5},{2,10},{6,14},... | collective-permute-start | bytes 147464 | tf_op jit(solution)/shard_map/ppermute | solution.py:319
  132.7 8.6 %collective-permute-start.20 = (f32[4,16,192]{2,1,0:T(8,128)S(1)}, f32[4,16,192]{2,1,0:T(8,128)S(1)}, u32[]{:S(2)}, u32[]{:S(2)}) collective-permute-start(f32[4,16,192]{2,1,0:T(8,128)S(1)} %add_up.3.refs_0_), channel_id=1, source_target_pairs={{0,12},{4,8},{8,4},{12,0},{1,13},{5,9},{9,5},{13,1},{2,14},{6,10},... | collective-permute-start | bytes 147464 | tf_op jit(solution)/shard_map/ppermute | solution.py:319
  134.4 20.5 %collective-permute-start.17 = (f32[16,10240]{1,0:T(8,128)S(1)}, f32[16,10240]{1,0:T(8,128)S(1)}, u32[]{:S(2)}, u32[]{:S(2)}) collective-permute-start(f32[16,10240]{1,0:T(8,128)S(1)} %add.40), channel_id=1, source_target_pairs={{8,4},{4,8},{9,5},{5,9},{10,6},{6,10},{11,7},{7,11},{24,20},{20,24... | collective-permute-start | bytes 1966088 | tf_op jit(solution)/shard_map/ppermute | solution.py:298
  145.2 17.7 %collective-permute-start.15 = (f32[16,10240]{1,0:T(8,128)S(1)}, f32[16,10240]{1,0:T(8,128)S(1)}, u32[]{:S(2)}, u32[]{:S(2)}) collective-permute-start(f32[16,10240]{1,0:T(8,128)S(1)} %add.39), channel_id=1, source_target_pairs={{4,0},{0,4},{12,8},{8,12},{5,1},{1,5},{13,9},{9,13},{6,2},{2,6},{1... | collective-permute-start | bytes 1966088 | tf_op jit(solution)/shard_map/ppermute | solution.py:298
  145.3 31.7 %collective-permute-start.21 = (f32[16,10240]{1,0:T(8,128)S(1)}, f32[16,10240]{1,0:T(8,128)S(1)}, u32[]{:S(2)}, u32[]{:S(2)}) collective-permute-start(f32[16,10240]{1,0:T(8,128)S(1)} %get-tuple-element.49), channel_id=1, source_target_pairs={{0,4},{12,8},{1,5},{13,9},{2,6},{14,10},{3,7},{15,11},{16,20},{28,... | collective-permute-start | bytes 1966088 | tf_op jit(solution)/shard_map/ppermute | solution.py:298
  146.6 42.4 %collective-permute-start.24 = (f32[16,10240]{1,0:T(8,128)S(1)}, f32[16,10240]{1,0:T(8,128)S(1)}, u32[]{:S(2)}, u32[]{:S(2)}) collective-permute-start(f32[16,10240]{1,0:T(8,128)S(1)} %get-tuple-element.48), channel_id=1, source_target_pairs={{0,4},{12,8},{1,5},{13,9},{2,6},{14,10},{3,7},{15,11},{16,20},{28,... | collective-permute-start | bytes 1966088 | tf_op jit(solution)/shard_map/ppermute | solution.py:298
  177.1 14.7 %collective-permute-start.22 = (f32[16,10240]{1,0:T(8,128)S(1)}, f32[16,10240]{1,0:T(8,128)S(1)}, u32[]{:S(2)}, u32[]{:S(2)}) collective-permute-start(f32[16,10240]{1,0:T(8,128)S(1)} %add.41), channel_id=1, source_target_pairs={{8,4},{4,8},{9,5},{5,9},{10,6},{6,10},{11,7},{7,11},{24,20},{20,24... | collective-permute-start | bytes 1966088 | tf_op jit(solution)/shard_map/ppermute | solution.py:298
  189.0 16.6 %collective-permute-start.25 = (f32[16,10240]{1,0:T(8,128)S(1)}, f32[16,10240]{1,0:T(8,128)S(1)}, u32[]{:S(2)}, u32[]{:S(2)}) collective-permute-start(f32[16,10240]{1,0:T(8,128)S(1)} %add.43), channel_id=1, source_target_pairs={{8,4},{4,8},{9,5},{5,9},{10,6},{6,10},{11,7},{7,11},{24,20},{20,24... | collective-permute-start | bytes 1966088 | tf_op jit(solution)/shard_map/ppermute | solution.py:298
  191.8 15.0 %collective-permute-start.23 = (f32[16,10240]{1,0:T(8,128)S(1)}, f32[16,10240]{1,0:T(8,128)S(1)}, u32[]{:S(2)}, u32[]{:S(2)}) collective-permute-start(f32[16,10240]{1,0:T(8,128)S(1)} %add.42), channel_id=1, source_target_pairs={{4,0},{0,4},{12,8},{8,12},{5,1},{1,5},{13,9},{9,13},{6,2},{2,6},{1... | collective-permute-start | bytes 1966088 | tf_op jit(solution)/shard_map/ppermute | solution.py:298

commit v6 on v5

--- a/solution.py
+++ b/solution.py
@@ -13,7 +13,7 @@
 
 
 SHORT = cost(1)
-LONG = cost(12_000_000)
+LONG = cost(200_000_000)
 HIGHEST = lax.Precision.HIGHEST
 ALONG = (((1,), (1,)), ((), ()))
 ACROSS = (((1,), (0,)), ((), ()))
@@ -33,12 +33,13 @@
     return first[:height] + (first[height:] + last)
 
 
-def split_design(design):
+def split_design(design, earlier):
     components, epochs, coefficients = design.shape
     samples = components * epochs
     width = math.gcd(coefficients, 2048)
 
-    def kernel(design_ref, high_ref, low_ref, tall_high_ref, tall_low_ref):
+    def kernel(design_ref, *refs):
+        high_ref, low_ref, tall_high_ref, tall_low_ref = refs[-4:]
         block = design_ref[...].reshape(samples, width)
         high_ref[...], low_ref[...] = split(block)
         tall_high_ref[...], tall_low_ref[...] = split(block.T)
@@ -48,14 +49,15 @@
     return pl.pallas_call(
         kernel,
         grid=(coefficients // width,),
-        in_specs=[pl.BlockSpec((components, epochs, width), lambda p: (0, 0, p))],
+        in_specs=[pl.BlockSpec((components, epochs, width), lambda p: (0, 0, p))]
+        + [pl.BlockSpec(memory_space=pl.ANY)] * len(earlier),
         out_specs=[pl.BlockSpec((samples, width), lambda p: (0, p))] * 2
         + [pl.BlockSpec((width, samples), lambda p: (p, 0))] * 2,
         out_shape=[flat, flat, tall, tall],
         compiler_params=pltpu.CompilerParams(vmem_limit_bytes=16 << 20),
         cost_estimate=SHORT,
         name="split_design",
-    )(design)
+    )(design, *earlier)
 
 
 def normal_rows(filter_taps, block_index, epochs, total):
@@ -91,7 +93,7 @@
     )(jnp.reshape(block_index, (1,)).astype(jnp.int32), filter_taps)
 
 
-def project(tall_high, tall_low, own, chunk, arrivals, shards):
+def project(tall_high, tall_low, own, chunk, arrivals, shards, tile):
     coefficients, samples = tall_high.shape
     slots = len(arrivals) + 1
     rows = arrivals[0][0].shape[0]
@@ -100,7 +102,7 @@
     pieces = [piece for group in arrivals for piece in group]
 
     def kernel(shard_ref, high_ref, low_ref, own_ref, *refs):
-        *piece_refs, out_ref = refs
+        *piece_refs, _, out_ref = refs
         values = [own_ref[...]]
         start = 0
         for count in counts:
@@ -128,17 +130,18 @@
                 pl.BlockSpec((width, samples), lambda p, shard: (p, 0)),
                 pl.BlockSpec((rows, width), lambda p, shard: (chunk, p)),
             ]
-            + [pl.BlockSpec((rows, width), lambda p, shard: (0, p)) for _ in pieces],
+            + [pl.BlockSpec((rows, width), lambda p, shard: (0, p)) for _ in pieces]
+            + [pl.BlockSpec(memory_space=pl.ANY)],
             out_specs=pl.BlockSpec((slots, rows, samples), lambda p, shard: (0, 0, 0)),
         ),
         out_shape=jax.ShapeDtypeStruct((slots, rows, samples), jnp.float32),
         compiler_params=pltpu.CompilerParams(vmem_limit_bytes=24 << 20),
-        cost_estimate=LONG,
+        cost_estimate=SHORT,
         name="project",
-    )(shards, tall_high, tall_low, own, *pieces)
-
-
-def multiply(high, low, taps, blocks, places, shards):
+    )(shards, tall_high, tall_low, own, *pieces, tile)
+
+
+def multiply(high, low, taps, blocks, places, shards, tile):
     samples, coefficients = high.shape
     _, components, epochs, _ = taps.shape
     slots, rows, _ = blocks[0].shape
@@ -147,7 +150,7 @@
 
     def kernel(shard_ref, place_ref, high_ref, low_ref, taps_ref, *refs):
         block_refs = refs[:count]
-        out_refs = refs[count:-1]
+        out_refs = refs[count + 1 : -1]
         weighted_ref = refs[-1]
 
         @pl.when(pl.program_id(0) == 0)
@@ -178,7 +181,8 @@
                 pl.BlockSpec((samples, width), lambda p, shard, place: (0, p)),
                 pl.BlockSpec(taps.shape, lambda p, shard, place: (0, 0, 0, 0)),
             ]
-            + [pl.BlockSpec((slots, rows, samples), lambda p, shard, place: (0, 0, 0)) for _ in blocks],
+            + [pl.BlockSpec((slots, rows, samples), lambda p, shard, place: (0, 0, 0)) for _ in blocks]
+            + [pl.BlockSpec(memory_space=pl.ANY)],
             out_specs=[pl.BlockSpec((rows, width), lambda p, shard, place: (0, p)) for _ in range(slots)],
             scratch_shapes=[pltpu.VMEM((slots, rows, samples), jnp.float32)],
         ),
@@ -186,7 +190,7 @@
         compiler_params=pltpu.CompilerParams(vmem_limit_bytes=24 << 20),
         cost_estimate=SHORT,
         name="multiply",
-    )(shards, places, high, low, taps, *blocks)
+    )(shards, places, high, low, taps, *blocks, tile)
 
 
 def add_up(shares):
@@ -207,26 +211,26 @@
     )(shares)
 
 
-def total_of(values):
+def total_of(values, tile):
     rows, coefficients = values[0].shape
     width = math.gcd(coefficients, 5120)
 
     def kernel(*refs):
         value = refs[0][...]
-        for ref in refs[1:-1]:
+        for ref in refs[1:-2]:
             value = value + ref[...]
         refs[-1][...] = value
 
     return pl.pallas_call(
         kernel,
         grid=(coefficients // width,),
-        in_specs=[pl.BlockSpec((rows, width), lambda p: (0, p)) for _ in values],
+        in_specs=[pl.BlockSpec((rows, width), lambda p: (0, p)) for _ in values] + [pl.BlockSpec(memory_space=pl.ANY)],
         out_specs=pl.BlockSpec((rows, width), lambda p: (0, p)),
         out_shape=jax.ShapeDtypeStruct((rows, coefficients), jnp.float32),
         compiler_params=pltpu.CompilerParams(vmem_limit_bytes=8 << 20),
         cost_estimate=LONG,
         name="total_of",
-    )(*values)
+    )(*values, tile)
 
 
 def step_pairs(length, step, parity):
@@ -239,8 +243,20 @@
     return pairs
 
 
-def after(value, *others):
-    return lax.optimization_barrier((value,) + others)[0]
+def mark(tile, *values):
+    count = len(values)
+
+    def kernel(tile_ref, *refs):
+        refs[count][...] = tile_ref[...]
+
+    return pl.pallas_call(
+        kernel,
+        in_specs=[pl.BlockSpec(memory_space=pltpu.VMEM)] + [pl.BlockSpec(memory_space=pl.ANY)] * count,
+        out_shape=jax.ShapeDtypeStruct(tile.shape, tile.dtype),
+        compiler_params=pltpu.CompilerParams(vmem_limit_bytes=1 << 20),
+        cost_estimate=LONG,
+        name="mark",
+    )(tile, *values)
 
 
 class Gather:
@@ -248,31 +264,28 @@
         self.length = length
         self.arrived = {(0, 0): value, (1, 0): value}
         self.done = 0
-        self.latest = [value]
-
-    def step(self, count=1, behind=()):
+
+    def step(self, count=1):
         for _ in range(min(count, self.length - 1 - self.done)):
             self.done += 1
-            self.latest = []
             for parity in (0, 1):
                 pairs = step_pairs(self.length, self.done, parity)
                 if pairs:
-                    value = self.arrived[1 - parity, self.done - 1]
-                    if behind:
-                        value = after(value, *behind)
-                    value = lax.ppermute(value, "tm", pairs)
-                    self.arrived[parity, self.done] = value
-                    self.latest.append(value)
-
-    def slots(self, behind=()):
+                    self.arrived[parity, self.done] = lax.ppermute(self.arrived[1 - parity, self.done - 1], "tm", pairs)
+
+    def tie(self, tile, parities=(0, 1)):
+        for parity in parities:
+            if (parity, self.done) in self.arrived:
+                tile, value = lax.optimization_barrier((tile, self.arrived[parity, self.done]))
+                self.arrived[parity, self.done] = value
+        return tile
+
+    def slots(self):
         self.step(self.length)
-        slots = [
+        return [
             [self.arrived[key] for key in ((0, slot), (1, self.length - slot)) if key in self.arrived]
             for slot in range(1, self.length)
         ]
-        if behind:
-            slots[-1][-1] = after(slots[-1][-1], *behind)
-        return slots
 
 
 class Reduction:
@@ -280,29 +293,30 @@
         self.length = length
         self.slots = slots
         self.pending = {}
-        self.left = length - 1
-        self.latest = []
-
-    def step(self, count=1, behind=()):
-        for _ in range(min(count, self.left)):
-            self.latest = []
+        self.left = length
+
+    def step(self, count=1):
+        for _ in range(min(count, self.left - 1)):
+            self.left -= 1
             for parity in (0, 1):
                 pairs = step_pairs(self.length, self.left, parity)
                 if pairs:
                     value = self.slots[self.left] if parity == 0 else self.slots[self.length - self.left]
                     if (1 - parity, self.left + 1) in self.pending:
-                        waiting = self.pending[1 - parity, self.left + 1]
-                        if behind:
-                            waiting = after(waiting, *behind)
-                        value = value + waiting
-                    value = lax.ppermute(value, "tm", [(b, a) for a, b in pairs])
-                    self.pending[parity, self.left] = value
-                    self.latest.append(value)
-            self.left -= 1
-
-    def result(self):
+                        value = value + self.pending[1 - parity, self.left + 1]
+                    self.pending[parity, self.left] = lax.ppermute(value, "tm", [(b, a) for a, b in pairs])
+
+    def tie(self, tile, parities=(0, 1)):
+        for parity in parities:
+            if (parity, self.left) in self.pending:
+                tile, value = lax.optimization_barrier((tile, self.pending[parity, self.left]))
+                self.pending[parity, self.left] = value
+        return tile
+
+    def result(self, tile):
         self.step(self.length)
-        return total_of([self.slots[0]] + [self.pending[key] for key in ((0, 1), (1, 1)) if key in self.pending])
+        waiting = [self.pending[key] for key in ((0, 1), (1, 1)) if key in self.pending]
+        return total_of([self.slots[0]] + waiting, tile)
 
 
 def is_direct(length):
@@ -333,39 +347,57 @@
     shards = (place + direction * jnp.arange(length, dtype=jnp.int32)) % length
     places = places_of(length)
     taps = normal_rows(filter_taps, place, epochs, length * epochs)
-    high, low, tall_high, tall_low = split_design(after(design, taps, shards, places))
+    tile = jnp.zeros((8, 128), jnp.float32)
+    high, low, tall_high, tall_low = split_design(design, [taps, shards, places, tile])
 
     def summed(partial):
         return add_up(lax.all_gather(partial, "param", axis=0))
 
-    def multiplied(blocks):
-        return Reduction(multiply(high, low, taps, blocks, places, shards), length)
+    def multiplied(blocks, tile):
+        slots = multiply(high, low, taps, blocks, places, shards, tile)
+        tile, *slots = lax.optimization_barrier((tile, *slots))
+        return Reduction(slots, length), tile
 
     first = Gather(own[:rows], length)
     first.step()
-    first.step(behind=[high])
-    waited = first.latest
+    tile, taps, shards, places, high, low = lax.optimization_barrier((tile, taps, shards, places, high, low))
+    tile = first.tie(tile)
+    first.step()
+    if chunks == 1:
+        partial = project(tall_high, tall_low, own, 0, first.slots(), shards, tile)
+        ahead, tile = multiplied(exchange(summed(partial), length), tile)
+        return ahead.result(tile).T
+    tile = first.tie(tile, (1,))
     first.step(length)
-    if chunks == 1:
-        partial = project(tall_high, tall_low, own, 0, first.slots(), shards)
-        return multiplied(exchange(summed(partial), length)).result().T
-    second = Gather(after(own[rows:], *waited), length)
+    tile = mark(tile)
+    tile, value = lax.optimization_barrier((tile, own[rows:]))
+    second = Gather(value, length)
     second.step()
-    partial = project(tall_high, tall_low, own, 0, first.slots(), shards)
+    partial = project(tall_high, tall_low, own, 0, first.slots(), shards, tile)
     projected = summed(partial)
-    second.step(behind=[projected])
-    ahead = multiplied(exchange(projected, length))
+    blocks = exchange(projected, length)
+    tile, *blocks = lax.optimization_barrier((tile, *blocks))
+    tile = second.tie(tile)
+    second.step()
+    ahead, tile = multiplied(blocks, mark(tile))
     ahead.step()
-    second.step(length, behind=[ahead.slots[0]])
-    partial = project(tall_high, tall_low, own, 1, second.slots(behind=ahead.latest[:1]), shards)
+    tile = second.tie(tile)
+    second.step(length)
+    tile = ahead.tie(mark(tile), (0,))
     ahead.step()
+    partial = project(tall_high, tall_low, own, 1, second.slots(), shards, mark(tile))
     projected = summed(partial)
-    ahead.step(length, behind=[projected])
-    start = ahead.result()
-    trailing = multiplied(exchange(projected, length))
+    blocks = exchange(projected, length)
+    tile = ahead.tie(mark(tile, projected))
+    ahead.step(length)
+    trailing, tile = multiplied(blocks, mark(tile))
     trailing.step()
-    trailing.step(behind=[start])
-    return jnp.concatenate([start, trailing.result()], axis=0).T
+    tile = ahead.tie(tile)
+    start = ahead.result(tile)
+    tile, start = lax.optimization_barrier((tile, start))
+    tile = trailing.tie(tile)
+    trailing.step()
+    return jnp.concatenate([start, trailing.result(tile)], axis=0).T
 
 
 def solution(mesh):

time: 210 us -> 186 us (0.89)
  waiting for transfers between devices: 123 us -> 96.1 us
  starting transfers between devices: 48.2 us -> 50.4 us
    ppermute x20, waiting for transfers between devices: 103 us -> 89.2 us  [the longest x10 52.5 us: step(): lax.ppermute(value, 'tm', [(b, a) for a, b in pairs])]
    ppermute x6, waiting for transfers between devices: 20.1 us -> 6.87 us  [exchange(): lax.ppermute(value, 'tm', [(i, i ^ by) for i in range(length)])]
  transfers between devices with their start and end apart: 26 -> 26, of which waited for: 17 -> 18; matrix products, arithmetic and copies ran while one was open for 0% -> 0% of each run, Pallas kernels for 9% -> 10%
where the time goes in v6:
time: 186 us; the launch traced here: 184 us
  waiting for transfers between devices  96.1 us (52%)
  starting transfers between devices  50.4 us (27%)
  Pallas kernels  19.3 us (10%)
  blocking collectives  11.6 us (6%)
  local copies, waits for them, and re-layouts  4.62 us (2%)
    ppermute x10, waiting for transfers between devices, step(): lax.ppermute(value, 'tm', [(b, a) for a, b in pairs])  52.5 us
    ppermute x10, waiting for transfers between devices, step(): lax.ppermute(self.arrived[1 - parity, self.done - 1], 'tm', pairs)  36.8 us
    ppermute x10, starting transfers between devices, step(): lax.ppermute(self.arrived[1 - parity, self.done - 1], 'tm', pairs)  22.1 us
    ppermute x10, starting transfers between devices, step(): lax.ppermute(value, 'tm', [(b, a) for a, b in pairs])  20.1 us
    all_gather x2, blocking collectives, summed(): return add_up(lax.all_gather(partial, 'param', axis=0))  11.6 us
    ppermute x6, starting transfers between devices, exchange(): lax.ppermute(value, 'tm', [(i, i ^ by) for i in range(length)])  8.21 us
    pallas_call x2, Pallas kernels, multiply(): pl.pallas_call(kernel, grid_spec=pltpu.PrefetchScalarGridSpec(num_scalar_...  7.46 us
    ppermute x6, waiting for transfers between devices, exchange(): lax.ppermute(value, 'tm', [(i, i ^ by) for i in range(length)])  6.87 us
  transfers between devices with their start and end apart: 26, of which 18 were waited for; matrix products, arithmetic and copies ran while one was open for 0% of the time, Pallas kernels for 10%

profile of v6, /device:TPU:8, one launch (start us, length us, event | category | flops | bytes accessed | tf_op | source)
XLA Modules:
  0.0 184.0 jit_solution(8347969734475995152)
XLA Ops:
  1.5 5.0 %collective-permute-start.1 = (f32[16,10240]{1,0:T(8,128)S(1)}, f32[16,10240]{1,0:T(8,128)S(1)}, u32[]{:S(2)}, u32[]{:S(2)}) collective-permute-start(f32[16,10240]{1,0:T(8,128)S(1)} %get-tuple-element.132), channel_id=1, source_target_pairs={{4,8},{8,4},{5,9},{9,5},{6,10},{10,6},{7,11},{11,7},{20,24},{24,20... | collective-permute-start | bytes 1966088 | tf_op jit(solution)/shard_map/ppermute | solution.py:274
  7.7 3.2 %copy-done.1 = f32[3,64,10240]{2,1,0:T(8,128)S(1)} copy-done((f32[3,64,10240]{2,1,0:T(8,128)S(1)}, f32[3,64,10240]{2,1,0:T(8,128)}, u32[]{:S(2)}) %copy-start.1) | copy-done | bytes 7864344
  11.0 4.3 %split_design.1 = (bf16[192,10240]{1,0:T(8,128)(2,1)S(1)}, bf16[192,10240]{1,0:T(8,128)(2,1)S(1)}, bf16[10240,192]{1,0:T(8,128)(2,1)S(1)}, bf16[10240,192]{1,0:T(8,128)(2,1)S(1)}) custom-call(f32[3,64,10240]{2,1,0:T(8,128)S(1)} %copy-done.1, f32[4,3,64,64]{3,2,1,0:T(8,128)S(1)} %normal_rows.1.refs_0_.taps_ref, s32[4]{0:T(128)S(1)} %get-tuple-element.76.refs_1_.shard_ref, ...), custom_call_target="tpu_custom_call" | custom-call | flops 1 | bytes 1 | tf_op jit(solution)/shard_map/split_design/pallas_call | solution.py:49
  15.2 2.7 %collective-permute-done.refs_0_ = f32[16,10240]{1,0:T(8,128)S(1)} collective-permute-done((f32[16,10240]{1,0:T(8,128)S(1)}, f32[16,10240]{1,0:T(8,128)S(1)}, u32[]{:S(2)}, u32[]{:S(2)}) %collective-permute-start) | collective-permute-done | bytes 655392 | tf_op jit(solution)/shard_map/ppermute | solution.py:274
  17.9 3.5 %collective-permute-start.2 = (f32[16,10240]{1,0:T(8,128)S(1)}, f32[16,10240]{1,0:T(8,128)S(1)}, u32[]{:S(2)}, u32[]{:S(2)}) collective-permute-start(f32[16,10240]{1,0:T(8,128)S(1)} %collective-permute-done.refs_0_), channel_id=1, source_target_pairs={{4,8},{8,4},{5,9},{9,5},{6,10},{10,6},{7,11},{11,7},{20,24},{24,20... | collective-permute-start | bytes 1966088 | tf_op jit(solution)/shard_map/ppermute | solution.py:274
  22.8 12.7 %collective-permute-done.2.refs_2_ = f32[16,10240]{1,0:T(8,128)S(1)} collective-permute-done((f32[16,10240]{1,0:T(8,128)S(1)}, f32[16,10240]{1,0:T(8,128)S(1)}, u32[]{:S(2)}, u32[]{:S(2)}) %collective-permute-start.2) | collective-permute-done | bytes 655392 | tf_op jit(solution)/shard_map/ppermute | solution.py:274
  36.8 3.5 %collective-permute-start.9 = (f32[16,10240]{1,0:T(8,128)S(1)}, f32[16,10240]{1,0:T(8,128)S(1)}, u32[]{:S(2)}, u32[]{:S(2)}) collective-permute-start(f32[16,10240]{1,0:T(8,128)S(1)} %get-tuple-element.82), channel_id=1, source_target_pairs={{4,8},{8,4},{5,9},{9,5},{6,10},{10,6},{7,11},{11,7},{20,24},{24,20... | collective-permute-start | bytes 1966088 | tf_op jit(solution)/shard_map/ppermute | solution.py:274
  40.3 11.5 %collective-permute-done.4.refs_3_ = f32[16,10240]{1,0:T(8,128)S(1)} collective-permute-done((f32[16,10240]{1,0:T(8,128)S(1)}, f32[16,10240]{1,0:T(8,128)S(1)}, u32[]{:S(2)}, u32[]{:S(2)}) %collective-permute-start.4) | collective-permute-done | bytes 655392 | tf_op jit(solution)/shard_map/ppermute | solution.py:274
  51.9 2.8 %project.2 = f32[4,16,192]{2,1,0:T(8,128)S(1)} custom-call(s32[4]{0:T(128)S(1)} %get-tuple-element.76.refs_1_.shard_ref, bf16[10240,192]{1,0:T(8,128)(2,1)S(1)} %get-tuple-element.77.high_ref, bf16[10240,192]{1,0:T(8,128)(2,1)S(1)} %get-tuple-element.78.low_ref, f32[32,10240]{1,0:T(8,128)S(1)} %bitcast.7, f32[16,10240]{1,0:T(8,128)S(1)} %collective-permute-done.refs_0_, ...), custom_call_target="tpu_custom_call" | custom-call | flops 1 | bytes 1 | tf_op jit(solution)/shard_map/project/pallas_call | solution.py:123
  54.7 5.8 %all-gather = f32[16,16,192]{2,1,0:T(8,128)S(1)} all-gather(f32[4,16,192]{2,1,0:T(8,128)S(1)} %project.2), channel_id=2, replica_groups=mesh['groups'=2,'tm'=4,'param'=4] {'param'}, dimensions={0}, use_global_device_ids=true | all-gather | bytes 245760 | tf_op jit(solution)/shard_map/all_gather | solution.py:354
  60.5 2.6 %collective-permute-start.5 = (f32[4,16,192]{2,1,0:T(8,128)S(1)}, f32[4,16,192]{2,1,0:T(8,128)S(1)}, u32[]{:S(2)}, u32[]{:S(2)}) collective-permute-start(f32[4,16,192]{2,1,0:T(8,128)S(1)} %add_up.2.refs_0_), channel_id=1, source_target_pairs={{0,4},{4,0},{8,12},{12,8},{1,5},{5,1},{9,13},{13,9},{2,6},{6,2},{1... | collective-permute-start | bytes 147464 | tf_op jit(solution)/shard_map/ppermute | solution.py:333
  66.5 2.8 %collective-permute-done.6.refs_2_ = f32[4,16,192]{2,1,0:T(8,128)S(1)} collective-permute-done((f32[4,16,192]{2,1,0:T(8,128)S(1)}, f32[4,16,192]{2,1,0:T(8,128)S(1)}, u32[]{:S(2)}, u32[]{:S(2)}) %collective-permute-start.6) | collective-permute-done | bytes 49184 | tf_op jit(solution)/shard_map/ppermute | solution.py:333
  69.3 2.0 %collective-permute-done.7.refs_3_ = f32[4,16,192]{2,1,0:T(8,128)S(1)} collective-permute-done((f32[4,16,192]{2,1,0:T(8,128)S(1)}, f32[4,16,192]{2,1,0:T(8,128)S(1)}, u32[]{:S(2)}, u32[]{:S(2)}) %collective-permute-start.7) | collective-permute-done | bytes 49184 | tf_op jit(solution)/shard_map/ppermute | solution.py:333
  71.2 2.9 %collective-permute-start.10 = (f32[16,10240]{1,0:T(8,128)S(1)}, f32[16,10240]{1,0:T(8,128)S(1)}, u32[]{:S(2)}, u32[]{:S(2)}) collective-permute-start(f32[16,10240]{1,0:T(8,128)S(1)} %collective-permute-done.9.refs_4_), channel_id=1, source_target_pairs={{4,0},{8,12},{5,1},{9,13},{6,2},{10,14},{7,3},{11,15},{20,16},{24,... | collective-permute-start | bytes 1966088 | tf_op jit(solution)/shard_map/ppermute | solution.py:274
  74.2 3.0 %collective-permute-start.11 = (f32[16,10240]{1,0:T(8,128)S(1)}, f32[16,10240]{1,0:T(8,128)S(1)}, u32[]{:S(2)}, u32[]{:S(2)}) collective-permute-start(f32[16,10240]{1,0:T(8,128)S(1)} %collective-permute-done.8.refs_0_), channel_id=1, source_target_pairs={{4,8},{8,4},{5,9},{9,5},{6,10},{10,6},{7,11},{11,7},{20,24},{24,20... | collective-permute-start | bytes 1966088 | tf_op jit(solution)/shard_map/ppermute | solution.py:274
  77.2 3.7 %multiply.2 = (f32[16,10240]{1,0:T(8,128)S(1)}, f32[16,10240]{1,0:T(8,128)S(1)}, f32[16,10240]{1,0:T(8,128)S(1)}, f32[16,10240]{1,0:T(8,128)S(1)}) custom-call(s32[4]{0:T(128)S(1)} %get-tuple-element.76.refs_1_.shard_ref, s32[4]{0:T(128)S(1)} %get-tuple-element.85.refs_2_.place_ref, bf16[192,10240]{1,0:T(8,128)(2,1)S(1)} %get-tuple-element.86.high_ref, ...), custom_call_target="tpu_custom_call" | custom-call | flops 1 | bytes 1 | tf_op jit(solution)/shard_map/multiply/pallas_call | solution.py:174
  82.3 4.7 %collective-permute-done.10.refs_1_ = f32[16,10240]{1,0:T(8,128)S(1)} collective-permute-done((f32[16,10240]{1,0:T(8,128)S(1)}, f32[16,10240]{1,0:T(8,128)S(1)}, u32[]{:S(2)}, u32[]{:S(2)}) %collective-permute-start.10) | collective-permute-done | bytes 655392 | tf_op jit(solution)/shard_map/ppermute | solution.py:274
  87.0 4.2 %collective-permute-done.11.refs_2_ = f32[16,10240]{1,0:T(8,128)S(1)} collective-permute-done((f32[16,10240]{1,0:T(8,128)S(1)}, f32[16,10240]{1,0:T(8,128)S(1)}, u32[]{:S(2)}, u32[]{:S(2)}) %collective-permute-start.11) | collective-permute-done | bytes 655392 | tf_op jit(solution)/shard_map/ppermute | solution.py:274
  93.8 6.8 %collective-permute-done.12 = f32[16,10240]{1,0:T(8,128)S(1)} collective-permute-done((f32[16,10240]{1,0:T(8,128)S(1)}, f32[16,10240]{1,0:T(8,128)S(1)}, u32[]{:S(2)}, u32[]{:S(2)}) %collective-permute-start.12) | collective-permute-done | bytes 655392 | tf_op jit(solution)/shard_map/ppermute | solution.py:307
  100.6 2.7 %collective-permute-start.15 = (f32[16,10240]{1,0:T(8,128)S(1)}, f32[16,10240]{1,0:T(8,128)S(1)}, u32[]{:S(2)}, u32[]{:S(2)}) collective-permute-start(f32[16,10240]{1,0:T(8,128)S(1)} %add.38), channel_id=1, source_target_pairs={{8,4},{4,8},{9,5},{5,9},{10,6},{6,10},{11,7},{7,11},{24,20},{20,24... | collective-permute-start | bytes 1966088 | tf_op jit(solution)/shard_map/ppermute | solution.py:307
  104.3 2.9 %project.3 = f32[4,16,192]{2,1,0:T(8,128)S(1)} custom-call(s32[4]{0:T(128)S(1)} %get-tuple-element.76.refs_1_.shard_ref, bf16[10240,192]{1,0:T(8,128)(2,1)S(1)} %get-tuple-element.77.high_ref, bf16[10240,192]{1,0:T(8,128)(2,1)S(1)} %get-tuple-element.78.low_ref, f32[32,10240]{1,0:T(8,128)S(1)} %bitcast.8, f32[16,10240]{1,0:T(8,128)S(1)} %collective-permute-done.8.refs_0_, ...), custom_call_target="tpu_custom_call" | custom-call | flops 1 | bytes 1 | tf_op jit(solution)/shard_map/project/pallas_call | solution.py:123
  107.2 5.8 %all-gather.1 = f32[16,16,192]{2,1,0:T(8,128)S(1)} all-gather(f32[4,16,192]{2,1,0:T(8,128)S(1)} %project.3), channel_id=3, replica_groups=mesh['groups'=2,'tm'=4,'param'=4] {'param'}, dimensions={0}, use_global_device_ids=true | all-gather | bytes 245760 | tf_op jit(solution)/shard_map/all_gather | solution.py:354
  113.0 2.5 %collective-permute-start.16 = (f32[4,16,192]{2,1,0:T(8,128)S(1)}, f32[4,16,192]{2,1,0:T(8,128)S(1)}, u32[]{:S(2)}, u32[]{:S(2)}) collective-permute-start(f32[4,16,192]{2,1,0:T(8,128)S(1)} %add_up.3.refs_0_), channel_id=1, source_target_pairs={{0,4},{4,0},{8,12},{12,8},{1,5},{5,1},{9,13},{13,9},{2,6},{6,2},{1... | collective-permute-start | bytes 147464 | tf_op jit(solution)/shard_map/ppermute | solution.py:333
  117.2 2.9 %collective-permute-start.19 = (f32[16,10240]{1,0:T(8,128)S(1)}, f32[16,10240]{1,0:T(8,128)S(1)}, u32[]{:S(2)}, u32[]{:S(2)}) collective-permute-start(f32[16,10240]{1,0:T(8,128)S(1)} %add.39), channel_id=1, source_target_pairs={{4,0},{0,4},{12,8},{8,12},{5,1},{1,5},{13,9},{9,13},{6,2},{2,6},{1... | collective-permute-start | bytes 1966088 | tf_op jit(solution)/shard_map/ppermute | solution.py:307
  120.2 3.2 %collective-permute-start.20 = (f32[16,10240]{1,0:T(8,128)S(1)}, f32[16,10240]{1,0:T(8,128)S(1)}, u32[]{:S(2)}, u32[]{:S(2)}) collective-permute-start(f32[16,10240]{1,0:T(8,128)S(1)} %add.40), channel_id=1, source_target_pairs={{8,4},{4,8},{9,5},{5,9},{10,6},{6,10},{11,7},{7,11},{24,20},{20,24... | collective-permute-start | bytes 1966088 | tf_op jit(solution)/shard_map/ppermute | solution.py:307
  123.7 3.7 %multiply.3 = (f32[16,10240]{1,0:T(8,128)S(1)}, f32[16,10240]{1,0:T(8,128)S(1)}, f32[16,10240]{1,0:T(8,128)S(1)}, f32[16,10240]{1,0:T(8,128)S(1)}) custom-call(s32[4]{0:T(128)S(1)} %get-tuple-element.76.refs_1_.shard_ref, s32[4]{0:T(128)S(1)} %get-tuple-element.85.refs_2_.place_ref, bf16[192,10240]{1,0:T(8,128)(2,1)S(1)} %get-tuple-element.86.high_ref, ...), custom_call_target="tpu_custom_call" | custom-call | flops 1 | bytes 1 | tf_op jit(solution)/shard_map/multiply/pallas_call | solution.py:174
  130.0 6.9 %collective-permute-done.19.refs_1_ = f32[16,10240]{1,0:T(8,128)S(1)} collective-permute-done((f32[16,10240]{1,0:T(8,128)S(1)}, f32[16,10240]{1,0:T(8,128)S(1)}, u32[]{:S(2)}, u32[]{:S(2)}) %collective-permute-start.19) | collective-permute-done | bytes 655392 | tf_op jit(solution)/shard_map/ppermute | solution.py:307
  138.3 12.7 %collective-permute-done.21 = f32[16,10240]{1,0:T(8,128)S(1)} collective-permute-done((f32[16,10240]{1,0:T(8,128)S(1)}, f32[16,10240]{1,0:T(8,128)S(1)}, u32[]{:S(2)}, u32[]{:S(2)}) %collective-permute-start.21) | collective-permute-done | bytes 655392 | tf_op jit(solution)/shard_map/ppermute | solution.py:307
  151.1 3.2 %collective-permute-start.22 = (f32[16,10240]{1,0:T(8,128)S(1)}, f32[16,10240]{1,0:T(8,128)S(1)}, u32[]{:S(2)}, u32[]{:S(2)}) collective-permute-start(f32[16,10240]{1,0:T(8,128)S(1)} %add.41), channel_id=1, source_target_pairs={{8,4},{4,8},{9,5},{5,9},{10,6},{6,10},{11,7},{7,11},{24,20},{20,24... | collective-permute-start | bytes 1966088 | tf_op jit(solution)/shard_map/ppermute | solution.py:307
  154.2 9.8 %collective-permute-done.24 = f32[16,10240]{1,0:T(8,128)S(1)} collective-permute-done((f32[16,10240]{1,0:T(8,128)S(1)}, f32[16,10240]{1,0:T(8,128)S(1)}, u32[]{:S(2)}, u32[]{:S(2)}) %collective-permute-start.24) | collective-permute-done | bytes 655392 | tf_op jit(solution)/shard_map/ppermute | solution.py:307
  164.1 2.9 %collective-permute-start.25 = (f32[16,10240]{1,0:T(8,128)S(1)}, f32[16,10240]{1,0:T(8,128)S(1)}, u32[]{:S(2)}, u32[]{:S(2)}) collective-permute-start(f32[16,10240]{1,0:T(8,128)S(1)} %add.43), channel_id=1, source_target_pairs={{8,4},{4,8},{9,5},{5,9},{10,6},{6,10},{11,7},{7,11},{24,20},{20,24... | collective-permute-start | bytes 1966088 | tf_op jit(solution)/shard_map/ppermute | solution.py:307
  167.9 13.9 %collective-permute-done.25.refs_2_ = f32[16,10240]{1,0:T(8,128)S(1)} collective-permute-done((f32[16,10240]{1,0:T(8,128)S(1)}, f32[16,10240]{1,0:T(8,128)S(1)}, u32[]{:S(2)}, u32[]{:S(2)}) %collective-permute-start.25) | collective-permute-done | bytes 655392 | tf_op jit(solution)/shard_map/ppermute | solution.py:307
  (54 shorter events, 22.8 us)
Async XLA Ops:
  0.0 6.5 %copy-start.2 = (f32[3,512]{1,0:T(4,128)S(1)}, f32[3,512]{1,0:T(4,128)}, u32[]{:S(2)}) copy-start(f32[3,512]{1,0:T(4,128)} %taps_ref.1) | copy-start | bytes 18436
  1.4 16.5 %collective-permute-start = (f32[16,10240]{1,0:T(8,128)S(1)}, f32[16,10240]{1,0:T(8,128)S(1)}, u32[]{:S(2)}, u32[]{:S(2)}) collective-permute-start(f32[16,10240]{1,0:T(8,128)S(1)} %get-tuple-element.132), channel_id=1, source_target_pairs={{0,4},{4,0},{8,12},{12,8},{1,5},{5,1},{9,13},{13,9},{2,6},{6,2},{1... | collective-permute-start | bytes 1966088 | tf_op jit(solution)/shard_map/ppermute | solution.py:274
  1.5 19.9 %collective-permute-start.1 = (f32[16,10240]{1,0:T(8,128)S(1)}, f32[16,10240]{1,0:T(8,128)S(1)}, u32[]{:S(2)}, u32[]{:S(2)}) collective-permute-start(f32[16,10240]{1,0:T(8,128)S(1)} %get-tuple-element.132), channel_id=1, source_target_pairs={{4,8},{8,4},{5,9},{9,5},{6,10},{10,6},{7,11},{11,7},{20,24},{24,20... | collective-permute-start | bytes 1966088 | tf_op jit(solution)/shard_map/ppermute | solution.py:274
  7.7 3.2 %copy-start.1 = (f32[3,64,10240]{2,1,0:T(8,128)S(1)}, f32[3,64,10240]{2,1,0:T(8,128)}, u32[]{:S(2)}) copy-start(f32[3,64,10240]{2,1,0:T(8,128)} %design_ref.1) | copy-start | bytes 23592964
  11.0 40.9 %copy-start = (f32[10240,32]{0,1:T(8,128)S(1)}, f32[10240,32]{0,1:T(8,128)}, u32[]{:S(2)}) copy-start(f32[10240,32]{0,1:T(8,128)} %param.5) | copy-start | bytes 3932164
  17.9 17.5 %collective-permute-start.2 = (f32[16,10240]{1,0:T(8,128)S(1)}, f32[16,10240]{1,0:T(8,128)S(1)}, u32[]{:S(2)}, u32[]{:S(2)}) collective-permute-start(f32[16,10240]{1,0:T(8,128)S(1)} %collective-permute-done.refs_0_), channel_id=1, source_target_pairs={{4,8},{8,4},{5,9},{9,5},{6,10},{10,6},{7,11},{11,7},{20,24},{24,20... | collective-permute-start | bytes 1966088 | tf_op jit(solution)/shard_map/ppermute | solution.py:274
  21.4 18.9 %collective-permute-start.3 = (f32[16,10240]{1,0:T(8,128)S(1)}, f32[16,10240]{1,0:T(8,128)S(1)}, u32[]{:S(2)}, u32[]{:S(2)}) collective-permute-start(f32[16,10240]{1,0:T(8,128)S(1)} %collective-permute-done.1.refs_4_), channel_id=1, source_target_pairs={{4,0},{8,12},{5,1},{9,13},{6,2},{10,14},{7,3},{11,15},{20,16},{24,... | collective-permute-start | bytes 1966088 | tf_op jit(solution)/shard_map/ppermute | solution.py:274
  35.4 16.5 %collective-permute-start.4 = (f32[16,10240]{1,0:T(8,128)S(1)}, f32[16,10240]{1,0:T(8,128)S(1)}, u32[]{:S(2)}, u32[]{:S(2)}) collective-permute-start(f32[16,10240]{1,0:T(8,128)S(1)} %collective-permute-done.2.refs_2_), channel_id=1, source_target_pairs={{4,0},{8,12},{5,1},{9,13},{6,2},{10,14},{7,3},{11,15},{20,16},{24,... | collective-permute-start | bytes 1966088 | tf_op jit(solution)/shard_map/ppermute | solution.py:274
  36.7 34.5 %collective-permute-start.8 = (f32[16,10240]{1,0:T(8,128)S(1)}, f32[16,10240]{1,0:T(8,128)S(1)}, u32[]{:S(2)}, u32[]{:S(2)}) collective-permute-start(f32[16,10240]{1,0:T(8,128)S(1)} %get-tuple-element.82), channel_id=1, source_target_pairs={{0,4},{4,0},{8,12},{12,8},{1,5},{5,1},{9,13},{13,9},{2,6},{6,2},{1... | collective-permute-start | bytes 1966088 | tf_op jit(solution)/shard_map/ppermute | solution.py:274
  36.8 34.4 %collective-permute-start.9 = (f32[16,10240]{1,0:T(8,128)S(1)}, f32[16,10240]{1,0:T(8,128)S(1)}, u32[]{:S(2)}, u32[]{:S(2)}) collective-permute-start(f32[16,10240]{1,0:T(8,128)S(1)} %get-tuple-element.82), channel_id=1, source_target_pairs={{4,8},{8,4},{5,9},{9,5},{6,10},{10,6},{7,11},{11,7},{20,24},{24,20... | collective-permute-start | bytes 1966088 | tf_op jit(solution)/shard_map/ppermute | solution.py:274
  60.5 5.9 %collective-permute-start.5 = (f32[4,16,192]{2,1,0:T(8,128)S(1)}, f32[4,16,192]{2,1,0:T(8,128)S(1)}, u32[]{:S(2)}, u32[]{:S(2)}) collective-permute-start(f32[4,16,192]{2,1,0:T(8,128)S(1)} %add_up.2.refs_0_), channel_id=1, source_target_pairs={{0,4},{4,0},{8,12},{12,8},{1,5},{5,1},{9,13},{13,9},{2,6},{6,2},{1... | collective-permute-start | bytes 147464 | tf_op jit(solution)/shard_map/ppermute | solution.py:333
  63.1 6.2 %collective-permute-start.6 = (f32[4,16,192]{2,1,0:T(8,128)S(1)}, f32[4,16,192]{2,1,0:T(8,128)S(1)}, u32[]{:S(2)}, u32[]{:S(2)}) collective-permute-start(f32[4,16,192]{2,1,0:T(8,128)S(1)} %add_up.2.refs_0_), channel_id=1, source_target_pairs={{0,8},{4,12},{8,0},{12,4},{1,9},{5,13},{9,1},{13,5},{2,10},{6,14},... | collective-permute-start | bytes 147464 | tf_op jit(solution)/shard_map/ppermute | solution.py:333
  64.2 7.1 %collective-permute-start.7 = (f32[4,16,192]{2,1,0:T(8,128)S(1)}, f32[4,16,192]{2,1,0:T(8,128)S(1)}, u32[]{:S(2)}, u32[]{:S(2)}) collective-permute-start(f32[4,16,192]{2,1,0:T(8,128)S(1)} %add_up.2.refs_0_), channel_id=1, source_target_pairs={{0,12},{4,8},{8,4},{12,0},{1,13},{5,9},{9,5},{13,1},{2,14},{6,10},... | collective-permute-start | bytes 147464 | tf_op jit(solution)/shard_map/ppermute | solution.py:333
  71.2 15.7 %collective-permute-start.10 = (f32[16,10240]{1,0:T(8,128)S(1)}, f32[16,10240]{1,0:T(8,128)S(1)}, u32[]{:S(2)}, u32[]{:S(2)}) collective-permute-start(f32[16,10240]{1,0:T(8,128)S(1)} %collective-permute-done.9.refs_4_), channel_id=1, source_target_pairs={{4,0},{8,12},{5,1},{9,13},{6,2},{10,14},{7,3},{11,15},{20,16},{24,... | collective-permute-start | bytes 1966088 | tf_op jit(solution)/shard_map/ppermute | solution.py:274
  74.2 16.9 %collective-permute-start.11 = (f32[16,10240]{1,0:T(8,128)S(1)}, f32[16,10240]{1,0:T(8,128)S(1)}, u32[]{:S(2)}, u32[]{:S(2)}) collective-permute-start(f32[16,10240]{1,0:T(8,128)S(1)} %collective-permute-done.8.refs_0_), channel_id=1, source_target_pairs={{4,8},{8,4},{5,9},{9,5},{6,10},{10,6},{7,11},{11,7},{20,24},{24,20... | collective-permute-start | bytes 1966088 | tf_op jit(solution)/shard_map/ppermute | solution.py:274
  81.0 19.6 %collective-permute-start.12 = (f32[16,10240]{1,0:T(8,128)S(1)}, f32[16,10240]{1,0:T(8,128)S(1)}, u32[]{:S(2)}, u32[]{:S(2)}) collective-permute-start(f32[16,10240]{1,0:T(8,128)S(1)} %get-tuple-element.102), channel_id=1, source_target_pairs={{0,4},{12,8},{1,5},{13,9},{2,6},{14,10},{3,7},{15,11},{16,20},{28,... | collective-permute-start | bytes 1966088 | tf_op jit(solution)/shard_map/ppermute | solution.py:307
  91.1 13.2 %collective-permute-start.13 = (f32[16,10240]{1,0:T(8,128)S(1)}, f32[16,10240]{1,0:T(8,128)S(1)}, u32[]{:S(2)}, u32[]{:S(2)}) collective-permute-start(f32[16,10240]{1,0:T(8,128)S(1)} %collective-permute-done.11.refs_2_), channel_id=1, source_target_pairs={{4,0},{8,12},{5,1},{9,13},{6,2},{10,14},{7,3},{11,15},{20,16},{24,... | collective-permute-start | bytes 1966088 | tf_op jit(solution)/shard_map/ppermute | solution.py:274
  92.5 24.6 %collective-permute-start.14 = (f32[16,10240]{1,0:T(8,128)S(1)}, f32[16,10240]{1,0:T(8,128)S(1)}, u32[]{:S(2)}, u32[]{:S(2)}) collective-permute-start(f32[16,10240]{1,0:T(8,128)S(1)} %get-tuple-element.106), channel_id=1, source_target_pairs={{0,4},{12,8},{1,5},{13,9},{2,6},{14,10},{3,7},{15,11},{16,20},{28,... | collective-permute-start | bytes 1966088 | tf_op jit(solution)/shard_map/ppermute | solution.py:307
  100.6 16.5 %collective-permute-start.15 = (f32[16,10240]{1,0:T(8,128)S(1)}, f32[16,10240]{1,0:T(8,128)S(1)}, u32[]{:S(2)}, u32[]{:S(2)}) collective-permute-start(f32[16,10240]{1,0:T(8,128)S(1)} %add.38), channel_id=1, source_target_pairs={{8,4},{4,8},{9,5},{5,9},{10,6},{6,10},{11,7},{7,11},{24,20},{20,24... | collective-permute-start | bytes 1966088 | tf_op jit(solution)/shard_map/ppermute | solution.py:307
  113.0 10.4 %collective-permute-start.16 = (f32[4,16,192]{2,1,0:T(8,128)S(1)}, f32[4,16,192]{2,1,0:T(8,128)S(1)}, u32[]{:S(2)}, u32[]{:S(2)}) collective-permute-start(f32[4,16,192]{2,1,0:T(8,128)S(1)} %add_up.3.refs_0_), channel_id=1, source_target_pairs={{0,4},{4,0},{8,12},{12,8},{1,5},{5,1},{9,13},{13,9},{2,6},{6,2},{1... | collective-permute-start | bytes 147464 | tf_op jit(solution)/shard_map/ppermute | solution.py:333
  115.5 7.8 %collective-permute-start.17 = (f32[4,16,192]{2,1,0:T(8,128)S(1)}, f32[4,16,192]{2,1,0:T(8,128)S(1)}, u32[]{:S(2)}, u32[]{:S(2)}) collective-permute-start(f32[4,16,192]{2,1,0:T(8,128)S(1)} %add_up.3.refs_0_), channel_id=1, source_target_pairs={{0,8},{4,12},{8,0},{12,4},{1,9},{5,13},{9,1},{13,5},{2,10},{6,14},... | collective-permute-start | bytes 147464 | tf_op jit(solution)/shard_map/ppermute | solution.py:333
  116.3 7.3 %collective-permute-start.18 = (f32[4,16,192]{2,1,0:T(8,128)S(1)}, f32[4,16,192]{2,1,0:T(8,128)S(1)}, u32[]{:S(2)}, u32[]{:S(2)}) collective-permute-start(f32[4,16,192]{2,1,0:T(8,128)S(1)} %add_up.3.refs_0_), channel_id=1, source_target_pairs={{0,12},{4,8},{8,4},{12,0},{1,13},{5,9},{9,5},{13,1},{2,14},{6,10},... | collective-permute-start | bytes 147464 | tf_op jit(solution)/shard_map/ppermute | solution.py:333
  117.2 19.8 %collective-permute-start.19 = (f32[16,10240]{1,0:T(8,128)S(1)}, f32[16,10240]{1,0:T(8,128)S(1)}, u32[]{:S(2)}, u32[]{:S(2)}) collective-permute-start(f32[16,10240]{1,0:T(8,128)S(1)} %add.39), channel_id=1, source_target_pairs={{4,0},{0,4},{12,8},{8,12},{5,1},{1,5},{13,9},{9,13},{6,2},{2,6},{1... | collective-permute-start | bytes 1966088 | tf_op jit(solution)/shard_map/ppermute | solution.py:307
  120.2 17.8 %collective-permute-start.20 = (f32[16,10240]{1,0:T(8,128)S(1)}, f32[16,10240]{1,0:T(8,128)S(1)}, u32[]{:S(2)}, u32[]{:S(2)}) collective-permute-start(f32[16,10240]{1,0:T(8,128)S(1)} %add.40), channel_id=1, source_target_pairs={{8,4},{4,8},{9,5},{5,9},{10,6},{6,10},{11,7},{7,11},{24,20},{20,24... | collective-permute-start | bytes 1966088 | tf_op jit(solution)/shard_map/ppermute | solution.py:307
  127.4 23.6 %collective-permute-start.21 = (f32[16,10240]{1,0:T(8,128)S(1)}, f32[16,10240]{1,0:T(8,128)S(1)}, u32[]{:S(2)}, u32[]{:S(2)}) collective-permute-start(f32[16,10240]{1,0:T(8,128)S(1)} %get-tuple-element.128), channel_id=1, source_target_pairs={{0,4},{12,8},{1,5},{13,9},{2,6},{14,10},{3,7},{15,11},{16,20},{28,... | collective-permute-start | bytes 1966088 | tf_op jit(solution)/shard_map/ppermute | solution.py:307
  128.7 35.3 %collective-permute-start.24 = (f32[16,10240]{1,0:T(8,128)S(1)}, f32[16,10240]{1,0:T(8,128)S(1)}, u32[]{:S(2)}, u32[]{:S(2)}) collective-permute-start(f32[16,10240]{1,0:T(8,128)S(1)} %get-tuple-element.126), channel_id=1, source_target_pairs={{0,4},{12,8},{1,5},{13,9},{2,6},{14,10},{3,7},{15,11},{16,20},{28,... | collective-permute-start | bytes 1966088 | tf_op jit(solution)/shard_map/ppermute | solution.py:307
  151.1 16.7 %collective-permute-start.22 = (f32[16,10240]{1,0:T(8,128)S(1)}, f32[16,10240]{1,0:T(8,128)S(1)}, u32[]{:S(2)}, u32[]{:S(2)}) collective-permute-start(f32[16,10240]{1,0:T(8,128)S(1)} %add.41), channel_id=1, source_target_pairs={{8,4},{4,8},{9,5},{5,9},{10,6},{6,10},{11,7},{7,11},{24,20},{20,24... | collective-permute-start | bytes 1966088 | tf_op jit(solution)/shard_map/ppermute | solution.py:307
  164.1 17.7 %collective-permute-start.25 = (f32[16,10240]{1,0:T(8,128)S(1)}, f32[16,10240]{1,0:T(8,128)S(1)}, u32[]{:S(2)}, u32[]{:S(2)}) collective-permute-start(f32[16,10240]{1,0:T(8,128)S(1)} %add.43), channel_id=1, source_target_pairs={{8,4},{4,8},{9,5},{5,9},{10,6},{6,10},{11,7},{7,11},{24,20},{20,24... | collective-permute-start | bytes 1966088 | tf_op jit(solution)/shard_map/ppermute | solution.py:307
  167.8 14.7 %collective-permute-start.23 = (f32[16,10240]{1,0:T(8,128)S(1)}, f32[16,10240]{1,0:T(8,128)S(1)}, u32[]{:S(2)}, u32[]{:S(2)}) collective-permute-start(f32[16,10240]{1,0:T(8,128)S(1)} %add.42), channel_id=1, source_target_pairs={{4,0},{0,4},{12,8},{8,12},{5,1},{1,5},{13,9},{9,13},{6,2},{2,6},{1... | collective-permute-start | bytes 1966088 | tf_op jit(solution)/shard_map/ppermute | solution.py:307

commit v7 on v6

--- a/solution.py
+++ b/solution.py
@@ -211,25 +211,29 @@
     )(shares)
 
 
-def total_of(values, tile):
-    rows, coefficients = values[0].shape
+def totals_of(groups, tile):
+    rows, coefficients = groups[0][0].shape
     width = math.gcd(coefficients, 5120)
+    values = [value for group in groups for value in group]
 
     def kernel(*refs):
-        value = refs[0][...]
-        for ref in refs[1:-2]:
-            value = value + ref[...]
-        refs[-1][...] = value
+        start = 0
+        for index, group in enumerate(groups):
+            value = refs[start][...]
+            for ref in refs[start + 1 : start + len(group)]:
+                value = value + ref[...]
+            refs[-1][index * rows : (index + 1) * rows, :] = value
+            start += len(group)
 
     return pl.pallas_call(
         kernel,
         grid=(coefficients // width,),
         in_specs=[pl.BlockSpec((rows, width), lambda p: (0, p)) for _ in values] + [pl.BlockSpec(memory_space=pl.ANY)],
-        out_specs=pl.BlockSpec((rows, width), lambda p: (0, p)),
-        out_shape=jax.ShapeDtypeStruct((rows, coefficients), jnp.float32),
-        compiler_params=pltpu.CompilerParams(vmem_limit_bytes=8 << 20),
+        out_specs=pl.BlockSpec((rows * len(groups), width), lambda p: (0, p)),
+        out_shape=jax.ShapeDtypeStruct((rows * len(groups), coefficients), jnp.float32),
+        compiler_params=pltpu.CompilerParams(vmem_limit_bytes=12 << 20),
         cost_estimate=LONG,
-        name="total_of",
+        name="totals_of",
     )(*values, tile)
 
 
@@ -313,10 +317,9 @@
                 self.pending[parity, self.left] = value
         return tile
 
-    def result(self, tile):
+    def addends(self):
         self.step(self.length)
-        waiting = [self.pending[key] for key in ((0, 1), (1, 1)) if key in self.pending]
-        return total_of([self.slots[0]] + waiting, tile)
+        return [self.slots[0]] + [self.pending[key] for key in ((0, 1), (1, 1)) if key in self.pending]
 
 
 def is_direct(length):
@@ -366,38 +369,37 @@
     if chunks == 1:
         partial = project(tall_high, tall_low, own, 0, first.slots(), shards, tile)
         ahead, tile = multiplied(exchange(summed(partial), length), tile)
-        return ahead.result(tile).T
-    tile = first.tie(tile, (1,))
-    first.step(length)
-    tile = mark(tile)
-    tile, value = lax.optimization_barrier((tile, own[rows:]))
+        return totals_of([ahead.addends()], tile).T
+    tile, value = lax.optimization_barrier((mark(tile), own[rows:]))
     second = Gather(value, length)
     second.step()
-    partial = project(tall_high, tall_low, own, 0, first.slots(), shards, tile)
+    tile = first.tie(tile)
+    first.step(length)
+    tile = second.tie(mark(tile))
+    second.step()
+    partial = project(tall_high, tall_low, own, 0, first.slots(), shards, mark(tile))
     projected = summed(partial)
     blocks = exchange(projected, length)
     tile, *blocks = lax.optimization_barrier((tile, *blocks))
     tile = second.tie(tile)
-    second.step()
+    second.step(length)
     ahead, tile = multiplied(blocks, mark(tile))
-    ahead.step()
-    tile = second.tie(tile)
-    second.step(length)
-    tile = ahead.tie(mark(tile), (0,))
     ahead.step()
     partial = project(tall_high, tall_low, own, 1, second.slots(), shards, mark(tile))
     projected = summed(partial)
     blocks = exchange(projected, length)
-    tile = ahead.tie(mark(tile, projected))
-    ahead.step(length)
+    tile = ahead.tie(mark(tile, projected), (0,))
+    ahead.step()
     trailing, tile = multiplied(blocks, mark(tile))
     trailing.step()
-    tile = ahead.tie(tile)
-    start = ahead.result(tile)
-    tile, start = lax.optimization_barrier((tile, start))
-    tile = trailing.tie(tile)
+    tile = ahead.tie(mark(tile))
+    ahead.step(length)
+    tile = trailing.tie(mark(tile), (0,))
     trailing.step()
-    return jnp.concatenate([start, trailing.result(tile)], axis=0).T
+    tile = trailing.tie(mark(tile))
+    trailing.step(length)
+    tile = ahead.tie(mark(tile))
+    return totals_of([ahead.addends(), trailing.addends()], tile).T
 
 
 def solution(mesh):

time: 186 us -> 195 us (1.048)
  waiting for transfers between devices: 96.1 us -> 109 us
  starting transfers between devices: 50.4 us -> 47.7 us
    ppermute x10, waiting for transfers between devices: 36.8 us -> 43 us  [step(): lax.ppermute(self.arrived[1 - parity, self.done - 1], 'tm', pairs)]
    ppermute x10, waiting for transfers between devices: 52.5 us -> 56.5 us  [step(): lax.ppermute(value, 'tm', [(b, a) for a, b in pairs])]
    ppermute x10, starting transfers between devices: 20.1 us -> 17 us  [step(): lax.ppermute(value, 'tm', [(b, a) for a, b in pairs])]
    ppermute x6, waiting for transfers between devices: 6.87 us -> 9.28 us  [exchange(): lax.ppermute(value, 'tm', [(i, i ^ by) for i in range(length)])]
  transfers between devices with their start and end apart: 26 -> 26, of which waited for: 18 -> 19; matrix products, arithmetic and copies ran while one was open for 0% -> 0% of each run, Pallas kernels for 10% -> 10%
where the time goes in v7:
time: 195 us; the launch traced here: 194 us
  waiting for transfers between devices  109 us (56%)
  starting transfers between devices  47.7 us (24%)
  Pallas kernels  20.1 us (10%)
  blocking collectives  11.6 us (6%)
  local copies, waits for them, and re-layouts  5.3 us (3%)
    ppermute x10, waiting for transfers between devices, step(): lax.ppermute(value, 'tm', [(b, a) for a, b in pairs])  56.5 us
    ppermute x10, waiting for transfers between devices, step(): lax.ppermute(self.arrived[1 - parity, self.done - 1], 'tm', pairs)  43 us
    ppermute x10, starting transfers between devices, step(): lax.ppermute(self.arrived[1 - parity, self.done - 1], 'tm', pairs)  22.3 us
    ppermute x10, starting transfers between devices, step(): lax.ppermute(value, 'tm', [(b, a) for a, b in pairs])  17 us
    all_gather x2, blocking collectives, summed(): return add_up(lax.all_gather(partial, 'param', axis=0))  11.6 us
    ppermute x6, waiting for transfers between devices, exchange(): lax.ppermute(value, 'tm', [(i, i ^ by) for i in range(length)])  9.28 us
    ppermute x6, starting transfers between devices, exchange(): lax.ppermute(value, 'tm', [(i, i ^ by) for i in range(length)])  8.38 us
    pallas_call x2, Pallas kernels, multiply(): pl.pallas_call(kernel, grid_spec=pltpu.PrefetchScalarGridSpec(num_scalar_...  7.48 us
  transfers between devices with their start and end apart: 26, of which 19 were waited for; matrix products, arithmetic and copies ran while one was open for 0% of the time, Pallas kernels for 10%

profile of v7, /device:TPU:8, one launch (start us, length us, event | category | flops | bytes accessed | tf_op | source)
XLA Modules:
  0.0 194.3 jit_solution(15799467728936744052)
XLA Ops:
  1.5 5.0 %collective-permute-start.1 = (f32[16,10240]{1,0:T(8,128)S(1)}, f32[16,10240]{1,0:T(8,128)S(1)}, u32[]{:S(2)}, u32[]{:S(2)}) collective-permute-start(f32[16,10240]{1,0:T(8,128)S(1)} %get-tuple-element.140), channel_id=1, source_target_pairs={{4,8},{8,4},{5,9},{9,5},{6,10},{10,6},{7,11},{11,7},{20,24},{24,20... | collective-permute-start | bytes 1966088 | tf_op jit(solution)/shard_map/ppermute | solution.py:278
  8.4 3.2 %copy-done.1 = f32[3,64,10240]{2,1,0:T(8,128)S(1)} copy-done((f32[3,64,10240]{2,1,0:T(8,128)S(1)}, f32[3,64,10240]{2,1,0:T(8,128)}, u32[]{:S(2)}) %copy-start.1) | copy-done | bytes 7864344
  11.6 4.3 %split_design.1 = (bf16[192,10240]{1,0:T(8,128)(2,1)S(1)}, bf16[192,10240]{1,0:T(8,128)(2,1)S(1)}, bf16[10240,192]{1,0:T(8,128)(2,1)S(1)}, bf16[10240,192]{1,0:T(8,128)(2,1)S(1)}) custom-call(f32[3,64,10240]{2,1,0:T(8,128)S(1)} %copy-done.1, f32[4,3,64,64]{3,2,1,0:T(8,128)S(1)} %normal_rows.1.refs_0_.taps_ref, s32[4]{0:T(128)S(1)} %get-tuple-element.85.refs_1_.shard_ref, ...), custom_call_target="tpu_custom_call" | custom-call | flops 1 | bytes 1 | tf_op jit(solution)/shard_map/split_design/pallas_call | solution.py:49
  17.9 3.0 %collective-permute-done.1.refs_4_ = f32[16,10240]{1,0:T(8,128)S(1)} collective-permute-done((f32[16,10240]{1,0:T(8,128)S(1)}, f32[16,10240]{1,0:T(8,128)S(1)}, u32[]{:S(2)}, u32[]{:S(2)}) %collective-permute-start.1) | collective-permute-done | bytes 655392 | tf_op jit(solution)/shard_map/ppermute | solution.py:278
  22.3 3.6 %collective-permute-start.3 = (f32[16,10240]{1,0:T(8,128)S(1)}, f32[16,10240]{1,0:T(8,128)S(1)}, u32[]{:S(2)}, u32[]{:S(2)}) collective-permute-start(f32[16,10240]{1,0:T(8,128)S(1)} %collective-permute-done.refs_0_), channel_id=1, source_target_pairs={{4,8},{8,4},{5,9},{9,5},{6,10},{10,6},{7,11},{11,7},{20,24},{24,20... | collective-permute-start | bytes 1966088 | tf_op jit(solution)/shard_map/ppermute | solution.py:278
  28.2 9.2 %collective-permute-done.2.refs_1_ = f32[16,10240]{1,0:T(8,128)S(1)} collective-permute-done((f32[16,10240]{1,0:T(8,128)S(1)}, f32[16,10240]{1,0:T(8,128)S(1)}, u32[]{:S(2)}, u32[]{:S(2)}) %collective-permute-start.2) | collective-permute-done | bytes 655392 | tf_op jit(solution)/shard_map/ppermute | solution.py:278
  37.4 4.4 %collective-permute-done.3.refs_2_ = f32[16,10240]{1,0:T(8,128)S(1)} collective-permute-done((f32[16,10240]{1,0:T(8,128)S(1)}, f32[16,10240]{1,0:T(8,128)S(1)}, u32[]{:S(2)}, u32[]{:S(2)}) %collective-permute-start.3) | collective-permute-done | bytes 655392 | tf_op jit(solution)/shard_map/ppermute | solution.py:278
  43.2 8.3 %collective-permute-done.4.refs_0_ = f32[16,10240]{1,0:T(8,128)S(1)} collective-permute-done((f32[16,10240]{1,0:T(8,128)S(1)}, f32[16,10240]{1,0:T(8,128)S(1)}, u32[]{:S(2)}, u32[]{:S(2)}) %collective-permute-start.4) | collective-permute-done | bytes 655392 | tf_op jit(solution)/shard_map/ppermute | solution.py:278
  55.9 3.6 %collective-permute-start.11 = (f32[16,10240]{1,0:T(8,128)S(1)}, f32[16,10240]{1,0:T(8,128)S(1)}, u32[]{:S(2)}, u32[]{:S(2)}) collective-permute-start(f32[16,10240]{1,0:T(8,128)S(1)} %collective-permute-done.4.refs_0_), channel_id=1, source_target_pairs={{4,8},{8,4},{5,9},{9,5},{6,10},{10,6},{7,11},{11,7},{20,24},{24,20... | collective-permute-start | bytes 1966088 | tf_op jit(solution)/shard_map/ppermute | solution.py:278
  59.5 6.0 %collective-permute-done.6.refs_3_ = f32[16,10240]{1,0:T(8,128)S(1)} collective-permute-done((f32[16,10240]{1,0:T(8,128)S(1)}, f32[16,10240]{1,0:T(8,128)S(1)}, u32[]{:S(2)}, u32[]{:S(2)}) %collective-permute-start.6) | collective-permute-done | bytes 655392 | tf_op jit(solution)/shard_map/ppermute | solution.py:278
  65.5 2.8 %project.2 = f32[4,16,192]{2,1,0:T(8,128)S(1)} custom-call(s32[4]{0:T(128)S(1)} %get-tuple-element.85.refs_1_.shard_ref, bf16[10240,192]{1,0:T(8,128)(2,1)S(1)} %get-tuple-element.86.high_ref, bf16[10240,192]{1,0:T(8,128)(2,1)S(1)} %get-tuple-element.87.low_ref, f32[32,10240]{1,0:T(8,128)S(1)} %bitcast.6, f32[16,10240]{1,0:T(8,128)S(1)} %collective-permute-done.refs_0_, ...), custom_call_target="tpu_custom_call" | custom-call | flops 1 | bytes 1 | tf_op jit(solution)/shard_map/project/pallas_call | solution.py:123
  68.3 5.8 %all-gather = f32[16,16,192]{2,1,0:T(8,128)S(1)} all-gather(f32[4,16,192]{2,1,0:T(8,128)S(1)} %project.2), channel_id=2, replica_groups=mesh['groups'=2,'tm'=4,'param'=4] {'param'}, dimensions={0}, use_global_device_ids=true | all-gather | bytes 245760 | tf_op jit(solution)/shard_map/all_gather | solution.py:357
  80.2 2.8 %collective-permute-done.8.refs_2_ = f32[4,16,192]{2,1,0:T(8,128)S(1)} collective-permute-done((f32[4,16,192]{2,1,0:T(8,128)S(1)}, f32[4,16,192]{2,1,0:T(8,128)S(1)}, u32[]{:S(2)}, u32[]{:S(2)}) %collective-permute-start.8) | collective-permute-done | bytes 49184 | tf_op jit(solution)/shard_map/ppermute | solution.py:336
  85.0 3.0 %collective-permute-start.12 = (f32[16,10240]{1,0:T(8,128)S(1)}, f32[16,10240]{1,0:T(8,128)S(1)}, u32[]{:S(2)}, u32[]{:S(2)}) collective-permute-start(f32[16,10240]{1,0:T(8,128)S(1)} %collective-permute-done.11.refs_2_), channel_id=1, source_target_pairs={{4,0},{8,12},{5,1},{9,13},{6,2},{10,14},{7,3},{11,15},{20,16},{24,... | collective-permute-start | bytes 1966088 | tf_op jit(solution)/shard_map/ppermute | solution.py:278
  88.0 3.7 %multiply.2 = (f32[16,10240]{1,0:T(8,128)S(1)}, f32[16,10240]{1,0:T(8,128)S(1)}, f32[16,10240]{1,0:T(8,128)S(1)}, f32[16,10240]{1,0:T(8,128)S(1)}) custom-call(s32[4]{0:T(128)S(1)} %get-tuple-element.85.refs_1_.shard_ref, s32[4]{0:T(128)S(1)} %get-tuple-element.95.refs_2_.place_ref, bf16[192,10240]{1,0:T(8,128)(2,1)S(1)} %get-tuple-element.96.high_ref, ...), custom_call_target="tpu_custom_call" | custom-call | flops 1 | bytes 1 | tf_op jit(solution)/shard_map/multiply/pallas_call | solution.py:174
  93.1 7.7 %collective-permute-done.12.refs_3_ = f32[16,10240]{1,0:T(8,128)S(1)} collective-permute-done((f32[16,10240]{1,0:T(8,128)S(1)}, f32[16,10240]{1,0:T(8,128)S(1)}, u32[]{:S(2)}, u32[]{:S(2)}) %collective-permute-start.12) | collective-permute-done | bytes 655392 | tf_op jit(solution)/shard_map/ppermute | solution.py:278
  100.8 2.8 %project.3 = f32[4,16,192]{2,1,0:T(8,128)S(1)} custom-call(s32[4]{0:T(128)S(1)} %get-tuple-element.85.refs_1_.shard_ref, bf16[10240,192]{1,0:T(8,128)(2,1)S(1)} %get-tuple-element.86.high_ref, bf16[10240,192]{1,0:T(8,128)(2,1)S(1)} %get-tuple-element.87.low_ref, f32[32,10240]{1,0:T(8,128)S(1)} %bitcast.7, f32[16,10240]{1,0:T(8,128)S(1)} %collective-permute-done.4.refs_0_, ...), custom_call_target="tpu_custom_call" | custom-call | flops 1 | bytes 1 | tf_op jit(solution)/shard_map/project/pallas_call | solution.py:123
  103.6 5.8 %all-gather.1 = f32[16,16,192]{2,1,0:T(8,128)S(1)} all-gather(f32[4,16,192]{2,1,0:T(8,128)S(1)} %project.3), channel_id=3, replica_groups=mesh['groups'=2,'tm'=4,'param'=4] {'param'}, dimensions={0}, use_global_device_ids=true | all-gather | bytes 245760 | tf_op jit(solution)/shard_map/all_gather | solution.py:357
  109.4 2.6 %collective-permute-start.14 = (f32[4,16,192]{2,1,0:T(8,128)S(1)}, f32[4,16,192]{2,1,0:T(8,128)S(1)}, u32[]{:S(2)}, u32[]{:S(2)}) collective-permute-start(f32[4,16,192]{2,1,0:T(8,128)S(1)} %add_up.3.refs_0_), channel_id=1, source_target_pairs={{0,4},{4,0},{8,12},{12,8},{1,5},{5,1},{9,13},{13,9},{2,6},{6,2},{1... | collective-permute-start | bytes 147464 | tf_op jit(solution)/shard_map/ppermute | solution.py:336
  114.9 2.9 %collective-permute-start.18 = (f32[16,10240]{1,0:T(8,128)S(1)}, f32[16,10240]{1,0:T(8,128)S(1)}, u32[]{:S(2)}, u32[]{:S(2)}) collective-permute-start(f32[16,10240]{1,0:T(8,128)S(1)} %add.38), channel_id=1, source_target_pairs={{8,4},{4,8},{9,5},{5,9},{10,6},{6,10},{11,7},{7,11},{24,20},{20,24... | collective-permute-start | bytes 1966088 | tf_op jit(solution)/shard_map/ppermute | solution.py:311
  117.9 2.7 %collective-permute-done.16.refs_3_ = f32[4,16,192]{2,1,0:T(8,128)S(1)} collective-permute-done((f32[4,16,192]{2,1,0:T(8,128)S(1)}, f32[4,16,192]{2,1,0:T(8,128)S(1)}, u32[]{:S(2)}, u32[]{:S(2)}) %collective-permute-start.16) | collective-permute-done | bytes 49184 | tf_op jit(solution)/shard_map/ppermute | solution.py:336
  120.6 3.7 %multiply.3 = (f32[16,10240]{1,0:T(8,128)S(1)}, f32[16,10240]{1,0:T(8,128)S(1)}, f32[16,10240]{1,0:T(8,128)S(1)}, f32[16,10240]{1,0:T(8,128)S(1)}) custom-call(s32[4]{0:T(128)S(1)} %get-tuple-element.85.refs_1_.shard_ref, s32[4]{0:T(128)S(1)} %get-tuple-element.95.refs_2_.place_ref, bf16[192,10240]{1,0:T(8,128)(2,1)S(1)} %get-tuple-element.96.high_ref, ...), custom_call_target="tpu_custom_call" | custom-call | flops 1 | bytes 1 | tf_op jit(solution)/shard_map/multiply/pallas_call | solution.py:174
  125.7 7.6 %collective-permute-done.17 = f32[16,10240]{1,0:T(8,128)S(1)} collective-permute-done((f32[16,10240]{1,0:T(8,128)S(1)}, f32[16,10240]{1,0:T(8,128)S(1)}, u32[]{:S(2)}, u32[]{:S(2)}) %collective-permute-start.17) | collective-permute-done | bytes 655392 | tf_op jit(solution)/shard_map/ppermute | solution.py:311
  134.6 12.7 %collective-permute-done.19 = f32[16,10240]{1,0:T(8,128)S(1)} collective-permute-done((f32[16,10240]{1,0:T(8,128)S(1)}, f32[16,10240]{1,0:T(8,128)S(1)}, u32[]{:S(2)}, u32[]{:S(2)}) %collective-permute-start.19) | collective-permute-done | bytes 655392 | tf_op jit(solution)/shard_map/ppermute | solution.py:311
  147.4 2.9 %collective-permute-start.21 = (f32[16,10240]{1,0:T(8,128)S(1)}, f32[16,10240]{1,0:T(8,128)S(1)}, u32[]{:S(2)}, u32[]{:S(2)}) collective-permute-start(f32[16,10240]{1,0:T(8,128)S(1)} %add.39), channel_id=1, source_target_pairs={{8,4},{4,8},{9,5},{5,9},{10,6},{6,10},{11,7},{7,11},{24,20},{20,24... | collective-permute-start | bytes 1966088 | tf_op jit(solution)/shard_map/ppermute | solution.py:311
  150.4 2.9 %collective-permute-start.23 = (f32[16,10240]{1,0:T(8,128)S(1)}, f32[16,10240]{1,0:T(8,128)S(1)}, u32[]{:S(2)}, u32[]{:S(2)}) collective-permute-start(f32[16,10240]{1,0:T(8,128)S(1)} %add.41), channel_id=1, source_target_pairs={{8,4},{4,8},{9,5},{5,9},{10,6},{6,10},{11,7},{7,11},{24,20},{20,24... | collective-permute-start | bytes 1966088 | tf_op jit(solution)/shard_map/ppermute | solution.py:311
  153.5 7.8 %collective-permute-done.20 = f32[16,10240]{1,0:T(8,128)S(1)} collective-permute-done((f32[16,10240]{1,0:T(8,128)S(1)}, f32[16,10240]{1,0:T(8,128)S(1)}, u32[]{:S(2)}, u32[]{:S(2)}) %collective-permute-start.20) | collective-permute-done | bytes 655392 | tf_op jit(solution)/shard_map/ppermute | solution.py:311
  161.4 2.9 %collective-permute-start.25 = (f32[16,10240]{1,0:T(8,128)S(1)}, f32[16,10240]{1,0:T(8,128)S(1)}, u32[]{:S(2)}, u32[]{:S(2)}) collective-permute-start(f32[16,10240]{1,0:T(8,128)S(1)} %add.43), channel_id=1, source_target_pairs={{8,4},{4,8},{9,5},{5,9},{10,6},{6,10},{11,7},{7,11},{24,20},{20,24... | collective-permute-start | bytes 1966088 | tf_op jit(solution)/shard_map/ppermute | solution.py:311
  164.4 2.6 %collective-permute-done.21 = f32[16,10240]{1,0:T(8,128)S(1)} collective-permute-done((f32[16,10240]{1,0:T(8,128)S(1)}, f32[16,10240]{1,0:T(8,128)S(1)}, u32[]{:S(2)}, u32[]{:S(2)}) %collective-permute-start.21) | collective-permute-done | bytes 655392 | tf_op jit(solution)/shard_map/ppermute | solution.py:311
  167.1 8.3 %collective-permute-done.22.refs_1_ = f32[16,10240]{1,0:T(8,128)S(1)} collective-permute-done((f32[16,10240]{1,0:T(8,128)S(1)}, f32[16,10240]{1,0:T(8,128)S(1)}, u32[]{:S(2)}, u32[]{:S(2)}) %collective-permute-start.22) | collective-permute-done | bytes 655392 | tf_op jit(solution)/shard_map/ppermute | solution.py:311
  175.4 5.6 %collective-permute-done.23.refs_2_ = f32[16,10240]{1,0:T(8,128)S(1)} collective-permute-done((f32[16,10240]{1,0:T(8,128)S(1)}, f32[16,10240]{1,0:T(8,128)S(1)}, u32[]{:S(2)}, u32[]{:S(2)}) %collective-permute-start.23) | collective-permute-done | bytes 655392 | tf_op jit(solution)/shard_map/ppermute | solution.py:311
  181.0 11.9 %collective-permute-done.25.refs_5_ = f32[16,10240]{1,0:T(8,128)S(1)} collective-permute-done((f32[16,10240]{1,0:T(8,128)S(1)}, f32[16,10240]{1,0:T(8,128)S(1)}, u32[]{:S(2)}, u32[]{:S(2)}) %collective-permute-start.25) | collective-permute-done | bytes 655392 | tf_op jit(solution)/shard_map/ppermute | solution.py:311
  (57 shorter events, 31.5 us)
Async XLA Ops:
  1.4 16.5 %collective-permute-start = (f32[16,10240]{1,0:T(8,128)S(1)}, f32[16,10240]{1,0:T(8,128)S(1)}, u32[]{:S(2)}, u32[]{:S(2)}) collective-permute-start(f32[16,10240]{1,0:T(8,128)S(1)} %get-tuple-element.140), channel_id=1, source_target_pairs={{0,4},{4,0},{8,12},{12,8},{1,5},{5,1},{9,13},{13,9},{2,6},{6,2},{1... | collective-permute-start | bytes 1966088 | tf_op jit(solution)/shard_map/ppermute | solution.py:278
  1.5 19.5 %collective-permute-start.1 = (f32[16,10240]{1,0:T(8,128)S(1)}, f32[16,10240]{1,0:T(8,128)S(1)}, u32[]{:S(2)}, u32[]{:S(2)}) collective-permute-start(f32[16,10240]{1,0:T(8,128)S(1)} %get-tuple-element.140), channel_id=1, source_target_pairs={{4,8},{8,4},{5,9},{9,5},{6,10},{10,6},{7,11},{11,7},{20,24},{24,20... | collective-permute-start | bytes 1966088 | tf_op jit(solution)/shard_map/ppermute | solution.py:278
  6.5 0.7 copy-start.2
  8.4 3.2 %copy-start.1 = (f32[3,64,10240]{2,1,0:T(8,128)S(1)}, f32[3,64,10240]{2,1,0:T(8,128)}, u32[]{:S(2)}) copy-start(f32[3,64,10240]{2,1,0:T(8,128)} %design_ref.1) | copy-start | bytes 23592964
  11.6 53.9 %copy-start = (f32[10240,32]{0,1:T(8,128)S(1)}, f32[10240,32]{0,1:T(8,128)}, u32[]{:S(2)}) copy-start(f32[10240,32]{0,1:T(8,128)} %param.5) | copy-start | bytes 3932164
  20.9 16.5 %collective-permute-start.2 = (f32[16,10240]{1,0:T(8,128)S(1)}, f32[16,10240]{1,0:T(8,128)S(1)}, u32[]{:S(2)}, u32[]{:S(2)}) collective-permute-start(f32[16,10240]{1,0:T(8,128)S(1)} %collective-permute-done.1.refs_4_), channel_id=1, source_target_pairs={{4,0},{8,12},{5,1},{9,13},{6,2},{10,14},{7,3},{11,15},{20,16},{24,... | collective-permute-start | bytes 1966088 | tf_op jit(solution)/shard_map/ppermute | solution.py:278
  22.3 19.6 %collective-permute-start.3 = (f32[16,10240]{1,0:T(8,128)S(1)}, f32[16,10240]{1,0:T(8,128)S(1)}, u32[]{:S(2)}, u32[]{:S(2)}) collective-permute-start(f32[16,10240]{1,0:T(8,128)S(1)} %collective-permute-done.refs_0_), channel_id=1, source_target_pairs={{4,8},{8,4},{5,9},{9,5},{6,10},{10,6},{7,11},{11,7},{20,24},{24,20... | collective-permute-start | bytes 1966088 | tf_op jit(solution)/shard_map/ppermute | solution.py:278
  25.9 25.5 %collective-permute-start.4 = (f32[16,10240]{1,0:T(8,128)S(1)}, f32[16,10240]{1,0:T(8,128)S(1)}, u32[]{:S(2)}, u32[]{:S(2)}) collective-permute-start(f32[16,10240]{1,0:T(8,128)S(1)} %get-tuple-element.82), channel_id=1, source_target_pairs={{0,4},{4,0},{8,12},{12,8},{1,5},{5,1},{9,13},{13,9},{2,6},{6,2},{1... | collective-permute-start | bytes 1966088 | tf_op jit(solution)/shard_map/ppermute | solution.py:278
  26.0 27.8 %collective-permute-start.5 = (f32[16,10240]{1,0:T(8,128)S(1)}, f32[16,10240]{1,0:T(8,128)S(1)}, u32[]{:S(2)}, u32[]{:S(2)}) collective-permute-start(f32[16,10240]{1,0:T(8,128)S(1)} %get-tuple-element.82), channel_id=1, source_target_pairs={{4,8},{8,4},{5,9},{9,5},{6,10},{10,6},{7,11},{11,7},{20,24},{24,20... | collective-permute-start | bytes 1966088 | tf_op jit(solution)/shard_map/ppermute | solution.py:278
  41.8 23.7 %collective-permute-start.6 = (f32[16,10240]{1,0:T(8,128)S(1)}, f32[16,10240]{1,0:T(8,128)S(1)}, u32[]{:S(2)}, u32[]{:S(2)}) collective-permute-start(f32[16,10240]{1,0:T(8,128)S(1)} %collective-permute-done.3.refs_2_), channel_id=1, source_target_pairs={{4,0},{8,12},{5,1},{9,13},{6,2},{10,14},{7,3},{11,15},{20,16},{24,... | collective-permute-start | bytes 1966088 | tf_op jit(solution)/shard_map/ppermute | solution.py:278
  53.8 31.2 %collective-permute-start.10 = (f32[16,10240]{1,0:T(8,128)S(1)}, f32[16,10240]{1,0:T(8,128)S(1)}, u32[]{:S(2)}, u32[]{:S(2)}) collective-permute-start(f32[16,10240]{1,0:T(8,128)S(1)} %collective-permute-done.5.refs_4_), channel_id=1, source_target_pairs={{4,0},{8,12},{5,1},{9,13},{6,2},{10,14},{7,3},{11,15},{20,16},{24,... | collective-permute-start | bytes 1966088 | tf_op jit(solution)/shard_map/ppermute | solution.py:278
  55.9 29.1 %collective-permute-start.11 = (f32[16,10240]{1,0:T(8,128)S(1)}, f32[16,10240]{1,0:T(8,128)S(1)}, u32[]{:S(2)}, u32[]{:S(2)}) collective-permute-start(f32[16,10240]{1,0:T(8,128)S(1)} %collective-permute-done.4.refs_0_), channel_id=1, source_target_pairs={{4,8},{8,4},{5,9},{9,5},{6,10},{10,6},{7,11},{11,7},{20,24},{24,20... | collective-permute-start | bytes 1966088 | tf_op jit(solution)/shard_map/ppermute | solution.py:278
  74.2 6.1 %collective-permute-start.7 = (f32[4,16,192]{2,1,0:T(8,128)S(1)}, f32[4,16,192]{2,1,0:T(8,128)S(1)}, u32[]{:S(2)}, u32[]{:S(2)}) collective-permute-start(f32[4,16,192]{2,1,0:T(8,128)S(1)} %add_up.2.refs_0_), channel_id=1, source_target_pairs={{0,4},{4,0},{8,12},{12,8},{1,5},{5,1},{9,13},{13,9},{2,6},{6,2},{1... | collective-permute-start | bytes 147464 | tf_op jit(solution)/shard_map/ppermute | solution.py:336
  76.7 6.3 %collective-permute-start.8 = (f32[4,16,192]{2,1,0:T(8,128)S(1)}, f32[4,16,192]{2,1,0:T(8,128)S(1)}, u32[]{:S(2)}, u32[]{:S(2)}) collective-permute-start(f32[4,16,192]{2,1,0:T(8,128)S(1)} %add_up.2.refs_0_), channel_id=1, source_target_pairs={{0,8},{4,12},{8,0},{12,4},{1,9},{5,13},{9,1},{13,5},{2,10},{6,14},... | collective-permute-start | bytes 147464 | tf_op jit(solution)/shard_map/ppermute | solution.py:336
  78.0 7.0 %collective-permute-start.9 = (f32[4,16,192]{2,1,0:T(8,128)S(1)}, f32[4,16,192]{2,1,0:T(8,128)S(1)}, u32[]{:S(2)}, u32[]{:S(2)}) collective-permute-start(f32[4,16,192]{2,1,0:T(8,128)S(1)} %add_up.2.refs_0_), channel_id=1, source_target_pairs={{0,12},{4,8},{8,4},{12,0},{1,13},{5,9},{9,5},{13,1},{2,14},{6,10},... | collective-permute-start | bytes 147464 | tf_op jit(solution)/shard_map/ppermute | solution.py:336
  85.0 15.8 %collective-permute-start.12 = (f32[16,10240]{1,0:T(8,128)S(1)}, f32[16,10240]{1,0:T(8,128)S(1)}, u32[]{:S(2)}, u32[]{:S(2)}) collective-permute-start(f32[16,10240]{1,0:T(8,128)S(1)} %collective-permute-done.11.refs_2_), channel_id=1, source_target_pairs={{4,0},{8,12},{5,1},{9,13},{6,2},{10,14},{7,3},{11,15},{20,16},{24,... | collective-permute-start | bytes 1966088 | tf_op jit(solution)/shard_map/ppermute | solution.py:278
  91.7 23.1 %collective-permute-start.13 = (f32[16,10240]{1,0:T(8,128)S(1)}, f32[16,10240]{1,0:T(8,128)S(1)}, u32[]{:S(2)}, u32[]{:S(2)}) collective-permute-start(f32[16,10240]{1,0:T(8,128)S(1)} %get-tuple-element.111), channel_id=1, source_target_pairs={{0,4},{12,8},{1,5},{13,9},{2,6},{14,10},{3,7},{15,11},{16,20},{28,... | collective-permute-start | bytes 1966088 | tf_op jit(solution)/shard_map/ppermute | solution.py:311
  109.4 8.4 %collective-permute-start.14 = (f32[4,16,192]{2,1,0:T(8,128)S(1)}, f32[4,16,192]{2,1,0:T(8,128)S(1)}, u32[]{:S(2)}, u32[]{:S(2)}) collective-permute-start(f32[4,16,192]{2,1,0:T(8,128)S(1)} %add_up.3.refs_0_), channel_id=1, source_target_pairs={{0,4},{4,0},{8,12},{12,8},{1,5},{5,1},{9,13},{13,9},{2,6},{6,2},{1... | collective-permute-start | bytes 147464 | tf_op jit(solution)/shard_map/ppermute | solution.py:336
  112.0 5.9 %collective-permute-start.15 = (f32[4,16,192]{2,1,0:T(8,128)S(1)}, f32[4,16,192]{2,1,0:T(8,128)S(1)}, u32[]{:S(2)}, u32[]{:S(2)}) collective-permute-start(f32[4,16,192]{2,1,0:T(8,128)S(1)} %add_up.3.refs_0_), channel_id=1, source_target_pairs={{0,8},{4,12},{8,0},{12,4},{1,9},{5,13},{9,1},{13,5},{2,10},{6,14},... | collective-permute-start | bytes 147464 | tf_op jit(solution)/shard_map/ppermute | solution.py:336
  112.5 8.1 %collective-permute-start.16 = (f32[4,16,192]{2,1,0:T(8,128)S(1)}, f32[4,16,192]{2,1,0:T(8,128)S(1)}, u32[]{:S(2)}, u32[]{:S(2)}) collective-permute-start(f32[4,16,192]{2,1,0:T(8,128)S(1)} %add_up.3.refs_0_), channel_id=1, source_target_pairs={{0,12},{4,8},{8,4},{12,0},{1,13},{5,9},{9,5},{13,1},{2,14},{6,10},... | collective-permute-start | bytes 147464 | tf_op jit(solution)/shard_map/ppermute | solution.py:336
  113.5 19.7 %collective-permute-start.17 = (f32[16,10240]{1,0:T(8,128)S(1)}, f32[16,10240]{1,0:T(8,128)S(1)}, u32[]{:S(2)}, u32[]{:S(2)}) collective-permute-start(f32[16,10240]{1,0:T(8,128)S(1)} %get-tuple-element.118), channel_id=1, source_target_pairs={{0,4},{12,8},{1,5},{13,9},{2,6},{14,10},{3,7},{15,11},{16,20},{28,... | collective-permute-start | bytes 1966088 | tf_op jit(solution)/shard_map/ppermute | solution.py:311
  114.9 19.6 %collective-permute-start.18 = (f32[16,10240]{1,0:T(8,128)S(1)}, f32[16,10240]{1,0:T(8,128)S(1)}, u32[]{:S(2)}, u32[]{:S(2)}) collective-permute-start(f32[16,10240]{1,0:T(8,128)S(1)} %add.38), channel_id=1, source_target_pairs={{8,4},{4,8},{9,5},{5,9},{10,6},{6,10},{11,7},{7,11},{24,20},{20,24... | collective-permute-start | bytes 1966088 | tf_op jit(solution)/shard_map/ppermute | solution.py:311
  124.4 23.0 %collective-permute-start.19 = (f32[16,10240]{1,0:T(8,128)S(1)}, f32[16,10240]{1,0:T(8,128)S(1)}, u32[]{:S(2)}, u32[]{:S(2)}) collective-permute-start(f32[16,10240]{1,0:T(8,128)S(1)} %get-tuple-element.122), channel_id=1, source_target_pairs={{0,4},{12,8},{1,5},{13,9},{2,6},{14,10},{3,7},{15,11},{16,20},{28,... | collective-permute-start | bytes 1966088 | tf_op jit(solution)/shard_map/ppermute | solution.py:311
  133.3 28.1 %collective-permute-start.20 = (f32[16,10240]{1,0:T(8,128)S(1)}, f32[16,10240]{1,0:T(8,128)S(1)}, u32[]{:S(2)}, u32[]{:S(2)}) collective-permute-start(f32[16,10240]{1,0:T(8,128)S(1)} %get-tuple-element.124), channel_id=1, source_target_pairs={{0,4},{12,8},{1,5},{13,9},{2,6},{14,10},{3,7},{15,11},{16,20},{28,... | collective-permute-start | bytes 1966088 | tf_op jit(solution)/shard_map/ppermute | solution.py:311
  147.4 19.6 %collective-permute-start.21 = (f32[16,10240]{1,0:T(8,128)S(1)}, f32[16,10240]{1,0:T(8,128)S(1)}, u32[]{:S(2)}, u32[]{:S(2)}) collective-permute-start(f32[16,10240]{1,0:T(8,128)S(1)} %add.39), channel_id=1, source_target_pairs={{8,4},{4,8},{9,5},{5,9},{10,6},{6,10},{11,7},{7,11},{24,20},{20,24... | collective-permute-start | bytes 1966088 | tf_op jit(solution)/shard_map/ppermute | solution.py:311
  150.4 30.6 %collective-permute-start.23 = (f32[16,10240]{1,0:T(8,128)S(1)}, f32[16,10240]{1,0:T(8,128)S(1)}, u32[]{:S(2)}, u32[]{:S(2)}) collective-permute-start(f32[16,10240]{1,0:T(8,128)S(1)} %add.41), channel_id=1, source_target_pairs={{8,4},{4,8},{9,5},{5,9},{10,6},{6,10},{11,7},{7,11},{24,20},{20,24... | collective-permute-start | bytes 1966088 | tf_op jit(solution)/shard_map/ppermute | solution.py:311
  153.5 21.9 %collective-permute-start.22 = (f32[16,10240]{1,0:T(8,128)S(1)}, f32[16,10240]{1,0:T(8,128)S(1)}, u32[]{:S(2)}, u32[]{:S(2)}) collective-permute-start(f32[16,10240]{1,0:T(8,128)S(1)} %add.40), channel_id=1, source_target_pairs={{4,0},{0,4},{12,8},{8,12},{5,1},{1,5},{13,9},{9,13},{6,2},{2,6},{1... | collective-permute-start | bytes 1966088 | tf_op jit(solution)/shard_map/ppermute | solution.py:311
  161.4 31.5 %collective-permute-start.25 = (f32[16,10240]{1,0:T(8,128)S(1)}, f32[16,10240]{1,0:T(8,128)S(1)}, u32[]{:S(2)}, u32[]{:S(2)}) collective-permute-start(f32[16,10240]{1,0:T(8,128)S(1)} %add.43), channel_id=1, source_target_pairs={{8,4},{4,8},{9,5},{5,9},{10,6},{6,10},{11,7},{7,11},{24,20},{20,24... | collective-permute-start | bytes 1966088 | tf_op jit(solution)/shard_map/ppermute | solution.py:311
  167.0 25.9 %collective-permute-start.24 = (f32[16,10240]{1,0:T(8,128)S(1)}, f32[16,10240]{1,0:T(8,128)S(1)}, u32[]{:S(2)}, u32[]{:S(2)}) collective-permute-start(f32[16,10240]{1,0:T(8,128)S(1)} %add.42), channel_id=1, source_target_pairs={{4,0},{0,4},{12,8},{8,12},{5,1},{1,5},{13,9},{9,13},{6,2},{2,6},{1... | collective-permute-start | bytes 1966088 | tf_op jit(solution)/shard_map/ppermute | solution.py:311

commit v8 on v7

--- a/solution.py
+++ b/solution.py
@@ -266,28 +266,34 @@
 class Gather:
     def __init__(self, value, length):
         self.length = length
-        self.arrived = {(0, 0): value, (1, 0): value}
-        self.done = 0
-
-    def step(self, count=1):
-        for _ in range(min(count, self.length - 1 - self.done)):
-            self.done += 1
-            for parity in (0, 1):
-                pairs = step_pairs(self.length, self.done, parity)
-                if pairs:
-                    self.arrived[parity, self.done] = lax.ppermute(self.arrived[1 - parity, self.done - 1], "tm", pairs)
-
-    def tie(self, tile, parities=(0, 1)):
-        for parity in parities:
-            if (parity, self.done) in self.arrived:
-                tile, value = lax.optimization_barrier((tile, self.arrived[parity, self.done]))
-                self.arrived[parity, self.done] = value
+        self.onward = {(0, 0): value, (1, 0): value}
+        self.arrived = {}
+
+    def pairs(self, parity, step, onward):
+        sources = {source for source, _ in step_pairs(self.length, step + 1, 1 - parity)}
+        return [pair for pair in step_pairs(self.length, step, parity) if (pair[1] in sources) == onward]
+
+    def send(self, parity, step, kinds=(True, False)):
+        pairs = [pair for onward in kinds for pair in self.pairs(parity, step, onward)]
+        if pairs:
+            value = lax.ppermute(self.onward[1 - parity, step - 1], "tm", pairs)
+            self.arrived.setdefault((parity, step), []).append(value)
+            if True in kinds:
+                self.onward[parity, step] = value
+
+    def tie(self, tile, parity, step):
+        values = self.arrived.get((parity, step), [])
+        if values:
+            places = [index for index, value in enumerate(values) if value is self.onward.get((parity, step))]
+            tile, *values = lax.optimization_barrier((tile, *values))
+            self.arrived[parity, step] = values
+            for index in places:
+                self.onward[parity, step] = values[index]
         return tile
 
     def slots(self):
-        self.step(self.length)
         return [
-            [self.arrived[key] for key in ((0, slot), (1, self.length - slot)) if key in self.arrived]
+            self.arrived.get((0, slot), []) + self.arrived.get((1, self.length - slot), [])
             for slot in range(1, self.length)
         ]
 
@@ -297,29 +303,30 @@
         self.length = length
         self.slots = slots
         self.pending = {}
-        self.left = length
-
-    def step(self, count=1):
-        for _ in range(min(count, self.left - 1)):
-            self.left -= 1
-            for parity in (0, 1):
-                pairs = step_pairs(self.length, self.left, parity)
-                if pairs:
-                    value = self.slots[self.left] if parity == 0 else self.slots[self.length - self.left]
-                    if (1 - parity, self.left + 1) in self.pending:
-                        value = value + self.pending[1 - parity, self.left + 1]
-                    self.pending[parity, self.left] = lax.ppermute(value, "tm", [(b, a) for a, b in pairs])
-
-    def tie(self, tile, parities=(0, 1)):
-        for parity in parities:
-            if (parity, self.left) in self.pending:
-                tile, value = lax.optimization_barrier((tile, self.pending[parity, self.left]))
-                self.pending[parity, self.left] = value
+
+    def pairs(self, parity, step, free):
+        receivers = {source for source, _ in step_pairs(self.length, step + 1, 1 - parity)}
+        pairs = [(b, a) for a, b in step_pairs(self.length, step, parity)]
+        return [pair for pair in pairs if (pair[0] not in receivers) == free]
+
+    def send(self, parity, step, kinds=(True, False)):
+        pairs = [pair for free in kinds for pair in self.pairs(parity, step, free)]
+        if pairs:
+            value = self.slots[step] if parity == 0 else self.slots[self.length - step]
+            if False in kinds:
+                for other in self.pending.get((1 - parity, step + 1), []):
+                    value = value + other
+            self.pending.setdefault((parity, step), []).append(lax.ppermute(value, "tm", pairs))
+
+    def tie(self, tile, parity, step):
+        values = self.pending.get((parity, step), [])
+        if values:
+            tile, *values = lax.optimization_barrier((tile, *values))
+            self.pending[parity, step] = values
         return tile
 
     def addends(self):
-        self.step(self.length)
-        return [self.slots[0]] + [self.pending[key] for key in ((0, 1), (1, 1)) if key in self.pending]
+        return [self.slots[0]] + self.pending.get((0, 1), []) + self.pending.get((1, 1), [])
 
 
 def is_direct(length):
@@ -361,44 +368,74 @@
         tile, *slots = lax.optimization_barrier((tile, *slots))
         return Reduction(slots, length), tile
 
+    if chunks == 1 or length != 4:
+        totals = []
+        for chunk in range(chunks):
+            gather = Gather(own[chunk * rows : (chunk + 1) * rows], length)
+            for step in range(1, length):
+                gather.send(0, step)
+                gather.send(1, step)
+            partial = project(tall_high, tall_low, own, chunk, gather.slots(), shards, tile)
+            reduction, tile = multiplied(exchange(summed(partial), length), tile)
+            for step in range(length - 1, 0, -1):
+                reduction.send(0, step)
+                reduction.send(1, step)
+            totals.append(reduction.addends())
+        return totals_of(totals, tile).T
+
     first = Gather(own[:rows], length)
-    first.step()
+    first.send(0, 1)
+    first.send(1, 1)
     tile, taps, shards, places, high, low = lax.optimization_barrier((tile, taps, shards, places, high, low))
-    tile = first.tie(tile)
-    first.step()
-    if chunks == 1:
-        partial = project(tall_high, tall_low, own, 0, first.slots(), shards, tile)
-        ahead, tile = multiplied(exchange(summed(partial), length), tile)
-        return totals_of([ahead.addends()], tile).T
+    tile = first.tie(tile, 0, 1)
+    tile = first.tie(tile, 1, 1)
+    first.send(0, 2)
+    first.send(1, 2)
+    tile = first.tie(tile, 1, 2)
+    first.send(0, 3)
     tile, value = lax.optimization_barrier((mark(tile), own[rows:]))
     second = Gather(value, length)
-    second.step()
-    tile = first.tie(tile)
-    first.step(length)
-    tile = second.tie(mark(tile))
-    second.step()
-    partial = project(tall_high, tall_low, own, 0, first.slots(), shards, mark(tile))
+    second.send(0, 1)
+    second.send(1, 1)
+    partial = project(tall_high, tall_low, own, 0, first.slots(), shards, tile)
     projected = summed(partial)
     blocks = exchange(projected, length)
     tile, *blocks = lax.optimization_barrier((tile, *blocks))
-    tile = second.tie(tile)
-    second.step(length)
+    tile = second.tie(tile, 0, 1)
+    tile = second.tie(tile, 1, 1)
+    second.send(0, 2)
+    second.send(1, 2)
     ahead, tile = multiplied(blocks, mark(tile))
-    ahead.step()
+    ahead.send(0, 3)
+    ahead.send(0, 1, (True,))
+    tile = second.tie(tile, 0, 2)
+    tile = second.tie(tile, 1, 2)
+    second.send(0, 3)
+    tile = ahead.tie(mark(tile), 0, 3)
+    ahead.send(0, 2)
+    ahead.send(1, 2)
     partial = project(tall_high, tall_low, own, 1, second.slots(), shards, mark(tile))
     projected = summed(partial)
     blocks = exchange(projected, length)
-    tile = ahead.tie(mark(tile, projected), (0,))
-    ahead.step()
+    tile = ahead.tie(mark(tile, projected), 0, 2)
+    tile = ahead.tie(tile, 1, 2)
+    ahead.send(0, 1, (False,))
+    ahead.send(1, 1)
+    free = ahead.pending[0, 1][:1]
+    tile, *free = lax.optimization_barrier((tile, *free))
+    ahead.pending[0, 1][:1] = free
     trailing, tile = multiplied(blocks, mark(tile))
-    trailing.step()
-    tile = ahead.tie(mark(tile))
-    ahead.step(length)
-    tile = trailing.tie(mark(tile), (0,))
-    trailing.step()
-    tile = trailing.tie(mark(tile))
-    trailing.step(length)
-    tile = ahead.tie(mark(tile))
+    trailing.send(0, 3)
+    tile = ahead.tie(mark(tile), 0, 1)
+    tile = ahead.tie(tile, 1, 1)
+    tile, later = lax.optimization_barrier((tile, trailing.slots[2]))
+    tile = mark(tile)
+    tile = trailing.tie(tile, 0, 3)
+    trailing.send(1, 2)
+    trailing.slots[2] = later
+    trailing.send(0, 2)
+    trailing.send(0, 1)
+    trailing.send(1, 1)
     return totals_of([ahead.addends(), trailing.addends()], tile).T
 
 

time: 195 us -> 182 us (0.933)
  waiting for transfers between devices: 109 us -> 92.7 us
  starting transfers between devices: 47.7 us -> 50.5 us
    ppermute x20 -> x21, waiting for transfers between devices: 99.5 us -> 85.9 us  [the longest x11 50.8 us: send(): lax.ppermute(value, 'tm', pairs)]
    ppermute x20 -> x21, starting transfers between devices: 39.3 us -> 42.1 us  [the longest x10 22.1 us: send(): value = lax.ppermute(self.onward[1 - parity, step - 1], 'tm', pairs)]
    ppermute x6, waiting for transfers between devices: 9.28 us -> 6.82 us  [exchange(): lax.ppermute(value, 'tm', [(i, i ^ by) for i in range(length)])]
  transfers between devices with their start and end apart: 26 -> 27, of which waited for: 19 -> 16; matrix products, arithmetic and copies ran while one was open for 0% -> 0% of each run, Pallas kernels for 10% -> 10%
where the time goes in v8:
time: 182 us; the launch traced here: 181 us
  waiting for transfers between devices  92.7 us (51%)
  starting transfers between devices  50.5 us (28%)
  Pallas kernels  20.1 us (11%)
  blocking collectives  11.6 us (6%)
  local copies, waits for them, and re-layouts  5.3 us (3%)
    ppermute x11, waiting for transfers between devices, send(): lax.ppermute(value, 'tm', pairs)  50.8 us
    ppermute x10, waiting for transfers between devices, send(): value = lax.ppermute(self.onward[1 - parity, step - 1], 'tm', pairs)  35.1 us
    ppermute x10, starting transfers between devices, send(): value = lax.ppermute(self.onward[1 - parity, step - 1], 'tm', pairs)  22.1 us
    ppermute x11, starting transfers between devices, send(): lax.ppermute(value, 'tm', pairs)  20 us
    all_gather x2, blocking collectives, summed(): return add_up(lax.all_gather(partial, 'param', axis=0))  11.6 us
    ppermute x6, starting transfers between devices, exchange(): lax.ppermute(value, 'tm', [(i, i ^ by) for i in range(length)])  8.41 us
    pallas_call x2, Pallas kernels, multiply(): pl.pallas_call(kernel, grid_spec=pltpu.PrefetchScalarGridSpec(num_scalar_...  7.46 us
    ppermute x6, waiting for transfers between devices, exchange(): lax.ppermute(value, 'tm', [(i, i ^ by) for i in range(length)])  6.82 us
  transfers between devices with their start and end apart: 27, of which 16 were waited for; matrix products, arithmetic and copies ran while one was open for 0% of the time, Pallas kernels for 10%

profile of v8, /device:TPU:8, one launch (start us, length us, event | category | flops | bytes accessed | tf_op | source)
XLA Modules:
  0.0 181.1 jit_solution(16190738003061778746)
XLA Ops:
  1.5 5.0 %collective-permute-start.1 = (f32[16,10240]{1,0:T(8,128)S(1)}, f32[16,10240]{1,0:T(8,128)S(1)}, u32[]{:S(2)}, u32[]{:S(2)}) collective-permute-start(f32[16,10240]{1,0:T(8,128)S(1)} %get-tuple-element.138), channel_id=1, source_target_pairs={{4,8},{8,4},{5,9},{9,5},{6,10},{10,6},{7,11},{11,7},{20,24},{24,20... | collective-permute-start | bytes 1966088 | tf_op jit(solution)/shard_map/ppermute | solution.py:279
  8.4 3.2 %copy-done.1 = f32[3,64,10240]{2,1,0:T(8,128)S(1)} copy-done((f32[3,64,10240]{2,1,0:T(8,128)S(1)}, f32[3,64,10240]{2,1,0:T(8,128)}, u32[]{:S(2)}) %copy-start.1) | copy-done | bytes 7864344
  11.6 4.3 %split_design.1 = (bf16[192,10240]{1,0:T(8,128)(2,1)S(1)}, bf16[192,10240]{1,0:T(8,128)(2,1)S(1)}, bf16[10240,192]{1,0:T(8,128)(2,1)S(1)}, bf16[10240,192]{1,0:T(8,128)(2,1)S(1)}) custom-call(f32[3,64,10240]{2,1,0:T(8,128)S(1)} %copy-done.1, f32[4,3,64,64]{3,2,1,0:T(8,128)S(1)} %normal_rows.1.refs_0_.taps_ref, s32[4]{0:T(128)S(1)} %get-tuple-element.79.refs_1_.shard_ref, ...), custom_call_target="tpu_custom_call" | custom-call | flops 1 | bytes 1 | tf_op jit(solution)/shard_map/split_design/pallas_call | solution.py:49
  15.9 2.0 %collective-permute-done.refs_0_ = f32[16,10240]{1,0:T(8,128)S(1)} collective-permute-done((f32[16,10240]{1,0:T(8,128)S(1)}, f32[16,10240]{1,0:T(8,128)S(1)}, u32[]{:S(2)}, u32[]{:S(2)}) %collective-permute-start) | collective-permute-done | bytes 655392 | tf_op jit(solution)/shard_map/ppermute | solution.py:279
  17.9 3.5 %collective-permute-start.2 = (f32[16,10240]{1,0:T(8,128)S(1)}, f32[16,10240]{1,0:T(8,128)S(1)}, u32[]{:S(2)}, u32[]{:S(2)}) collective-permute-start(f32[16,10240]{1,0:T(8,128)S(1)} %collective-permute-done.refs_0_), channel_id=1, source_target_pairs={{4,8},{8,4},{5,9},{9,5},{6,10},{10,6},{7,11},{11,7},{20,24},{24,20... | collective-permute-start | bytes 1966088 | tf_op jit(solution)/shard_map/ppermute | solution.py:279
  22.8 12.7 %collective-permute-done.2.refs_2_ = f32[16,10240]{1,0:T(8,128)S(1)} collective-permute-done((f32[16,10240]{1,0:T(8,128)S(1)}, f32[16,10240]{1,0:T(8,128)S(1)}, u32[]{:S(2)}, u32[]{:S(2)}) %collective-permute-start.2) | collective-permute-done | bytes 655392 | tf_op jit(solution)/shard_map/ppermute | solution.py:279
  36.8 3.5 %collective-permute-start.9 = (f32[16,10240]{1,0:T(8,128)S(1)}, f32[16,10240]{1,0:T(8,128)S(1)}, u32[]{:S(2)}, u32[]{:S(2)}) collective-permute-start(f32[16,10240]{1,0:T(8,128)S(1)} %get-tuple-element.85), channel_id=1, source_target_pairs={{4,8},{8,4},{5,9},{9,5},{6,10},{10,6},{7,11},{11,7},{20,24},{24,20... | collective-permute-start | bytes 1966088 | tf_op jit(solution)/shard_map/ppermute | solution.py:279
  40.3 11.5 %collective-permute-done.4.refs_3_ = f32[16,10240]{1,0:T(8,128)S(1)} collective-permute-done((f32[16,10240]{1,0:T(8,128)S(1)}, f32[16,10240]{1,0:T(8,128)S(1)}, u32[]{:S(2)}, u32[]{:S(2)}) %collective-permute-start.4) | collective-permute-done | bytes 655392 | tf_op jit(solution)/shard_map/ppermute | solution.py:279
  51.9 2.9 %project.2 = f32[4,16,192]{2,1,0:T(8,128)S(1)} custom-call(s32[4]{0:T(128)S(1)} %get-tuple-element.79.refs_1_.shard_ref, bf16[10240,192]{1,0:T(8,128)(2,1)S(1)} %get-tuple-element.80.high_ref, bf16[10240,192]{1,0:T(8,128)(2,1)S(1)} %get-tuple-element.81.low_ref, f32[32,10240]{1,0:T(8,128)S(1)} %bitcast.6, f32[16,10240]{1,0:T(8,128)S(1)} %collective-permute-done.refs_0_, ...), custom_call_target="tpu_custom_call" | custom-call | flops 1 | bytes 1 | tf_op jit(solution)/shard_map/project/pallas_call | solution.py:123
  54.7 5.8 %all-gather = f32[16,16,192]{2,1,0:T(8,128)S(1)} all-gather(f32[4,16,192]{2,1,0:T(8,128)S(1)} %project.2), channel_id=2, replica_groups=mesh['groups'=2,'tm'=4,'param'=4] {'param'}, dimensions={0}, use_global_device_ids=true | all-gather | bytes 245760 | tf_op jit(solution)/shard_map/all_gather | solution.py:364
  60.5 2.5 %collective-permute-start.5 = (f32[4,16,192]{2,1,0:T(8,128)S(1)}, f32[4,16,192]{2,1,0:T(8,128)S(1)}, u32[]{:S(2)}, u32[]{:S(2)}) collective-permute-start(f32[4,16,192]{2,1,0:T(8,128)S(1)} %add_up.2.refs_0_), channel_id=1, source_target_pairs={{0,4},{4,0},{8,12},{12,8},{1,5},{5,1},{9,13},{13,9},{2,6},{6,2},{1... | collective-permute-start | bytes 147464 | tf_op jit(solution)/shard_map/ppermute | solution.py:343
  66.5 2.8 %collective-permute-done.6.refs_2_ = f32[4,16,192]{2,1,0:T(8,128)S(1)} collective-permute-done((f32[4,16,192]{2,1,0:T(8,128)S(1)}, f32[4,16,192]{2,1,0:T(8,128)S(1)}, u32[]{:S(2)}, u32[]{:S(2)}) %collective-permute-start.6) | collective-permute-done | bytes 49184 | tf_op jit(solution)/shard_map/ppermute | solution.py:343
  71.2 2.9 %collective-permute-start.10 = (f32[16,10240]{1,0:T(8,128)S(1)}, f32[16,10240]{1,0:T(8,128)S(1)}, u32[]{:S(2)}, u32[]{:S(2)}) collective-permute-start(f32[16,10240]{1,0:T(8,128)S(1)} %collective-permute-done.9.refs_4_), channel_id=1, source_target_pairs={{4,0},{8,12},{5,1},{9,13},{6,2},{10,14},{7,3},{11,15},{20,16},{24,... | collective-permute-start | bytes 1966088 | tf_op jit(solution)/shard_map/ppermute | solution.py:279
  74.2 3.0 %collective-permute-start.11 = (f32[16,10240]{1,0:T(8,128)S(1)}, f32[16,10240]{1,0:T(8,128)S(1)}, u32[]{:S(2)}, u32[]{:S(2)}) collective-permute-start(f32[16,10240]{1,0:T(8,128)S(1)} %collective-permute-done.8.refs_0_), channel_id=1, source_target_pairs={{4,8},{8,4},{5,9},{9,5},{6,10},{10,6},{7,11},{11,7},{20,24},{24,20... | collective-permute-start | bytes 1966088 | tf_op jit(solution)/shard_map/ppermute | solution.py:279
  77.2 3.7 %multiply.2 = (f32[16,10240]{1,0:T(8,128)S(1)}, f32[16,10240]{1,0:T(8,128)S(1)}, f32[16,10240]{1,0:T(8,128)S(1)}, f32[16,10240]{1,0:T(8,128)S(1)}) custom-call(s32[4]{0:T(128)S(1)} %get-tuple-element.79.refs_1_.shard_ref, s32[4]{0:T(128)S(1)} %get-tuple-element.88.refs_2_.place_ref, bf16[192,10240]{1,0:T(8,128)(2,1)S(1)} %get-tuple-element.89.high_ref, ...), custom_call_target="tpu_custom_call" | custom-call | flops 1 | bytes 1 | tf_op jit(solution)/shard_map/multiply/pallas_call | solution.py:174
  82.3 4.7 %collective-permute-done.10.refs_1_ = f32[16,10240]{1,0:T(8,128)S(1)} collective-permute-done((f32[16,10240]{1,0:T(8,128)S(1)}, f32[16,10240]{1,0:T(8,128)S(1)}, u32[]{:S(2)}, u32[]{:S(2)}) %collective-permute-start.10) | collective-permute-done | bytes 655392 | tf_op jit(solution)/shard_map/ppermute | solution.py:279
  87.0 4.2 %collective-permute-done.11.refs_2_ = f32[16,10240]{1,0:T(8,128)S(1)} collective-permute-done((f32[16,10240]{1,0:T(8,128)S(1)}, f32[16,10240]{1,0:T(8,128)S(1)}, u32[]{:S(2)}, u32[]{:S(2)}) %collective-permute-start.11) | collective-permute-done | bytes 655392 | tf_op jit(solution)/shard_map/ppermute | solution.py:279
  93.8 6.8 %collective-permute-done.12 = f32[16,10240]{1,0:T(8,128)S(1)} collective-permute-done((f32[16,10240]{1,0:T(8,128)S(1)}, f32[16,10240]{1,0:T(8,128)S(1)}, u32[]{:S(2)}, u32[]{:S(2)}) %collective-permute-start.12) | collective-permute-done | bytes 655392 | tf_op jit(solution)/shard_map/ppermute | solution.py:319
  100.6 2.7 %collective-permute-start.15 = (f32[16,10240]{1,0:T(8,128)S(1)}, f32[16,10240]{1,0:T(8,128)S(1)}, u32[]{:S(2)}, u32[]{:S(2)}) collective-permute-start(f32[16,10240]{1,0:T(8,128)S(1)} %add.38), channel_id=1, source_target_pairs={{8,4},{4,8},{9,5},{5,9},{10,6},{6,10},{11,7},{7,11},{24,20},{20,24... | collective-permute-start | bytes 1966088 | tf_op jit(solution)/shard_map/ppermute | solution.py:319
  104.6 2.9 %project.3 = f32[4,16,192]{2,1,0:T(8,128)S(1)} custom-call(s32[4]{0:T(128)S(1)} %get-tuple-element.79.refs_1_.shard_ref, bf16[10240,192]{1,0:T(8,128)(2,1)S(1)} %get-tuple-element.80.high_ref, bf16[10240,192]{1,0:T(8,128)(2,1)S(1)} %get-tuple-element.81.low_ref, f32[32,10240]{1,0:T(8,128)S(1)} %bitcast.7, f32[16,10240]{1,0:T(8,128)S(1)} %collective-permute-done.8.refs_0_, ...), custom_call_target="tpu_custom_call" | custom-call | flops 1 | bytes 1 | tf_op jit(solution)/shard_map/project/pallas_call | solution.py:123
  107.5 5.8 %all-gather.1 = f32[16,16,192]{2,1,0:T(8,128)S(1)} all-gather(f32[4,16,192]{2,1,0:T(8,128)S(1)} %project.3), channel_id=3, replica_groups=mesh['groups'=2,'tm'=4,'param'=4] {'param'}, dimensions={0}, use_global_device_ids=true | all-gather | bytes 245760 | tf_op jit(solution)/shard_map/all_gather | solution.py:364
  113.3 2.7 %collective-permute-start.17 = (f32[4,16,192]{2,1,0:T(8,128)S(1)}, f32[4,16,192]{2,1,0:T(8,128)S(1)}, u32[]{:S(2)}, u32[]{:S(2)}) collective-permute-start(f32[4,16,192]{2,1,0:T(8,128)S(1)} %add_up.3.refs_0_), channel_id=1, source_target_pairs={{0,4},{4,0},{8,12},{12,8},{1,5},{5,1},{9,13},{13,9},{2,6},{6,2},{1... | collective-permute-start | bytes 147464 | tf_op jit(solution)/shard_map/ppermute | solution.py:343
  117.7 3.2 %collective-permute-start.21 = (f32[16,10240]{1,0:T(8,128)S(1)}, f32[16,10240]{1,0:T(8,128)S(1)}, u32[]{:S(2)}, u32[]{:S(2)}) collective-permute-start(f32[16,10240]{1,0:T(8,128)S(1)} %add.40), channel_id=1, source_target_pairs={{8,4},{4,8},{9,5},{5,9},{10,6},{6,10},{11,7},{7,11},{24,20},{20,24... | collective-permute-start | bytes 1966088 | tf_op jit(solution)/shard_map/ppermute | solution.py:319
  120.9 7.0 %collective-permute-done.16.refs_1_ = f32[16,10240]{1,0:T(8,128)S(1)} collective-permute-done((f32[16,10240]{1,0:T(8,128)S(1)}, f32[16,10240]{1,0:T(8,128)S(1)}, u32[]{:S(2)}, u32[]{:S(2)}) %collective-permute-start.16) | collective-permute-done | bytes 655392 | tf_op jit(solution)/shard_map/ppermute | solution.py:319
  129.7 3.7 %multiply.3 = (f32[16,10240]{1,0:T(8,128)S(1)}, f32[16,10240]{1,0:T(8,128)S(1)}, f32[16,10240]{1,0:T(8,128)S(1)}, f32[16,10240]{1,0:T(8,128)S(1)}) custom-call(s32[4]{0:T(128)S(1)} %get-tuple-element.79.refs_1_.shard_ref, s32[4]{0:T(128)S(1)} %get-tuple-element.88.refs_2_.place_ref, bf16[192,10240]{1,0:T(8,128)(2,1)S(1)} %get-tuple-element.89.high_ref, ...), custom_call_target="tpu_custom_call" | custom-call | flops 1 | bytes 1 | tf_op jit(solution)/shard_map/multiply/pallas_call | solution.py:174
  134.7 5.5 %collective-permute-done.20.refs_2_ = f32[16,10240]{1,0:T(8,128)S(1)} collective-permute-done((f32[16,10240]{1,0:T(8,128)S(1)}, f32[16,10240]{1,0:T(8,128)S(1)}, u32[]{:S(2)}, u32[]{:S(2)}) %collective-permute-start.20) | collective-permute-done | bytes 655392 | tf_op jit(solution)/shard_map/ppermute | solution.py:319
  141.5 11.5 %collective-permute-done.22 = f32[16,10240]{1,0:T(8,128)S(1)} collective-permute-done((f32[16,10240]{1,0:T(8,128)S(1)}, f32[16,10240]{1,0:T(8,128)S(1)}, u32[]{:S(2)}, u32[]{:S(2)}) %collective-permute-start.22) | collective-permute-done | bytes 655392 | tf_op jit(solution)/shard_map/ppermute | solution.py:319
  153.1 3.1 %collective-permute-start.23 = (f32[16,10240]{1,0:T(8,128)S(1)}, f32[16,10240]{1,0:T(8,128)S(1)}, u32[]{:S(2)}, u32[]{:S(2)}) collective-permute-start(f32[16,10240]{1,0:T(8,128)S(1)} %add.41), channel_id=1, source_target_pairs={{8,4},{4,8},{9,5},{5,9},{10,6},{6,10},{11,7},{7,11},{24,20},{20,24... | collective-permute-start | bytes 1966088 | tf_op jit(solution)/shard_map/ppermute | solution.py:319
  156.2 6.6 %collective-permute-done.25 = f32[16,10240]{1,0:T(8,128)S(1)} collective-permute-done((f32[16,10240]{1,0:T(8,128)S(1)}, f32[16,10240]{1,0:T(8,128)S(1)}, u32[]{:S(2)}, u32[]{:S(2)}) %collective-permute-start.25) | collective-permute-done | bytes 655392 | tf_op jit(solution)/shard_map/ppermute | solution.py:319
  162.8 3.1 %collective-permute-start.26 = (f32[16,10240]{1,0:T(8,128)S(1)}, f32[16,10240]{1,0:T(8,128)S(1)}, u32[]{:S(2)}, u32[]{:S(2)}) collective-permute-start(f32[16,10240]{1,0:T(8,128)S(1)} %add.43), channel_id=1, source_target_pairs={{8,4},{4,8},{9,5},{5,9},{10,6},{6,10},{11,7},{7,11},{24,20},{20,24... | collective-permute-start | bytes 1966088 | tf_op jit(solution)/shard_map/ppermute | solution.py:319
  165.9 2.0 %collective-permute-done.23 = f32[16,10240]{1,0:T(8,128)S(1)} collective-permute-done((f32[16,10240]{1,0:T(8,128)S(1)}, f32[16,10240]{1,0:T(8,128)S(1)}, u32[]{:S(2)}, u32[]{:S(2)}) %collective-permute-start.23) | collective-permute-done | bytes 655392 | tf_op jit(solution)/shard_map/ppermute | solution.py:319
  168.1 11.5 %collective-permute-done.26.refs_6_ = f32[16,10240]{1,0:T(8,128)S(1)} collective-permute-done((f32[16,10240]{1,0:T(8,128)S(1)}, f32[16,10240]{1,0:T(8,128)S(1)}, u32[]{:S(2)}, u32[]{:S(2)}) %collective-permute-start.26) | collective-permute-done | bytes 655392 | tf_op jit(solution)/shard_map/ppermute | solution.py:319
  (56 shorter events, 24.5 us)
Async XLA Ops:
  1.4 16.5 %collective-permute-start = (f32[16,10240]{1,0:T(8,128)S(1)}, f32[16,10240]{1,0:T(8,128)S(1)}, u32[]{:S(2)}, u32[]{:S(2)}) collective-permute-start(f32[16,10240]{1,0:T(8,128)S(1)} %get-tuple-element.138), channel_id=1, source_target_pairs={{0,4},{12,8},{4,0},{8,12},{1,5},{13,9},{5,1},{9,13},{2,6},{14,10},... | collective-permute-start | bytes 1966088 | tf_op jit(solution)/shard_map/ppermute | solution.py:279
  1.5 19.9 %collective-permute-start.1 = (f32[16,10240]{1,0:T(8,128)S(1)}, f32[16,10240]{1,0:T(8,128)S(1)}, u32[]{:S(2)}, u32[]{:S(2)}) collective-permute-start(f32[16,10240]{1,0:T(8,128)S(1)} %get-tuple-element.138), channel_id=1, source_target_pairs={{4,8},{8,4},{5,9},{9,5},{6,10},{10,6},{7,11},{11,7},{20,24},{24,20... | collective-permute-start | bytes 1966088 | tf_op jit(solution)/shard_map/ppermute | solution.py:279
  6.5 0.7 copy-start.2
  8.4 3.2 %copy-start.1 = (f32[3,64,10240]{2,1,0:T(8,128)S(1)}, f32[3,64,10240]{2,1,0:T(8,128)}, u32[]{:S(2)}) copy-start(f32[3,64,10240]{2,1,0:T(8,128)} %design_ref.1) | copy-start | bytes 23592964
  11.6 40.2 %copy-start = (f32[10240,32]{0,1:T(8,128)S(1)}, f32[10240,32]{0,1:T(8,128)}, u32[]{:S(2)}) copy-start(f32[10240,32]{0,1:T(8,128)} %param.5) | copy-start | bytes 3932164
  17.9 17.5 %collective-permute-start.2 = (f32[16,10240]{1,0:T(8,128)S(1)}, f32[16,10240]{1,0:T(8,128)S(1)}, u32[]{:S(2)}, u32[]{:S(2)}) collective-permute-start(f32[16,10240]{1,0:T(8,128)S(1)} %collective-permute-done.refs_0_), channel_id=1, source_target_pairs={{4,8},{8,4},{5,9},{9,5},{6,10},{10,6},{7,11},{11,7},{20,24},{24,20... | collective-permute-start | bytes 1966088 | tf_op jit(solution)/shard_map/ppermute | solution.py:279
  21.4 18.9 %collective-permute-start.3 = (f32[16,10240]{1,0:T(8,128)S(1)}, f32[16,10240]{1,0:T(8,128)S(1)}, u32[]{:S(2)}, u32[]{:S(2)}) collective-permute-start(f32[16,10240]{1,0:T(8,128)S(1)} %collective-permute-done.1.refs_4_), channel_id=1, source_target_pairs={{4,0},{8,12},{5,1},{9,13},{6,2},{10,14},{7,3},{11,15},{20,16},{24,... | collective-permute-start | bytes 1966088 | tf_op jit(solution)/shard_map/ppermute | solution.py:279
  35.4 16.5 %collective-permute-start.4 = (f32[16,10240]{1,0:T(8,128)S(1)}, f32[16,10240]{1,0:T(8,128)S(1)}, u32[]{:S(2)}, u32[]{:S(2)}) collective-permute-start(f32[16,10240]{1,0:T(8,128)S(1)} %collective-permute-done.2.refs_2_), channel_id=1, source_target_pairs={{4,0},{8,12},{5,1},{9,13},{6,2},{10,14},{7,3},{11,15},{20,16},{24,... | collective-permute-start | bytes 1966088 | tf_op jit(solution)/shard_map/ppermute | solution.py:279
  36.7 34.5 %collective-permute-start.8 = (f32[16,10240]{1,0:T(8,128)S(1)}, f32[16,10240]{1,0:T(8,128)S(1)}, u32[]{:S(2)}, u32[]{:S(2)}) collective-permute-start(f32[16,10240]{1,0:T(8,128)S(1)} %get-tuple-element.85), channel_id=1, source_target_pairs={{0,4},{12,8},{4,0},{8,12},{1,5},{13,9},{5,1},{9,13},{2,6},{14,10},... | collective-permute-start | bytes 1966088 | tf_op jit(solution)/shard_map/ppermute | solution.py:279
  36.8 34.4 %collective-permute-start.9 = (f32[16,10240]{1,0:T(8,128)S(1)}, f32[16,10240]{1,0:T(8,128)S(1)}, u32[]{:S(2)}, u32[]{:S(2)}) collective-permute-start(f32[16,10240]{1,0:T(8,128)S(1)} %get-tuple-element.85), channel_id=1, source_target_pairs={{4,8},{8,4},{5,9},{9,5},{6,10},{10,6},{7,11},{11,7},{20,24},{24,20... | collective-permute-start | bytes 1966088 | tf_op jit(solution)/shard_map/ppermute | solution.py:279
  60.5 5.9 %collective-permute-start.5 = (f32[4,16,192]{2,1,0:T(8,128)S(1)}, f32[4,16,192]{2,1,0:T(8,128)S(1)}, u32[]{:S(2)}, u32[]{:S(2)}) collective-permute-start(f32[4,16,192]{2,1,0:T(8,128)S(1)} %add_up.2.refs_0_), channel_id=1, source_target_pairs={{0,4},{4,0},{8,12},{12,8},{1,5},{5,1},{9,13},{13,9},{2,6},{6,2},{1... | collective-permute-start | bytes 147464 | tf_op jit(solution)/shard_map/ppermute | solution.py:343
  63.1 6.2 %collective-permute-start.6 = (f32[4,16,192]{2,1,0:T(8,128)S(1)}, f32[4,16,192]{2,1,0:T(8,128)S(1)}, u32[]{:S(2)}, u32[]{:S(2)}) collective-permute-start(f32[4,16,192]{2,1,0:T(8,128)S(1)} %add_up.2.refs_0_), channel_id=1, source_target_pairs={{0,8},{4,12},{8,0},{12,4},{1,9},{5,13},{9,1},{13,5},{2,10},{6,14},... | collective-permute-start | bytes 147464 | tf_op jit(solution)/shard_map/ppermute | solution.py:343
  64.2 7.1 %collective-permute-start.7 = (f32[4,16,192]{2,1,0:T(8,128)S(1)}, f32[4,16,192]{2,1,0:T(8,128)S(1)}, u32[]{:S(2)}, u32[]{:S(2)}) collective-permute-start(f32[4,16,192]{2,1,0:T(8,128)S(1)} %add_up.2.refs_0_), channel_id=1, source_target_pairs={{0,12},{4,8},{8,4},{12,0},{1,13},{5,9},{9,5},{13,1},{2,14},{6,10},... | collective-permute-start | bytes 147464 | tf_op jit(solution)/shard_map/ppermute | solution.py:343
  71.2 15.7 %collective-permute-start.10 = (f32[16,10240]{1,0:T(8,128)S(1)}, f32[16,10240]{1,0:T(8,128)S(1)}, u32[]{:S(2)}, u32[]{:S(2)}) collective-permute-start(f32[16,10240]{1,0:T(8,128)S(1)} %collective-permute-done.9.refs_4_), channel_id=1, source_target_pairs={{4,0},{8,12},{5,1},{9,13},{6,2},{10,14},{7,3},{11,15},{20,16},{24,... | collective-permute-start | bytes 1966088 | tf_op jit(solution)/shard_map/ppermute | solution.py:279
  74.2 16.9 %collective-permute-start.11 = (f32[16,10240]{1,0:T(8,128)S(1)}, f32[16,10240]{1,0:T(8,128)S(1)}, u32[]{:S(2)}, u32[]{:S(2)}) collective-permute-start(f32[16,10240]{1,0:T(8,128)S(1)} %collective-permute-done.8.refs_0_), channel_id=1, source_target_pairs={{4,8},{8,4},{5,9},{9,5},{6,10},{10,6},{7,11},{11,7},{20,24},{24,20... | collective-permute-start | bytes 1966088 | tf_op jit(solution)/shard_map/ppermute | solution.py:279
  81.0 19.6 %collective-permute-start.12 = (f32[16,10240]{1,0:T(8,128)S(1)}, f32[16,10240]{1,0:T(8,128)S(1)}, u32[]{:S(2)}, u32[]{:S(2)}) collective-permute-start(f32[16,10240]{1,0:T(8,128)S(1)} %get-tuple-element.106), channel_id=1, source_target_pairs={{0,4},{12,8},{1,5},{13,9},{2,6},{14,10},{3,7},{15,11},{16,20},{28,... | collective-permute-start | bytes 1966088 | tf_op jit(solution)/shard_map/ppermute | solution.py:319
  91.1 13.5 %collective-permute-start.13 = (f32[16,10240]{1,0:T(8,128)S(1)}, f32[16,10240]{1,0:T(8,128)S(1)}, u32[]{:S(2)}, u32[]{:S(2)}) collective-permute-start(f32[16,10240]{1,0:T(8,128)S(1)} %collective-permute-done.11.refs_2_), channel_id=1, source_target_pairs={{4,0},{8,12},{5,1},{9,13},{6,2},{10,14},{7,3},{11,15},{20,16},{24,... | collective-permute-start | bytes 1966088 | tf_op jit(solution)/shard_map/ppermute | solution.py:279
  92.5 24.4 %collective-permute-start.14 = (f32[16,10240]{1,0:T(8,128)S(1)}, f32[16,10240]{1,0:T(8,128)S(1)}, u32[]{:S(2)}, u32[]{:S(2)}) collective-permute-start(f32[16,10240]{1,0:T(8,128)S(1)} %get-tuple-element.110), channel_id=1, source_target_pairs={{0,4},{12,8},{1,5},{13,9},{2,6},{14,10},{3,7},{15,11},{16,20},{28,... | collective-permute-start | bytes 1966088 | tf_op jit(solution)/shard_map/ppermute | solution.py:319
  100.6 17.0 %collective-permute-start.15 = (f32[16,10240]{1,0:T(8,128)S(1)}, f32[16,10240]{1,0:T(8,128)S(1)}, u32[]{:S(2)}, u32[]{:S(2)}) collective-permute-start(f32[16,10240]{1,0:T(8,128)S(1)} %add.38), channel_id=1, source_target_pairs={{8,4},{4,8},{9,5},{5,9},{10,6},{6,10},{11,7},{7,11},{24,20},{20,24... | collective-permute-start | bytes 1966088 | tf_op jit(solution)/shard_map/ppermute | solution.py:319
  103.3 24.6 %collective-permute-start.16 = (f32[16,10240]{1,0:T(8,128)S(1)}, f32[16,10240]{1,0:T(8,128)S(1)}, u32[]{:S(2)}, u32[]{:S(2)}) collective-permute-start(f32[16,10240]{1,0:T(8,128)S(1)} %get-tuple-element.114), channel_id=1, source_target_pairs={{0,4},{12,8},{1,5},{13,9},{2,6},{14,10},{3,7},{15,11},{16,20},{28,... | collective-permute-start | bytes 1966088 | tf_op jit(solution)/shard_map/ppermute | solution.py:319
  113.3 16.1 %collective-permute-start.17 = (f32[4,16,192]{2,1,0:T(8,128)S(1)}, f32[4,16,192]{2,1,0:T(8,128)S(1)}, u32[]{:S(2)}, u32[]{:S(2)}) collective-permute-start(f32[4,16,192]{2,1,0:T(8,128)S(1)} %add_up.3.refs_0_), channel_id=1, source_target_pairs={{0,4},{4,0},{8,12},{12,8},{1,5},{5,1},{9,13},{13,9},{2,6},{6,2},{1... | collective-permute-start | bytes 147464 | tf_op jit(solution)/shard_map/ppermute | solution.py:343
  116.0 13.6 %collective-permute-start.18 = (f32[4,16,192]{2,1,0:T(8,128)S(1)}, f32[4,16,192]{2,1,0:T(8,128)S(1)}, u32[]{:S(2)}, u32[]{:S(2)}) collective-permute-start(f32[4,16,192]{2,1,0:T(8,128)S(1)} %add_up.3.refs_0_), channel_id=1, source_target_pairs={{0,8},{4,12},{8,0},{12,4},{1,9},{5,13},{9,1},{13,5},{2,10},{6,14},... | collective-permute-start | bytes 147464 | tf_op jit(solution)/shard_map/ppermute | solution.py:343
  116.8 12.9 %collective-permute-start.19 = (f32[4,16,192]{2,1,0:T(8,128)S(1)}, f32[4,16,192]{2,1,0:T(8,128)S(1)}, u32[]{:S(2)}, u32[]{:S(2)}) collective-permute-start(f32[4,16,192]{2,1,0:T(8,128)S(1)} %add_up.3.refs_0_), channel_id=1, source_target_pairs={{0,12},{4,8},{8,4},{12,0},{1,13},{5,9},{9,5},{13,1},{2,14},{6,10},... | collective-permute-start | bytes 147464 | tf_op jit(solution)/shard_map/ppermute | solution.py:343
  117.7 22.6 %collective-permute-start.21 = (f32[16,10240]{1,0:T(8,128)S(1)}, f32[16,10240]{1,0:T(8,128)S(1)}, u32[]{:S(2)}, u32[]{:S(2)}) collective-permute-start(f32[16,10240]{1,0:T(8,128)S(1)} %add.40), channel_id=1, source_target_pairs={{8,4},{4,8},{9,5},{5,9},{10,6},{6,10},{11,7},{7,11},{24,20},{20,24... | collective-permute-start | bytes 1966088 | tf_op jit(solution)/shard_map/ppermute | solution.py:319
  127.9 12.3 %collective-permute-start.20 = (f32[16,10240]{1,0:T(8,128)S(1)}, f32[16,10240]{1,0:T(8,128)S(1)}, u32[]{:S(2)}, u32[]{:S(2)}) collective-permute-start(f32[16,10240]{1,0:T(8,128)S(1)} %add.39), channel_id=1, source_target_pairs={{4,0},{8,12},{5,1},{9,13},{6,2},{10,14},{7,3},{11,15},{20,16},{24,... | collective-permute-start | bytes 1966088 | tf_op jit(solution)/shard_map/ppermute | solution.py:319
  133.4 19.6 %collective-permute-start.22 = (f32[16,10240]{1,0:T(8,128)S(1)}, f32[16,10240]{1,0:T(8,128)S(1)}, u32[]{:S(2)}, u32[]{:S(2)}) collective-permute-start(f32[16,10240]{1,0:T(8,128)S(1)} %get-tuple-element.133), channel_id=1, source_target_pairs={{0,4},{12,8},{1,5},{13,9},{2,6},{14,10},{3,7},{15,11},{16,20},{28,... | collective-permute-start | bytes 1966088 | tf_op jit(solution)/shard_map/ppermute | solution.py:319
  140.2 22.5 %collective-permute-start.25 = (f32[16,10240]{1,0:T(8,128)S(1)}, f32[16,10240]{1,0:T(8,128)S(1)}, u32[]{:S(2)}, u32[]{:S(2)}) collective-permute-start(f32[16,10240]{1,0:T(8,128)S(1)} %get-tuple-element.135), channel_id=1, source_target_pairs={{0,4},{12,8},{1,5},{13,9},{2,6},{14,10},{3,7},{15,11},{16,20},{28,... | collective-permute-start | bytes 1966088 | tf_op jit(solution)/shard_map/ppermute | solution.py:319
  153.1 14.8 %collective-permute-start.23 = (f32[16,10240]{1,0:T(8,128)S(1)}, f32[16,10240]{1,0:T(8,128)S(1)}, u32[]{:S(2)}, u32[]{:S(2)}) collective-permute-start(f32[16,10240]{1,0:T(8,128)S(1)} %add.41), channel_id=1, source_target_pairs={{8,4},{4,8},{9,5},{5,9},{10,6},{6,10},{11,7},{7,11},{24,20},{20,24... | collective-permute-start | bytes 1966088 | tf_op jit(solution)/shard_map/ppermute | solution.py:319
  162.8 16.8 %collective-permute-start.26 = (f32[16,10240]{1,0:T(8,128)S(1)}, f32[16,10240]{1,0:T(8,128)S(1)}, u32[]{:S(2)}, u32[]{:S(2)}) collective-permute-start(f32[16,10240]{1,0:T(8,128)S(1)} %add.43), channel_id=1, source_target_pairs={{8,4},{4,8},{9,5},{5,9},{10,6},{6,10},{11,7},{7,11},{24,20},{20,24... | collective-permute-start | bytes 1966088 | tf_op jit(solution)/shard_map/ppermute | solution.py:319
  168.0 11.6 %collective-permute-start.24 = (f32[16,10240]{1,0:T(8,128)S(1)}, f32[16,10240]{1,0:T(8,128)S(1)}, u32[]{:S(2)}, u32[]{:S(2)}) collective-permute-start(f32[16,10240]{1,0:T(8,128)S(1)} %add.42), channel_id=1, source_target_pairs={{0,4},{12,8},{4,0},{8,12},{1,5},{13,9},{5,1},{9,13},{2,6},{14,10},... | collective-permute-start | bytes 1966088 | tf_op jit(solution)/shard_map/ppermute | solution.py:319

commit v9 on v8

--- a/solution.py
+++ b/solution.py
@@ -24,12 +24,12 @@
     return high, (value - high.astype(jnp.float32)).astype(jnp.bfloat16)
 
 
-def three_passes(left, right_high, right_low):
+def three_passes(left, right_high, right_low, dimensions=ACROSS):
     left_high, left_low = split(left)
     height = left.shape[0]
     both = jnp.concatenate([left_high, left_low], axis=0)
-    first = lax.dot_general(both, right_high, ACROSS, preferred_element_type=jnp.float32)
-    last = lax.dot_general(left_high, right_low, ACROSS, preferred_element_type=jnp.float32)
+    first = lax.dot_general(both, right_high, dimensions, preferred_element_type=jnp.float32)
+    last = lax.dot_general(left_high, right_low, dimensions, preferred_element_type=jnp.float32)
     return first[:height] + (first[height:] + last)
 
 
@@ -161,9 +161,7 @@
                 for c in range(components):
                     piece = block[:, c * epochs : (c + 1) * epochs]
                     factor = taps_ref[place_ref[source], c]
-                    sums[c] = sums[c] + lax.dot_general(
-                        piece, factor, ALONG, precision=HIGHEST, preferred_element_type=jnp.float32
-                    )
+                    sums[c] = sums[c] + three_passes(piece, *split(factor), ALONG)
             weighted_ref[...] = jnp.concatenate(sums, axis=1).reshape(slots, rows, samples)
 
         weighted = jnp.concatenate([weighted_ref[shard_ref[slot]] for slot in range(slots)], axis=0)
@@ -358,7 +356,6 @@
     places = places_of(length)
     taps = normal_rows(filter_taps, place, epochs, length * epochs)
     tile = jnp.zeros((8, 128), jnp.float32)
-    high, low, tall_high, tall_low = split_design(design, [taps, shards, places, tile])
 
     def summed(partial):
         return add_up(lax.all_gather(partial, "param", axis=0))
@@ -369,6 +366,7 @@
         return Reduction(slots, length), tile
 
     if chunks == 1 or length != 4:
+        high, low, tall_high, tall_low = split_design(design, [taps, shards, places, tile])
         totals = []
         for chunk in range(chunks):
             gather = Gather(own[chunk * rows : (chunk + 1) * rows], length)
@@ -384,16 +382,17 @@
         return totals_of(totals, tile).T
 
     first = Gather(own[:rows], length)
+    first.send(1, 1)
     first.send(0, 1)
-    first.send(1, 1)
-    tile, taps, shards, places, high, low = lax.optimization_barrier((tile, taps, shards, places, high, low))
+    tile, taps, shards, places = lax.optimization_barrier((tile, taps, shards, places))
     tile = first.tie(tile, 0, 1)
     tile = first.tie(tile, 1, 1)
     first.send(0, 2)
     first.send(1, 2)
     tile = first.tie(tile, 1, 2)
     first.send(0, 3)
-    tile, value = lax.optimization_barrier((mark(tile), own[rows:]))
+    high, low, tall_high, tall_low = split_design(design, [taps, shards, places, mark(tile)])
+    tile, high, low, value = lax.optimization_barrier((tile, high, low, own[rows:]))
     second = Gather(value, length)
     second.send(0, 1)
     second.send(1, 1)

time: 182 us -> 181 us (level)
  transfers between devices with their start and end apart: 27 -> 27, of which waited for: 16 -> 17; matrix products, arithmetic and copies ran while one was open for 0% -> 0% of each run, Pallas kernels for 10% -> 10%
where the time goes in v9:
time: 181 us; the launch traced here: 180 us
  waiting for transfers between devices  93.5 us (52%)
  starting transfers between devices  49.7 us (27%)
  Pallas kernels  19.4 us (11%)
  blocking collectives  11.6 us (6%)
  local copies, waits for them, and re-layouts  5.3 us (3%)
    ppermute x11, waiting for transfers between devices, send(): lax.ppermute(value, 'tm', pairs)  50.8 us
    ppermute x10, waiting for transfers between devices, send(): value = lax.ppermute(self.onward[1 - parity, step - 1], 'tm', pairs)  35.9 us
    ppermute x10, starting transfers between devices, send(): value = lax.ppermute(self.onward[1 - parity, step - 1], 'tm', pairs)  22.1 us
    ppermute x11, starting transfers between devices, send(): lax.ppermute(value, 'tm', pairs)  19.4 us
    all_gather x2, blocking collectives, summed(): return add_up(lax.all_gather(partial, 'param', axis=0))  11.6 us
    ppermute x6, starting transfers between devices, exchange(): lax.ppermute(value, 'tm', [(i, i ^ by) for i in range(length)])  8.21 us
    ppermute x6, waiting for transfers between devices, exchange(): lax.ppermute(value, 'tm', [(i, i ^ by) for i in range(length)])  6.83 us
    pallas_call x2, Pallas kernels, multiply(): pl.pallas_call(kernel, grid_spec=pltpu.PrefetchScalarGridSpec(num_scalar_...  6.72 us
  transfers between devices with their start and end apart: 27, of which 17 were waited for; matrix products, arithmetic and copies ran while one was open for 0% of the time, Pallas kernels for 10%

profile of v9, /device:TPU:8, one launch (start us, length us, event | category | flops | bytes accessed | tf_op | source)
XLA Modules:
  0.0 180.4 jit_solution(11794432513374260082)
XLA Ops:
  1.5 5.0 %collective-permute-start.1 = (f32[16,10240]{1,0:T(8,128)S(1)}, f32[16,10240]{1,0:T(8,128)S(1)}, u32[]{:S(2)}, u32[]{:S(2)}) collective-permute-start(f32[16,10240]{1,0:T(8,128)S(1)} %get-tuple-element.138), channel_id=1, source_target_pairs={{4,8},{8,4},{5,9},{9,5},{6,10},{10,6},{7,11},{11,7},{20,24},{24,20... | collective-permute-start | bytes 1966088 | tf_op jit(solution)/shard_map/ppermute | solution.py:277
  8.4 9.5 %collective-permute-done.refs_0_ = f32[16,10240]{1,0:T(8,128)S(1)} collective-permute-done((f32[16,10240]{1,0:T(8,128)S(1)}, f32[16,10240]{1,0:T(8,128)S(1)}, u32[]{:S(2)}, u32[]{:S(2)}) %collective-permute-start) | collective-permute-done | bytes 655392 | tf_op jit(solution)/shard_map/ppermute | solution.py:277
  17.9 3.5 %collective-permute-start.2 = (f32[16,10240]{1,0:T(8,128)S(1)}, f32[16,10240]{1,0:T(8,128)S(1)}, u32[]{:S(2)}, u32[]{:S(2)}) collective-permute-start(f32[16,10240]{1,0:T(8,128)S(1)} %collective-permute-done.refs_0_), channel_id=1, source_target_pairs={{4,8},{8,4},{5,9},{9,5},{6,10},{10,6},{7,11},{11,7},{20,24},{24,20... | collective-permute-start | bytes 1966088 | tf_op jit(solution)/shard_map/ppermute | solution.py:277
  22.8 12.7 %collective-permute-done.2.refs_2_ = f32[16,10240]{1,0:T(8,128)S(1)} collective-permute-done((f32[16,10240]{1,0:T(8,128)S(1)}, f32[16,10240]{1,0:T(8,128)S(1)}, u32[]{:S(2)}, u32[]{:S(2)}) %collective-permute-start.2) | collective-permute-done | bytes 655392 | tf_op jit(solution)/shard_map/ppermute | solution.py:277
  36.8 3.2 %copy-done.1 = f32[3,64,10240]{2,1,0:T(8,128)S(1)} copy-done((f32[3,64,10240]{2,1,0:T(8,128)S(1)}, f32[3,64,10240]{2,1,0:T(8,128)}, u32[]{:S(2)}) %copy-start.1) | copy-done | bytes 7864344
  40.0 4.3 %split_design.1 = (bf16[192,10240]{1,0:T(8,128)(2,1)S(1)}, bf16[192,10240]{1,0:T(8,128)(2,1)S(1)}, bf16[10240,192]{1,0:T(8,128)(2,1)S(1)}, bf16[10240,192]{1,0:T(8,128)(2,1)S(1)}) custom-call(f32[3,64,10240]{2,1,0:T(8,128)S(1)} %copy-done.1, f32[4,3,64,64]{3,2,1,0:T(8,128)S(1)} %normal_rows.1.refs_0_.taps_ref, s32[4]{0:T(128)S(1)} %get-tuple-element.77.refs_1_.shard_ref, ...), custom_call_target="tpu_custom_call" | custom-call | flops 1 | bytes 1 | tf_op jit(solution)/shard_map/split_design/pallas_call | solution.py:49
  44.3 3.5 %collective-permute-start.9 = (f32[16,10240]{1,0:T(8,128)S(1)}, f32[16,10240]{1,0:T(8,128)S(1)}, u32[]{:S(2)}, u32[]{:S(2)}) collective-permute-start(f32[16,10240]{1,0:T(8,128)S(1)} %get-tuple-element.87), channel_id=1, source_target_pairs={{4,8},{8,4},{5,9},{9,5},{6,10},{10,6},{7,11},{11,7},{20,24},{24,20... | collective-permute-start | bytes 1966088 | tf_op jit(solution)/shard_map/ppermute | solution.py:277
  47.8 4.0 %collective-permute-done.4.refs_3_ = f32[16,10240]{1,0:T(8,128)S(1)} collective-permute-done((f32[16,10240]{1,0:T(8,128)S(1)}, f32[16,10240]{1,0:T(8,128)S(1)}, u32[]{:S(2)}, u32[]{:S(2)}) %collective-permute-start.4) | collective-permute-done | bytes 655392 | tf_op jit(solution)/shard_map/ppermute | solution.py:277
  51.9 2.9 %project.2 = f32[4,16,192]{2,1,0:T(8,128)S(1)} custom-call(s32[4]{0:T(128)S(1)} %get-tuple-element.77.refs_1_.shard_ref, bf16[10240,192]{1,0:T(8,128)(2,1)S(1)} %get-tuple-element.82.high_ref, bf16[10240,192]{1,0:T(8,128)(2,1)S(1)} %get-tuple-element.83.low_ref, f32[32,10240]{1,0:T(8,128)S(1)} %bitcast.6, f32[16,10240]{1,0:T(8,128)S(1)} %collective-permute-done.refs_0_, ...), custom_call_target="tpu_custom_call" | custom-call | flops 1 | bytes 1 | tf_op jit(solution)/shard_map/project/pallas_call | solution.py:123
  54.7 5.8 %all-gather = f32[16,16,192]{2,1,0:T(8,128)S(1)} all-gather(f32[4,16,192]{2,1,0:T(8,128)S(1)} %project.2), channel_id=2, replica_groups=mesh['groups'=2,'tm'=4,'param'=4] {'param'}, dimensions={0}, use_global_device_ids=true | all-gather | bytes 245760 | tf_op jit(solution)/shard_map/all_gather | solution.py:361
  60.5 2.5 %collective-permute-start.5 = (f32[4,16,192]{2,1,0:T(8,128)S(1)}, f32[4,16,192]{2,1,0:T(8,128)S(1)}, u32[]{:S(2)}, u32[]{:S(2)}) collective-permute-start(f32[4,16,192]{2,1,0:T(8,128)S(1)} %add_up.2.refs_0_), channel_id=1, source_target_pairs={{0,4},{4,0},{8,12},{12,8},{1,5},{5,1},{9,13},{13,9},{2,6},{6,2},{1... | collective-permute-start | bytes 147464 | tf_op jit(solution)/shard_map/ppermute | solution.py:341
  66.5 2.8 %collective-permute-done.6.refs_2_ = f32[4,16,192]{2,1,0:T(8,128)S(1)} collective-permute-done((f32[4,16,192]{2,1,0:T(8,128)S(1)}, f32[4,16,192]{2,1,0:T(8,128)S(1)}, u32[]{:S(2)}, u32[]{:S(2)}) %collective-permute-start.6) | collective-permute-done | bytes 49184 | tf_op jit(solution)/shard_map/ppermute | solution.py:341
  69.3 2.0 %collective-permute-done.7.refs_3_ = f32[4,16,192]{2,1,0:T(8,128)S(1)} collective-permute-done((f32[4,16,192]{2,1,0:T(8,128)S(1)}, f32[4,16,192]{2,1,0:T(8,128)S(1)}, u32[]{:S(2)}, u32[]{:S(2)}) %collective-permute-start.7) | collective-permute-done | bytes 49184 | tf_op jit(solution)/shard_map/ppermute | solution.py:341
  71.2 2.9 %collective-permute-start.10 = (f32[16,10240]{1,0:T(8,128)S(1)}, f32[16,10240]{1,0:T(8,128)S(1)}, u32[]{:S(2)}, u32[]{:S(2)}) collective-permute-start(f32[16,10240]{1,0:T(8,128)S(1)} %collective-permute-done.9.refs_4_), channel_id=1, source_target_pairs={{4,0},{8,12},{5,1},{9,13},{6,2},{10,14},{7,3},{11,15},{20,16},{24,... | collective-permute-start | bytes 1966088 | tf_op jit(solution)/shard_map/ppermute | solution.py:277
  74.2 3.0 %collective-permute-start.11 = (f32[16,10240]{1,0:T(8,128)S(1)}, f32[16,10240]{1,0:T(8,128)S(1)}, u32[]{:S(2)}, u32[]{:S(2)}) collective-permute-start(f32[16,10240]{1,0:T(8,128)S(1)} %collective-permute-done.8.refs_0_), channel_id=1, source_target_pairs={{4,8},{8,4},{5,9},{9,5},{6,10},{10,6},{7,11},{11,7},{20,24},{24,20... | collective-permute-start | bytes 1966088 | tf_op jit(solution)/shard_map/ppermute | solution.py:277
  77.2 3.4 %multiply.2 = (f32[16,10240]{1,0:T(8,128)S(1)}, f32[16,10240]{1,0:T(8,128)S(1)}, f32[16,10240]{1,0:T(8,128)S(1)}, f32[16,10240]{1,0:T(8,128)S(1)}) custom-call(s32[4]{0:T(128)S(1)} %get-tuple-element.77.refs_1_.shard_ref, s32[4]{0:T(128)S(1)} %get-tuple-element.78.refs_2_.place_ref, bf16[192,10240]{1,0:T(8,128)(2,1)S(1)} %get-tuple-element.90.high_ref, ...), custom_call_target="tpu_custom_call" | custom-call | flops 1 | bytes 1 | tf_op jit(solution)/shard_map/multiply/pallas_call | solution.py:172
  81.9 5.1 %collective-permute-done.10.refs_1_ = f32[16,10240]{1,0:T(8,128)S(1)} collective-permute-done((f32[16,10240]{1,0:T(8,128)S(1)}, f32[16,10240]{1,0:T(8,128)S(1)}, u32[]{:S(2)}, u32[]{:S(2)}) %collective-permute-start.10) | collective-permute-done | bytes 655392 | tf_op jit(solution)/shard_map/ppermute | solution.py:277
  87.0 4.2 %collective-permute-done.11.refs_2_ = f32[16,10240]{1,0:T(8,128)S(1)} collective-permute-done((f32[16,10240]{1,0:T(8,128)S(1)}, f32[16,10240]{1,0:T(8,128)S(1)}, u32[]{:S(2)}, u32[]{:S(2)}) %collective-permute-start.11) | collective-permute-done | bytes 655392 | tf_op jit(solution)/shard_map/ppermute | solution.py:277
  93.8 6.4 %collective-permute-done.12 = f32[16,10240]{1,0:T(8,128)S(1)} collective-permute-done((f32[16,10240]{1,0:T(8,128)S(1)}, f32[16,10240]{1,0:T(8,128)S(1)}, u32[]{:S(2)}, u32[]{:S(2)}) %collective-permute-start.12) | collective-permute-done | bytes 655392 | tf_op jit(solution)/shard_map/ppermute | solution.py:317
  100.3 2.3 %collective-permute-start.15 = (f32[16,10240]{1,0:T(8,128)S(1)}, f32[16,10240]{1,0:T(8,128)S(1)}, u32[]{:S(2)}, u32[]{:S(2)}) collective-permute-start(f32[16,10240]{1,0:T(8,128)S(1)} %add.38), channel_id=1, source_target_pairs={{8,4},{4,8},{9,5},{5,9},{10,6},{6,10},{11,7},{7,11},{24,20},{20,24... | collective-permute-start | bytes 1966088 | tf_op jit(solution)/shard_map/ppermute | solution.py:317
  104.3 2.9 %project.3 = f32[4,16,192]{2,1,0:T(8,128)S(1)} custom-call(s32[4]{0:T(128)S(1)} %get-tuple-element.77.refs_1_.shard_ref, bf16[10240,192]{1,0:T(8,128)(2,1)S(1)} %get-tuple-element.82.high_ref, bf16[10240,192]{1,0:T(8,128)(2,1)S(1)} %get-tuple-element.83.low_ref, f32[32,10240]{1,0:T(8,128)S(1)} %bitcast.7, f32[16,10240]{1,0:T(8,128)S(1)} %collective-permute-done.8.refs_0_, ...), custom_call_target="tpu_custom_call" | custom-call | flops 1 | bytes 1 | tf_op jit(solution)/shard_map/project/pallas_call | solution.py:123
  107.2 5.8 %all-gather.1 = f32[16,16,192]{2,1,0:T(8,128)S(1)} all-gather(f32[4,16,192]{2,1,0:T(8,128)S(1)} %project.3), channel_id=3, replica_groups=mesh['groups'=2,'tm'=4,'param'=4] {'param'}, dimensions={0}, use_global_device_ids=true | all-gather | bytes 245760 | tf_op jit(solution)/shard_map/all_gather | solution.py:361
  113.0 2.5 %collective-permute-start.17 = (f32[4,16,192]{2,1,0:T(8,128)S(1)}, f32[4,16,192]{2,1,0:T(8,128)S(1)}, u32[]{:S(2)}, u32[]{:S(2)}) collective-permute-start(f32[4,16,192]{2,1,0:T(8,128)S(1)} %add_up.3.refs_0_), channel_id=1, source_target_pairs={{0,4},{4,0},{8,12},{12,8},{1,5},{5,1},{9,13},{13,9},{2,6},{6,2},{1... | collective-permute-start | bytes 147464 | tf_op jit(solution)/shard_map/ppermute | solution.py:341
  117.2 3.3 %collective-permute-start.21 = (f32[16,10240]{1,0:T(8,128)S(1)}, f32[16,10240]{1,0:T(8,128)S(1)}, u32[]{:S(2)}, u32[]{:S(2)}) collective-permute-start(f32[16,10240]{1,0:T(8,128)S(1)} %add.40), channel_id=1, source_target_pairs={{8,4},{4,8},{9,5},{5,9},{10,6},{6,10},{11,7},{7,11},{24,20},{20,24... | collective-permute-start | bytes 1966088 | tf_op jit(solution)/shard_map/ppermute | solution.py:317
  120.6 7.0 %collective-permute-done.16.refs_1_ = f32[16,10240]{1,0:T(8,128)S(1)} collective-permute-done((f32[16,10240]{1,0:T(8,128)S(1)}, f32[16,10240]{1,0:T(8,128)S(1)}, u32[]{:S(2)}, u32[]{:S(2)}) %collective-permute-start.16) | collective-permute-done | bytes 655392 | tf_op jit(solution)/shard_map/ppermute | solution.py:317
  129.3 3.4 %multiply.3 = (f32[16,10240]{1,0:T(8,128)S(1)}, f32[16,10240]{1,0:T(8,128)S(1)}, f32[16,10240]{1,0:T(8,128)S(1)}, f32[16,10240]{1,0:T(8,128)S(1)}) custom-call(s32[4]{0:T(128)S(1)} %get-tuple-element.77.refs_1_.shard_ref, s32[4]{0:T(128)S(1)} %get-tuple-element.78.refs_2_.place_ref, bf16[192,10240]{1,0:T(8,128)(2,1)S(1)} %get-tuple-element.90.high_ref, ...), custom_call_target="tpu_custom_call" | custom-call | flops 1 | bytes 1 | tf_op jit(solution)/shard_map/multiply/pallas_call | solution.py:172
  134.0 5.9 %collective-permute-done.20.refs_2_ = f32[16,10240]{1,0:T(8,128)S(1)} collective-permute-done((f32[16,10240]{1,0:T(8,128)S(1)}, f32[16,10240]{1,0:T(8,128)S(1)}, u32[]{:S(2)}, u32[]{:S(2)}) %collective-permute-start.20) | collective-permute-done | bytes 655392 | tf_op jit(solution)/shard_map/ppermute | solution.py:317
  141.2 11.1 %collective-permute-done.22 = f32[16,10240]{1,0:T(8,128)S(1)} collective-permute-done((f32[16,10240]{1,0:T(8,128)S(1)}, f32[16,10240]{1,0:T(8,128)S(1)}, u32[]{:S(2)}, u32[]{:S(2)}) %collective-permute-start.22) | collective-permute-done | bytes 655392 | tf_op jit(solution)/shard_map/ppermute | solution.py:317
  152.3 3.1 %collective-permute-start.23 = (f32[16,10240]{1,0:T(8,128)S(1)}, f32[16,10240]{1,0:T(8,128)S(1)}, u32[]{:S(2)}, u32[]{:S(2)}) collective-permute-start(f32[16,10240]{1,0:T(8,128)S(1)} %add.41), channel_id=1, source_target_pairs={{8,4},{4,8},{9,5},{5,9},{10,6},{6,10},{11,7},{7,11},{24,20},{20,24... | collective-permute-start | bytes 1966088 | tf_op jit(solution)/shard_map/ppermute | solution.py:317
  155.5 6.9 %collective-permute-done.25 = f32[16,10240]{1,0:T(8,128)S(1)} collective-permute-done((f32[16,10240]{1,0:T(8,128)S(1)}, f32[16,10240]{1,0:T(8,128)S(1)}, u32[]{:S(2)}, u32[]{:S(2)}) %collective-permute-start.25) | collective-permute-done | bytes 655392 | tf_op jit(solution)/shard_map/ppermute | solution.py:317
  162.5 2.7 %collective-permute-start.26 = (f32[16,10240]{1,0:T(8,128)S(1)}, f32[16,10240]{1,0:T(8,128)S(1)}, u32[]{:S(2)}, u32[]{:S(2)}) collective-permute-start(f32[16,10240]{1,0:T(8,128)S(1)} %add.43), channel_id=1, source_target_pairs={{8,4},{4,8},{9,5},{5,9},{10,6},{6,10},{11,7},{7,11},{24,20},{20,24... | collective-permute-start | bytes 1966088 | tf_op jit(solution)/shard_map/ppermute | solution.py:317
  166.5 12.3 %collective-permute-done.26.refs_6_ = f32[16,10240]{1,0:T(8,128)S(1)} collective-permute-done((f32[16,10240]{1,0:T(8,128)S(1)}, f32[16,10240]{1,0:T(8,128)S(1)}, u32[]{:S(2)}, u32[]{:S(2)}) %collective-permute-start.26) | collective-permute-done | bytes 655392 | tf_op jit(solution)/shard_map/ppermute | solution.py:317
  (56 shorter events, 24.2 us)
Async XLA Ops:
  1.4 16.5 %collective-permute-start = (f32[16,10240]{1,0:T(8,128)S(1)}, f32[16,10240]{1,0:T(8,128)S(1)}, u32[]{:S(2)}, u32[]{:S(2)}) collective-permute-start(f32[16,10240]{1,0:T(8,128)S(1)} %get-tuple-element.138), channel_id=1, source_target_pairs={{0,4},{12,8},{4,0},{8,12},{1,5},{13,9},{5,1},{9,13},{2,6},{14,10},... | collective-permute-start | bytes 1966088 | tf_op jit(solution)/shard_map/ppermute | solution.py:277
  1.5 19.9 %collective-permute-start.1 = (f32[16,10240]{1,0:T(8,128)S(1)}, f32[16,10240]{1,0:T(8,128)S(1)}, u32[]{:S(2)}, u32[]{:S(2)}) collective-permute-start(f32[16,10240]{1,0:T(8,128)S(1)} %get-tuple-element.138), channel_id=1, source_target_pairs={{4,8},{8,4},{5,9},{9,5},{6,10},{10,6},{7,11},{11,7},{20,24},{24,20... | collective-permute-start | bytes 1966088 | tf_op jit(solution)/shard_map/ppermute | solution.py:277
  6.5 0.7 copy-start.2
  17.9 17.5 %collective-permute-start.2 = (f32[16,10240]{1,0:T(8,128)S(1)}, f32[16,10240]{1,0:T(8,128)S(1)}, u32[]{:S(2)}, u32[]{:S(2)}) collective-permute-start(f32[16,10240]{1,0:T(8,128)S(1)} %collective-permute-done.refs_0_), channel_id=1, source_target_pairs={{4,8},{8,4},{5,9},{9,5},{6,10},{10,6},{7,11},{11,7},{20,24},{24,20... | collective-permute-start | bytes 1966088 | tf_op jit(solution)/shard_map/ppermute | solution.py:277
  21.4 26.4 %collective-permute-start.3 = (f32[16,10240]{1,0:T(8,128)S(1)}, f32[16,10240]{1,0:T(8,128)S(1)}, u32[]{:S(2)}, u32[]{:S(2)}) collective-permute-start(f32[16,10240]{1,0:T(8,128)S(1)} %collective-permute-done.1.refs_4_), channel_id=1, source_target_pairs={{4,0},{8,12},{5,1},{9,13},{6,2},{10,14},{7,3},{11,15},{20,16},{24,... | collective-permute-start | bytes 1966088 | tf_op jit(solution)/shard_map/ppermute | solution.py:277
  35.4 16.5 %collective-permute-start.4 = (f32[16,10240]{1,0:T(8,128)S(1)}, f32[16,10240]{1,0:T(8,128)S(1)}, u32[]{:S(2)}, u32[]{:S(2)}) collective-permute-start(f32[16,10240]{1,0:T(8,128)S(1)} %collective-permute-done.2.refs_2_), channel_id=1, source_target_pairs={{4,0},{8,12},{5,1},{9,13},{6,2},{10,14},{7,3},{11,15},{20,16},{24,... | collective-permute-start | bytes 1966088 | tf_op jit(solution)/shard_map/ppermute | solution.py:277
  36.8 3.2 %copy-start.1 = (f32[3,64,10240]{2,1,0:T(8,128)S(1)}, f32[3,64,10240]{2,1,0:T(8,128)}, u32[]{:S(2)}) copy-start(f32[3,64,10240]{2,1,0:T(8,128)} %design_ref.1) | copy-start | bytes 23592964
  40.0 11.9 %copy-start = (f32[10240,32]{0,1:T(8,128)S(1)}, f32[10240,32]{0,1:T(8,128)}, u32[]{:S(2)}) copy-start(f32[10240,32]{0,1:T(8,128)} %param.5) | copy-start | bytes 3932164
  44.3 27.0 %collective-permute-start.8 = (f32[16,10240]{1,0:T(8,128)S(1)}, f32[16,10240]{1,0:T(8,128)S(1)}, u32[]{:S(2)}, u32[]{:S(2)}) collective-permute-start(f32[16,10240]{1,0:T(8,128)S(1)} %get-tuple-element.87), channel_id=1, source_target_pairs={{0,4},{12,8},{4,0},{8,12},{1,5},{13,9},{5,1},{9,13},{2,6},{14,10},... | collective-permute-start | bytes 1966088 | tf_op jit(solution)/shard_map/ppermute | solution.py:277
  44.3 26.9 %collective-permute-start.9 = (f32[16,10240]{1,0:T(8,128)S(1)}, f32[16,10240]{1,0:T(8,128)S(1)}, u32[]{:S(2)}, u32[]{:S(2)}) collective-permute-start(f32[16,10240]{1,0:T(8,128)S(1)} %get-tuple-element.87), channel_id=1, source_target_pairs={{4,8},{8,4},{5,9},{9,5},{6,10},{10,6},{7,11},{11,7},{20,24},{24,20... | collective-permute-start | bytes 1966088 | tf_op jit(solution)/shard_map/ppermute | solution.py:277
  60.5 5.9 %collective-permute-start.5 = (f32[4,16,192]{2,1,0:T(8,128)S(1)}, f32[4,16,192]{2,1,0:T(8,128)S(1)}, u32[]{:S(2)}, u32[]{:S(2)}) collective-permute-start(f32[4,16,192]{2,1,0:T(8,128)S(1)} %add_up.2.refs_0_), channel_id=1, source_target_pairs={{0,4},{4,0},{8,12},{12,8},{1,5},{5,1},{9,13},{13,9},{2,6},{6,2},{1... | collective-permute-start | bytes 147464 | tf_op jit(solution)/shard_map/ppermute | solution.py:341
  63.1 6.2 %collective-permute-start.6 = (f32[4,16,192]{2,1,0:T(8,128)S(1)}, f32[4,16,192]{2,1,0:T(8,128)S(1)}, u32[]{:S(2)}, u32[]{:S(2)}) collective-permute-start(f32[4,16,192]{2,1,0:T(8,128)S(1)} %add_up.2.refs_0_), channel_id=1, source_target_pairs={{0,8},{4,12},{8,0},{12,4},{1,9},{5,13},{9,1},{13,5},{2,10},{6,14},... | collective-permute-start | bytes 147464 | tf_op jit(solution)/shard_map/ppermute | solution.py:341
  64.2 7.1 %collective-permute-start.7 = (f32[4,16,192]{2,1,0:T(8,128)S(1)}, f32[4,16,192]{2,1,0:T(8,128)S(1)}, u32[]{:S(2)}, u32[]{:S(2)}) collective-permute-start(f32[4,16,192]{2,1,0:T(8,128)S(1)} %add_up.2.refs_0_), channel_id=1, source_target_pairs={{0,12},{4,8},{8,4},{12,0},{1,13},{5,9},{9,5},{13,1},{2,14},{6,10},... | collective-permute-start | bytes 147464 | tf_op jit(solution)/shard_map/ppermute | solution.py:341
  71.2 15.7 %collective-permute-start.10 = (f32[16,10240]{1,0:T(8,128)S(1)}, f32[16,10240]{1,0:T(8,128)S(1)}, u32[]{:S(2)}, u32[]{:S(2)}) collective-permute-start(f32[16,10240]{1,0:T(8,128)S(1)} %collective-permute-done.9.refs_4_), channel_id=1, source_target_pairs={{4,0},{8,12},{5,1},{9,13},{6,2},{10,14},{7,3},{11,15},{20,16},{24,... | collective-permute-start | bytes 1966088 | tf_op jit(solution)/shard_map/ppermute | solution.py:277
  74.2 16.9 %collective-permute-start.11 = (f32[16,10240]{1,0:T(8,128)S(1)}, f32[16,10240]{1,0:T(8,128)S(1)}, u32[]{:S(2)}, u32[]{:S(2)}) collective-permute-start(f32[16,10240]{1,0:T(8,128)S(1)} %collective-permute-done.8.refs_0_), channel_id=1, source_target_pairs={{4,8},{8,4},{5,9},{9,5},{6,10},{10,6},{7,11},{11,7},{20,24},{24,20... | collective-permute-start | bytes 1966088 | tf_op jit(solution)/shard_map/ppermute | solution.py:277
  80.6 19.6 %collective-permute-start.12 = (f32[16,10240]{1,0:T(8,128)S(1)}, f32[16,10240]{1,0:T(8,128)S(1)}, u32[]{:S(2)}, u32[]{:S(2)}) collective-permute-start(f32[16,10240]{1,0:T(8,128)S(1)} %get-tuple-element.106), channel_id=1, source_target_pairs={{0,4},{12,8},{1,5},{13,9},{2,6},{14,10},{3,7},{15,11},{16,20},{28,... | collective-permute-start | bytes 1966088 | tf_op jit(solution)/shard_map/ppermute | solution.py:317
  91.1 13.2 %collective-permute-start.13 = (f32[16,10240]{1,0:T(8,128)S(1)}, f32[16,10240]{1,0:T(8,128)S(1)}, u32[]{:S(2)}, u32[]{:S(2)}) collective-permute-start(f32[16,10240]{1,0:T(8,128)S(1)} %collective-permute-done.11.refs_2_), channel_id=1, source_target_pairs={{4,0},{8,12},{5,1},{9,13},{6,2},{10,14},{7,3},{11,15},{20,16},{24,... | collective-permute-start | bytes 1966088 | tf_op jit(solution)/shard_map/ppermute | solution.py:277
  92.5 24.0 %collective-permute-start.14 = (f32[16,10240]{1,0:T(8,128)S(1)}, f32[16,10240]{1,0:T(8,128)S(1)}, u32[]{:S(2)}, u32[]{:S(2)}) collective-permute-start(f32[16,10240]{1,0:T(8,128)S(1)} %get-tuple-element.110), channel_id=1, source_target_pairs={{0,4},{12,8},{1,5},{13,9},{2,6},{14,10},{3,7},{15,11},{16,20},{28,... | collective-permute-start | bytes 1966088 | tf_op jit(solution)/shard_map/ppermute | solution.py:317
  100.3 16.9 %collective-permute-start.15 = (f32[16,10240]{1,0:T(8,128)S(1)}, f32[16,10240]{1,0:T(8,128)S(1)}, u32[]{:S(2)}, u32[]{:S(2)}) collective-permute-start(f32[16,10240]{1,0:T(8,128)S(1)} %add.38), channel_id=1, source_target_pairs={{8,4},{4,8},{9,5},{5,9},{10,6},{6,10},{11,7},{7,11},{24,20},{20,24... | collective-permute-start | bytes 1966088 | tf_op jit(solution)/shard_map/ppermute | solution.py:317
  102.6 25.0 %collective-permute-start.16 = (f32[16,10240]{1,0:T(8,128)S(1)}, f32[16,10240]{1,0:T(8,128)S(1)}, u32[]{:S(2)}, u32[]{:S(2)}) collective-permute-start(f32[16,10240]{1,0:T(8,128)S(1)} %get-tuple-element.114), channel_id=1, source_target_pairs={{0,4},{12,8},{1,5},{13,9},{2,6},{14,10},{3,7},{15,11},{16,20},{28,... | collective-permute-start | bytes 1966088 | tf_op jit(solution)/shard_map/ppermute | solution.py:317
  113.0 16.1 %collective-permute-start.17 = (f32[4,16,192]{2,1,0:T(8,128)S(1)}, f32[4,16,192]{2,1,0:T(8,128)S(1)}, u32[]{:S(2)}, u32[]{:S(2)}) collective-permute-start(f32[4,16,192]{2,1,0:T(8,128)S(1)} %add_up.3.refs_0_), channel_id=1, source_target_pairs={{0,4},{4,0},{8,12},{12,8},{1,5},{5,1},{9,13},{13,9},{2,6},{6,2},{1... | collective-permute-start | bytes 147464 | tf_op jit(solution)/shard_map/ppermute | solution.py:341
  115.5 13.8 %collective-permute-start.18 = (f32[4,16,192]{2,1,0:T(8,128)S(1)}, f32[4,16,192]{2,1,0:T(8,128)S(1)}, u32[]{:S(2)}, u32[]{:S(2)}) collective-permute-start(f32[4,16,192]{2,1,0:T(8,128)S(1)} %add_up.3.refs_0_), channel_id=1, source_target_pairs={{0,8},{4,12},{8,0},{12,4},{1,9},{5,13},{9,1},{13,5},{2,10},{6,14},... | collective-permute-start | bytes 147464 | tf_op jit(solution)/shard_map/ppermute | solution.py:341
  116.5 12.9 %collective-permute-start.19 = (f32[4,16,192]{2,1,0:T(8,128)S(1)}, f32[4,16,192]{2,1,0:T(8,128)S(1)}, u32[]{:S(2)}, u32[]{:S(2)}) collective-permute-start(f32[4,16,192]{2,1,0:T(8,128)S(1)} %add_up.3.refs_0_), channel_id=1, source_target_pairs={{0,12},{4,8},{8,4},{12,0},{1,13},{5,9},{9,5},{13,1},{2,14},{6,10},... | collective-permute-start | bytes 147464 | tf_op jit(solution)/shard_map/ppermute | solution.py:341
  117.2 22.7 %collective-permute-start.21 = (f32[16,10240]{1,0:T(8,128)S(1)}, f32[16,10240]{1,0:T(8,128)S(1)}, u32[]{:S(2)}, u32[]{:S(2)}) collective-permute-start(f32[16,10240]{1,0:T(8,128)S(1)} %add.40), channel_id=1, source_target_pairs={{8,4},{4,8},{9,5},{5,9},{10,6},{6,10},{11,7},{7,11},{24,20},{20,24... | collective-permute-start | bytes 1966088 | tf_op jit(solution)/shard_map/ppermute | solution.py:317
  127.6 12.3 %collective-permute-start.20 = (f32[16,10240]{1,0:T(8,128)S(1)}, f32[16,10240]{1,0:T(8,128)S(1)}, u32[]{:S(2)}, u32[]{:S(2)}) collective-permute-start(f32[16,10240]{1,0:T(8,128)S(1)} %add.39), channel_id=1, source_target_pairs={{4,0},{8,12},{5,1},{9,13},{6,2},{10,14},{7,3},{11,15},{20,16},{24,... | collective-permute-start | bytes 1966088 | tf_op jit(solution)/shard_map/ppermute | solution.py:317
  132.7 19.6 %collective-permute-start.22 = (f32[16,10240]{1,0:T(8,128)S(1)}, f32[16,10240]{1,0:T(8,128)S(1)}, u32[]{:S(2)}, u32[]{:S(2)}) collective-permute-start(f32[16,10240]{1,0:T(8,128)S(1)} %get-tuple-element.133), channel_id=1, source_target_pairs={{0,4},{12,8},{1,5},{13,9},{2,6},{14,10},{3,7},{15,11},{16,20},{28,... | collective-permute-start | bytes 1966088 | tf_op jit(solution)/shard_map/ppermute | solution.py:317
  139.9 22.5 %collective-permute-start.25 = (f32[16,10240]{1,0:T(8,128)S(1)}, f32[16,10240]{1,0:T(8,128)S(1)}, u32[]{:S(2)}, u32[]{:S(2)}) collective-permute-start(f32[16,10240]{1,0:T(8,128)S(1)} %get-tuple-element.135), channel_id=1, source_target_pairs={{0,4},{12,8},{1,5},{13,9},{2,6},{14,10},{3,7},{15,11},{16,20},{28,... | collective-permute-start | bytes 1966088 | tf_op jit(solution)/shard_map/ppermute | solution.py:317
  152.3 14.0 %collective-permute-start.23 = (f32[16,10240]{1,0:T(8,128)S(1)}, f32[16,10240]{1,0:T(8,128)S(1)}, u32[]{:S(2)}, u32[]{:S(2)}) collective-permute-start(f32[16,10240]{1,0:T(8,128)S(1)} %add.41), channel_id=1, source_target_pairs={{8,4},{4,8},{9,5},{5,9},{10,6},{6,10},{11,7},{7,11},{24,20},{20,24... | collective-permute-start | bytes 1966088 | tf_op jit(solution)/shard_map/ppermute | solution.py:317
  162.5 16.4 %collective-permute-start.26 = (f32[16,10240]{1,0:T(8,128)S(1)}, f32[16,10240]{1,0:T(8,128)S(1)}, u32[]{:S(2)}, u32[]{:S(2)}) collective-permute-start(f32[16,10240]{1,0:T(8,128)S(1)} %add.43), channel_id=1, source_target_pairs={{8,4},{4,8},{9,5},{5,9},{10,6},{6,10},{11,7},{7,11},{24,20},{20,24... | collective-permute-start | bytes 1966088 | tf_op jit(solution)/shard_map/ppermute | solution.py:317
  166.5 12.4 %collective-permute-start.24 = (f32[16,10240]{1,0:T(8,128)S(1)}, f32[16,10240]{1,0:T(8,128)S(1)}, u32[]{:S(2)}, u32[]{:S(2)}) collective-permute-start(f32[16,10240]{1,0:T(8,128)S(1)} %add.42), channel_id=1, source_target_pairs={{0,4},{12,8},{4,0},{8,12},{1,5},{13,9},{5,1},{9,13},{2,6},{14,10},... | collective-permute-start | bytes 1966088 | tf_op jit(solution)/shard_map/ppermute | solution.py:317

commit v10 on v9

--- a/solution.py
+++ b/solution.py
@@ -97,7 +97,7 @@
     coefficients, samples = tall_high.shape
     slots = len(arrivals) + 1
     rows = arrivals[0][0].shape[0]
-    width = math.gcd(coefficients, 5120)
+    width = math.gcd(coefficients, 10240)
     counts = [len(pieces) for pieces in arrivals]
     pieces = [piece for group in arrivals for piece in group]
 
@@ -145,7 +145,7 @@
     samples, coefficients = high.shape
     _, components, epochs, _ = taps.shape
     slots, rows, _ = blocks[0].shape
-    width = math.gcd(coefficients, 5120)
+    width = math.gcd(coefficients, 10240)
     count = len(blocks)
 
     def kernel(shard_ref, place_ref, high_ref, low_ref, taps_ref, *refs):

time: 181 us -> 180 us (level)
  Pallas kernels: 19.4 us -> 16.4 us
    ppermute x10, waiting for transfers between devices: 35.9 us -> 38.7 us  [send(): value = lax.ppermute(self.onward[1 - parity, step - 1], 'tm', pairs)]
    ppermute x11, waiting for transfers between devices: 50.8 us -> 48.4 us  [send(): lax.ppermute(value, 'tm', pairs)]
    pallas_call x2, Pallas kernels: 6.72 us -> 4.82 us  [multiply(): pl.pallas_call(kernel, grid_spec=pltpu.PrefetchScalarGridSpec(num_scalar_...]
  transfers between devices with their start and end apart: 27 -> 27, of which waited for: 17 -> 17; matrix products, arithmetic and copies ran while one was open for 0% -> 0% of each run, Pallas kernels for 10% -> 8%
where the time goes in v10:
time: 180 us; the launch traced here: 178 us
  waiting for transfers between devices  94.2 us (52%)
  starting transfers between devices  50 us (28%)
  Pallas kernels  16.4 us (9%)
  blocking collectives  11.6 us (6%)
  local copies, waits for them, and re-layouts  5.3 us (3%)
    ppermute x11, waiting for transfers between devices, send(): lax.ppermute(value, 'tm', pairs)  48.4 us
    ppermute x10, waiting for transfers between devices, send(): value = lax.ppermute(self.onward[1 - parity, step - 1], 'tm', pairs)  38.7 us
    ppermute x10, starting transfers between devices, send(): value = lax.ppermute(self.onward[1 - parity, step - 1], 'tm', pairs)  22.1 us
    ppermute x11, starting transfers between devices, send(): lax.ppermute(value, 'tm', pairs)  19.7 us
    all_gather x2, blocking collectives, summed(): return add_up(lax.all_gather(partial, 'param', axis=0))  11.6 us
    ppermute x6, starting transfers between devices, exchange(): lax.ppermute(value, 'tm', [(i, i ^ by) for i in range(length)])  8.23 us
    ppermute x6, waiting for transfers between devices, exchange(): lax.ppermute(value, 'tm', [(i, i ^ by) for i in range(length)])  6.99 us
    pallas_call x2, Pallas kernels, multiply(): pl.pallas_call(kernel, grid_spec=pltpu.PrefetchScalarGridSpec(num_scalar_...  4.82 us
  transfers between devices with their start and end apart: 27, of which 17 were waited for; matrix products, arithmetic and copies ran while one was open for 0% of the time, Pallas kernels for 8%

profile of v10, /device:TPU:8, one launch (start us, length us, event | category | flops | bytes accessed | tf_op | source)
XLA Modules:
  0.0 178.4 jit_solution(11729955347313920102)
XLA Ops:
  1.5 5.0 %collective-permute-start.1 = (f32[16,10240]{1,0:T(8,128)S(1)}, f32[16,10240]{1,0:T(8,128)S(1)}, u32[]{:S(2)}, u32[]{:S(2)}) collective-permute-start(f32[16,10240]{1,0:T(8,128)S(1)} %get-tuple-element.138), channel_id=1, source_target_pairs={{4,8},{8,4},{5,9},{9,5},{6,10},{10,6},{7,11},{11,7},{20,24},{24,20... | collective-permute-start | bytes 1966088 | tf_op jit(solution)/shard_map/ppermute | solution.py:277
  8.4 9.5 %collective-permute-done.refs_0_ = f32[16,10240]{1,0:T(8,128)S(1)} collective-permute-done((f32[16,10240]{1,0:T(8,128)S(1)}, f32[16,10240]{1,0:T(8,128)S(1)}, u32[]{:S(2)}, u32[]{:S(2)}) %collective-permute-start) | collective-permute-done | bytes 655392 | tf_op jit(solution)/shard_map/ppermute | solution.py:277
  17.9 3.5 %collective-permute-start.2 = (f32[16,10240]{1,0:T(8,128)S(1)}, f32[16,10240]{1,0:T(8,128)S(1)}, u32[]{:S(2)}, u32[]{:S(2)}) collective-permute-start(f32[16,10240]{1,0:T(8,128)S(1)} %collective-permute-done.refs_0_), channel_id=1, source_target_pairs={{4,8},{8,4},{5,9},{9,5},{6,10},{10,6},{7,11},{11,7},{20,24},{24,20... | collective-permute-start | bytes 1966088 | tf_op jit(solution)/shard_map/ppermute | solution.py:277
  22.8 12.7 %collective-permute-done.2.refs_2_ = f32[16,10240]{1,0:T(8,128)S(1)} collective-permute-done((f32[16,10240]{1,0:T(8,128)S(1)}, f32[16,10240]{1,0:T(8,128)S(1)}, u32[]{:S(2)}, u32[]{:S(2)}) %collective-permute-start.2) | collective-permute-done | bytes 655392 | tf_op jit(solution)/shard_map/ppermute | solution.py:277
  36.8 3.2 %copy-done.1 = f32[3,64,10240]{2,1,0:T(8,128)S(1)} copy-done((f32[3,64,10240]{2,1,0:T(8,128)S(1)}, f32[3,64,10240]{2,1,0:T(8,128)}, u32[]{:S(2)}) %copy-start.1) | copy-done | bytes 7864344
  40.0 4.3 %split_design.1 = (bf16[192,10240]{1,0:T(8,128)(2,1)S(1)}, bf16[192,10240]{1,0:T(8,128)(2,1)S(1)}, bf16[10240,192]{1,0:T(8,128)(2,1)S(1)}, bf16[10240,192]{1,0:T(8,128)(2,1)S(1)}) custom-call(f32[3,64,10240]{2,1,0:T(8,128)S(1)} %copy-done.1, f32[4,3,64,64]{3,2,1,0:T(8,128)S(1)} %normal_rows.1.refs_0_.taps_ref, s32[4]{0:T(128)S(1)} %get-tuple-element.77.refs_1_.shard_ref, ...), custom_call_target="tpu_custom_call" | custom-call | flops 1 | bytes 1 | tf_op jit(solution)/shard_map/split_design/pallas_call | solution.py:49
  44.3 3.5 %collective-permute-start.9 = (f32[16,10240]{1,0:T(8,128)S(1)}, f32[16,10240]{1,0:T(8,128)S(1)}, u32[]{:S(2)}, u32[]{:S(2)}) collective-permute-start(f32[16,10240]{1,0:T(8,128)S(1)} %get-tuple-element.87), channel_id=1, source_target_pairs={{4,8},{8,4},{5,9},{9,5},{6,10},{10,6},{7,11},{11,7},{20,24},{24,20... | collective-permute-start | bytes 1966088 | tf_op jit(solution)/shard_map/ppermute | solution.py:277
  47.8 4.0 %collective-permute-done.4.refs_3_ = f32[16,10240]{1,0:T(8,128)S(1)} collective-permute-done((f32[16,10240]{1,0:T(8,128)S(1)}, f32[16,10240]{1,0:T(8,128)S(1)}, u32[]{:S(2)}, u32[]{:S(2)}) %collective-permute-start.4) | collective-permute-done | bytes 655392 | tf_op jit(solution)/shard_map/ppermute | solution.py:277
  51.9 2.3 %project.2 = f32[4,16,192]{2,1,0:T(8,128)S(1)} custom-call(s32[4]{0:T(128)S(1)} %get-tuple-element.77.refs_1_.shard_ref, bf16[10240,192]{1,0:T(8,128)(2,1)S(1)} %get-tuple-element.82.high_ref, bf16[10240,192]{1,0:T(8,128)(2,1)S(1)} %get-tuple-element.83.low_ref, f32[32,10240]{1,0:T(8,128)S(1)} %bitcast.6, f32[16,10240]{1,0:T(8,128)S(1)} %collective-permute-done.refs_0_, ...), custom_call_target="tpu_custom_call" | custom-call | flops 1 | bytes 1 | tf_op jit(solution)/shard_map/project/pallas_call | solution.py:123
  54.2 5.8 %all-gather = f32[16,16,192]{2,1,0:T(8,128)S(1)} all-gather(f32[4,16,192]{2,1,0:T(8,128)S(1)} %project.2), channel_id=2, replica_groups=mesh['groups'=2,'tm'=4,'param'=4] {'param'}, dimensions={0}, use_global_device_ids=true | all-gather | bytes 245760 | tf_op jit(solution)/shard_map/all_gather | solution.py:361
  60.0 2.5 %collective-permute-start.5 = (f32[4,16,192]{2,1,0:T(8,128)S(1)}, f32[4,16,192]{2,1,0:T(8,128)S(1)}, u32[]{:S(2)}, u32[]{:S(2)}) collective-permute-start(f32[4,16,192]{2,1,0:T(8,128)S(1)} %add_up.2.refs_0_), channel_id=1, source_target_pairs={{0,4},{4,0},{8,12},{12,8},{1,5},{5,1},{9,13},{13,9},{2,6},{6,2},{1... | collective-permute-start | bytes 147464 | tf_op jit(solution)/shard_map/ppermute | solution.py:341
  64.2 2.3 %collective-permute-done.5.refs_1_ = f32[4,16,192]{2,1,0:T(8,128)S(1)} collective-permute-done((f32[4,16,192]{2,1,0:T(8,128)S(1)}, f32[4,16,192]{2,1,0:T(8,128)S(1)}, u32[]{:S(2)}, u32[]{:S(2)}) %collective-permute-start.5) | collective-permute-done | bytes 49184 | tf_op jit(solution)/shard_map/ppermute | solution.py:341
  66.5 2.3 %collective-permute-done.6.refs_2_ = f32[4,16,192]{2,1,0:T(8,128)S(1)} collective-permute-done((f32[4,16,192]{2,1,0:T(8,128)S(1)}, f32[4,16,192]{2,1,0:T(8,128)S(1)}, u32[]{:S(2)}, u32[]{:S(2)}) %collective-permute-start.6) | collective-permute-done | bytes 49184 | tf_op jit(solution)/shard_map/ppermute | solution.py:341
  70.7 2.9 %collective-permute-start.10 = (f32[16,10240]{1,0:T(8,128)S(1)}, f32[16,10240]{1,0:T(8,128)S(1)}, u32[]{:S(2)}, u32[]{:S(2)}) collective-permute-start(f32[16,10240]{1,0:T(8,128)S(1)} %collective-permute-done.9.refs_4_), channel_id=1, source_target_pairs={{4,0},{8,12},{5,1},{9,13},{6,2},{10,14},{7,3},{11,15},{20,16},{24,... | collective-permute-start | bytes 1966088 | tf_op jit(solution)/shard_map/ppermute | solution.py:277
  73.7 3.0 %collective-permute-start.11 = (f32[16,10240]{1,0:T(8,128)S(1)}, f32[16,10240]{1,0:T(8,128)S(1)}, u32[]{:S(2)}, u32[]{:S(2)}) collective-permute-start(f32[16,10240]{1,0:T(8,128)S(1)} %collective-permute-done.8.refs_0_), channel_id=1, source_target_pairs={{4,8},{8,4},{5,9},{9,5},{6,10},{10,6},{7,11},{11,7},{20,24},{24,20... | collective-permute-start | bytes 1966088 | tf_op jit(solution)/shard_map/ppermute | solution.py:277
  76.7 2.4 %multiply.2 = (f32[16,10240]{1,0:T(8,128)S(1)}, f32[16,10240]{1,0:T(8,128)S(1)}, f32[16,10240]{1,0:T(8,128)S(1)}, f32[16,10240]{1,0:T(8,128)S(1)}) custom-call(s32[4]{0:T(128)S(1)} %get-tuple-element.77.refs_1_.shard_ref, s32[4]{0:T(128)S(1)} %get-tuple-element.78.refs_2_.place_ref, bf16[192,10240]{1,0:T(8,128)(2,1)S(1)} %get-tuple-element.90.high_ref, ...), custom_call_target="tpu_custom_call" | custom-call | flops 1 | bytes 1 | tf_op jit(solution)/shard_map/multiply/pallas_call | solution.py:172
  80.4 6.0 %collective-permute-done.10.refs_1_ = f32[16,10240]{1,0:T(8,128)S(1)} collective-permute-done((f32[16,10240]{1,0:T(8,128)S(1)}, f32[16,10240]{1,0:T(8,128)S(1)}, u32[]{:S(2)}, u32[]{:S(2)}) %collective-permute-start.10) | collective-permute-done | bytes 655392 | tf_op jit(solution)/shard_map/ppermute | solution.py:277
  86.5 4.2 %collective-permute-done.11.refs_2_ = f32[16,10240]{1,0:T(8,128)S(1)} collective-permute-done((f32[16,10240]{1,0:T(8,128)S(1)}, f32[16,10240]{1,0:T(8,128)S(1)}, u32[]{:S(2)}, u32[]{:S(2)}) %collective-permute-start.11) | collective-permute-done | bytes 655392 | tf_op jit(solution)/shard_map/ppermute | solution.py:277
  93.3 4.6 %collective-permute-done.12 = f32[16,10240]{1,0:T(8,128)S(1)} collective-permute-done((f32[16,10240]{1,0:T(8,128)S(1)}, f32[16,10240]{1,0:T(8,128)S(1)}, u32[]{:S(2)}, u32[]{:S(2)}) %collective-permute-start.12) | collective-permute-done | bytes 655392 | tf_op jit(solution)/shard_map/ppermute | solution.py:317
  101.4 2.4 %collective-permute-done.13.refs_3_ = f32[16,10240]{1,0:T(8,128)S(1)} collective-permute-done((f32[16,10240]{1,0:T(8,128)S(1)}, f32[16,10240]{1,0:T(8,128)S(1)}, u32[]{:S(2)}, u32[]{:S(2)}) %collective-permute-start.13) | collective-permute-done | bytes 655392 | tf_op jit(solution)/shard_map/ppermute | solution.py:277
  103.8 2.3 %project.3 = f32[4,16,192]{2,1,0:T(8,128)S(1)} custom-call(s32[4]{0:T(128)S(1)} %get-tuple-element.77.refs_1_.shard_ref, bf16[10240,192]{1,0:T(8,128)(2,1)S(1)} %get-tuple-element.82.high_ref, bf16[10240,192]{1,0:T(8,128)(2,1)S(1)} %get-tuple-element.83.low_ref, f32[32,10240]{1,0:T(8,128)S(1)} %bitcast.7, f32[16,10240]{1,0:T(8,128)S(1)} %collective-permute-done.8.refs_0_, ...), custom_call_target="tpu_custom_call" | custom-call | flops 1 | bytes 1 | tf_op jit(solution)/shard_map/project/pallas_call | solution.py:123
  106.1 5.8 %all-gather.1 = f32[16,16,192]{2,1,0:T(8,128)S(1)} all-gather(f32[4,16,192]{2,1,0:T(8,128)S(1)} %project.3), channel_id=3, replica_groups=mesh['groups'=2,'tm'=4,'param'=4] {'param'}, dimensions={0}, use_global_device_ids=true | all-gather | bytes 245760 | tf_op jit(solution)/shard_map/all_gather | solution.py:361
  111.9 2.6 %collective-permute-start.17 = (f32[4,16,192]{2,1,0:T(8,128)S(1)}, f32[4,16,192]{2,1,0:T(8,128)S(1)}, u32[]{:S(2)}, u32[]{:S(2)}) collective-permute-start(f32[4,16,192]{2,1,0:T(8,128)S(1)} %add_up.3.refs_0_), channel_id=1, source_target_pairs={{0,4},{4,0},{8,12},{12,8},{1,5},{5,1},{9,13},{13,9},{2,6},{6,2},{1... | collective-permute-start | bytes 147464 | tf_op jit(solution)/shard_map/ppermute | solution.py:341
  116.1 3.2 %collective-permute-start.21 = (f32[16,10240]{1,0:T(8,128)S(1)}, f32[16,10240]{1,0:T(8,128)S(1)}, u32[]{:S(2)}, u32[]{:S(2)}) collective-permute-start(f32[16,10240]{1,0:T(8,128)S(1)} %add.40), channel_id=1, source_target_pairs={{8,4},{4,8},{9,5},{5,9},{10,6},{6,10},{11,7},{7,11},{24,20},{20,24... | collective-permute-start | bytes 1966088 | tf_op jit(solution)/shard_map/ppermute | solution.py:317
  119.4 6.5 %collective-permute-done.16.refs_1_ = f32[16,10240]{1,0:T(8,128)S(1)} collective-permute-done((f32[16,10240]{1,0:T(8,128)S(1)}, f32[16,10240]{1,0:T(8,128)S(1)}, u32[]{:S(2)}, u32[]{:S(2)}) %collective-permute-start.16) | collective-permute-done | bytes 655392 | tf_op jit(solution)/shard_map/ppermute | solution.py:317
  127.9 2.4 %multiply.3 = (f32[16,10240]{1,0:T(8,128)S(1)}, f32[16,10240]{1,0:T(8,128)S(1)}, f32[16,10240]{1,0:T(8,128)S(1)}, f32[16,10240]{1,0:T(8,128)S(1)}) custom-call(s32[4]{0:T(128)S(1)} %get-tuple-element.77.refs_1_.shard_ref, s32[4]{0:T(128)S(1)} %get-tuple-element.78.refs_2_.place_ref, bf16[192,10240]{1,0:T(8,128)(2,1)S(1)} %get-tuple-element.90.high_ref, ...), custom_call_target="tpu_custom_call" | custom-call | flops 1 | bytes 1 | tf_op jit(solution)/shard_map/multiply/pallas_call | solution.py:172
  131.6 7.7 %collective-permute-done.20.refs_2_ = f32[16,10240]{1,0:T(8,128)S(1)} collective-permute-done((f32[16,10240]{1,0:T(8,128)S(1)}, f32[16,10240]{1,0:T(8,128)S(1)}, u32[]{:S(2)}, u32[]{:S(2)}) %collective-permute-start.20) | collective-permute-done | bytes 655392 | tf_op jit(solution)/shard_map/ppermute | solution.py:317
  140.6 9.2 %collective-permute-done.22 = f32[16,10240]{1,0:T(8,128)S(1)} collective-permute-done((f32[16,10240]{1,0:T(8,128)S(1)}, f32[16,10240]{1,0:T(8,128)S(1)}, u32[]{:S(2)}, u32[]{:S(2)}) %collective-permute-start.22) | collective-permute-done | bytes 655392 | tf_op jit(solution)/shard_map/ppermute | solution.py:317
  149.9 3.1 %collective-permute-start.23 = (f32[16,10240]{1,0:T(8,128)S(1)}, f32[16,10240]{1,0:T(8,128)S(1)}, u32[]{:S(2)}, u32[]{:S(2)}) collective-permute-start(f32[16,10240]{1,0:T(8,128)S(1)} %add.41), channel_id=1, source_target_pairs={{8,4},{4,8},{9,5},{5,9},{10,6},{6,10},{11,7},{7,11},{24,20},{20,24... | collective-permute-start | bytes 1966088 | tf_op jit(solution)/shard_map/ppermute | solution.py:317
  153.1 7.3 %collective-permute-done.25 = f32[16,10240]{1,0:T(8,128)S(1)} collective-permute-done((f32[16,10240]{1,0:T(8,128)S(1)}, f32[16,10240]{1,0:T(8,128)S(1)}, u32[]{:S(2)}, u32[]{:S(2)}) %collective-permute-start.25) | collective-permute-done | bytes 655392 | tf_op jit(solution)/shard_map/ppermute | solution.py:317
  160.5 3.2 %collective-permute-start.26 = (f32[16,10240]{1,0:T(8,128)S(1)}, f32[16,10240]{1,0:T(8,128)S(1)}, u32[]{:S(2)}, u32[]{:S(2)}) collective-permute-start(f32[16,10240]{1,0:T(8,128)S(1)} %add.43), channel_id=1, source_target_pairs={{8,4},{4,8},{9,5},{5,9},{10,6},{6,10},{11,7},{7,11},{24,20},{20,24... | collective-permute-start | bytes 1966088 | tf_op jit(solution)/shard_map/ppermute | solution.py:317
  163.9 12.6 %collective-permute-done.26.refs_6_ = f32[16,10240]{1,0:T(8,128)S(1)} collective-permute-done((f32[16,10240]{1,0:T(8,128)S(1)}, f32[16,10240]{1,0:T(8,128)S(1)}, u32[]{:S(2)}, u32[]{:S(2)}) %collective-permute-start.26) | collective-permute-done | bytes 655392 | tf_op jit(solution)/shard_map/ppermute | solution.py:317
  (56 shorter events, 25.6 us)
Async XLA Ops:
  1.4 16.5 %collective-permute-start = (f32[16,10240]{1,0:T(8,128)S(1)}, f32[16,10240]{1,0:T(8,128)S(1)}, u32[]{:S(2)}, u32[]{:S(2)}) collective-permute-start(f32[16,10240]{1,0:T(8,128)S(1)} %get-tuple-element.138), channel_id=1, source_target_pairs={{0,4},{12,8},{4,0},{8,12},{1,5},{13,9},{5,1},{9,13},{2,6},{14,10},... | collective-permute-start | bytes 1966088 | tf_op jit(solution)/shard_map/ppermute | solution.py:277
  1.5 19.9 %collective-permute-start.1 = (f32[16,10240]{1,0:T(8,128)S(1)}, f32[16,10240]{1,0:T(8,128)S(1)}, u32[]{:S(2)}, u32[]{:S(2)}) collective-permute-start(f32[16,10240]{1,0:T(8,128)S(1)} %get-tuple-element.138), channel_id=1, source_target_pairs={{4,8},{8,4},{5,9},{9,5},{6,10},{10,6},{7,11},{11,7},{20,24},{24,20... | collective-permute-start | bytes 1966088 | tf_op jit(solution)/shard_map/ppermute | solution.py:277
  6.5 0.7 copy-start.2
  17.9 17.5 %collective-permute-start.2 = (f32[16,10240]{1,0:T(8,128)S(1)}, f32[16,10240]{1,0:T(8,128)S(1)}, u32[]{:S(2)}, u32[]{:S(2)}) collective-permute-start(f32[16,10240]{1,0:T(8,128)S(1)} %collective-permute-done.refs_0_), channel_id=1, source_target_pairs={{4,8},{8,4},{5,9},{9,5},{6,10},{10,6},{7,11},{11,7},{20,24},{24,20... | collective-permute-start | bytes 1966088 | tf_op jit(solution)/shard_map/ppermute | solution.py:277
  21.4 26.4 %collective-permute-start.3 = (f32[16,10240]{1,0:T(8,128)S(1)}, f32[16,10240]{1,0:T(8,128)S(1)}, u32[]{:S(2)}, u32[]{:S(2)}) collective-permute-start(f32[16,10240]{1,0:T(8,128)S(1)} %collective-permute-done.1.refs_4_), channel_id=1, source_target_pairs={{4,0},{8,12},{5,1},{9,13},{6,2},{10,14},{7,3},{11,15},{20,16},{24,... | collective-permute-start | bytes 1966088 | tf_op jit(solution)/shard_map/ppermute | solution.py:277
  35.4 16.5 %collective-permute-start.4 = (f32[16,10240]{1,0:T(8,128)S(1)}, f32[16,10240]{1,0:T(8,128)S(1)}, u32[]{:S(2)}, u32[]{:S(2)}) collective-permute-start(f32[16,10240]{1,0:T(8,128)S(1)} %collective-permute-done.2.refs_2_), channel_id=1, source_target_pairs={{4,0},{8,12},{5,1},{9,13},{6,2},{10,14},{7,3},{11,15},{20,16},{24,... | collective-permute-start | bytes 1966088 | tf_op jit(solution)/shard_map/ppermute | solution.py:277
  36.8 3.2 %copy-start.1 = (f32[3,64,10240]{2,1,0:T(8,128)S(1)}, f32[3,64,10240]{2,1,0:T(8,128)}, u32[]{:S(2)}) copy-start(f32[3,64,10240]{2,1,0:T(8,128)} %design_ref.1) | copy-start | bytes 23592964
  40.0 11.9 %copy-start = (f32[10240,32]{0,1:T(8,128)S(1)}, f32[10240,32]{0,1:T(8,128)}, u32[]{:S(2)}) copy-start(f32[10240,32]{0,1:T(8,128)} %param.5) | copy-start | bytes 3932164
  44.3 26.5 %collective-permute-start.8 = (f32[16,10240]{1,0:T(8,128)S(1)}, f32[16,10240]{1,0:T(8,128)S(1)}, u32[]{:S(2)}, u32[]{:S(2)}) collective-permute-start(f32[16,10240]{1,0:T(8,128)S(1)} %get-tuple-element.87), channel_id=1, source_target_pairs={{0,4},{12,8},{4,0},{8,12},{1,5},{13,9},{5,1},{9,13},{2,6},{14,10},... | collective-permute-start | bytes 1966088 | tf_op jit(solution)/shard_map/ppermute | solution.py:277
  44.3 26.4 %collective-permute-start.9 = (f32[16,10240]{1,0:T(8,128)S(1)}, f32[16,10240]{1,0:T(8,128)S(1)}, u32[]{:S(2)}, u32[]{:S(2)}) collective-permute-start(f32[16,10240]{1,0:T(8,128)S(1)} %get-tuple-element.87), channel_id=1, source_target_pairs={{4,8},{8,4},{5,9},{9,5},{6,10},{10,6},{7,11},{11,7},{20,24},{24,20... | collective-permute-start | bytes 1966088 | tf_op jit(solution)/shard_map/ppermute | solution.py:277
  60.0 6.5 %collective-permute-start.5 = (f32[4,16,192]{2,1,0:T(8,128)S(1)}, f32[4,16,192]{2,1,0:T(8,128)S(1)}, u32[]{:S(2)}, u32[]{:S(2)}) collective-permute-start(f32[4,16,192]{2,1,0:T(8,128)S(1)} %add_up.2.refs_0_), channel_id=1, source_target_pairs={{0,4},{4,0},{8,12},{12,8},{1,5},{5,1},{9,13},{13,9},{2,6},{6,2},{1... | collective-permute-start | bytes 147464 | tf_op jit(solution)/shard_map/ppermute | solution.py:341
  62.6 6.2 %collective-permute-start.6 = (f32[4,16,192]{2,1,0:T(8,128)S(1)}, f32[4,16,192]{2,1,0:T(8,128)S(1)}, u32[]{:S(2)}, u32[]{:S(2)}) collective-permute-start(f32[4,16,192]{2,1,0:T(8,128)S(1)} %add_up.2.refs_0_), channel_id=1, source_target_pairs={{0,8},{4,12},{8,0},{12,4},{1,9},{5,13},{9,1},{13,5},{2,10},{6,14},... | collective-permute-start | bytes 147464 | tf_op jit(solution)/shard_map/ppermute | solution.py:341
  63.7 7.1 %collective-permute-start.7 = (f32[4,16,192]{2,1,0:T(8,128)S(1)}, f32[4,16,192]{2,1,0:T(8,128)S(1)}, u32[]{:S(2)}, u32[]{:S(2)}) collective-permute-start(f32[4,16,192]{2,1,0:T(8,128)S(1)} %add_up.2.refs_0_), channel_id=1, source_target_pairs={{0,12},{4,8},{8,4},{12,0},{1,13},{5,9},{9,5},{13,1},{2,14},{6,10},... | collective-permute-start | bytes 147464 | tf_op jit(solution)/shard_map/ppermute | solution.py:341
  70.7 15.7 %collective-permute-start.10 = (f32[16,10240]{1,0:T(8,128)S(1)}, f32[16,10240]{1,0:T(8,128)S(1)}, u32[]{:S(2)}, u32[]{:S(2)}) collective-permute-start(f32[16,10240]{1,0:T(8,128)S(1)} %collective-permute-done.9.refs_4_), channel_id=1, source_target_pairs={{4,0},{8,12},{5,1},{9,13},{6,2},{10,14},{7,3},{11,15},{20,16},{24,... | collective-permute-start | bytes 1966088 | tf_op jit(solution)/shard_map/ppermute | solution.py:277
  73.7 16.9 %collective-permute-start.11 = (f32[16,10240]{1,0:T(8,128)S(1)}, f32[16,10240]{1,0:T(8,128)S(1)}, u32[]{:S(2)}, u32[]{:S(2)}) collective-permute-start(f32[16,10240]{1,0:T(8,128)S(1)} %collective-permute-done.8.refs_0_), channel_id=1, source_target_pairs={{4,8},{8,4},{5,9},{9,5},{6,10},{10,6},{7,11},{11,7},{20,24},{24,20... | collective-permute-start | bytes 1966088 | tf_op jit(solution)/shard_map/ppermute | solution.py:277
  79.1 18.7 %collective-permute-start.12 = (f32[16,10240]{1,0:T(8,128)S(1)}, f32[16,10240]{1,0:T(8,128)S(1)}, u32[]{:S(2)}, u32[]{:S(2)}) collective-permute-start(f32[16,10240]{1,0:T(8,128)S(1)} %get-tuple-element.106), channel_id=1, source_target_pairs={{0,4},{12,8},{1,5},{13,9},{2,6},{14,10},{3,7},{15,11},{16,20},{28,... | collective-permute-start | bytes 1966088 | tf_op jit(solution)/shard_map/ppermute | solution.py:317
  90.6 13.2 %collective-permute-start.13 = (f32[16,10240]{1,0:T(8,128)S(1)}, f32[16,10240]{1,0:T(8,128)S(1)}, u32[]{:S(2)}, u32[]{:S(2)}) collective-permute-start(f32[16,10240]{1,0:T(8,128)S(1)} %collective-permute-done.11.refs_2_), channel_id=1, source_target_pairs={{4,0},{8,12},{5,1},{9,13},{6,2},{10,14},{7,3},{11,15},{20,16},{24,... | collective-permute-start | bytes 1966088 | tf_op jit(solution)/shard_map/ppermute | solution.py:277
  91.9 23.3 %collective-permute-start.14 = (f32[16,10240]{1,0:T(8,128)S(1)}, f32[16,10240]{1,0:T(8,128)S(1)}, u32[]{:S(2)}, u32[]{:S(2)}) collective-permute-start(f32[16,10240]{1,0:T(8,128)S(1)} %get-tuple-element.110), channel_id=1, source_target_pairs={{0,4},{12,8},{1,5},{13,9},{2,6},{14,10},{3,7},{15,11},{16,20},{28,... | collective-permute-start | bytes 1966088 | tf_op jit(solution)/shard_map/ppermute | solution.py:317
  97.9 18.2 %collective-permute-start.15 = (f32[16,10240]{1,0:T(8,128)S(1)}, f32[16,10240]{1,0:T(8,128)S(1)}, u32[]{:S(2)}, u32[]{:S(2)}) collective-permute-start(f32[16,10240]{1,0:T(8,128)S(1)} %add.38), channel_id=1, source_target_pairs={{8,4},{4,8},{9,5},{5,9},{10,6},{6,10},{11,7},{7,11},{24,20},{20,24... | collective-permute-start | bytes 1966088 | tf_op jit(solution)/shard_map/ppermute | solution.py:317
  100.1 25.8 %collective-permute-start.16 = (f32[16,10240]{1,0:T(8,128)S(1)}, f32[16,10240]{1,0:T(8,128)S(1)}, u32[]{:S(2)}, u32[]{:S(2)}) collective-permute-start(f32[16,10240]{1,0:T(8,128)S(1)} %get-tuple-element.114), channel_id=1, source_target_pairs={{0,4},{12,8},{1,5},{13,9},{2,6},{14,10},{3,7},{15,11},{16,20},{28,... | collective-permute-start | bytes 1966088 | tf_op jit(solution)/shard_map/ppermute | solution.py:317
  111.9 15.5 %collective-permute-start.17 = (f32[4,16,192]{2,1,0:T(8,128)S(1)}, f32[4,16,192]{2,1,0:T(8,128)S(1)}, u32[]{:S(2)}, u32[]{:S(2)}) collective-permute-start(f32[4,16,192]{2,1,0:T(8,128)S(1)} %add_up.3.refs_0_), channel_id=1, source_target_pairs={{0,4},{4,0},{8,12},{12,8},{1,5},{5,1},{9,13},{13,9},{2,6},{6,2},{1... | collective-permute-start | bytes 147464 | tf_op jit(solution)/shard_map/ppermute | solution.py:341
  114.5 13.4 %collective-permute-start.18 = (f32[4,16,192]{2,1,0:T(8,128)S(1)}, f32[4,16,192]{2,1,0:T(8,128)S(1)}, u32[]{:S(2)}, u32[]{:S(2)}) collective-permute-start(f32[4,16,192]{2,1,0:T(8,128)S(1)} %add_up.3.refs_0_), channel_id=1, source_target_pairs={{0,8},{4,12},{8,0},{12,4},{1,9},{5,13},{9,1},{13,5},{2,10},{6,14},... | collective-permute-start | bytes 147464 | tf_op jit(solution)/shard_map/ppermute | solution.py:341
  115.3 12.6 %collective-permute-start.19 = (f32[4,16,192]{2,1,0:T(8,128)S(1)}, f32[4,16,192]{2,1,0:T(8,128)S(1)}, u32[]{:S(2)}, u32[]{:S(2)}) collective-permute-start(f32[4,16,192]{2,1,0:T(8,128)S(1)} %add_up.3.refs_0_), channel_id=1, source_target_pairs={{0,12},{4,8},{8,4},{12,0},{1,13},{5,9},{9,5},{13,1},{2,14},{6,10},... | collective-permute-start | bytes 147464 | tf_op jit(solution)/shard_map/ppermute | solution.py:341
  116.1 23.2 %collective-permute-start.21 = (f32[16,10240]{1,0:T(8,128)S(1)}, f32[16,10240]{1,0:T(8,128)S(1)}, u32[]{:S(2)}, u32[]{:S(2)}) collective-permute-start(f32[16,10240]{1,0:T(8,128)S(1)} %add.40), channel_id=1, source_target_pairs={{8,4},{4,8},{9,5},{5,9},{10,6},{6,10},{11,7},{7,11},{24,20},{20,24... | collective-permute-start | bytes 1966088 | tf_op jit(solution)/shard_map/ppermute | solution.py:317
  125.9 13.4 %collective-permute-start.20 = (f32[16,10240]{1,0:T(8,128)S(1)}, f32[16,10240]{1,0:T(8,128)S(1)}, u32[]{:S(2)}, u32[]{:S(2)}) collective-permute-start(f32[16,10240]{1,0:T(8,128)S(1)} %add.39), channel_id=1, source_target_pairs={{4,0},{8,12},{5,1},{9,13},{6,2},{10,14},{7,3},{11,15},{20,16},{24,... | collective-permute-start | bytes 1966088 | tf_op jit(solution)/shard_map/ppermute | solution.py:317
  130.3 19.6 %collective-permute-start.22 = (f32[16,10240]{1,0:T(8,128)S(1)}, f32[16,10240]{1,0:T(8,128)S(1)}, u32[]{:S(2)}, u32[]{:S(2)}) collective-permute-start(f32[16,10240]{1,0:T(8,128)S(1)} %get-tuple-element.133), channel_id=1, source_target_pairs={{0,4},{12,8},{1,5},{13,9},{2,6},{14,10},{3,7},{15,11},{16,20},{28,... | collective-permute-start | bytes 1966088 | tf_op jit(solution)/shard_map/ppermute | solution.py:317
  139.3 21.1 %collective-permute-start.25 = (f32[16,10240]{1,0:T(8,128)S(1)}, f32[16,10240]{1,0:T(8,128)S(1)}, u32[]{:S(2)}, u32[]{:S(2)}) collective-permute-start(f32[16,10240]{1,0:T(8,128)S(1)} %get-tuple-element.135), channel_id=1, source_target_pairs={{0,4},{12,8},{1,5},{13,9},{2,6},{14,10},{3,7},{15,11},{16,20},{28,... | collective-permute-start | bytes 1966088 | tf_op jit(solution)/shard_map/ppermute | solution.py:317
  149.9 13.8 %collective-permute-start.23 = (f32[16,10240]{1,0:T(8,128)S(1)}, f32[16,10240]{1,0:T(8,128)S(1)}, u32[]{:S(2)}, u32[]{:S(2)}) collective-permute-start(f32[16,10240]{1,0:T(8,128)S(1)} %add.41), channel_id=1, source_target_pairs={{8,4},{4,8},{9,5},{5,9},{10,6},{6,10},{11,7},{7,11},{24,20},{20,24... | collective-permute-start | bytes 1966088 | tf_op jit(solution)/shard_map/ppermute | solution.py:317
  160.5 16.0 %collective-permute-start.26 = (f32[16,10240]{1,0:T(8,128)S(1)}, f32[16,10240]{1,0:T(8,128)S(1)}, u32[]{:S(2)}, u32[]{:S(2)}) collective-permute-start(f32[16,10240]{1,0:T(8,128)S(1)} %add.43), channel_id=1, source_target_pairs={{8,4},{4,8},{9,5},{5,9},{10,6},{6,10},{11,7},{7,11},{24,20},{20,24... | collective-permute-start | bytes 1966088 | tf_op jit(solution)/shard_map/ppermute | solution.py:317
  163.8 13.1 %collective-permute-start.24 = (f32[16,10240]{1,0:T(8,128)S(1)}, f32[16,10240]{1,0:T(8,128)S(1)}, u32[]{:S(2)}, u32[]{:S(2)}) collective-permute-start(f32[16,10240]{1,0:T(8,128)S(1)} %add.42), channel_id=1, source_target_pairs={{0,4},{12,8},{4,0},{8,12},{1,5},{13,9},{5,1},{9,13},{2,6},{14,10},... | collective-permute-start | bytes 1966088 | tf_op jit(solution)/shard_map/ppermute | solution.py:317

commit v11 on v10

--- a/solution.py
+++ b/solution.py
@@ -211,7 +211,7 @@
 
 def totals_of(groups, tile):
     rows, coefficients = groups[0][0].shape
-    width = math.gcd(coefficients, 5120)
+    width = math.gcd(coefficients, 2560)
     values = [value for group in groups for value in group]
 
     def kernel(*refs):
@@ -392,7 +392,8 @@
     tile = first.tie(tile, 1, 2)
     first.send(0, 3)
     high, low, tall_high, tall_low = split_design(design, [taps, shards, places, mark(tile)])
-    tile, high, low, value = lax.optimization_barrier((tile, high, low, own[rows:]))
+    tile, high, low, held = lax.optimization_barrier((tile, high, low, own))
+    value = held[rows:]
     second = Gather(value, length)
     second.send(0, 1)
     second.send(1, 1)

time: 180 us -> 180 us (level)
  no operation moved by 1% of the time
where the time goes in v11:
time: 180 us; the launch traced here: 179 us
  waiting for transfers between devices  94.1 us (52%)
  starting transfers between devices  50 us (28%)
  Pallas kernels  16.9 us (9%)
  blocking collectives  11.6 us (6%)
  local copies, waits for them, and re-layouts  5.1 us (3%)
    ppermute x11, waiting for transfers between devices, send(): lax.ppermute(value, 'tm', pairs)  48.4 us
    ppermute x10, waiting for transfers between devices, send(): value = lax.ppermute(self.onward[1 - parity, step - 1], 'tm', pairs)  38.7 us
    ppermute x10, starting transfers between devices, send(): value = lax.ppermute(self.onward[1 - parity, step - 1], 'tm', pairs)  22.1 us
    ppermute x11, starting transfers between devices, send(): lax.ppermute(value, 'tm', pairs)  19.8 us
    all_gather x2, blocking collectives, summed(): return add_up(lax.all_gather(partial, 'param', axis=0))  11.6 us
    ppermute x6, starting transfers between devices, exchange(): lax.ppermute(value, 'tm', [(i, i ^ by) for i in range(length)])  8.21 us
    ppermute x6, waiting for transfers between devices, exchange(): lax.ppermute(value, 'tm', [(i, i ^ by) for i in range(length)])  7.05 us
    pallas_call x2, Pallas kernels, multiply(): pl.pallas_call(kernel, grid_spec=pltpu.PrefetchScalarGridSpec(num_scalar_...  4.85 us
  transfers between devices with their start and end apart: 27, of which 17 were waited for; matrix products, arithmetic and copies ran while one was open for 0% of the time, Pallas kernels for 8%

profile of v11, /device:TPU:8, one launch (start us, length us, event | category | flops | bytes accessed | tf_op | source)
XLA Modules:
  0.0 178.6 jit_solution(113009184796552569)
XLA Ops:
  1.2 5.0 %collective-permute-start.1 = (f32[16,10240]{1,0:T(8,128)S(1)}, f32[16,10240]{1,0:T(8,128)S(1)}, u32[]{:S(2)}, u32[]{:S(2)}) collective-permute-start(f32[16,10240]{1,0:T(8,128)S(1)} %slice.8), channel_id=1, source_target_pairs={{4,8},{8,4},{5,9},{9,5},{6,10},{10,6},{7,11},{11,7},{20,24},{24,20... | collective-permute-start | bytes 1966088 | tf_op jit(solution)/shard_map/ppermute | solution.py:277
  8.1 9.5 %collective-permute-done.refs_0_ = f32[16,10240]{1,0:T(8,128)S(1)} collective-permute-done((f32[16,10240]{1,0:T(8,128)S(1)}, f32[16,10240]{1,0:T(8,128)S(1)}, u32[]{:S(2)}, u32[]{:S(2)}) %collective-permute-start) | collective-permute-done | bytes 655392 | tf_op jit(solution)/shard_map/ppermute | solution.py:277
  17.7 3.5 %collective-permute-start.2 = (f32[16,10240]{1,0:T(8,128)S(1)}, f32[16,10240]{1,0:T(8,128)S(1)}, u32[]{:S(2)}, u32[]{:S(2)}) collective-permute-start(f32[16,10240]{1,0:T(8,128)S(1)} %collective-permute-done.refs_0_), channel_id=1, source_target_pairs={{4,8},{8,4},{5,9},{9,5},{6,10},{10,6},{7,11},{11,7},{20,24},{24,20... | collective-permute-start | bytes 1966088 | tf_op jit(solution)/shard_map/ppermute | solution.py:277
  22.5 12.7 %collective-permute-done.2.refs_2_ = f32[16,10240]{1,0:T(8,128)S(1)} collective-permute-done((f32[16,10240]{1,0:T(8,128)S(1)}, f32[16,10240]{1,0:T(8,128)S(1)}, u32[]{:S(2)}, u32[]{:S(2)}) %collective-permute-start.2) | collective-permute-done | bytes 655392 | tf_op jit(solution)/shard_map/ppermute | solution.py:277
  36.5 3.2 %copy-done.1 = f32[3,64,10240]{2,1,0:T(8,128)S(1)} copy-done((f32[3,64,10240]{2,1,0:T(8,128)S(1)}, f32[3,64,10240]{2,1,0:T(8,128)}, u32[]{:S(2)}) %copy-start.1) | copy-done | bytes 7864344
  39.7 4.3 %split_design.1 = (bf16[192,10240]{1,0:T(8,128)(2,1)S(1)}, bf16[192,10240]{1,0:T(8,128)(2,1)S(1)}, bf16[10240,192]{1,0:T(8,128)(2,1)S(1)}, bf16[10240,192]{1,0:T(8,128)(2,1)S(1)}) custom-call(f32[3,64,10240]{2,1,0:T(8,128)S(1)} %copy-done.1, f32[4,3,64,64]{3,2,1,0:T(8,128)S(1)} %normal_rows.1.refs_0_.taps_ref, s32[4]{0:T(128)S(1)} %get-tuple-element.77.refs_1_.shard_ref, ...), custom_call_target="tpu_custom_call" | custom-call | flops 1 | bytes 1 | tf_op jit(solution)/shard_map/split_design/pallas_call | solution.py:49
  44.1 3.5 %collective-permute-start.9 = (f32[16,10240]{1,0:T(8,128)S(1)}, f32[16,10240]{1,0:T(8,128)S(1)}, u32[]{:S(2)}, u32[]{:S(2)}) collective-permute-start(f32[16,10240]{1,0:T(8,128)S(1)} %slice.7), channel_id=1, source_target_pairs={{4,8},{8,4},{5,9},{9,5},{6,10},{10,6},{7,11},{11,7},{20,24},{24,20... | collective-permute-start | bytes 1966088 | tf_op jit(solution)/shard_map/ppermute | solution.py:277
  47.7 4.0 %collective-permute-done.4.refs_3_ = f32[16,10240]{1,0:T(8,128)S(1)} collective-permute-done((f32[16,10240]{1,0:T(8,128)S(1)}, f32[16,10240]{1,0:T(8,128)S(1)}, u32[]{:S(2)}, u32[]{:S(2)}) %collective-permute-start.4) | collective-permute-done | bytes 655392 | tf_op jit(solution)/shard_map/ppermute | solution.py:277
  51.6 2.3 %project.2 = f32[4,16,192]{2,1,0:T(8,128)S(1)} custom-call(s32[4]{0:T(128)S(1)} %get-tuple-element.77.refs_1_.shard_ref, bf16[10240,192]{1,0:T(8,128)(2,1)S(1)} %get-tuple-element.82.high_ref, bf16[10240,192]{1,0:T(8,128)(2,1)S(1)} %get-tuple-element.83.low_ref, f32[32,10240]{1,0:T(8,128)S(1)} %bitcast.7, f32[16,10240]{1,0:T(8,128)S(1)} %collective-permute-done.refs_0_, ...), custom_call_target="tpu_custom_call" | custom-call | flops 1 | bytes 1 | tf_op jit(solution)/shard_map/project/pallas_call | solution.py:123
  54.0 5.8 %all-gather = f32[16,16,192]{2,1,0:T(8,128)S(1)} all-gather(f32[4,16,192]{2,1,0:T(8,128)S(1)} %project.2), channel_id=2, replica_groups=mesh['groups'=2,'tm'=4,'param'=4] {'param'}, dimensions={0}, use_global_device_ids=true | all-gather | bytes 245760 | tf_op jit(solution)/shard_map/all_gather | solution.py:361
  59.8 2.6 %collective-permute-start.5 = (f32[4,16,192]{2,1,0:T(8,128)S(1)}, f32[4,16,192]{2,1,0:T(8,128)S(1)}, u32[]{:S(2)}, u32[]{:S(2)}) collective-permute-start(f32[4,16,192]{2,1,0:T(8,128)S(1)} %add_up.2.refs_0_), channel_id=1, source_target_pairs={{0,4},{4,0},{8,12},{12,8},{1,5},{5,1},{9,13},{13,9},{2,6},{6,2},{1... | collective-permute-start | bytes 147464 | tf_op jit(solution)/shard_map/ppermute | solution.py:341
  63.9 2.4 %collective-permute-done.5.refs_1_ = f32[4,16,192]{2,1,0:T(8,128)S(1)} collective-permute-done((f32[4,16,192]{2,1,0:T(8,128)S(1)}, f32[4,16,192]{2,1,0:T(8,128)S(1)}, u32[]{:S(2)}, u32[]{:S(2)}) %collective-permute-start.5) | collective-permute-done | bytes 49184 | tf_op jit(solution)/shard_map/ppermute | solution.py:341
  70.5 2.9 %collective-permute-start.10 = (f32[16,10240]{1,0:T(8,128)S(1)}, f32[16,10240]{1,0:T(8,128)S(1)}, u32[]{:S(2)}, u32[]{:S(2)}) collective-permute-start(f32[16,10240]{1,0:T(8,128)S(1)} %collective-permute-done.9.refs_4_), channel_id=1, source_target_pairs={{4,0},{8,12},{5,1},{9,13},{6,2},{10,14},{7,3},{11,15},{20,16},{24,... | collective-permute-start | bytes 1966088 | tf_op jit(solution)/shard_map/ppermute | solution.py:277
  73.4 3.0 %collective-permute-start.11 = (f32[16,10240]{1,0:T(8,128)S(1)}, f32[16,10240]{1,0:T(8,128)S(1)}, u32[]{:S(2)}, u32[]{:S(2)}) collective-permute-start(f32[16,10240]{1,0:T(8,128)S(1)} %collective-permute-done.8.refs_0_), channel_id=1, source_target_pairs={{4,8},{8,4},{5,9},{9,5},{6,10},{10,6},{7,11},{11,7},{20,24},{24,20... | collective-permute-start | bytes 1966088 | tf_op jit(solution)/shard_map/ppermute | solution.py:277
  76.5 2.4 %multiply.2 = (f32[16,10240]{1,0:T(8,128)S(1)}, f32[16,10240]{1,0:T(8,128)S(1)}, f32[16,10240]{1,0:T(8,128)S(1)}, f32[16,10240]{1,0:T(8,128)S(1)}) custom-call(s32[4]{0:T(128)S(1)} %get-tuple-element.77.refs_1_.shard_ref, s32[4]{0:T(128)S(1)} %get-tuple-element.78.refs_2_.place_ref, bf16[192,10240]{1,0:T(8,128)(2,1)S(1)} %get-tuple-element.90.high_ref, ...), custom_call_target="tpu_custom_call" | custom-call | flops 1 | bytes 1 | tf_op jit(solution)/shard_map/multiply/pallas_call | solution.py:172
  80.2 6.0 %collective-permute-done.10.refs_1_ = f32[16,10240]{1,0:T(8,128)S(1)} collective-permute-done((f32[16,10240]{1,0:T(8,128)S(1)}, f32[16,10240]{1,0:T(8,128)S(1)}, u32[]{:S(2)}, u32[]{:S(2)}) %collective-permute-start.10) | collective-permute-done | bytes 655392 | tf_op jit(solution)/shard_map/ppermute | solution.py:277
  86.2 4.2 %collective-permute-done.11.refs_2_ = f32[16,10240]{1,0:T(8,128)S(1)} collective-permute-done((f32[16,10240]{1,0:T(8,128)S(1)}, f32[16,10240]{1,0:T(8,128)S(1)}, u32[]{:S(2)}, u32[]{:S(2)}) %collective-permute-start.11) | collective-permute-done | bytes 655392 | tf_op jit(solution)/shard_map/ppermute | solution.py:277
  93.0 4.5 %collective-permute-done.12 = f32[16,10240]{1,0:T(8,128)S(1)} collective-permute-done((f32[16,10240]{1,0:T(8,128)S(1)}, f32[16,10240]{1,0:T(8,128)S(1)}, u32[]{:S(2)}, u32[]{:S(2)}) %collective-permute-start.12) | collective-permute-done | bytes 655392 | tf_op jit(solution)/shard_map/ppermute | solution.py:317
  97.6 2.3 %collective-permute-start.15 = (f32[16,10240]{1,0:T(8,128)S(1)}, f32[16,10240]{1,0:T(8,128)S(1)}, u32[]{:S(2)}, u32[]{:S(2)}) collective-permute-start(f32[16,10240]{1,0:T(8,128)S(1)} %add.38), channel_id=1, source_target_pairs={{8,4},{4,8},{9,5},{5,9},{10,6},{6,10},{11,7},{7,11},{24,20},{20,24... | collective-permute-start | bytes 1966088 | tf_op jit(solution)/shard_map/ppermute | solution.py:317
  101.2 2.3 %collective-permute-done.13.refs_3_ = f32[16,10240]{1,0:T(8,128)S(1)} collective-permute-done((f32[16,10240]{1,0:T(8,128)S(1)}, f32[16,10240]{1,0:T(8,128)S(1)}, u32[]{:S(2)}, u32[]{:S(2)}) %collective-permute-start.13) | collective-permute-done | bytes 655392 | tf_op jit(solution)/shard_map/ppermute | solution.py:277
  103.5 2.3 %project.3 = f32[4,16,192]{2,1,0:T(8,128)S(1)} custom-call(s32[4]{0:T(128)S(1)} %get-tuple-element.77.refs_1_.shard_ref, bf16[10240,192]{1,0:T(8,128)(2,1)S(1)} %get-tuple-element.82.high_ref, bf16[10240,192]{1,0:T(8,128)(2,1)S(1)} %get-tuple-element.83.low_ref, f32[32,10240]{1,0:T(8,128)S(1)} %bitcast.8, f32[16,10240]{1,0:T(8,128)S(1)} %collective-permute-done.8.refs_0_, ...), custom_call_target="tpu_custom_call" | custom-call | flops 1 | bytes 1 | tf_op jit(solution)/shard_map/project/pallas_call | solution.py:123
  105.9 5.8 %all-gather.1 = f32[16,16,192]{2,1,0:T(8,128)S(1)} all-gather(f32[4,16,192]{2,1,0:T(8,128)S(1)} %project.3), channel_id=3, replica_groups=mesh['groups'=2,'tm'=4,'param'=4] {'param'}, dimensions={0}, use_global_device_ids=true | all-gather | bytes 245760 | tf_op jit(solution)/shard_map/all_gather | solution.py:361
  111.7 2.5 %collective-permute-start.17 = (f32[4,16,192]{2,1,0:T(8,128)S(1)}, f32[4,16,192]{2,1,0:T(8,128)S(1)}, u32[]{:S(2)}, u32[]{:S(2)}) collective-permute-start(f32[4,16,192]{2,1,0:T(8,128)S(1)} %add_up.3.refs_0_), channel_id=1, source_target_pairs={{0,4},{4,0},{8,12},{12,8},{1,5},{5,1},{9,13},{13,9},{2,6},{6,2},{1... | collective-permute-start | bytes 147464 | tf_op jit(solution)/shard_map/ppermute | solution.py:341
  115.8 3.2 %collective-permute-start.21 = (f32[16,10240]{1,0:T(8,128)S(1)}, f32[16,10240]{1,0:T(8,128)S(1)}, u32[]{:S(2)}, u32[]{:S(2)}) collective-permute-start(f32[16,10240]{1,0:T(8,128)S(1)} %add.40), channel_id=1, source_target_pairs={{8,4},{4,8},{9,5},{5,9},{10,6},{6,10},{11,7},{7,11},{24,20},{20,24... | collective-permute-start | bytes 1966088 | tf_op jit(solution)/shard_map/ppermute | solution.py:317
  119.1 6.5 %collective-permute-done.16.refs_1_ = f32[16,10240]{1,0:T(8,128)S(1)} collective-permute-done((f32[16,10240]{1,0:T(8,128)S(1)}, f32[16,10240]{1,0:T(8,128)S(1)}, u32[]{:S(2)}, u32[]{:S(2)}) %collective-permute-start.16) | collective-permute-done | bytes 655392 | tf_op jit(solution)/shard_map/ppermute | solution.py:317
  127.6 2.4 %multiply.3 = (f32[16,10240]{1,0:T(8,128)S(1)}, f32[16,10240]{1,0:T(8,128)S(1)}, f32[16,10240]{1,0:T(8,128)S(1)}, f32[16,10240]{1,0:T(8,128)S(1)}) custom-call(s32[4]{0:T(128)S(1)} %get-tuple-element.77.refs_1_.shard_ref, s32[4]{0:T(128)S(1)} %get-tuple-element.78.refs_2_.place_ref, bf16[192,10240]{1,0:T(8,128)(2,1)S(1)} %get-tuple-element.90.high_ref, ...), custom_call_target="tpu_custom_call" | custom-call | flops 1 | bytes 1 | tf_op jit(solution)/shard_map/multiply/pallas_call | solution.py:172
  131.3 7.7 %collective-permute-done.20.refs_2_ = f32[16,10240]{1,0:T(8,128)S(1)} collective-permute-done((f32[16,10240]{1,0:T(8,128)S(1)}, f32[16,10240]{1,0:T(8,128)S(1)}, u32[]{:S(2)}, u32[]{:S(2)}) %collective-permute-start.20) | collective-permute-done | bytes 655392 | tf_op jit(solution)/shard_map/ppermute | solution.py:317
  140.3 9.3 %collective-permute-done.22 = f32[16,10240]{1,0:T(8,128)S(1)} collective-permute-done((f32[16,10240]{1,0:T(8,128)S(1)}, f32[16,10240]{1,0:T(8,128)S(1)}, u32[]{:S(2)}, u32[]{:S(2)}) %collective-permute-start.22) | collective-permute-done | bytes 655392 | tf_op jit(solution)/shard_map/ppermute | solution.py:317
  149.7 3.1 %collective-permute-start.23 = (f32[16,10240]{1,0:T(8,128)S(1)}, f32[16,10240]{1,0:T(8,128)S(1)}, u32[]{:S(2)}, u32[]{:S(2)}) collective-permute-start(f32[16,10240]{1,0:T(8,128)S(1)} %add.41), channel_id=1, source_target_pairs={{8,4},{4,8},{9,5},{5,9},{10,6},{6,10},{11,7},{7,11},{24,20},{20,24... | collective-permute-start | bytes 1966088 | tf_op jit(solution)/shard_map/ppermute | solution.py:317
  152.8 7.4 %collective-permute-done.25 = f32[16,10240]{1,0:T(8,128)S(1)} collective-permute-done((f32[16,10240]{1,0:T(8,128)S(1)}, f32[16,10240]{1,0:T(8,128)S(1)}, u32[]{:S(2)}, u32[]{:S(2)}) %collective-permute-start.25) | collective-permute-done | bytes 655392 | tf_op jit(solution)/shard_map/ppermute | solution.py:317
  160.2 3.2 %collective-permute-start.26 = (f32[16,10240]{1,0:T(8,128)S(1)}, f32[16,10240]{1,0:T(8,128)S(1)}, u32[]{:S(2)}, u32[]{:S(2)}) collective-permute-start(f32[16,10240]{1,0:T(8,128)S(1)} %add.43), channel_id=1, source_target_pairs={{8,4},{4,8},{9,5},{5,9},{10,6},{6,10},{11,7},{7,11},{24,20},{20,24... | collective-permute-start | bytes 1966088 | tf_op jit(solution)/shard_map/ppermute | solution.py:317
  163.6 12.6 %collective-permute-done.26.refs_6_ = f32[16,10240]{1,0:T(8,128)S(1)} collective-permute-done((f32[16,10240]{1,0:T(8,128)S(1)}, f32[16,10240]{1,0:T(8,128)S(1)}, u32[]{:S(2)}, u32[]{:S(2)}) %collective-permute-start.26) | collective-permute-done | bytes 655392 | tf_op jit(solution)/shard_map/ppermute | solution.py:317
  (57 shorter events, 25.9 us)
Async XLA Ops:
  1.1 16.5 %collective-permute-start = (f32[16,10240]{1,0:T(8,128)S(1)}, f32[16,10240]{1,0:T(8,128)S(1)}, u32[]{:S(2)}, u32[]{:S(2)}) collective-permute-start(f32[16,10240]{1,0:T(8,128)S(1)} %slice.8), channel_id=1, source_target_pairs={{0,4},{12,8},{4,0},{8,12},{1,5},{13,9},{5,1},{9,13},{2,6},{14,10},... | collective-permute-start | bytes 1966088 | tf_op jit(solution)/shard_map/ppermute | solution.py:277
  1.2 19.9 %collective-permute-start.1 = (f32[16,10240]{1,0:T(8,128)S(1)}, f32[16,10240]{1,0:T(8,128)S(1)}, u32[]{:S(2)}, u32[]{:S(2)}) collective-permute-start(f32[16,10240]{1,0:T(8,128)S(1)} %slice.8), channel_id=1, source_target_pairs={{4,8},{8,4},{5,9},{9,5},{6,10},{10,6},{7,11},{11,7},{20,24},{24,20... | collective-permute-start | bytes 1966088 | tf_op jit(solution)/shard_map/ppermute | solution.py:277
  6.3 0.7 copy-start.2
  17.7 17.5 %collective-permute-start.2 = (f32[16,10240]{1,0:T(8,128)S(1)}, f32[16,10240]{1,0:T(8,128)S(1)}, u32[]{:S(2)}, u32[]{:S(2)}) collective-permute-start(f32[16,10240]{1,0:T(8,128)S(1)} %collective-permute-done.refs_0_), channel_id=1, source_target_pairs={{4,8},{8,4},{5,9},{9,5},{6,10},{10,6},{7,11},{11,7},{20,24},{24,20... | collective-permute-start | bytes 1966088 | tf_op jit(solution)/shard_map/ppermute | solution.py:277
  21.2 26.5 %collective-permute-start.3 = (f32[16,10240]{1,0:T(8,128)S(1)}, f32[16,10240]{1,0:T(8,128)S(1)}, u32[]{:S(2)}, u32[]{:S(2)}) collective-permute-start(f32[16,10240]{1,0:T(8,128)S(1)} %collective-permute-done.1.refs_4_), channel_id=1, source_target_pairs={{4,0},{8,12},{5,1},{9,13},{6,2},{10,14},{7,3},{11,15},{20,16},{24,... | collective-permute-start | bytes 1966088 | tf_op jit(solution)/shard_map/ppermute | solution.py:277
  35.2 16.5 %collective-permute-start.4 = (f32[16,10240]{1,0:T(8,128)S(1)}, f32[16,10240]{1,0:T(8,128)S(1)}, u32[]{:S(2)}, u32[]{:S(2)}) collective-permute-start(f32[16,10240]{1,0:T(8,128)S(1)} %collective-permute-done.2.refs_2_), channel_id=1, source_target_pairs={{4,0},{8,12},{5,1},{9,13},{6,2},{10,14},{7,3},{11,15},{20,16},{24,... | collective-permute-start | bytes 1966088 | tf_op jit(solution)/shard_map/ppermute | solution.py:277
  36.5 3.2 %copy-start.1 = (f32[3,64,10240]{2,1,0:T(8,128)S(1)}, f32[3,64,10240]{2,1,0:T(8,128)}, u32[]{:S(2)}) copy-start(f32[3,64,10240]{2,1,0:T(8,128)} %design_ref.1) | copy-start | bytes 23592964
  39.7 4.3 %copy-start = (f32[10240,32]{0,1:T(8,128)S(1)}, f32[10240,32]{0,1:T(8,128)}, u32[]{:S(2)}) copy-start(f32[10240,32]{0,1:T(8,128)} %param.5) | copy-start | bytes 3932164
  44.1 26.4 %collective-permute-start.8 = (f32[16,10240]{1,0:T(8,128)S(1)}, f32[16,10240]{1,0:T(8,128)S(1)}, u32[]{:S(2)}, u32[]{:S(2)}) collective-permute-start(f32[16,10240]{1,0:T(8,128)S(1)} %slice.7), channel_id=1, source_target_pairs={{0,4},{12,8},{4,0},{8,12},{1,5},{13,9},{5,1},{9,13},{2,6},{14,10},... | collective-permute-start | bytes 1966088 | tf_op jit(solution)/shard_map/ppermute | solution.py:277
  44.1 26.3 %collective-permute-start.9 = (f32[16,10240]{1,0:T(8,128)S(1)}, f32[16,10240]{1,0:T(8,128)S(1)}, u32[]{:S(2)}, u32[]{:S(2)}) collective-permute-start(f32[16,10240]{1,0:T(8,128)S(1)} %slice.7), channel_id=1, source_target_pairs={{4,8},{8,4},{5,9},{9,5},{6,10},{10,6},{7,11},{11,7},{20,24},{24,20... | collective-permute-start | bytes 1966088 | tf_op jit(solution)/shard_map/ppermute | solution.py:277
  59.8 6.5 %collective-permute-start.5 = (f32[4,16,192]{2,1,0:T(8,128)S(1)}, f32[4,16,192]{2,1,0:T(8,128)S(1)}, u32[]{:S(2)}, u32[]{:S(2)}) collective-permute-start(f32[4,16,192]{2,1,0:T(8,128)S(1)} %add_up.2.refs_0_), channel_id=1, source_target_pairs={{0,4},{4,0},{8,12},{12,8},{1,5},{5,1},{9,13},{13,9},{2,6},{6,2},{1... | collective-permute-start | bytes 147464 | tf_op jit(solution)/shard_map/ppermute | solution.py:341
  62.3 6.2 %collective-permute-start.6 = (f32[4,16,192]{2,1,0:T(8,128)S(1)}, f32[4,16,192]{2,1,0:T(8,128)S(1)}, u32[]{:S(2)}, u32[]{:S(2)}) collective-permute-start(f32[4,16,192]{2,1,0:T(8,128)S(1)} %add_up.2.refs_0_), channel_id=1, source_target_pairs={{0,8},{4,12},{8,0},{12,4},{1,9},{5,13},{9,1},{13,5},{2,10},{6,14},... | collective-permute-start | bytes 147464 | tf_op jit(solution)/shard_map/ppermute | solution.py:341
  63.4 7.1 %collective-permute-start.7 = (f32[4,16,192]{2,1,0:T(8,128)S(1)}, f32[4,16,192]{2,1,0:T(8,128)S(1)}, u32[]{:S(2)}, u32[]{:S(2)}) collective-permute-start(f32[4,16,192]{2,1,0:T(8,128)S(1)} %add_up.2.refs_0_), channel_id=1, source_target_pairs={{0,12},{4,8},{8,4},{12,0},{1,13},{5,9},{9,5},{13,1},{2,14},{6,10},... | collective-permute-start | bytes 147464 | tf_op jit(solution)/shard_map/ppermute | solution.py:341
  70.5 15.7 %collective-permute-start.10 = (f32[16,10240]{1,0:T(8,128)S(1)}, f32[16,10240]{1,0:T(8,128)S(1)}, u32[]{:S(2)}, u32[]{:S(2)}) collective-permute-start(f32[16,10240]{1,0:T(8,128)S(1)} %collective-permute-done.9.refs_4_), channel_id=1, source_target_pairs={{4,0},{8,12},{5,1},{9,13},{6,2},{10,14},{7,3},{11,15},{20,16},{24,... | collective-permute-start | bytes 1966088 | tf_op jit(solution)/shard_map/ppermute | solution.py:277
  73.4 16.9 %collective-permute-start.11 = (f32[16,10240]{1,0:T(8,128)S(1)}, f32[16,10240]{1,0:T(8,128)S(1)}, u32[]{:S(2)}, u32[]{:S(2)}) collective-permute-start(f32[16,10240]{1,0:T(8,128)S(1)} %collective-permute-done.8.refs_0_), channel_id=1, source_target_pairs={{4,8},{8,4},{5,9},{9,5},{6,10},{10,6},{7,11},{11,7},{20,24},{24,20... | collective-permute-start | bytes 1966088 | tf_op jit(solution)/shard_map/ppermute | solution.py:277
  78.9 18.6 %collective-permute-start.12 = (f32[16,10240]{1,0:T(8,128)S(1)}, f32[16,10240]{1,0:T(8,128)S(1)}, u32[]{:S(2)}, u32[]{:S(2)}) collective-permute-start(f32[16,10240]{1,0:T(8,128)S(1)} %get-tuple-element.106), channel_id=1, source_target_pairs={{0,4},{12,8},{1,5},{13,9},{2,6},{14,10},{3,7},{15,11},{16,20},{28,... | collective-permute-start | bytes 1966088 | tf_op jit(solution)/shard_map/ppermute | solution.py:317
  90.4 13.2 %collective-permute-start.13 = (f32[16,10240]{1,0:T(8,128)S(1)}, f32[16,10240]{1,0:T(8,128)S(1)}, u32[]{:S(2)}, u32[]{:S(2)}) collective-permute-start(f32[16,10240]{1,0:T(8,128)S(1)} %collective-permute-done.11.refs_2_), channel_id=1, source_target_pairs={{4,0},{8,12},{5,1},{9,13},{6,2},{10,14},{7,3},{11,15},{20,16},{24,... | collective-permute-start | bytes 1966088 | tf_op jit(solution)/shard_map/ppermute | solution.py:277
  91.7 23.3 %collective-permute-start.14 = (f32[16,10240]{1,0:T(8,128)S(1)}, f32[16,10240]{1,0:T(8,128)S(1)}, u32[]{:S(2)}, u32[]{:S(2)}) collective-permute-start(f32[16,10240]{1,0:T(8,128)S(1)} %get-tuple-element.110), channel_id=1, source_target_pairs={{0,4},{12,8},{1,5},{13,9},{2,6},{14,10},{3,7},{15,11},{16,20},{28,... | collective-permute-start | bytes 1966088 | tf_op jit(solution)/shard_map/ppermute | solution.py:317
  97.6 18.2 %collective-permute-start.15 = (f32[16,10240]{1,0:T(8,128)S(1)}, f32[16,10240]{1,0:T(8,128)S(1)}, u32[]{:S(2)}, u32[]{:S(2)}) collective-permute-start(f32[16,10240]{1,0:T(8,128)S(1)} %add.38), channel_id=1, source_target_pairs={{8,4},{4,8},{9,5},{5,9},{10,6},{6,10},{11,7},{7,11},{24,20},{20,24... | collective-permute-start | bytes 1966088 | tf_op jit(solution)/shard_map/ppermute | solution.py:317
  99.9 25.7 %collective-permute-start.16 = (f32[16,10240]{1,0:T(8,128)S(1)}, f32[16,10240]{1,0:T(8,128)S(1)}, u32[]{:S(2)}, u32[]{:S(2)}) collective-permute-start(f32[16,10240]{1,0:T(8,128)S(1)} %get-tuple-element.114), channel_id=1, source_target_pairs={{0,4},{12,8},{1,5},{13,9},{2,6},{14,10},{3,7},{15,11},{16,20},{28,... | collective-permute-start | bytes 1966088 | tf_op jit(solution)/shard_map/ppermute | solution.py:317
  111.7 15.4 %collective-permute-start.17 = (f32[4,16,192]{2,1,0:T(8,128)S(1)}, f32[4,16,192]{2,1,0:T(8,128)S(1)}, u32[]{:S(2)}, u32[]{:S(2)}) collective-permute-start(f32[4,16,192]{2,1,0:T(8,128)S(1)} %add_up.3.refs_0_), channel_id=1, source_target_pairs={{0,4},{4,0},{8,12},{12,8},{1,5},{5,1},{9,13},{13,9},{2,6},{6,2},{1... | collective-permute-start | bytes 147464 | tf_op jit(solution)/shard_map/ppermute | solution.py:341
  114.2 13.4 %collective-permute-start.18 = (f32[4,16,192]{2,1,0:T(8,128)S(1)}, f32[4,16,192]{2,1,0:T(8,128)S(1)}, u32[]{:S(2)}, u32[]{:S(2)}) collective-permute-start(f32[4,16,192]{2,1,0:T(8,128)S(1)} %add_up.3.refs_0_), channel_id=1, source_target_pairs={{0,8},{4,12},{8,0},{12,4},{1,9},{5,13},{9,1},{13,5},{2,10},{6,14},... | collective-permute-start | bytes 147464 | tf_op jit(solution)/shard_map/ppermute | solution.py:341
  115.0 12.6 %collective-permute-start.19 = (f32[4,16,192]{2,1,0:T(8,128)S(1)}, f32[4,16,192]{2,1,0:T(8,128)S(1)}, u32[]{:S(2)}, u32[]{:S(2)}) collective-permute-start(f32[4,16,192]{2,1,0:T(8,128)S(1)} %add_up.3.refs_0_), channel_id=1, source_target_pairs={{0,12},{4,8},{8,4},{12,0},{1,13},{5,9},{9,5},{13,1},{2,14},{6,10},... | collective-permute-start | bytes 147464 | tf_op jit(solution)/shard_map/ppermute | solution.py:341
  115.8 23.2 %collective-permute-start.21 = (f32[16,10240]{1,0:T(8,128)S(1)}, f32[16,10240]{1,0:T(8,128)S(1)}, u32[]{:S(2)}, u32[]{:S(2)}) collective-permute-start(f32[16,10240]{1,0:T(8,128)S(1)} %add.40), channel_id=1, source_target_pairs={{8,4},{4,8},{9,5},{5,9},{10,6},{6,10},{11,7},{7,11},{24,20},{20,24... | collective-permute-start | bytes 1966088 | tf_op jit(solution)/shard_map/ppermute | solution.py:317
  125.6 13.4 %collective-permute-start.20 = (f32[16,10240]{1,0:T(8,128)S(1)}, f32[16,10240]{1,0:T(8,128)S(1)}, u32[]{:S(2)}, u32[]{:S(2)}) collective-permute-start(f32[16,10240]{1,0:T(8,128)S(1)} %add.39), channel_id=1, source_target_pairs={{4,0},{8,12},{5,1},{9,13},{6,2},{10,14},{7,3},{11,15},{20,16},{24,... | collective-permute-start | bytes 1966088 | tf_op jit(solution)/shard_map/ppermute | solution.py:317
  130.0 19.6 %collective-permute-start.22 = (f32[16,10240]{1,0:T(8,128)S(1)}, f32[16,10240]{1,0:T(8,128)S(1)}, u32[]{:S(2)}, u32[]{:S(2)}) collective-permute-start(f32[16,10240]{1,0:T(8,128)S(1)} %get-tuple-element.133), channel_id=1, source_target_pairs={{0,4},{12,8},{1,5},{13,9},{2,6},{14,10},{3,7},{15,11},{16,20},{28,... | collective-permute-start | bytes 1966088 | tf_op jit(solution)/shard_map/ppermute | solution.py:317
  139.0 21.1 %collective-permute-start.25 = (f32[16,10240]{1,0:T(8,128)S(1)}, f32[16,10240]{1,0:T(8,128)S(1)}, u32[]{:S(2)}, u32[]{:S(2)}) collective-permute-start(f32[16,10240]{1,0:T(8,128)S(1)} %get-tuple-element.135), channel_id=1, source_target_pairs={{0,4},{12,8},{1,5},{13,9},{2,6},{14,10},{3,7},{15,11},{16,20},{28,... | collective-permute-start | bytes 1966088 | tf_op jit(solution)/shard_map/ppermute | solution.py:317
  149.7 13.7 %collective-permute-start.23 = (f32[16,10240]{1,0:T(8,128)S(1)}, f32[16,10240]{1,0:T(8,128)S(1)}, u32[]{:S(2)}, u32[]{:S(2)}) collective-permute-start(f32[16,10240]{1,0:T(8,128)S(1)} %add.41), channel_id=1, source_target_pairs={{8,4},{4,8},{9,5},{5,9},{10,6},{6,10},{11,7},{7,11},{24,20},{20,24... | collective-permute-start | bytes 1966088 | tf_op jit(solution)/shard_map/ppermute | solution.py:317
  160.2 16.0 %collective-permute-start.26 = (f32[16,10240]{1,0:T(8,128)S(1)}, f32[16,10240]{1,0:T(8,128)S(1)}, u32[]{:S(2)}, u32[]{:S(2)}) collective-permute-start(f32[16,10240]{1,0:T(8,128)S(1)} %add.43), channel_id=1, source_target_pairs={{8,4},{4,8},{9,5},{5,9},{10,6},{6,10},{11,7},{7,11},{24,20},{20,24... | collective-permute-start | bytes 1966088 | tf_op jit(solution)/shard_map/ppermute | solution.py:317
  163.5 13.1 %collective-permute-start.24 = (f32[16,10240]{1,0:T(8,128)S(1)}, f32[16,10240]{1,0:T(8,128)S(1)}, u32[]{:S(2)}, u32[]{:S(2)}) collective-permute-start(f32[16,10240]{1,0:T(8,128)S(1)} %add.42), channel_id=1, source_target_pairs={{0,4},{12,8},{4,0},{8,12},{1,5},{13,9},{5,1},{9,13},{2,6},{14,10},... | collective-permute-start | bytes 1966088 | tf_op jit(solution)/shard_map/ppermute | solution.py:317

commit v12 on v10

--- a/solution.py
+++ b/solution.py
@@ -338,7 +338,8 @@
 
 def exchange(value, length):
     if is_direct(length):
-        return [value] + [lax.ppermute(value, "tm", [(i, i ^ by) for i in range(length)]) for by in range(1, length)]
+        others = [lax.ppermute(value, "tm", [(i, i ^ by) for i in range(length)]) for by in range(length - 1, 0, -1)]
+        return [value] + others[::-1]
     gathered = lax.all_gather(value, "tm", axis=0)
     return [gathered[i] for i in range(length)]
 

time: 180 us -> 180 us (level)
  no operation moved by 1% of the time
where the time goes in v12:
time: 180 us; the launch traced here: 178 us
  waiting for transfers between devices  94.2 us (52%)
  starting transfers between devices  50 us (28%)
  Pallas kernels  16.4 us (9%)
  blocking collectives  11.6 us (6%)
  local copies, waits for them, and re-layouts  5.3 us (3%)
    ppermute x11, waiting for transfers between devices, send(): lax.ppermute(value, 'tm', pairs)  48.4 us
    ppermute x10, waiting for transfers between devices, send(): value = lax.ppermute(self.onward[1 - parity, step - 1], 'tm', pairs)  38.7 us
    ppermute x10, starting transfers between devices, send(): value = lax.ppermute(self.onward[1 - parity, step - 1], 'tm', pairs)  22.1 us
    ppermute x11, starting transfers between devices, send(): lax.ppermute(value, 'tm', pairs)  19.7 us
    all_gather x2, blocking collectives, summed(): return add_up(lax.all_gather(partial, 'param', axis=0))  11.6 us
    ppermute x6, starting transfers between devices, exchange(): lax.ppermute(value, 'tm', [(i, i ^ by) for i in range(length)])  8.23 us
    ppermute x6, waiting for transfers between devices, exchange(): lax.ppermute(value, 'tm', [(i, i ^ by) for i in range(length)])  6.99 us
    pallas_call x2, Pallas kernels, multiply(): pl.pallas_call(kernel, grid_spec=pltpu.PrefetchScalarGridSpec(num_scalar_...  4.82 us
  transfers between devices with their start and end apart: 27, of which 17 were waited for; matrix products, arithmetic and copies ran while one was open for 0% of the time, Pallas kernels for 8%

profile of v12, /device:TPU:8, one launch (start us, length us, event | category | flops | bytes accessed | tf_op | source)
XLA Modules:
  0.0 178.4 jit_solution(11729955347313920102)
XLA Ops:
  1.5 5.0 %collective-permute-start.1 = (f32[16,10240]{1,0:T(8,128)S(1)}, f32[16,10240]{1,0:T(8,128)S(1)}, u32[]{:S(2)}, u32[]{:S(2)}) collective-permute-start(f32[16,10240]{1,0:T(8,128)S(1)} %get-tuple-element.138), channel_id=1, source_target_pairs={{4,8},{8,4},{5,9},{9,5},{6,10},{10,6},{7,11},{11,7},{20,24},{24,20... | collective-permute-start | bytes 1966088 | tf_op jit(solution)/shard_map/ppermute | solution.py:277
  8.4 9.5 %collective-permute-done.refs_0_ = f32[16,10240]{1,0:T(8,128)S(1)} collective-permute-done((f32[16,10240]{1,0:T(8,128)S(1)}, f32[16,10240]{1,0:T(8,128)S(1)}, u32[]{:S(2)}, u32[]{:S(2)}) %collective-permute-start) | collective-permute-done | bytes 655392 | tf_op jit(solution)/shard_map/ppermute | solution.py:277
  17.9 3.5 %collective-permute-start.2 = (f32[16,10240]{1,0:T(8,128)S(1)}, f32[16,10240]{1,0:T(8,128)S(1)}, u32[]{:S(2)}, u32[]{:S(2)}) collective-permute-start(f32[16,10240]{1,0:T(8,128)S(1)} %collective-permute-done.refs_0_), channel_id=1, source_target_pairs={{4,8},{8,4},{5,9},{9,5},{6,10},{10,6},{7,11},{11,7},{20,24},{24,20... | collective-permute-start | bytes 1966088 | tf_op jit(solution)/shard_map/ppermute | solution.py:277
  22.8 12.7 %collective-permute-done.2.refs_2_ = f32[16,10240]{1,0:T(8,128)S(1)} collective-permute-done((f32[16,10240]{1,0:T(8,128)S(1)}, f32[16,10240]{1,0:T(8,128)S(1)}, u32[]{:S(2)}, u32[]{:S(2)}) %collective-permute-start.2) | collective-permute-done | bytes 655392 | tf_op jit(solution)/shard_map/ppermute | solution.py:277
  36.8 3.2 %copy-done.1 = f32[3,64,10240]{2,1,0:T(8,128)S(1)} copy-done((f32[3,64,10240]{2,1,0:T(8,128)S(1)}, f32[3,64,10240]{2,1,0:T(8,128)}, u32[]{:S(2)}) %copy-start.1) | copy-done | bytes 7864344
  40.0 4.3 %split_design.1 = (bf16[192,10240]{1,0:T(8,128)(2,1)S(1)}, bf16[192,10240]{1,0:T(8,128)(2,1)S(1)}, bf16[10240,192]{1,0:T(8,128)(2,1)S(1)}, bf16[10240,192]{1,0:T(8,128)(2,1)S(1)}) custom-call(f32[3,64,10240]{2,1,0:T(8,128)S(1)} %copy-done.1, f32[4,3,64,64]{3,2,1,0:T(8,128)S(1)} %normal_rows.1.refs_0_.taps_ref, s32[4]{0:T(128)S(1)} %get-tuple-element.77.refs_1_.shard_ref, ...), custom_call_target="tpu_custom_call" | custom-call | flops 1 | bytes 1 | tf_op jit(solution)/shard_map/split_design/pallas_call | solution.py:49
  44.3 3.5 %collective-permute-start.9 = (f32[16,10240]{1,0:T(8,128)S(1)}, f32[16,10240]{1,0:T(8,128)S(1)}, u32[]{:S(2)}, u32[]{:S(2)}) collective-permute-start(f32[16,10240]{1,0:T(8,128)S(1)} %get-tuple-element.87), channel_id=1, source_target_pairs={{4,8},{8,4},{5,9},{9,5},{6,10},{10,6},{7,11},{11,7},{20,24},{24,20... | collective-permute-start | bytes 1966088 | tf_op jit(solution)/shard_map/ppermute | solution.py:277
  47.8 4.0 %collective-permute-done.4.refs_3_ = f32[16,10240]{1,0:T(8,128)S(1)} collective-permute-done((f32[16,10240]{1,0:T(8,128)S(1)}, f32[16,10240]{1,0:T(8,128)S(1)}, u32[]{:S(2)}, u32[]{:S(2)}) %collective-permute-start.4) | collective-permute-done | bytes 655392 | tf_op jit(solution)/shard_map/ppermute | solution.py:277
  51.9 2.3 %project.2 = f32[4,16,192]{2,1,0:T(8,128)S(1)} custom-call(s32[4]{0:T(128)S(1)} %get-tuple-element.77.refs_1_.shard_ref, bf16[10240,192]{1,0:T(8,128)(2,1)S(1)} %get-tuple-element.82.high_ref, bf16[10240,192]{1,0:T(8,128)(2,1)S(1)} %get-tuple-element.83.low_ref, f32[32,10240]{1,0:T(8,128)S(1)} %bitcast.6, f32[16,10240]{1,0:T(8,128)S(1)} %collective-permute-done.refs_0_, ...), custom_call_target="tpu_custom_call" | custom-call | flops 1 | bytes 1 | tf_op jit(solution)/shard_map/project/pallas_call | solution.py:123
  54.2 5.8 %all-gather = f32[16,16,192]{2,1,0:T(8,128)S(1)} all-gather(f32[4,16,192]{2,1,0:T(8,128)S(1)} %project.2), channel_id=2, replica_groups=mesh['groups'=2,'tm'=4,'param'=4] {'param'}, dimensions={0}, use_global_device_ids=true | all-gather | bytes 245760 | tf_op jit(solution)/shard_map/all_gather | solution.py:362
  60.0 2.5 %collective-permute-start.5 = (f32[4,16,192]{2,1,0:T(8,128)S(1)}, f32[4,16,192]{2,1,0:T(8,128)S(1)}, u32[]{:S(2)}, u32[]{:S(2)}) collective-permute-start(f32[4,16,192]{2,1,0:T(8,128)S(1)} %add_up.2.refs_0_), channel_id=1, source_target_pairs={{0,4},{4,0},{8,12},{12,8},{1,5},{5,1},{9,13},{13,9},{2,6},{6,2},{1... | collective-permute-start | bytes 147464 | tf_op jit(solution)/shard_map/ppermute | solution.py:341
  64.2 2.3 %collective-permute-done.5.refs_1_ = f32[4,16,192]{2,1,0:T(8,128)S(1)} collective-permute-done((f32[4,16,192]{2,1,0:T(8,128)S(1)}, f32[4,16,192]{2,1,0:T(8,128)S(1)}, u32[]{:S(2)}, u32[]{:S(2)}) %collective-permute-start.5) | collective-permute-done | bytes 49184 | tf_op jit(solution)/shard_map/ppermute | solution.py:341
  66.5 2.3 %collective-permute-done.6.refs_2_ = f32[4,16,192]{2,1,0:T(8,128)S(1)} collective-permute-done((f32[4,16,192]{2,1,0:T(8,128)S(1)}, f32[4,16,192]{2,1,0:T(8,128)S(1)}, u32[]{:S(2)}, u32[]{:S(2)}) %collective-permute-start.6) | collective-permute-done | bytes 49184 | tf_op jit(solution)/shard_map/ppermute | solution.py:341
  70.7 2.9 %collective-permute-start.10 = (f32[16,10240]{1,0:T(8,128)S(1)}, f32[16,10240]{1,0:T(8,128)S(1)}, u32[]{:S(2)}, u32[]{:S(2)}) collective-permute-start(f32[16,10240]{1,0:T(8,128)S(1)} %collective-permute-done.9.refs_4_), channel_id=1, source_target_pairs={{4,0},{8,12},{5,1},{9,13},{6,2},{10,14},{7,3},{11,15},{20,16},{24,... | collective-permute-start | bytes 1966088 | tf_op jit(solution)/shard_map/ppermute | solution.py:277
  73.7 3.0 %collective-permute-start.11 = (f32[16,10240]{1,0:T(8,128)S(1)}, f32[16,10240]{1,0:T(8,128)S(1)}, u32[]{:S(2)}, u32[]{:S(2)}) collective-permute-start(f32[16,10240]{1,0:T(8,128)S(1)} %collective-permute-done.8.refs_0_), channel_id=1, source_target_pairs={{4,8},{8,4},{5,9},{9,5},{6,10},{10,6},{7,11},{11,7},{20,24},{24,20... | collective-permute-start | bytes 1966088 | tf_op jit(solution)/shard_map/ppermute | solution.py:277
  76.7 2.4 %multiply.2 = (f32[16,10240]{1,0:T(8,128)S(1)}, f32[16,10240]{1,0:T(8,128)S(1)}, f32[16,10240]{1,0:T(8,128)S(1)}, f32[16,10240]{1,0:T(8,128)S(1)}) custom-call(s32[4]{0:T(128)S(1)} %get-tuple-element.77.refs_1_.shard_ref, s32[4]{0:T(128)S(1)} %get-tuple-element.78.refs_2_.place_ref, bf16[192,10240]{1,0:T(8,128)(2,1)S(1)} %get-tuple-element.90.high_ref, ...), custom_call_target="tpu_custom_call" | custom-call | flops 1 | bytes 1 | tf_op jit(solution)/shard_map/multiply/pallas_call | solution.py:172
  80.4 6.0 %collective-permute-done.10.refs_1_ = f32[16,10240]{1,0:T(8,128)S(1)} collective-permute-done((f32[16,10240]{1,0:T(8,128)S(1)}, f32[16,10240]{1,0:T(8,128)S(1)}, u32[]{:S(2)}, u32[]{:S(2)}) %collective-permute-start.10) | collective-permute-done | bytes 655392 | tf_op jit(solution)/shard_map/ppermute | solution.py:277
  86.5 4.2 %collective-permute-done.11.refs_2_ = f32[16,10240]{1,0:T(8,128)S(1)} collective-permute-done((f32[16,10240]{1,0:T(8,128)S(1)}, f32[16,10240]{1,0:T(8,128)S(1)}, u32[]{:S(2)}, u32[]{:S(2)}) %collective-permute-start.11) | collective-permute-done | bytes 655392 | tf_op jit(solution)/shard_map/ppermute | solution.py:277
  93.3 4.6 %collective-permute-done.12 = f32[16,10240]{1,0:T(8,128)S(1)} collective-permute-done((f32[16,10240]{1,0:T(8,128)S(1)}, f32[16,10240]{1,0:T(8,128)S(1)}, u32[]{:S(2)}, u32[]{:S(2)}) %collective-permute-start.12) | collective-permute-done | bytes 655392 | tf_op jit(solution)/shard_map/ppermute | solution.py:317
  101.4 2.4 %collective-permute-done.13.refs_3_ = f32[16,10240]{1,0:T(8,128)S(1)} collective-permute-done((f32[16,10240]{1,0:T(8,128)S(1)}, f32[16,10240]{1,0:T(8,128)S(1)}, u32[]{:S(2)}, u32[]{:S(2)}) %collective-permute-start.13) | collective-permute-done | bytes 655392 | tf_op jit(solution)/shard_map/ppermute | solution.py:277
  103.8 2.3 %project.3 = f32[4,16,192]{2,1,0:T(8,128)S(1)} custom-call(s32[4]{0:T(128)S(1)} %get-tuple-element.77.refs_1_.shard_ref, bf16[10240,192]{1,0:T(8,128)(2,1)S(1)} %get-tuple-element.82.high_ref, bf16[10240,192]{1,0:T(8,128)(2,1)S(1)} %get-tuple-element.83.low_ref, f32[32,10240]{1,0:T(8,128)S(1)} %bitcast.7, f32[16,10240]{1,0:T(8,128)S(1)} %collective-permute-done.8.refs_0_, ...), custom_call_target="tpu_custom_call" | custom-call | flops 1 | bytes 1 | tf_op jit(solution)/shard_map/project/pallas_call | solution.py:123
  106.1 5.8 %all-gather.1 = f32[16,16,192]{2,1,0:T(8,128)S(1)} all-gather(f32[4,16,192]{2,1,0:T(8,128)S(1)} %project.3), channel_id=3, replica_groups=mesh['groups'=2,'tm'=4,'param'=4] {'param'}, dimensions={0}, use_global_device_ids=true | all-gather | bytes 245760 | tf_op jit(solution)/shard_map/all_gather | solution.py:362
  111.9 2.6 %collective-permute-start.17 = (f32[4,16,192]{2,1,0:T(8,128)S(1)}, f32[4,16,192]{2,1,0:T(8,128)S(1)}, u32[]{:S(2)}, u32[]{:S(2)}) collective-permute-start(f32[4,16,192]{2,1,0:T(8,128)S(1)} %add_up.3.refs_0_), channel_id=1, source_target_pairs={{0,4},{4,0},{8,12},{12,8},{1,5},{5,1},{9,13},{13,9},{2,6},{6,2},{1... | collective-permute-start | bytes 147464 | tf_op jit(solution)/shard_map/ppermute | solution.py:341
  116.1 3.2 %collective-permute-start.21 = (f32[16,10240]{1,0:T(8,128)S(1)}, f32[16,10240]{1,0:T(8,128)S(1)}, u32[]{:S(2)}, u32[]{:S(2)}) collective-permute-start(f32[16,10240]{1,0:T(8,128)S(1)} %add.40), channel_id=1, source_target_pairs={{8,4},{4,8},{9,5},{5,9},{10,6},{6,10},{11,7},{7,11},{24,20},{20,24... | collective-permute-start | bytes 1966088 | tf_op jit(solution)/shard_map/ppermute | solution.py:317
  119.4 6.5 %collective-permute-done.16.refs_1_ = f32[16,10240]{1,0:T(8,128)S(1)} collective-permute-done((f32[16,10240]{1,0:T(8,128)S(1)}, f32[16,10240]{1,0:T(8,128)S(1)}, u32[]{:S(2)}, u32[]{:S(2)}) %collective-permute-start.16) | collective-permute-done | bytes 655392 | tf_op jit(solution)/shard_map/ppermute | solution.py:317
  127.9 2.4 %multiply.3 = (f32[16,10240]{1,0:T(8,128)S(1)}, f32[16,10240]{1,0:T(8,128)S(1)}, f32[16,10240]{1,0:T(8,128)S(1)}, f32[16,10240]{1,0:T(8,128)S(1)}) custom-call(s32[4]{0:T(128)S(1)} %get-tuple-element.77.refs_1_.shard_ref, s32[4]{0:T(128)S(1)} %get-tuple-element.78.refs_2_.place_ref, bf16[192,10240]{1,0:T(8,128)(2,1)S(1)} %get-tuple-element.90.high_ref, ...), custom_call_target="tpu_custom_call" | custom-call | flops 1 | bytes 1 | tf_op jit(solution)/shard_map/multiply/pallas_call | solution.py:172
  131.6 7.7 %collective-permute-done.20.refs_2_ = f32[16,10240]{1,0:T(8,128)S(1)} collective-permute-done((f32[16,10240]{1,0:T(8,128)S(1)}, f32[16,10240]{1,0:T(8,128)S(1)}, u32[]{:S(2)}, u32[]{:S(2)}) %collective-permute-start.20) | collective-permute-done | bytes 655392 | tf_op jit(solution)/shard_map/ppermute | solution.py:317
  140.6 9.2 %collective-permute-done.22 = f32[16,10240]{1,0:T(8,128)S(1)} collective-permute-done((f32[16,10240]{1,0:T(8,128)S(1)}, f32[16,10240]{1,0:T(8,128)S(1)}, u32[]{:S(2)}, u32[]{:S(2)}) %collective-permute-start.22) | collective-permute-done | bytes 655392 | tf_op jit(solution)/shard_map/ppermute | solution.py:317
  149.9 3.1 %collective-permute-start.23 = (f32[16,10240]{1,0:T(8,128)S(1)}, f32[16,10240]{1,0:T(8,128)S(1)}, u32[]{:S(2)}, u32[]{:S(2)}) collective-permute-start(f32[16,10240]{1,0:T(8,128)S(1)} %add.41), channel_id=1, source_target_pairs={{8,4},{4,8},{9,5},{5,9},{10,6},{6,10},{11,7},{7,11},{24,20},{20,24... | collective-permute-start | bytes 1966088 | tf_op jit(solution)/shard_map/ppermute | solution.py:317
  153.1 7.3 %collective-permute-done.25 = f32[16,10240]{1,0:T(8,128)S(1)} collective-permute-done((f32[16,10240]{1,0:T(8,128)S(1)}, f32[16,10240]{1,0:T(8,128)S(1)}, u32[]{:S(2)}, u32[]{:S(2)}) %collective-permute-start.25) | collective-permute-done | bytes 655392 | tf_op jit(solution)/shard_map/ppermute | solution.py:317
  160.5 3.2 %collective-permute-start.26 = (f32[16,10240]{1,0:T(8,128)S(1)}, f32[16,10240]{1,0:T(8,128)S(1)}, u32[]{:S(2)}, u32[]{:S(2)}) collective-permute-start(f32[16,10240]{1,0:T(8,128)S(1)} %add.43), channel_id=1, source_target_pairs={{8,4},{4,8},{9,5},{5,9},{10,6},{6,10},{11,7},{7,11},{24,20},{20,24... | collective-permute-start | bytes 1966088 | tf_op jit(solution)/shard_map/ppermute | solution.py:317
  163.9 12.6 %collective-permute-done.26.refs_6_ = f32[16,10240]{1,0:T(8,128)S(1)} collective-permute-done((f32[16,10240]{1,0:T(8,128)S(1)}, f32[16,10240]{1,0:T(8,128)S(1)}, u32[]{:S(2)}, u32[]{:S(2)}) %collective-permute-start.26) | collective-permute-done | bytes 655392 | tf_op jit(solution)/shard_map/ppermute | solution.py:317
  (56 shorter events, 25.6 us)
Async XLA Ops:
  1.4 16.5 %collective-permute-start = (f32[16,10240]{1,0:T(8,128)S(1)}, f32[16,10240]{1,0:T(8,128)S(1)}, u32[]{:S(2)}, u32[]{:S(2)}) collective-permute-start(f32[16,10240]{1,0:T(8,128)S(1)} %get-tuple-element.138), channel_id=1, source_target_pairs={{0,4},{12,8},{4,0},{8,12},{1,5},{13,9},{5,1},{9,13},{2,6},{14,10},... | collective-permute-start | bytes 1966088 | tf_op jit(solution)/shard_map/ppermute | solution.py:277
  1.5 19.9 %collective-permute-start.1 = (f32[16,10240]{1,0:T(8,128)S(1)}, f32[16,10240]{1,0:T(8,128)S(1)}, u32[]{:S(2)}, u32[]{:S(2)}) collective-permute-start(f32[16,10240]{1,0:T(8,128)S(1)} %get-tuple-element.138), channel_id=1, source_target_pairs={{4,8},{8,4},{5,9},{9,5},{6,10},{10,6},{7,11},{11,7},{20,24},{24,20... | collective-permute-start | bytes 1966088 | tf_op jit(solution)/shard_map/ppermute | solution.py:277
  6.5 0.7 copy-start.2
  17.9 17.5 %collective-permute-start.2 = (f32[16,10240]{1,0:T(8,128)S(1)}, f32[16,10240]{1,0:T(8,128)S(1)}, u32[]{:S(2)}, u32[]{:S(2)}) collective-permute-start(f32[16,10240]{1,0:T(8,128)S(1)} %collective-permute-done.refs_0_), channel_id=1, source_target_pairs={{4,8},{8,4},{5,9},{9,5},{6,10},{10,6},{7,11},{11,7},{20,24},{24,20... | collective-permute-start | bytes 1966088 | tf_op jit(solution)/shard_map/ppermute | solution.py:277
  21.4 26.4 %collective-permute-start.3 = (f32[16,10240]{1,0:T(8,128)S(1)}, f32[16,10240]{1,0:T(8,128)S(1)}, u32[]{:S(2)}, u32[]{:S(2)}) collective-permute-start(f32[16,10240]{1,0:T(8,128)S(1)} %collective-permute-done.1.refs_4_), channel_id=1, source_target_pairs={{4,0},{8,12},{5,1},{9,13},{6,2},{10,14},{7,3},{11,15},{20,16},{24,... | collective-permute-start | bytes 1966088 | tf_op jit(solution)/shard_map/ppermute | solution.py:277
  35.4 16.5 %collective-permute-start.4 = (f32[16,10240]{1,0:T(8,128)S(1)}, f32[16,10240]{1,0:T(8,128)S(1)}, u32[]{:S(2)}, u32[]{:S(2)}) collective-permute-start(f32[16,10240]{1,0:T(8,128)S(1)} %collective-permute-done.2.refs_2_), channel_id=1, source_target_pairs={{4,0},{8,12},{5,1},{9,13},{6,2},{10,14},{7,3},{11,15},{20,16},{24,... | collective-permute-start | bytes 1966088 | tf_op jit(solution)/shard_map/ppermute | solution.py:277
  36.8 3.2 %copy-start.1 = (f32[3,64,10240]{2,1,0:T(8,128)S(1)}, f32[3,64,10240]{2,1,0:T(8,128)}, u32[]{:S(2)}) copy-start(f32[3,64,10240]{2,1,0:T(8,128)} %design_ref.1) | copy-start | bytes 23592964
  40.0 11.9 %copy-start = (f32[10240,32]{0,1:T(8,128)S(1)}, f32[10240,32]{0,1:T(8,128)}, u32[]{:S(2)}) copy-start(f32[10240,32]{0,1:T(8,128)} %param.5) | copy-start | bytes 3932164
  44.3 26.5 %collective-permute-start.8 = (f32[16,10240]{1,0:T(8,128)S(1)}, f32[16,10240]{1,0:T(8,128)S(1)}, u32[]{:S(2)}, u32[]{:S(2)}) collective-permute-start(f32[16,10240]{1,0:T(8,128)S(1)} %get-tuple-element.87), channel_id=1, source_target_pairs={{0,4},{12,8},{4,0},{8,12},{1,5},{13,9},{5,1},{9,13},{2,6},{14,10},... | collective-permute-start | bytes 1966088 | tf_op jit(solution)/shard_map/ppermute | solution.py:277
  44.3 26.4 %collective-permute-start.9 = (f32[16,10240]{1,0:T(8,128)S(1)}, f32[16,10240]{1,0:T(8,128)S(1)}, u32[]{:S(2)}, u32[]{:S(2)}) collective-permute-start(f32[16,10240]{1,0:T(8,128)S(1)} %get-tuple-element.87), channel_id=1, source_target_pairs={{4,8},{8,4},{5,9},{9,5},{6,10},{10,6},{7,11},{11,7},{20,24},{24,20... | collective-permute-start | bytes 1966088 | tf_op jit(solution)/shard_map/ppermute | solution.py:277
  60.0 6.5 %collective-permute-start.5 = (f32[4,16,192]{2,1,0:T(8,128)S(1)}, f32[4,16,192]{2,1,0:T(8,128)S(1)}, u32[]{:S(2)}, u32[]{:S(2)}) collective-permute-start(f32[4,16,192]{2,1,0:T(8,128)S(1)} %add_up.2.refs_0_), channel_id=1, source_target_pairs={{0,4},{4,0},{8,12},{12,8},{1,5},{5,1},{9,13},{13,9},{2,6},{6,2},{1... | collective-permute-start | bytes 147464 | tf_op jit(solution)/shard_map/ppermute | solution.py:341
  62.6 6.2 %collective-permute-start.6 = (f32[4,16,192]{2,1,0:T(8,128)S(1)}, f32[4,16,192]{2,1,0:T(8,128)S(1)}, u32[]{:S(2)}, u32[]{:S(2)}) collective-permute-start(f32[4,16,192]{2,1,0:T(8,128)S(1)} %add_up.2.refs_0_), channel_id=1, source_target_pairs={{0,8},{4,12},{8,0},{12,4},{1,9},{5,13},{9,1},{13,5},{2,10},{6,14},... | collective-permute-start | bytes 147464 | tf_op jit(solution)/shard_map/ppermute | solution.py:341
  63.7 7.1 %collective-permute-start.7 = (f32[4,16,192]{2,1,0:T(8,128)S(1)}, f32[4,16,192]{2,1,0:T(8,128)S(1)}, u32[]{:S(2)}, u32[]{:S(2)}) collective-permute-start(f32[4,16,192]{2,1,0:T(8,128)S(1)} %add_up.2.refs_0_), channel_id=1, source_target_pairs={{0,12},{4,8},{8,4},{12,0},{1,13},{5,9},{9,5},{13,1},{2,14},{6,10},... | collective-permute-start | bytes 147464 | tf_op jit(solution)/shard_map/ppermute | solution.py:341
  70.7 15.7 %collective-permute-start.10 = (f32[16,10240]{1,0:T(8,128)S(1)}, f32[16,10240]{1,0:T(8,128)S(1)}, u32[]{:S(2)}, u32[]{:S(2)}) collective-permute-start(f32[16,10240]{1,0:T(8,128)S(1)} %collective-permute-done.9.refs_4_), channel_id=1, source_target_pairs={{4,0},{8,12},{5,1},{9,13},{6,2},{10,14},{7,3},{11,15},{20,16},{24,... | collective-permute-start | bytes 1966088 | tf_op jit(solution)/shard_map/ppermute | solution.py:277
  73.7 16.9 %collective-permute-start.11 = (f32[16,10240]{1,0:T(8,128)S(1)}, f32[16,10240]{1,0:T(8,128)S(1)}, u32[]{:S(2)}, u32[]{:S(2)}) collective-permute-start(f32[16,10240]{1,0:T(8,128)S(1)} %collective-permute-done.8.refs_0_), channel_id=1, source_target_pairs={{4,8},{8,4},{5,9},{9,5},{6,10},{10,6},{7,11},{11,7},{20,24},{24,20... | collective-permute-start | bytes 1966088 | tf_op jit(solution)/shard_map/ppermute | solution.py:277
  79.1 18.7 %collective-permute-start.12 = (f32[16,10240]{1,0:T(8,128)S(1)}, f32[16,10240]{1,0:T(8,128)S(1)}, u32[]{:S(2)}, u32[]{:S(2)}) collective-permute-start(f32[16,10240]{1,0:T(8,128)S(1)} %get-tuple-element.106), channel_id=1, source_target_pairs={{0,4},{12,8},{1,5},{13,9},{2,6},{14,10},{3,7},{15,11},{16,20},{28,... | collective-permute-start | bytes 1966088 | tf_op jit(solution)/shard_map/ppermute | solution.py:317
  90.6 13.2 %collective-permute-start.13 = (f32[16,10240]{1,0:T(8,128)S(1)}, f32[16,10240]{1,0:T(8,128)S(1)}, u32[]{:S(2)}, u32[]{:S(2)}) collective-permute-start(f32[16,10240]{1,0:T(8,128)S(1)} %collective-permute-done.11.refs_2_), channel_id=1, source_target_pairs={{4,0},{8,12},{5,1},{9,13},{6,2},{10,14},{7,3},{11,15},{20,16},{24,... | collective-permute-start | bytes 1966088 | tf_op jit(solution)/shard_map/ppermute | solution.py:277
  91.9 23.3 %collective-permute-start.14 = (f32[16,10240]{1,0:T(8,128)S(1)}, f32[16,10240]{1,0:T(8,128)S(1)}, u32[]{:S(2)}, u32[]{:S(2)}) collective-permute-start(f32[16,10240]{1,0:T(8,128)S(1)} %get-tuple-element.110), channel_id=1, source_target_pairs={{0,4},{12,8},{1,5},{13,9},{2,6},{14,10},{3,7},{15,11},{16,20},{28,... | collective-permute-start | bytes 1966088 | tf_op jit(solution)/shard_map/ppermute | solution.py:317
  97.9 18.2 %collective-permute-start.15 = (f32[16,10240]{1,0:T(8,128)S(1)}, f32[16,10240]{1,0:T(8,128)S(1)}, u32[]{:S(2)}, u32[]{:S(2)}) collective-permute-start(f32[16,10240]{1,0:T(8,128)S(1)} %add.38), channel_id=1, source_target_pairs={{8,4},{4,8},{9,5},{5,9},{10,6},{6,10},{11,7},{7,11},{24,20},{20,24... | collective-permute-start | bytes 1966088 | tf_op jit(solution)/shard_map/ppermute | solution.py:317
  100.1 25.8 %collective-permute-start.16 = (f32[16,10240]{1,0:T(8,128)S(1)}, f32[16,10240]{1,0:T(8,128)S(1)}, u32[]{:S(2)}, u32[]{:S(2)}) collective-permute-start(f32[16,10240]{1,0:T(8,128)S(1)} %get-tuple-element.114), channel_id=1, source_target_pairs={{0,4},{12,8},{1,5},{13,9},{2,6},{14,10},{3,7},{15,11},{16,20},{28,... | collective-permute-start | bytes 1966088 | tf_op jit(solution)/shard_map/ppermute | solution.py:317
  111.9 15.5 %collective-permute-start.17 = (f32[4,16,192]{2,1,0:T(8,128)S(1)}, f32[4,16,192]{2,1,0:T(8,128)S(1)}, u32[]{:S(2)}, u32[]{:S(2)}) collective-permute-start(f32[4,16,192]{2,1,0:T(8,128)S(1)} %add_up.3.refs_0_), channel_id=1, source_target_pairs={{0,4},{4,0},{8,12},{12,8},{1,5},{5,1},{9,13},{13,9},{2,6},{6,2},{1... | collective-permute-start | bytes 147464 | tf_op jit(solution)/shard_map/ppermute | solution.py:341
  114.5 13.4 %collective-permute-start.18 = (f32[4,16,192]{2,1,0:T(8,128)S(1)}, f32[4,16,192]{2,1,0:T(8,128)S(1)}, u32[]{:S(2)}, u32[]{:S(2)}) collective-permute-start(f32[4,16,192]{2,1,0:T(8,128)S(1)} %add_up.3.refs_0_), channel_id=1, source_target_pairs={{0,8},{4,12},{8,0},{12,4},{1,9},{5,13},{9,1},{13,5},{2,10},{6,14},... | collective-permute-start | bytes 147464 | tf_op jit(solution)/shard_map/ppermute | solution.py:341
  115.3 12.6 %collective-permute-start.19 = (f32[4,16,192]{2,1,0:T(8,128)S(1)}, f32[4,16,192]{2,1,0:T(8,128)S(1)}, u32[]{:S(2)}, u32[]{:S(2)}) collective-permute-start(f32[4,16,192]{2,1,0:T(8,128)S(1)} %add_up.3.refs_0_), channel_id=1, source_target_pairs={{0,12},{4,8},{8,4},{12,0},{1,13},{5,9},{9,5},{13,1},{2,14},{6,10},... | collective-permute-start | bytes 147464 | tf_op jit(solution)/shard_map/ppermute | solution.py:341
  116.1 23.2 %collective-permute-start.21 = (f32[16,10240]{1,0:T(8,128)S(1)}, f32[16,10240]{1,0:T(8,128)S(1)}, u32[]{:S(2)}, u32[]{:S(2)}) collective-permute-start(f32[16,10240]{1,0:T(8,128)S(1)} %add.40), channel_id=1, source_target_pairs={{8,4},{4,8},{9,5},{5,9},{10,6},{6,10},{11,7},{7,11},{24,20},{20,24... | collective-permute-start | bytes 1966088 | tf_op jit(solution)/shard_map/ppermute | solution.py:317
  125.9 13.4 %collective-permute-start.20 = (f32[16,10240]{1,0:T(8,128)S(1)}, f32[16,10240]{1,0:T(8,128)S(1)}, u32[]{:S(2)}, u32[]{:S(2)}) collective-permute-start(f32[16,10240]{1,0:T(8,128)S(1)} %add.39), channel_id=1, source_target_pairs={{4,0},{8,12},{5,1},{9,13},{6,2},{10,14},{7,3},{11,15},{20,16},{24,... | collective-permute-start | bytes 1966088 | tf_op jit(solution)/shard_map/ppermute | solution.py:317
  130.3 19.6 %collective-permute-start.22 = (f32[16,10240]{1,0:T(8,128)S(1)}, f32[16,10240]{1,0:T(8,128)S(1)}, u32[]{:S(2)}, u32[]{:S(2)}) collective-permute-start(f32[16,10240]{1,0:T(8,128)S(1)} %get-tuple-element.133), channel_id=1, source_target_pairs={{0,4},{12,8},{1,5},{13,9},{2,6},{14,10},{3,7},{15,11},{16,20},{28,... | collective-permute-start | bytes 1966088 | tf_op jit(solution)/shard_map/ppermute | solution.py:317
  139.3 21.1 %collective-permute-start.25 = (f32[16,10240]{1,0:T(8,128)S(1)}, f32[16,10240]{1,0:T(8,128)S(1)}, u32[]{:S(2)}, u32[]{:S(2)}) collective-permute-start(f32[16,10240]{1,0:T(8,128)S(1)} %get-tuple-element.135), channel_id=1, source_target_pairs={{0,4},{12,8},{1,5},{13,9},{2,6},{14,10},{3,7},{15,11},{16,20},{28,... | collective-permute-start | bytes 1966088 | tf_op jit(solution)/shard_map/ppermute | solution.py:317
  149.9 13.8 %collective-permute-start.23 = (f32[16,10240]{1,0:T(8,128)S(1)}, f32[16,10240]{1,0:T(8,128)S(1)}, u32[]{:S(2)}, u32[]{:S(2)}) collective-permute-start(f32[16,10240]{1,0:T(8,128)S(1)} %add.41), channel_id=1, source_target_pairs={{8,4},{4,8},{9,5},{5,9},{10,6},{6,10},{11,7},{7,11},{24,20},{20,24... | collective-permute-start | bytes 1966088 | tf_op jit(solution)/shard_map/ppermute | solution.py:317
  160.5 16.0 %collective-permute-start.26 = (f32[16,10240]{1,0:T(8,128)S(1)}, f32[16,10240]{1,0:T(8,128)S(1)}, u32[]{:S(2)}, u32[]{:S(2)}) collective-permute-start(f32[16,10240]{1,0:T(8,128)S(1)} %add.43), channel_id=1, source_target_pairs={{8,4},{4,8},{9,5},{5,9},{10,6},{6,10},{11,7},{7,11},{24,20},{20,24... | collective-permute-start | bytes 1966088 | tf_op jit(solution)/shard_map/ppermute | solution.py:317
  163.8 13.1 %collective-permute-start.24 = (f32[16,10240]{1,0:T(8,128)S(1)}, f32[16,10240]{1,0:T(8,128)S(1)}, u32[]{:S(2)}, u32[]{:S(2)}) collective-permute-start(f32[16,10240]{1,0:T(8,128)S(1)} %add.42), channel_id=1, source_target_pairs={{0,4},{12,8},{4,0},{8,12},{1,5},{13,9},{5,1},{9,13},{2,6},{14,10},... | collective-permute-start | bytes 1966088 | tf_op jit(solution)/shard_map/ppermute | solution.py:317
